TPU v7x, 32 devices: a whole 2x2x4 slice. The times are simulated.
32 devices in a mesh: req: 8 (over z, x), tp: 4 (over y, core).
Axes of the slice: x: 2, y: 2, z: 4, core: 2. Of those that a mesh axis runs over, the one named last changes fastest.
Arguments:
- tokens: bfloat16 [4096, 1024], P('req', 'tp'), may hold values from -17.5 to 17.5
- prompt_lengths: int32 [64, 4], P('req'), may hold values from 1 to 32, 64 in all within a row
- adapter_ids: int32 [64, 4], P('req'), may hold values from 0 to 15, as said below
- adapter_slot: int32 [16], replicated, may hold values from 0 to 15, as said below
- w_qkv: bfloat16 [3, 1024, 1024], P(None, None, 'tp'), may hold values from -0.1875 to 0.1875
- w_out: bfloat16 [1024, 1024], P('tp'), may hold values from -0.1875 to 0.1875
- w_fc1: bfloat16 [1024, 4096], P(None, 'tp'), may hold values from -0.1875 to 0.1875
- w_fc2: bfloat16 [4096, 1024], P('tp'), may hold values from -0.09375 to 0.09375
- qkv_down: bfloat16 [3, 1024, 256], P(None, None, 'req'), may hold values from -0.1875 to 0.1875
- qkv_up: bfloat16 [3, 256, 1024], P(None, 'req', 'tp'), may hold values from -0.75 to 0.75
- out_down: bfloat16 [1024, 256], P('tp', 'req'), may hold values from -0.1875 to 0.1875
- out_up: bfloat16 [256, 1024], P('req'), may hold values from -0.75 to 0.75
- fc1_down: bfloat16 [1024, 256], P(None, 'req'), may hold values from -0.1875 to 0.1875
- fc1_up: bfloat16 [256, 4096], P('req', 'tp'), may hold values from -0.75 to 0.75
- fc2_down: bfloat16 [4096, 256], P('tp', 'req'), may hold values from -0.09375 to 0.09375
- fc2_up: bfloat16 [256, 1024], P('req'), may hold values from -0.75 to 0.75
- norm1_gain: float32 [1024], replicated, may hold values from 0.5 to 1.5
- norm1_bias: float32 [1024], replicated, may hold values from -1.75 to 1.75
- norm2_gain: float32 [1024], replicated, may hold values from 0.5 to 1.5
- norm2_bias: float32 [1024], replicated, may hold values from -1.75 to 1.75
Outputs:
- layer_out: bfloat16 [4096, 1024], P('req', 'tp')
Inputs may be any that keep to these rules, and one draw needn't show every extreme that they name: `prompt_lengths`: each row sums to 64, and its longest request has exactly 32 tokens. A permutation: adapter i is stored in slot adapter_slot[i] of the adapter arrays, and slot s lies on index s // 2 of req (its owner). `adapter_ids`: all requests of one block use adapters of one owner; the 8 blocks of one index of req use 8 different owners; the first block of every index of req uses one common owner.
All inputs are finite; a program needn't handle non-finite values.
Results may differ from a plain program's by a relative error of at most 0.015.
The roundings to bfloat16 on the way count: a program that leaves them out, or rounds other values in their place, can miss the bound.
Values may be sent and summed in bfloat16 or wider, within the bound.
No kernel may reach another device: no remote copies, remote signals or barrier semaphores. Data moves between devices by JAX's collectives and lax.ppermute only.
A program may use at most 64 MiB of HBM per device.

v0:
```python
import jax
import jax.numpy as jnp
from jax import lax
from jax.sharding import PartitionSpec as P

HEAD_DIM = 64
RANK = 16
ADAPT_DEV = 2
CAP = 64
SEQ_G = 4


norm_eps = 1e-05


def layer_norm(values, gain_vec, shift_vec):
    row_mean = jnp.mean(values, axis=-1, keepdims=True)
    centred = values - row_mean
    variance = jnp.mean(centred * centred, axis=-1, keepdims=True)
    return centred * lax.rsqrt(variance + norm_eps) * gain_vec + shift_vec


def block_codes(prompt_lengths, adapter_ids, adapter_slot):
    id_table = jnp.arange(adapter_slot.shape[0], dtype=jnp.int32)
    slot_of_req = jnp.sum(jnp.where(adapter_ids[..., None] == id_table, adapter_slot, 0), axis=-1)
    owner_of = slot_of_req[..., 0] // ADAPT_DEV
    local_pick = slot_of_req % ADAPT_DEV
    request_end = jnp.cumsum(prompt_lengths, axis=-1)
    position = jnp.arange(CAP, dtype=jnp.int32)
    segment = jnp.sum((position[:, None] >= request_end[..., None, :]).astype(jnp.int32), axis=-1)
    chosen = segment[..., None] == jnp.arange(SEQ_G, dtype=jnp.int32)
    row_local = jnp.sum(jnp.where(chosen, local_pick[..., None, :], 0), axis=-1)
    return (owner_of, 1 + segment * ADAPT_DEV + row_local)


def body(
    tokens,
    prompt_lengths,
    adapter_ids,
    adapter_slot,
    w_qkv,
    w_out,
    w_fc1,
    w_fc2,
    qkv_down,
    qkv_up,
    out_down,
    out_up,
    fc1_down,
    fc1_up,
    fc2_down,
    fc2_up,
    norm1_gain,
    norm1_bias,
    norm2_gain,
    norm2_bias,
):
    highest = lax.Precision.HIGHEST
    owner_count = lax.axis_size("req")
    tensor_count = lax.axis_size("tp")
    share_rows = CAP // tensor_count
    owner_of, row_codes = block_codes(prompt_lengths, adapter_ids, adapter_slot)
    blocks = owner_of.shape[0]
    onehot = owner_of[:, None] == jnp.arange(owner_count, dtype=jnp.int32)[None, :]
    routing = onehot.astype(jnp.bfloat16)
    sent_codes = jnp.sum(jnp.where(onehot[:, None, :], row_codes[:, :, None], 0), axis=0)
    outgoing = jnp.einsum(
        "gcf,gn->cnf", tokens.reshape(blocks, CAP, -1), routing, preferred_element_type=jnp.float32
    ).astype(jnp.bfloat16)
    pieces, arrived_codes = (
        lax.all_to_all(outgoing, "req", split_axis=1, concat_axis=1, tiled=True),
        lax.all_to_all(sent_codes, "req", split_axis=1, concat_axis=1, tiled=True),
    )
    arrived = lax.all_gather(pieces, "tp", axis=2, tiled=True)
    span_cols = ADAPT_DEV * RANK
    column_adapter = jnp.arange(span_cols, dtype=jnp.int32) // RANK
    selector = (column_adapter == ((arrived_codes - 1) % ADAPT_DEV)[..., None]).astype(jnp.float32)
    projected = jnp.einsum("cnd,kdo->kcno", arrived, w_qkv, preferred_element_type=jnp.float32)
    reduced = (
        jnp.einsum("cnd,kdr->kcnr", arrived, qkv_down, preferred_element_type=jnp.float32)
        * selector[None]
    )
    lifted = jnp.einsum("kcnr,kro->kcno", reduced, qkv_up.astype(jnp.float32), precision=highest)
    qkv = (projected + lifted).astype(jnp.bfloat16)
    local_heads = qkv.shape[-1] // HEAD_DIM
    per_head = qkv.reshape(3, CAP, owner_count, local_heads, HEAD_DIM)
    scores = jnp.einsum(
        "cnhd,enhd->nhce", per_head[0], per_head[1], preferred_element_type=jnp.float32
    ) * HEAD_DIM ** (-0.5)
    code_by_slot = arrived_codes.T
    same_request = code_by_slot[:, :, None] == code_by_slot[:, None, :]
    scores = jnp.where(same_request[:, None], scores, -1e30)
    row_max = jnp.max(scores, axis=-1, keepdims=True)
    expo = jnp.exp(scores - row_max)
    attn_weights = (expo / jnp.sum(expo, axis=-1, keepdims=True)).astype(jnp.bfloat16)
    attended = jnp.einsum(
        "nhce,enhd->cnhd", attn_weights, per_head[2], preferred_element_type=jnp.float32
    )
    attended = attended.astype(jnp.bfloat16).reshape(CAP, owner_count, -1)
    out_upper = out_up.astype(jnp.float32)
    fc1_upper = fc1_up.astype(jnp.float32)
    fc2_upper = fc2_up.astype(jnp.float32)
    own_start = lax.axis_index("tp") * share_rows
    window = attended
    chosen = selector
    out_low = (
        jnp.einsum("cnf,fr->cnr", window, out_down, preferred_element_type=jnp.float32) * chosen
    )
    base_term = jnp.einsum("cnf,fo->cno", window, w_out, preferred_element_type=jnp.float32)
    attn_total = lax.psum(
        (base_term + jnp.einsum("cnr,ro->cno", out_low, out_upper, precision=highest)).astype(
            jnp.bfloat16
        ),
        "tp",
    ).astype(jnp.float32)
    h1_full = layer_norm(arrived.astype(jnp.float32) + attn_total, norm1_gain, norm1_bias).astype(
        jnp.bfloat16
    )
    chosen = selector
    gate_in = jnp.einsum("cnd,df->cnf", h1_full, w_fc1, preferred_element_type=jnp.float32)
    fc1_low = (
        jnp.einsum("cnd,dr->cnr", h1_full, fc1_down, preferred_element_type=jnp.float32) * chosen
    )
    gate_in = gate_in + jnp.einsum("cnr,rf->cnf", fc1_low, fc1_upper, precision=highest)
    hidden = jax.nn.gelu(gate_in, approximate=False).astype(jnp.bfloat16)
    h1_share = lax.dynamic_slice_in_dim(h1_full, own_start, share_rows, 0)
    window = hidden
    chosen = selector
    fc2_low = (
        jnp.einsum("cnf,fr->cnr", window, fc2_down, preferred_element_type=jnp.float32) * chosen
    )
    base_term = jnp.einsum("cnf,fo->cno", window, w_fc2, preferred_element_type=jnp.float32)
    ffn_share = lax.psum_scatter(
        (base_term + jnp.einsum("cnr,ro->cno", fc2_low, fc2_upper, precision=highest)).astype(
            jnp.bfloat16
        ),
        "tp",
        scatter_dimension=0,
        tiled=True,
    ).astype(jnp.float32)
    finished = layer_norm(h1_share.astype(jnp.float32) + ffn_share, norm2_gain, norm2_bias).astype(
        jnp.bfloat16
    )
    returned = lax.all_to_all(
        lax.all_to_all(finished, "req", split_axis=1, concat_axis=1, tiled=True),
        "tp",
        split_axis=2,
        concat_axis=0,
        tiled=True,
    )
    result_rows = jnp.einsum(
        "cnf,gn->gcf", returned, routing, preferred_element_type=jnp.float32
    ).astype(jnp.bfloat16)
    return result_rows.reshape(blocks * CAP, -1)


def solution(mesh):
    placed = (
        P("req", "tp"),
        P("req", None),
        P("req", None),
        P(),
        P(None, None, "tp"),
        P("tp", None),
        P(None, "tp"),
        P("tp", None),
        P(None, None, "req"),
        P(None, "req", "tp"),
        P("tp", "req"),
        P("req", None),
        P(None, "req"),
        P("req", "tp"),
        P("tp", "req"),
        P("req", None),
        P(),
        P(),
        P(),
        P(),
    )
    return jax.shard_map(
        body, mesh=mesh, in_specs=placed, out_specs=P("req", "tp"), check_vma=False
    )
```

profile of v0, /device:TPU:0, one launch (start us, length us, event | category | flops | bytes accessed | tf_op | source)
XLA Modules:
  0.0 183.7 jit_solution(12121473320741959190)
XLA Ops:
  6.5 1.1 select_reduce_fusion.2
  7.6 1.3 fusion.24
  8.9 0.8 copy.90
  9.7 7.3 %all-to-all-start = ((bf16[64,8,256]{2,0,1:T(8,128)(2,1)}), bf16[64,8,256]{2,0,1:T(8,128)(2,1)S(1)}, u32[]{:S(2)}, u32[]{:S(2)}) async-start(bf16[64,8,256]{2,0,1:T(8,128)(2,1)} %copy.90), calls=%async_computation | async-start | bytes 524288 | tf_op jit(solution)/shard_map/all_to_all | solution.py:71
  17.0 0.7 reduce_window_sum.11
  17.7 8.2 %all-to-all-done = bf16[64,8,256]{2,0,1:T(8,128)(2,1)S(1)} async-done(((bf16[64,8,256]{2,0,1:T(8,128)(2,1)}), bf16[64,8,256]{2,0,1:T(8,128)(2,1)S(1)}, u32[]{:S(2)}, u32[]{:S(2)}) %all-to-all-start) | async-done | bytes 262176 | tf_op jit(solution)/shard_map/all_to_all | solution.py:71
  25.8 0.9 copy.91
  27.0 0.7 select_reduce_fusion
  27.6 3.6 %all-to-all-start.1 = ((s32[64,8,1]{0,2,1:T(1,128)}), s32[64,8,1]{0,2,1:T(1,128)S(1)}, u32[]{:S(2)}, u32[]{:S(2)}) async-start(s32[64,8,1]{0,2,1:T(1,128)} %bitcast.12), calls=%async_computation.1 | async-start | bytes 8192 | tf_op jit(solution)/shard_map/all_to_all | solution.py:72
  31.3 6.4 %all-to-all-done.1 = s32[64,8,1]{0,2,1:T(1,128)S(1)} async-done(((s32[64,8,1]{0,2,1:T(1,128)}), s32[64,8,1]{0,2,1:T(1,128)S(1)}, u32[]{:S(2)}, u32[]{:S(2)}) %all-to-all-start.1) | async-done | bytes 2080 | tf_op jit(solution)/shard_map/all_to_all | solution.py:72
  38.1 4.7 %all-gather.2.cloned.1.call-done = bf16[64,8,1024]{2,1,0:T(8,128)(2,1)} async-done(((bf16[64,8,256]{2,1,0:T(8,128)(2,1)}), bf16[64,8,1024]{2,1,0:T(8,128)(2,1)}) %all-gather.2.cloned.1.call-update) | async-done | bytes 1048592 | tf_op jit(solution)/shard_map/all_gather | solution.py:74
  42.8 2.8 %fusion.18 = f32[64,8,3,256]{3,1,2,0:T(8,128)S(1)} fusion(bf16[3,1024,256]{2,1,0:T(8,128)(2,1)} %param.24, bf16[64,8,1024]{2,1,0:T(8,128)(2,1)} %all-gather.2.cloned.1.call-done), kind=kOutput, calls=%fused_computation.33 | convolution fusion | flops 805306368 | bytes 4194304 | tf_op jit(solution)/shard_map/cnd,kdo->kcno/dot_general | solution.py:78
  45.6 0.7 fusion.23
  46.4 0.8 fusion.17
  47.2 0.9 fusion.52
  48.1 2.0 %squeeze.11 = bf16[64,8,4,64]{3,2,1,0:T(4,128)(2,1)} reshape(bf16[1,64,8,256]{3,2,0,1:T(8,128)(2,1)} %get-tuple-element.5) | data formatting | bytes 524288 | tf_op jit(solution)/shard_map/squeeze | solution.py:88
  50.1 2.0 %squeeze.12 = bf16[64,8,4,64]{3,2,1,0:T(4,128)(2,1)} reshape(bf16[1,64,8,256]{3,2,0,1:T(8,128)(2,1)} %get-tuple-element.6) | data formatting | bytes 524288 | tf_op jit(solution)/shard_map/squeeze | solution.py:88
  52.1 1.7 fusion.22
  53.9 1.0 copy-done.19
  54.8 0.3 fusion.53
  55.1 1.1 copy.112
  56.2 2.9 %convolution_convert_fusion = bf16[8,4,64,64]{3,2,1,0:T(8,128)(2,1)} fusion(bf16[64,8,4,64]{0,3,2,1:T(8,128)(2,1)} %bitcast.104, f32[8,4,64]{2,1,0:T(4,128)S(1)} %fusion.53, f32[8,4,64,64]{2,3,1,0:T(8,128)} %copy-done.19), kind=kOutput, calls=%fused_computation.39 | convolution fusion | flops 17303616 | bytes 1056768 | tf_op jit(solution)/shard_map/nhce,enhd->cnhd/dot_general | solution.py:96
  59.1 1.3 copy.99
  60.7 1.0 fusion.40
  61.6 1.5 add_convert_fusion.2
  63.2 0.2 reduce-scatter.2.cloned.1.call-start
  63.4 36.0 %all-reduce.2.cloned.1.call-done = bf16[64,8,1024]{2,1,0:T(8,128)(2,1)} async-done(((bf16[64,8,1024]{2,1,0:T(8,128)(2,1)}), bf16[64,8,1024]{2,1,0:T(8,128)(2,1)}) %all-reduce.2.cloned.1.call-update) | async-done | bytes 1048592 | tf_op jit(solution)/shard_map/psum | solution.py:110
  99.4 1.7 fusion.16
  101.1 0.5 multiply_reduce_fusion
  101.6 0.6 add_convert_fusion.1
  102.2 1.3 fusion.6
  103.5 0.4 convolution_select_fusion.2
  104.0 5.6 %fusion.3 = bf16[64,8,1024]{2,1,0:T(8,128)(2,1)S(1)} fusion(f32[64,8,1024]{2,1,0:T(8,128)S(1)} %fusion.6, f32[64,8,32]{2,1,0:T(8,128)S(1)} %convolution_select_fusion.2, bf16[32,1024]{1,0:T(8,128)(2,1)S(1)} %copy-done.18), kind=kOutput, calls=%fused_computation.4 | convolution fusion | flops 235929600 | bytes 3276800 | tf_op jit(solution)/shard_map/cnr,rf->cnf/dot_general | solution.py:124
  109.6 1.3 fusion.4
  110.9 0.4 convolution_select_fusion.1
  111.4 2.1 %add_convert_fusion = bf16[64,8,1024]{2,1,0:T(8,128)(2,1)} fusion(f32[64,8,1024]{2,1,0:T(8,128)S(1)} %fusion.4, f32[64,8,32]{2,1,0:T(8,128)S(1)} %convolution_select_fusion.1, bf16[32,1024]{1,0:T(8,128)(2,1)S(1)} %copy-done.9), kind=kOutput, calls=%fused_computation.9 | convolution fusion | flops 202375168 | bytes 3276800 | tf_op jit(solution)/shard_map/cnr,ro->cno/dot_general | solution.py:134
  113.5 25.4 %reduce-scatter.2.cloned.1.call-done = bf16[16,8,1024]{2,1,0:T(8,128)(2,1)} async-done(((bf16[64,8,1024]{2,1,0:T(8,128)(2,1)}), bf16[16,8,1024]{2,1,0:T(8,128)(2,1)}) %reduce-scatter.2.cloned.1.call-update) | async-done | bytes 262160 | tf_op jit(solution)/shard_map/reduce_scatter | solution.py:133
  138.9 1.1 fusion.33
  140.0 1.1 multiply_reduce_fusion.1
  141.2 1.1 add_convert_fusion.3
  142.5 14.2 %all_to_all.40 = bf16[16,8,1024]{2,0,1:T(8,128)(2,1)S(1)} all-to-all(bf16[16,8,1024]{2,0,1:T(8,128)(2,1)S(1)} %copy.101), channel_id=1, replica_groups=mesh['req'=8,'tp'=4] {'req'}, dimensions={1} | all-to-all | bytes 524288 | tf_op jit(solution)/shard_map/all_to_all | solution.py:145
  156.7 2.5 %copy.102 = bf16[16,8,1024]{0,1,2:T(8,128)(2,1)} copy(bf16[16,8,1024]{2,0,1:T(8,128)(2,1)S(1)} %all_to_all.40) | data formatting | bytes 524288 | tf_op jit(solution)/shard_map/all_to_all | solution.py:145
  159.2 3.4 %reshape.129 = bf16[4,2,16384]{2,1,0:T(2,128)(2,1)S(1)} reshape(bf16[1024,8,16]{2,1,0:T(8,128)(2,1)} %bitcast.101) | data formatting | bytes 524288
  162.6 8.4 %all_to_all.41 = bf16[4,2,16384]{2,1,0:T(2,128)(2,1)S(1)} all-to-all(bf16[4,2,16384]{2,1,0:T(2,128)(2,1)S(1)} %reshape.129), channel_id=1, replica_groups=mesh['req'=8,'tp'=4] {'tp'}, dimensions={0} | all-to-all | bytes 524288 | tf_op jit(solution)/shard_map/all_to_all | solution.py:144
  171.1 2.4 %reshape.130 = bf16[1024,8,16]{2,1,0:T(8,128)(2,1)} reshape(bf16[4,2,16384]{2,1,0:T(2,128)(2,1)S(1)} %all_to_all.41) | data formatting | bytes 524288
  173.5 2.6 %copy.103 = bf16[16,8,4,256]{3,1,0,2:T(8,128)(2,1)S(1)} copy(bf16[16,8,4,256]{0,1,3,2:T(8,128)(2,1)} %bitcast.102) | data formatting | bytes 524288 | tf_op jit(solution)/shard_map/all_to_all | solution.py:144
  176.1 0.3 convolution_convert_fusion.1
  176.4 0.8 copy.104
  (61 shorter events, 1.3 us)
Async XLA Ops:
  6.5 95.7 %copy-start = (bf16[1024,1024]{1,0:T(8,128)(2,1)S(1)}, bf16[1024,1024]{1,0:T(8,128)(2,1)}, u32[]{:S(2)}) copy-start(bf16[1024,1024]{1,0:T(8,128)(2,1)} %param.26) | copy-start | bytes 6291460
  9.7 16.2 %all-to-all-start = ((bf16[64,8,256]{2,0,1:T(8,128)(2,1)}), bf16[64,8,256]{2,0,1:T(8,128)(2,1)S(1)}, u32[]{:S(2)}, u32[]{:S(2)}) async-start(bf16[64,8,256]{2,0,1:T(8,128)(2,1)} %copy.90), calls=%async_computation | async-start | bytes 524288 | tf_op jit(solution)/shard_map/all_to_all | solution.py:71
  16.9 25.8 %all-gather.2.cloned.1.call-start = ((), (), s32[]{:S(2)}) async-start(), calls=%async_computation.5 | async-start | bytes 1310720 | tf_op jit(solution)/shard_map/all_gather | solution.py:74
  27.6 10.1 %all-to-all-start.1 = ((s32[64,8,1]{0,2,1:T(1,128)}), s32[64,8,1]{0,2,1:T(1,128)S(1)}, u32[]{:S(2)}, u32[]{:S(2)}) async-start(s32[64,8,1]{0,2,1:T(1,128)} %bitcast.12), calls=%async_computation.1 | async-start | bytes 8192 | tf_op jit(solution)/shard_map/all_to_all | solution.py:72
  31.2 68.2 %all-reduce.2.cloned.1.call-start = ((), (), s32[]{:S(2)}) async-start(), calls=%async_computation.6 | async-start | bytes 2097152 | tf_op jit(solution)/shard_map/psum | solution.py:110
  42.8 2.8 %copy-start.1 = (bf16[64,8,1024]{2,1,0:T(8,128)(2,1)S(1)}, bf16[64,8,1024]{2,1,0:T(8,128)(2,1)}, u32[]{:S(2)}) copy-start(bf16[64,8,1024]{2,1,0:T(8,128)(2,1)} %all-gather.2.cloned.1.call-done) | copy-start | bytes 3145732
  42.8 2.8 %copy-start.17 = (bf16[3,1024,32]{1,2,0:T(8,128)(2,1)S(1)}, bf16[3,1024,32]{1,2,0:T(8,128)(2,1)}, u32[]{:S(2)}) copy-start(bf16[3,1024,32]{1,2,0:T(8,128)(2,1)} %param.28) | copy-start | bytes 589828
  45.6 0.8 copy-start.10
  53.8 1.0 copy-start.19
  56.2 4.2 %copy-start.11 = (bf16[256,32]{0,1:T(8,128)(2,1)S(1)}, bf16[256,32]{0,1:T(8,128)(2,1)}, u32[]{:S(2)}) copy-start(bf16[256,32]{0,1:T(8,128)(2,1)} %param.30) | copy-start | bytes 49156
  56.2 4.5 %copy-start.6 = (bf16[32,1024]{1,0:T(8,128)(2,1)S(1)}, bf16[32,1024]{1,0:T(8,128)(2,1)}, u32[]{:S(2)}) copy-start(bf16[32,1024]{1,0:T(8,128)(2,1)} %param.31) | copy-start | bytes 196612
  60.4 1.2 copy-start.5
  63.2 38.4 %copy-start.12 = (f32[1024]{0:T(1024)S(1)}, f32[1024]{0:T(1024)}, u32[]{:S(2)}) copy-start(f32[1024]{0:T(1024)} %param.37) | copy-start | bytes 12292
  63.2 38.4 %copy-start.13 = (f32[1024]{0:T(1024)S(1)}, f32[1024]{0:T(1024)}, u32[]{:S(2)}) copy-start(f32[1024]{0:T(1024)} %param.36) | copy-start | bytes 12292
  63.2 75.7 %reduce-scatter.2.cloned.1.call-start = ((), (), s32[]{:S(2)}) async-start(), calls=%async_computation.7 | async-start | bytes 1310720 | tf_op jit(solution)/shard_map/reduce_scatter | solution.py:133
  99.4 1.7 copy-start.2
  102.2 1.3 copy-start.3
  102.2 1.3 copy-start.7
  102.2 1.7 copy-start.18
  104.0 5.6 %copy-start.16 = (bf16[1024,1024]{1,0:T(8,128)(2,1)S(1)}, bf16[1024,1024]{1,0:T(8,128)(2,1)}, u32[]{:S(2)}) copy-start(bf16[1024,1024]{1,0:T(8,128)(2,1)} %param.27) | copy-start | bytes 6291460
  109.6 1.3 copy-start.8
  109.6 1.7 copy-start.9
  111.4 27.6 %copy-start.4 = (bf16[64,8,1024]{2,1,0:T(8,128)(2,1)S(1)}, bf16[64,8,1024]{2,1,0:T(8,128)(2,1)}, u32[]{:S(2)}) copy-start(bf16[64,8,1024]{2,1,0:T(8,128)(2,1)} %copy-done.3) | copy-start | bytes 3145732
  111.4 29.8 %copy-start.14 = (f32[1024]{0:T(1024)S(1)}, f32[1024]{0:T(1024)}, u32[]{:S(2)}) copy-start(f32[1024]{0:T(1024)} %param.39) | copy-start | bytes 12292
  111.4 29.8 %copy-start.15 = (f32[1024]{0:T(1024)S(1)}, f32[1024]{0:T(1024)}, u32[]{:S(2)}) copy-start(f32[1024]{0:T(1024)} %param.38) | copy-start | bytes 12292
Sparse Core Ops, SparseCore 0:
  26.8 15.8 all-gather.1
  63.3 36.0 all-reduce.1
  113.6 25.2 reduce-scatter.1
where the time goes:
time: 184 us
  waiting for transfers between devices  80.7 us (44%)
  matrix products  24.3 us (13%)
  blocking collectives  22.7 us (12%)
  local copies, waits for them, and re-layouts  22 us (12%)
  between operations  13.5 us (7%)
  starting transfers between devices  11.1 us (6%)
  other arithmetic  9.38 us (5%)
    psum x1, waiting for transfers between devices, body(): lax.psum((base_term + jnp.einsum('cnr,ro->cno', out_low, out_upper, preci...  36 us
    reduce_scatter x1, waiting for transfers between devices, body(): lax.psum_scatter((base_term + jnp.einsum('cnr,ro->cno', fc2_low, fc2_uppe...  25.4 us
    all_to_all x1, blocking collectives, body(): lax.all_to_all(finished, 'req', split_axis=1, concat_axis=1, tiled=True)  14.2 us
    all_to_all x1, blocking collectives, body(): lax.all_to_all(lax.all_to_all(finished, 'req', split_axis=1, concat_axis=...  8.42 us
    all_to_all x1, waiting for transfers between devices, body(): lax.all_to_all(outgoing, 'req', split_axis=1, concat_axis=1, tiled=True)  8.15 us
    all_to_all x1, starting transfers between devices, body(): lax.all_to_all(outgoing, 'req', split_axis=1, concat_axis=1, tiled=True)  7.25 us
    unnamed x42, local copies, waits for them, and re-layouts  7.01 us
    all_to_all x1, waiting for transfers between devices, body(): lax.all_to_all(sent_codes, 'req', split_axis=1, concat_axis=1, tiled=True)  6.41 us
  transfers between devices with their start and end apart: 5, of which 5 were waited for; matrix products, arithmetic and copies ran while one was open for 1% of the time, Pallas kernels for 0%

commit v1 on v0

v1 whole, which is shorter than its diff:
```python
import functools

import jax
import jax.numpy as jnp
from jax import lax
from jax.experimental import pallas as pl
from jax.experimental.pallas import tpu as pltpu
from jax.sharding import PartitionSpec as P

HEAD_DIM = 64
RANK = 16
ADAPT_DEV = 2
CAP = 64
SEQ_G = 4
SPAN = ADAPT_DEV * RANK
PAD = 8
NORM_EPS = 1e-05
BF = jnp.bfloat16
F32 = jnp.float32
VMEM_LIMIT = 56 * 1024 * 1024


def dot(a, b):
    return lax.dot_general(a, b, (((1,), (0,)), ((), ())), preferred_element_type=F32)


def dot_t(a, b):
    return lax.dot_general(a, b, (((1,), (1,)), ((), ())), preferred_element_type=F32)


def layer_norm(values, gain, shift):
    mean = jnp.mean(values, axis=-1, keepdims=True)
    centred = values - mean
    variance = jnp.mean(centred * centred, axis=-1, keepdims=True)
    return centred * lax.rsqrt(variance + NORM_EPS) * gain + shift


def split_low(low, sel):
    low = low * sel
    high = low.astype(BF).astype(F32)
    lane = lax.broadcasted_iota(jnp.int32, low.shape, 1)
    return jnp.where((lane // SPAN) % 2 == 0, high, low - high).astype(BF)


def pack_kernel(lengths, ids, slots, tok, out):
    blocks = tok.shape[0]
    if out.shape[0] > blocks:
        out[...] = jnp.zeros(out.shape, out.dtype)
    width = out.shape[2]
    pos = lax.broadcasted_iota(jnp.int32, (PAD, width), 1) % CAP
    for g in range(blocks):
        slot = [slots[ids[g, k]] for k in range(SEQ_G)]
        owner = slot[0] // ADAPT_DEV
        code = jnp.full((PAD, width), 1 + slot[0] % ADAPT_DEV, jnp.int32)
        end = jnp.int32(0)
        for k in range(1, SEQ_G):
            end = end + lengths[g, k - 1]
            code = jnp.where(pos >= end, 1 + k * ADAPT_DEV + slot[k] % ADAPT_DEV, code)
        out[owner, :CAP, :] = tok[g]
        out[owner, CAP:, :] = code.astype(F32).astype(BF)


def attn_kernel(n_tp, me, *refs):
    parts, (w, down, up, att, sel_out, x_full) = refs[:n_tp], refs[n_tp:]
    blocks = parts[0].shape[0]
    width = parts[0].shape[2]
    rows = blocks * CAP
    tp = me[0]
    for r in range(n_tp):
        start = pl.multiple_of((tp ^ r) * width, width)
        x_full[:, pl.ds(start, width)] = parts[r][:, :CAP, :].reshape(rows, width)
    x = x_full[...]
    pair_lane = lax.broadcasted_iota(jnp.int32, (2 * CAP, 2 * CAP), 1)
    pair_row = lax.broadcasted_iota(jnp.int32, (2 * CAP, 2 * CAP), 0)
    eye = pair_lane == pair_row
    lane_sel = lax.broadcasted_iota(jnp.int32, (2 * CAP, sel_out.shape[1]), 1)
    lane_sel = ((lane_sel // RANK) % ADAPT_DEV).astype(F32)
    masks, sels = [], []
    for p in range(blocks // 2):
        c0 = parts[0][2 * p, CAP : CAP + 1, : 2 * CAP].astype(F32)
        c1 = parts[0][2 * p + 1, CAP : CAP + 1, : 2 * CAP].astype(F32) + 64.0
        idr = jnp.where(pair_lane < CAP, c0, c1)
        idc = jnp.sum(jnp.where(eye, idr, 0.0), axis=1, keepdims=True)
        masks.append(idr == idc)
        pick = idc - 1.0
        pick = pick - 2.0 * jnp.floor(pick * 0.5)
        sels.append((lane_sel == pick).astype(F32))
    sel = jnp.concatenate(sels, axis=0)
    sel_out[...] = sel.astype(BF)
    low = split_low(dot(x, down[...]), jnp.concatenate([sel, sel], axis=1)[:, : 6 * SPAN])
    qkv = []
    for k in range(3):
        full = dot(x, w[k]) + dot(low[:, 2 * k * SPAN : 2 * (k + 1) * SPAN], up[k])
        qkv.append(full.astype(BF))
    q, k_, v = qkv
    q = (q.astype(F32) * HEAD_DIM**-0.5).astype(BF)
    first = pair_lane < HEAD_DIM
    zero = jnp.zeros((), BF)
    for p in range(blocks // 2):
        r0 = p * 2 * CAP
        for h in range(width // (2 * HEAD_DIM)):
            c0 = h * 2 * HEAD_DIM
            qq = q[r0 : r0 + 2 * CAP, c0 : c0 + 2 * HEAD_DIM]
            kk = k_[r0 : r0 + 2 * CAP, c0 : c0 + 2 * HEAD_DIM]
            vv = v[r0 : r0 + 2 * CAP, c0 : c0 + 2 * HEAD_DIM]
            both = []
            for half in (first, ~first):
                s = dot_t(jnp.where(half, qq, zero), kk)
                s = jnp.where(masks[p], s, -1e30)
                e = jnp.exp(s - jnp.max(s, axis=-1, keepdims=True))
                prob = (e / jnp.sum(e, axis=-1, keepdims=True)).astype(BF)
                both.append(dot(prob, vv))
            att[r0 : r0 + 2 * CAP, c0 : c0 + 2 * HEAD_DIM] = jnp.where(first, *both).astype(BF)


def ffn_kernel(n_tp, me, *refs):
    atts, wouts, odowns = refs[:n_tp], refs[n_tp : 2 * n_tp], refs[2 * n_tp : 3 * n_tp]
    (x, sel_in, oup, w1, d1, u1, w2, d2, u2, g1, b1, even, odd, h_own, h_scr) = refs[3 * n_tp :]
    rows, feat = x.shape
    blocks = rows // CAP
    share = CAP // n_tp
    tp = me[0]
    step = min(rows, 256)
    for r0 in range(0, rows, step):
        rs = slice(r0, r0 + step)
        nb = step // CAP
        sel = sel_in[rs].astype(F32)[:, : 2 * SPAN]
        total = x[rs].astype(F32)
        low = None
        for r in range(n_tp):
            a = atts[r][rs]
            total = total + dot(a, wouts[r][...])
            part = dot(a, odowns[r][...])
            low = part if low is None else low + part
        total = total + dot(split_low(low, sel), oup[...])
        h1 = layer_norm(total, g1[...], b1[...]).astype(BF)
        h_scr[r0 // CAP : r0 // CAP + nb] = h1.reshape(nb, n_tp, share, feat)
        gate = dot(h1, w1[...]) + dot(split_low(dot(h1, d1[...]), sel), u1[...])
        hidden = (0.5 * gate * (1.0 + lax.erf(gate * 0.7071067811865476))).astype(BF)
        term = dot(hidden, w2[...]) + dot(split_low(dot(hidden, d2[...]), sel), u2[...])
        term = term.reshape(nb, n_tp, share, feat)
        own_rows = slice(r0 // n_tp, (r0 + step) // n_tp)
        for j in range(n_tp):
            rel = tp ^ j
            piece = term[:, j].reshape(nb * share, feat)

            @pl.when(rel % 2 == 0)
            def _():
                even[rel // 2, own_rows, :] = piece

            @pl.when(rel % 2 == 1)
            def _():
                odd[rel // 2, own_rows, :] = piece.astype(BF)

    h_own[...] = h_scr[:, tp].reshape(blocks * share, feat)


def last_kernel(n_tp, even, got, *refs):
    arrived, (h_own, g2, b2, out) = refs[: n_tp // 2 - 1], refs[n_tp // 2 - 1 :]
    total = h_own[...].astype(F32) + (even[0] + got[0].astype(F32))
    for a in arrived:
        total = total + a[...].astype(F32)
    done = layer_norm(total, g2[...], b2[...]).astype(BF)
    n, _, share, width = out.shape
    for f in range(n_tp):
        out[:, f] = done[:, f * width : (f + 1) * width].reshape(n, share, width)


def unpack_kernel(ids, slots, arrived, out):
    for g in range(out.shape[0]):
        out[g] = arrived[slots[ids[g, 0]] // ADAPT_DEV]


def whole(shape):
    zeros = (0,) * len(shape)
    return pl.BlockSpec(tuple(shape), lambda *_: zeros)


SMEM = pl.BlockSpec(memory_space=pltpu.SMEM)


def params():
    return pltpu.CompilerParams(vmem_limit_bytes=VMEM_LIMIT)


def body(
    tokens,
    prompt_lengths,
    adapter_ids,
    adapter_slot,
    w_qkv,
    w_out,
    w_fc1,
    w_fc2,
    qkv_down,
    qkv_up,
    out_down,
    out_up,
    fc1_down,
    fc1_up,
    fc2_down,
    fc2_up,
    norm1_gain,
    norm1_bias,
    norm2_gain,
    norm2_bias,
):
    n_req = lax.axis_size("req")
    n_tp = lax.axis_size("tp")
    feat = w_qkv.shape[1]
    width = tokens.shape[1]
    blocks = tokens.shape[0] // CAP
    share = CAP // n_tp
    me = jnp.reshape(lax.axis_index("tp"), (1,)).astype(jnp.int32)

    def swap(value, r):
        return lax.ppermute(value, "tp", [(i, i ^ r) for i in range(n_tp)])

    def gather(value):
        far = [value] + [swap(value, 2 * y) for y in range(1, n_tp // 2)]
        found = []
        for piece in far:
            found += [piece, swap(piece, 1)]
        return found

    def twice(value, axis):
        return jnp.concatenate([value, value], axis=axis)

    packed = pl.pallas_call(
        pack_kernel,
        out_shape=jax.ShapeDtypeStruct((n_req, CAP + PAD, width), BF),
        in_specs=[SMEM, SMEM, SMEM, pl.BlockSpec(memory_space=pltpu.VMEM)],
        out_specs=pl.BlockSpec(memory_space=pltpu.VMEM),
        name="pack",
    )(prompt_lengths, adapter_ids, adapter_slot, tokens.reshape(blocks, CAP, width))
    arrived = lax.all_to_all(packed, "req", split_axis=0, concat_axis=0, tiled=True)
    parts = gather(arrived)
    wouts = gather(w_out)
    odowns = gather(twice(out_down, 1))

    step_blocks = min(n_req, 8)
    steps = n_req // step_blocks
    step_rows = step_blocks * CAP
    rows = n_req * CAP

    def by_rows(cols):
        return pl.BlockSpec((step_rows, cols), lambda i: (i, 0))

    down = jnp.transpose(twice(qkv_down, 2), (1, 0, 2)).reshape(feat, 6 * SPAN)
    up = twice(qkv_up, 1)
    attended, sel, x_full = pl.pallas_call(
        functools.partial(attn_kernel, n_tp),
        grid=(steps,),
        out_shape=(
            jax.ShapeDtypeStruct((rows, width), BF),
            jax.ShapeDtypeStruct((rows, 4 * SPAN), BF),
            jax.ShapeDtypeStruct((rows, feat), BF),
        ),
        in_specs=[SMEM]
        + [pl.BlockSpec((step_blocks, CAP + PAD, width), lambda i: (i, 0, 0))] * n_tp
        + [whole(w_qkv.shape), whole(down.shape), whole(up.shape)],
        out_specs=(by_rows(width), by_rows(4 * SPAN), by_rows(feat)),
        compiler_params=params(),
        name="attend",
    )(me, *parts, w_qkv, down, up)

    atts = gather(attended)
    oup, u1, u2 = twice(out_up, 0), twice(fc1_up, 0), twice(fc2_up, 0)
    d1, d2 = twice(fc1_down, 1), twice(fc2_down, 1)
    g1, b1 = norm1_gain[None], norm1_bias[None]
    half = n_tp // 2
    own = rows // n_tp
    step_own = step_rows // n_tp
    consts = [oup, w_fc1, d1, u1, w_fc2, d2, u2, g1, b1]
    even, odd, h_own = pl.pallas_call(
        functools.partial(ffn_kernel, n_tp),
        grid=(steps,),
        out_shape=(
            jax.ShapeDtypeStruct((half, own, feat), F32),
            jax.ShapeDtypeStruct((half, own, feat), BF),
            jax.ShapeDtypeStruct((own, feat), BF),
        ),
        in_specs=[SMEM]
        + [by_rows(width)] * n_tp
        + [whole(w.shape) for w in wouts + odowns]
        + [by_rows(feat), by_rows(4 * SPAN)]
        + [whole(c.shape) for c in consts],
        out_specs=(
            pl.BlockSpec((half, step_own, feat), lambda i: (0, i, 0)),
            pl.BlockSpec((half, step_own, feat), lambda i: (0, i, 0)),
            pl.BlockSpec((step_own, feat), lambda i: (i, 0)),
        ),
        scratch_shapes=[pltpu.VMEM((step_blocks, n_tp, share, feat), BF)],
        compiler_params=params(),
        name="feed",
    )(me, *atts, *wouts, *odowns, x_full, sel, *consts)

    got = swap(odd, 1)
    sums = [
        swap((even[y] + got[y].astype(F32)).astype(BF), 2 * y) for y in range(1, half)
    ]
    vm = pl.BlockSpec(memory_space=pltpu.VMEM)
    done = pl.pallas_call(
        functools.partial(last_kernel, n_tp),
        out_shape=jax.ShapeDtypeStruct((n_req, n_tp, share, width), BF),
        in_specs=[vm] * (5 + len(sums)),
        out_specs=vm,
        compiler_params=params(),
        name="finish",
    )(even, got, *sums, h_own, norm2_gain[None], norm2_bias[None])
    back = lax.all_to_all(
        done.reshape(n_req * n_tp, share, width),
        ("req", "tp"),
        split_axis=0,
        concat_axis=0,
        tiled=True,
    )
    result = pl.pallas_call(
        unpack_kernel,
        out_shape=jax.ShapeDtypeStruct((blocks, CAP, width), BF),
        in_specs=[SMEM, SMEM, vm],
        out_specs=vm,
        name="unpack",
    )(adapter_ids, adapter_slot, back.reshape(n_req, CAP, width))
    return result.reshape(blocks * CAP, width)


def solution(mesh):
    placed = (
        P("req", "tp"),
        P("req", None),
        P("req", None),
        P(),
        P(None, None, "tp"),
        P("tp", None),
        P(None, "tp"),
        P("tp", None),
        P(None, None, "req"),
        P(None, "req", "tp"),
        P("tp", "req"),
        P("req", None),
        P(None, "req"),
        P("req", "tp"),
        P("tp", "req"),
        P("req", None),
        P(),
        P(),
        P(),
        P(),
    )
    return jax.shard_map(
        body, mesh=mesh, in_specs=placed, out_specs=P("req", "tp"), check_vma=False
    )
```

time: 184 us -> 102 us (0.55)
  waiting for transfers between devices: 80.7 us -> 23.2 us
  Pallas kernels: 0 us -> 27.2 us
  matrix products: 24.3 us -> 0 us
  local copies, waits for them, and re-layouts: 22 us -> 6.73 us
  between operations: 13.5 us -> 0.22 us
  blocking collectives: 22.7 us -> 31.5 us
  other arithmetic: 9.38 us -> 5.64 us
  starting transfers between devices: 11.1 us -> 7.5 us
    psum x1 -> x0, waiting for transfers between devices: 36 us -> none  [body(): lax.psum((base_term + jnp.einsum('cnr,ro->cno', out_low, out_upper, preci...]
    pallas_call x0 -> x5, Pallas kernels: none -> 27.2 us  [the longest x1 11.8 us: body(): pl.pallas_call(functools.partial(ffn_kernel, n_tp), grid=(steps,), out_sh...]
    reduce_scatter x1 -> x0, waiting for transfers between devices: 25.4 us -> none  [body(): lax.psum_scatter((base_term + jnp.einsum('cnr,ro->cno', fc2_low, fc2_uppe...]
    dot_general x16 -> x0, matrix products: 24.3 us -> none  [the longest x1 5.6 us: body(): jnp.einsum('cnr,rf->cnf', fc1_low, fc1_upper, precision=highest)]
    ppermute x0 -> x14, waiting for transfers between devices: none -> 23.2 us  [swap(): return lax.ppermute(value, 'tp', [(i, i ^ r) for i in range(n_tp)])]
    all_to_all x2 -> x0, waiting for transfers between devices: 14.6 us -> none  [the longest x1 8.15 us: body(): lax.all_to_all(outgoing, 'req', split_axis=1, concat_axis=1, tiled=True)]
    all_to_all x2 -> x0, starting transfers between devices: 10.8 us -> none  [the longest x1 7.25 us: body(): lax.all_to_all(outgoing, 'req', split_axis=1, concat_axis=1, tiled=True)]
    all_to_all x2, blocking collectives: 22.7 us -> 31.5 us  [the longest x1 17.6 us: body(): lax.all_to_all(packed, 'req', split_axis=0, concat_axis=0, tiled=True)]
  transfers between devices with their start and end apart: 5 -> 14, of which waited for: 5 -> 6; matrix products, arithmetic and copies ran while one was open for 1% -> 6% of each run, Pallas kernels for 0% -> 9%
where the time goes in v1:
time: 102 us
  blocking collectives  31.5 us (31%)
  Pallas kernels  27.2 us (27%)
  waiting for transfers between devices  23.2 us (23%)
  starting transfers between devices  7.5 us (7%)
  local copies, waits for them, and re-layouts  6.73 us (7%)
  other arithmetic  5.64 us (6%)
    ppermute x14, waiting for transfers between devices, swap(): return lax.ppermute(value, 'tp', [(i, i ^ r) for i in range(n_tp)])  23.2 us
    all_to_all x1, blocking collectives, body(): lax.all_to_all(packed, 'req', split_axis=0, concat_axis=0, tiled=True)  17.6 us
    all_to_all x1, blocking collectives, body(): lax.all_to_all(done.reshape(n_req * n_tp, share, width), ('req', 'tp'), s...  13.9 us
    pallas_call x1, Pallas kernels, body(): pl.pallas_call(functools.partial(ffn_kernel, n_tp), grid=(steps,), out_sh...  11.8 us
    pallas_call x1, Pallas kernels, body(): pl.pallas_call(functools.partial(attn_kernel, n_tp), grid=(steps,), out_s...  9.37 us
    ppermute x14, starting transfers between devices, swap(): return lax.ppermute(value, 'tp', [(i, i ^ r) for i in range(n_tp)])  7.5 us
    unnamed x53, local copies, waits for them, and re-layouts  5.74 us
    concatenate x6, other arithmetic, twice(): return jnp.concatenate([value, value], axis=axis)  4.36 us
  transfers between devices with their start and end apart: 14, of which 6 were waited for; matrix products, arithmetic and copies ran while one was open for 6% of the time, Pallas kernels for 9%

profile of v1, /device:TPU:0, one launch (start us, length us, event | category | flops | bytes accessed | tf_op | source)
XLA Modules:
  0.0 101.9 jit_solution(9226815309598651888)
XLA Ops:
  0.0 1.3 %copy.40.ids = s32[8,4]{1,0:T(8,128)} copy(s32[8,4]{0,1:T(4,128)} %param.22) | data formatting | bytes 256 | tf_op args[2]
  1.3 1.3 %copy.31.lengths = s32[8,4]{1,0:T(8,128)} copy(s32[8,4]{0,1:T(4,128)} %param.21) | data formatting | bytes 256 | tf_op args[1]
  2.7 1.8 %pack.1 = bf16[8,72,256]{2,1,0:T(8,128)(2,1)} custom-call(s32[8,4]{1,0:T(8,128)} %copy.31.lengths, s32[8,4]{1,0:T(8,128)} %copy.40.ids, s32[16]{0:T(128)} %slots.3, bf16[8,64,256]{2,1,0:T(8,128)(2,1)} %bitcast.17), custom_call_target="tpu_custom_call" | custom-call | tf_op jit(solution)/shard_map/pack/pallas_call | solution.py:229
  4.5 17.6 %all_to_all.10.refs_0_ = bf16[8,72,256]{2,1,0:T(8,128)(2,1)S(1)} all-to-all(bf16[8,72,256]{2,1,0:T(8,128)(2,1)} %pack.1), channel_id=1, replica_groups=mesh['req'=8,'tp'=4] {'req'}, dimensions={0} | all-to-all | bytes 589824 | tf_op jit(solution)/shard_map/all_to_all | solution.py:236
  22.1 1.5 %collective-permute-start.1 = (bf16[8,72,256]{2,1,0:T(8,128)(2,1)S(1)}, bf16[8,72,256]{2,1,0:T(8,128)(2,1)S(1)}, u32[]{:S(2)}, u32[]{:S(2)}) collective-permute-start(bf16[8,72,256]{2,1,0:T(8,128)(2,1)S(1)} %all_to_all.10.refs_0_), channel_id=1, source_target_pairs={{0,2},{1,3},{2,0},{3,1},{4,6},{5,7},{6,4},{7,5},{8,10},{9,11},{10,... | collective-permute-start | bytes 884744 | tf_op jit(solution)/shard_map/ppermute | solution.py:217
  23.6 0.5 collective-permute-start.7
  24.1 7.9 %collective-permute-done.1.refs_2_ = bf16[8,72,256]{2,1,0:T(8,128)(2,1)S(1)} collective-permute-done((bf16[8,72,256]{2,1,0:T(8,128)(2,1)S(1)}, bf16[8,72,256]{2,1,0:T(8,128)(2,1)S(1)}, u32[]{:S(2)}, u32[]{:S(2)}) %collective-permute-start.1) | collective-permute-done | bytes 294944 | tf_op jit(solution)/shard_map/ppermute | solution.py:217
  32.0 0.0 collective-permute-start.2
  32.1 1.2 %pad_maximum_fusion = bf16[3,1024,64]{1,2,0:T(8,128)(2,1)S(1)} fusion(bf16[3,1024,32]{1,2,0:T(8,128)(2,1)} %param.28), kind=kLoop, calls=%fused_computation.1 | loop fusion | flops 786432 | bytes 589824 | tf_op jit(solution)/shard_map/concatenate | solution.py:227
  33.2 0.0 copy-start.2
  33.2 0.0 copy-start.23
  33.2 1.0 copy.33.refs_5_
  34.2 0.7 pad_maximum_fusion.6.refs_6_
  34.9 0.7 copy-done.7
  35.6 0.1 copy-done.8
  35.7 9.4 %attend.1 = (bf16[512,256]{1,0:T(8,128)(2,1)}, bf16[512,128]{1,0:T(8,128)(2,1)}, bf16[512,1024]{1,0:T(8,128)(2,1)}) custom-call(s32[1]{0:T(128)} %bitcast.me, bf16[8,72,256]{2,1,0:T(8,128)(2,1)} %copy-done, bf16[8,72,256]{2,1,0:T(8,128)(2,1)} %copy-done.7, bf16[8,72,256]{2,1,0:T(8,128)(2,1)} %copy-done.6, bf16[8,72,256]{2,1,0:T(8,128)(2,1)} %copy-done.8, ...), custom_call_target="tpu_custom_call" | custom-call | tf_op jit(solution)/shard_map/attend/pallas_call | solution.py:251
  45.1 1.5 %collective-permute-start.4 = (bf16[512,256]{1,0:T(8,128)(2,1)}, bf16[512,256]{1,0:T(8,128)(2,1)S(1)}, u32[]{:S(2)}, u32[]{:S(2)}) collective-permute-start(bf16[512,256]{1,0:T(8,128)(2,1)} %get-tuple-element.11.refs_0_), channel_id=1, source_target_pairs={{0,2},{1,3},{2,0},{3,1},{4,6},{5,7},{6,4},{7,5},{8,10},{9,11},{10,... | collective-permute-start | bytes 786440 | tf_op jit(solution)/shard_map/ppermute | solution.py:217
  46.6 0.1 collective-permute-start.6
  46.8 0.4 collective-permute-start.8
  47.1 0.1 copy.34
  47.3 0.1 pad_maximum_fusion.7.refs_8_
  47.4 0.6 collective-permute-start.10
  47.9 0.2 copy.36
  48.1 0.2 copy.38
  48.3 0.1 collective-permute-start.3
  48.4 6.0 %collective-permute-done.4.refs_2_ = bf16[512,256]{1,0:T(8,128)(2,1)S(1)} collective-permute-done((bf16[512,256]{1,0:T(8,128)(2,1)}, bf16[512,256]{1,0:T(8,128)(2,1)S(1)}, u32[]{:S(2)}, u32[]{:S(2)}) %collective-permute-start.4) | collective-permute-done | bytes 262176 | tf_op jit(solution)/shard_map/ppermute | solution.py:217
  54.4 1.1 %pad_maximum_fusion.1 = (bf16[1024,64]{1,0:T(8,128)(2,1)}, bf16[1024,64]{1,0:T(8,128)(2,1)}) fusion(bf16[1024,32]{1,0:T(8,128)(2,1)S(1)} %copy.36, bf16[1024,32]{1,0:T(8,128)(2,1)S(1)} %copy.38), kind=kLoop, calls=%fused_computation.3 | loop fusion | flops 524288 | bytes 393216 | tf_op jit(solution)/shard_map/concatenate | solution.py:227
  55.5 0.5 collective-permute-start.9
  56.0 0.7 pad_maximum_fusion.3
  56.7 0.2 collective-permute-done.9.refs_9_
  56.9 0.4 collective-permute-start.11
  57.3 0.7 pad_maximum_fusion.5.refs_20_
  57.9 0.2 collective-permute-done.11.refs_11_
  58.3 0.5 copy-done.16
  58.8 0.2 copy-done.4
  59.0 0.2 copy-done.5
  59.2 0.1 copy-done.11
  59.2 0.1 copy-done.12
  59.3 11.8 %feed.1 = (f32[2,128,1024]{2,1,0:T(8,128)}, bf16[2,128,1024]{2,1,0:T(8,128)(2,1)}, bf16[128,1024]{1,0:T(8,128)(2,1)}) custom-call(s32[1]{0:T(128)} %bitcast.me, bf16[512,256]{1,0:T(8,128)(2,1)} %get-tuple-element.11.refs_0_, bf16[512,256]{1,0:T(8,128)(2,1)} %copy-done.11, bf16[512,256]{1,0:T(8,128)(2,1)} %copy-done.10, bf16[512,256]{1,0:T(8,128)(2,1)} %copy-done.12, ...), custom_call_target="tpu_custom_call" | custom-call | tf_op jit(solution)/shard_map/feed/pallas_call | solution.py:275
  71.1 0.4 collective-permute-start.12
  71.4 1.8 %collective-permute-done.12.got = bf16[2,128,1024]{2,1,0:T(8,128)(2,1)S(1)} collective-permute-done((bf16[2,128,1024]{2,1,0:T(8,128)(2,1)}, bf16[2,128,1024]{2,1,0:T(8,128)(2,1)S(1)}, u32[]{:S(2)}, u32[]{:S(2)}) %collective-permute-start.12) | collective-permute-done | bytes 524320 | tf_op jit(solution)/shard_map/ppermute | solution.py:217
  73.2 1.3 %fusion = bf16[128,1024]{1,0:T(8,128)(2,1)S(1)} fusion(f32[2,128,1024]{2,1,0:T(8,128)} %get-tuple-element.14.even, bf16[2,128,1024]{2,1,0:T(8,128)(2,1)S(1)} %collective-permute-done.12.got), kind=kLoop, calls=%fused_computation.2 | loop fusion | flops 393216 | bytes 1048576 | tf_op jit(solution)/shard_map/convert_element_type | solution.py:300
  74.5 1.6 %collective-permute-start.13 = (bf16[128,1024]{1,0:T(8,128)(2,1)S(1)}, bf16[128,1024]{1,0:T(8,128)(2,1)S(1)}, u32[]{:S(2)}, u32[]{:S(2)}) collective-permute-start(bf16[128,1024]{1,0:T(8,128)(2,1)S(1)} %fusion), channel_id=1, source_target_pairs={{0,2},{1,3},{2,0},{3,1},{4,6},{5,7},{6,4},{7,5},{8,10},{9,11},{10,... | collective-permute-start | bytes 786440 | tf_op jit(solution)/shard_map/ppermute | solution.py:217
  76.1 7.0 %collective-permute-done.13.refs_0_ = bf16[128,1024]{1,0:T(8,128)(2,1)S(1)} collective-permute-done((bf16[128,1024]{1,0:T(8,128)(2,1)S(1)}, bf16[128,1024]{1,0:T(8,128)(2,1)S(1)}, u32[]{:S(2)}, u32[]{:S(2)}) %collective-permute-start.13) | collective-permute-done | bytes 262176 | tf_op jit(solution)/shard_map/ppermute | solution.py:217
  83.1 0.7 copy-done.13
  83.8 2.5 %finish.1 = bf16[8,4,16,256]{3,2,1,0:T(8,128)(2,1)} custom-call(f32[2,128,1024]{2,1,0:T(8,128)} %get-tuple-element.14.even, bf16[2,128,1024]{2,1,0:T(8,128)(2,1)} %copy-done.1, bf16[128,1024]{1,0:T(8,128)(2,1)} %copy-done.13, bf16[128,1024]{1,0:T(8,128)(2,1)} %get-tuple-element.16.refs_1_, f32[1,1024]{1,0:T(1,128)} %bitcast.20, f32[1,1024]{1,0:T(1,128)} %bitcast.21), custom_call_target="tpu_custom_call" | custom-call | tf_op jit(solution)/shard_map/finish/pallas_call | solution.py:303
  86.3 13.9 %all_to_all.11 = bf16[32,16,256]{2,1,0:T(8,128)(2,1)} all-to-all(bf16[32,16,256]{2,1,0:T(8,128)(2,1)} %bitcast.15), channel_id=1, replica_groups=mesh['req'=8,'tp'=4] {'req','tp'}, dimensions={0} | all-to-all | bytes 524288 | tf_op jit(solution)/shard_map/all_to_all | solution.py:311
  100.2 1.7 %unpack.1 = bf16[8,64,256]{2,1,0:T(8,128)(2,1)} custom-call(s32[8,4]{1,0:T(8,128)} %copy.40.ids, s32[16]{0:T(128)} %slots.3, bf16[8,64,256]{2,1,0:T(8,128)(2,1)} %bitcast.16), custom_call_target="tpu_custom_call" | custom-call | tf_op jit(solution)/shard_map/unpack/pallas_call | solution.py:318
  (48 shorter events, 0.1 us)
Async XLA Ops:
  0.0 34.2 %copy-start.22 = (bf16[3,32,256]{2,1,0:T(8,128)(2,1)S(1)}, bf16[3,32,256]{2,1,0:T(8,128)(2,1)}, u32[]{:S(2)}) copy-start(bf16[3,32,256]{2,1,0:T(8,128)(2,1)} %param.29) | copy-start | bytes 147460
  22.1 12.8 %copy-start = (bf16[8,72,256]{2,1,0:T(8,128)(2,1)}, bf16[8,72,256]{2,1,0:T(8,128)(2,1)S(1)}, u32[]{:S(2)}) copy-start(bf16[8,72,256]{2,1,0:T(8,128)(2,1)S(1)} %all_to_all.10.refs_0_) | copy-start | bytes 884740
  22.1 9.9 %collective-permute-start.1 = (bf16[8,72,256]{2,1,0:T(8,128)(2,1)S(1)}, bf16[8,72,256]{2,1,0:T(8,128)(2,1)S(1)}, u32[]{:S(2)}, u32[]{:S(2)}) collective-permute-start(bf16[8,72,256]{2,1,0:T(8,128)(2,1)S(1)} %all_to_all.10.refs_0_), channel_id=1, source_target_pairs={{0,2},{1,3},{2,0},{3,1},{4,6},{5,7},{6,4},{7,5},{8,10},{9,11},{10,... | collective-permute-start | bytes 884744 | tf_op jit(solution)/shard_map/ppermute | solution.py:217
  23.6 23.1 %collective-permute-start.7 = (bf16[256,1024]{1,0:T(8,128)(2,1)}, bf16[256,1024]{1,0:T(8,128)(2,1)S(1)}, u32[]{:S(2)}, u32[]{:S(2)}) collective-permute-start(bf16[256,1024]{1,0:T(8,128)(2,1)} %refs_4_.3), channel_id=1, source_target_pairs={{0,2},{1,3},{2,0},{3,1},{4,6},{5,7},{6,4},{7,5},{8,10},{9,11},{10,... | collective-permute-start | bytes 1572872 | tf_op jit(solution)/shard_map/ppermute | solution.py:217
  24.1 10.8 %collective-permute-start = (bf16[8,72,256]{2,1,0:T(8,128)(2,1)S(1)}, bf16[8,72,256]{2,1,0:T(8,128)(2,1)S(1)}, u32[]{:S(2)}, u32[]{:S(2)}) collective-permute-start(bf16[8,72,256]{2,1,0:T(8,128)(2,1)S(1)} %all_to_all.10.refs_0_), channel_id=1, source_target_pairs={{0,1},{1,0},{2,3},{3,2},{4,5},{5,4},{6,7},{7,6},{8,9},{9,8},{10,11... | collective-permute-start | bytes 884744 | tf_op jit(solution)/shard_map/ppermute | solution.py:217
  32.0 2.9 %copy-start.6 = (bf16[8,72,256]{2,1,0:T(8,128)(2,1)}, bf16[8,72,256]{2,1,0:T(8,128)(2,1)S(1)}, u32[]{:S(2)}) copy-start(bf16[8,72,256]{2,1,0:T(8,128)(2,1)S(1)} %collective-permute-done.1.refs_2_) | copy-start | bytes 884740
  32.0 2.8 %collective-permute-start.2 = (bf16[8,72,256]{2,1,0:T(8,128)(2,1)S(1)}, bf16[8,72,256]{2,1,0:T(8,128)(2,1)S(1)}, u32[]{:S(2)}, u32[]{:S(2)}) collective-permute-start(bf16[8,72,256]{2,1,0:T(8,128)(2,1)S(1)} %collective-permute-done.1.refs_2_), channel_id=1, source_target_pairs={{0,1},{1,0},{2,3},{3,2},{4,5},{5,4},{6,7},{7,6},{8,9},{9,8},{10,11... | collective-permute-start | bytes 884744 | tf_op jit(solution)/shard_map/ppermute | solution.py:217
  33.2 13.4 %copy-start.2 = (bf16[256,1024]{1,0:T(8,128)(2,1)S(1)}, bf16[256,1024]{1,0:T(8,128)(2,1)}, u32[]{:S(2)}) copy-start(bf16[256,1024]{1,0:T(8,128)(2,1)} %refs_4_.3) | copy-start | bytes 1572868
  33.2 13.9 %copy-start.23 = (bf16[256,32]{0,1:T(8,128)(2,1)S(1)}, bf16[256,32]{0,1:T(8,128)(2,1)}, u32[]{:S(2)}) copy-start(bf16[256,32]{0,1:T(8,128)(2,1)} %param.30) | copy-start | bytes 49156
  34.2 13.7 %copy-start.17 = (bf16[1024,32]{0,1:T(8,128)(2,1)S(1)}, bf16[1024,32]{0,1:T(8,128)(2,1)}, u32[]{:S(2)}) copy-start(bf16[1024,32]{0,1:T(8,128)(2,1)} %param.32) | copy-start | bytes 196612
  34.2 13.9 %copy-start.18 = (bf16[1024,32]{0,1:T(8,128)(2,1)S(1)}, bf16[1024,32]{0,1:T(8,128)(2,1)}, u32[]{:S(2)}) copy-start(bf16[1024,32]{0,1:T(8,128)(2,1)} %param.34) | copy-start | bytes 196612
  34.9 0.7 copy-start.7
  34.9 0.8 copy-start.8
  35.7 20.3 %copy-start.20 = (bf16[32,1024]{1,0:T(8,128)(2,1)S(1)}, bf16[32,1024]{1,0:T(8,128)(2,1)}, u32[]{:S(2)}) copy-start(bf16[32,1024]{1,0:T(8,128)(2,1)} %param.31) | copy-start | bytes 196612
  35.7 20.3 %copy-start.21 = (bf16[32,1024]{1,0:T(8,128)(2,1)S(1)}, bf16[32,1024]{1,0:T(8,128)(2,1)}, u32[]{:S(2)}) copy-start(bf16[32,1024]{1,0:T(8,128)(2,1)} %param.33) | copy-start | bytes 196612
  35.7 21.5 %copy-start.19 = (bf16[32,1024]{1,0:T(8,128)(2,1)S(1)}, bf16[32,1024]{1,0:T(8,128)(2,1)}, u32[]{:S(2)}) copy-start(bf16[32,1024]{1,0:T(8,128)(2,1)} %param.35) | copy-start | bytes 196612
  45.1 9.3 %collective-permute-start.4 = (bf16[512,256]{1,0:T(8,128)(2,1)}, bf16[512,256]{1,0:T(8,128)(2,1)S(1)}, u32[]{:S(2)}, u32[]{:S(2)}) collective-permute-start(bf16[512,256]{1,0:T(8,128)(2,1)} %get-tuple-element.11.refs_0_), channel_id=1, source_target_pairs={{0,2},{1,3},{2,0},{3,1},{4,6},{5,7},{6,4},{7,5},{8,10},{9,11},{10,... | collective-permute-start | bytes 786440 | tf_op jit(solution)/shard_map/ppermute | solution.py:217
  46.6 11.6 %collective-permute-start.6 = (bf16[256,1024]{1,0:T(8,128)(2,1)S(1)}, bf16[256,1024]{1,0:T(8,128)(2,1)S(1)}, u32[]{:S(2)}, u32[]{:S(2)}) collective-permute-start(bf16[256,1024]{1,0:T(8,128)(2,1)S(1)} %copy-done.2), channel_id=1, source_target_pairs={{0,1},{1,0},{2,3},{3,2},{4,5},{5,4},{6,7},{7,6},{8,9},{9,8},{10,11... | collective-permute-start | bytes 1572872 | tf_op jit(solution)/shard_map/ppermute | solution.py:217
  46.8 11.5 %copy-start.3 = (bf16[256,1024]{1,0:T(8,128)(2,1)}, bf16[256,1024]{1,0:T(8,128)(2,1)S(1)}, u32[]{:S(2)}) copy-start(bf16[256,1024]{1,0:T(8,128)(2,1)S(1)} %collective-permute-done.7.refs_6_) | copy-start | bytes 1572868
  46.8 11.4 %collective-permute-start.8 = (bf16[256,1024]{1,0:T(8,128)(2,1)S(1)}, bf16[256,1024]{1,0:T(8,128)(2,1)S(1)}, u32[]{:S(2)}, u32[]{:S(2)}) collective-permute-start(bf16[256,1024]{1,0:T(8,128)(2,1)S(1)} %collective-permute-done.7.refs_6_), channel_id=1, source_target_pairs={{0,1},{1,0},{2,3},{3,2},{4,5},{5,4},{6,7},{7,6},{8,9},{9,8},{10,11... | collective-permute-start | bytes 1572872 | tf_op jit(solution)/shard_map/ppermute | solution.py:217
  47.4 10.9 %copy-start.9 = (bf16[256,64]{1,0:T(8,128)(2,1)}, bf16[256,64]{1,0:T(8,128)(2,1)S(1)}, u32[]{:S(2)}) copy-start(bf16[256,64]{1,0:T(8,128)(2,1)S(1)} %pad_maximum_fusion.7.refs_8_) | copy-start | bytes 98308
  47.4 8.1 %collective-permute-start.10 = (bf16[256,64]{1,0:T(8,128)(2,1)S(1)}, bf16[256,64]{1,0:T(8,128)(2,1)S(1)}, u32[]{:S(2)}, u32[]{:S(2)}) collective-permute-start(bf16[256,64]{1,0:T(8,128)(2,1)S(1)} %pad_maximum_fusion.7.refs_8_), channel_id=1, source_target_pairs={{0,2},{1,3},{2,0},{3,1},{4,6},{5,7},{6,4},{7,5},{8,10},{9,11},{10,... | collective-permute-start | bytes 98312 | tf_op jit(solution)/shard_map/ppermute | solution.py:217
  48.3 9.9 %collective-permute-start.3 = (bf16[512,256]{1,0:T(8,128)(2,1)}, bf16[512,256]{1,0:T(8,128)(2,1)S(1)}, u32[]{:S(2)}, u32[]{:S(2)}) collective-permute-start(bf16[512,256]{1,0:T(8,128)(2,1)} %get-tuple-element.11.refs_0_), channel_id=1, source_target_pairs={{0,1},{1,0},{2,3},{3,2},{4,5},{5,4},{6,7},{7,6},{8,9},{9,8},{10,11... | collective-permute-start | bytes 786440 | tf_op jit(solution)/shard_map/ppermute | solution.py:217
  54.4 3.8 %copy-start.10 = (bf16[512,256]{1,0:T(8,128)(2,1)}, bf16[512,256]{1,0:T(8,128)(2,1)S(1)}, u32[]{:S(2)}) copy-start(bf16[512,256]{1,0:T(8,128)(2,1)S(1)} %collective-permute-done.4.refs_2_) | copy-start | bytes 786436
  54.4 3.8 %collective-permute-start.5 = (bf16[512,256]{1,0:T(8,128)(2,1)S(1)}, bf16[512,256]{1,0:T(8,128)(2,1)S(1)}, u32[]{:S(2)}, u32[]{:S(2)}) collective-permute-start(bf16[512,256]{1,0:T(8,128)(2,1)S(1)} %collective-permute-done.4.refs_2_), channel_id=1, source_target_pairs={{0,1},{1,0},{2,3},{3,2},{4,5},{5,4},{6,7},{7,6},{8,9},{9,8},{10,11... | collective-permute-start | bytes 786440 | tf_op jit(solution)/shard_map/ppermute | solution.py:217
  55.5 2.8 %copy-start.14 = (bf16[256,64]{1,0:T(8,128)(2,1)}, bf16[256,64]{1,0:T(8,128)(2,1)S(1)}, u32[]{:S(2)}) copy-start(bf16[256,64]{1,0:T(8,128)(2,1)S(1)} %collective-permute-done.10.refs_10_) | copy-start | bytes 98308
  55.5 1.4 %collective-permute-start.9 = (bf16[256,64]{1,0:T(8,128)(2,1)S(1)}, bf16[256,64]{1,0:T(8,128)(2,1)S(1)}, u32[]{:S(2)}, u32[]{:S(2)}) collective-permute-start(bf16[256,64]{1,0:T(8,128)(2,1)S(1)} %pad_maximum_fusion.7.refs_8_), channel_id=1, source_target_pairs={{0,1},{1,0},{2,3},{3,2},{4,5},{5,4},{6,7},{7,6},{8,9},{9,8},{10,11... | collective-permute-start | bytes 98312 | tf_op jit(solution)/shard_map/ppermute | solution.py:217
  56.9 1.4 %copy-start.15 = (bf16[256,64]{1,0:T(8,128)(2,1)}, bf16[256,64]{1,0:T(8,128)(2,1)S(1)}, u32[]{:S(2)}) copy-start(bf16[256,64]{1,0:T(8,128)(2,1)S(1)} %collective-permute-done.9.refs_9_) | copy-start | bytes 98308
  56.9 1.3 %collective-permute-start.11 = (bf16[256,64]{1,0:T(8,128)(2,1)S(1)}, bf16[256,64]{1,0:T(8,128)(2,1)S(1)}, u32[]{:S(2)}, u32[]{:S(2)}) collective-permute-start(bf16[256,64]{1,0:T(8,128)(2,1)S(1)} %collective-permute-done.10.refs_10_), channel_id=1, source_target_pairs={{0,1},{1,0},{2,3},{3,2},{4,5},{5,4},{6,7},{7,6},{8,9},{9,8},{10,11... | collective-permute-start | bytes 98312 | tf_op jit(solution)/shard_map/ppermute | solution.py:217
  58.2 0.6 copy-start.16
  58.2 0.8 copy-start.4
  58.2 1.0 copy-start.5
  58.2 1.0 %copy-start.11 = (bf16[512,256]{1,0:T(8,128)(2,1)}, bf16[512,256]{1,0:T(8,128)(2,1)S(1)}, u32[]{:S(2)}) copy-start(bf16[512,256]{1,0:T(8,128)(2,1)S(1)} %collective-permute-done.3.refs_1_) | copy-start | bytes 786436
  58.2 1.1 %copy-start.12 = (bf16[512,256]{1,0:T(8,128)(2,1)}, bf16[512,256]{1,0:T(8,128)(2,1)S(1)}, u32[]{:S(2)}) copy-start(bf16[512,256]{1,0:T(8,128)(2,1)S(1)} %collective-permute-done.5.refs_3_) | copy-start | bytes 786436
  71.1 2.1 %collective-permute-start.12 = (bf16[2,128,1024]{2,1,0:T(8,128)(2,1)}, bf16[2,128,1024]{2,1,0:T(8,128)(2,1)S(1)}, u32[]{:S(2)}, u32[]{:S(2)}) collective-permute-start(bf16[2,128,1024]{2,1,0:T(8,128)(2,1)} %get-tuple-element.15), channel_id=1, source_target_pairs={{0,1},{1,0},{2,3},{3,2},{4,5},{5,4},{6,7},{7,6},{8,9},{9,8},{10,11... | collective-permute-start | bytes 1572872 | tf_op jit(solution)/shard_map/ppermute | solution.py:217
  73.2 9.9 %copy-start.1 = (bf16[2,128,1024]{2,1,0:T(8,128)(2,1)}, bf16[2,128,1024]{2,1,0:T(8,128)(2,1)S(1)}, u32[]{:S(2)}) copy-start(bf16[2,128,1024]{2,1,0:T(8,128)(2,1)S(1)} %collective-permute-done.12.got) | copy-start | bytes 1572868
  74.5 8.6 %collective-permute-start.13 = (bf16[128,1024]{1,0:T(8,128)(2,1)S(1)}, bf16[128,1024]{1,0:T(8,128)(2,1)S(1)}, u32[]{:S(2)}, u32[]{:S(2)}) collective-permute-start(bf16[128,1024]{1,0:T(8,128)(2,1)S(1)} %fusion), channel_id=1, source_target_pairs={{0,2},{1,3},{2,0},{3,1},{4,6},{5,7},{6,4},{7,5},{8,10},{9,11},{10,... | collective-permute-start | bytes 786440 | tf_op jit(solution)/shard_map/ppermute | solution.py:217
  83.1 0.7 copy-start.13

commit v2 on v1

v2 whole, which is shorter than its diff:
```python
import functools

import jax
import jax.numpy as jnp
from jax import lax
from jax.experimental import pallas as pl
from jax.experimental.pallas import tpu as pltpu
from jax.sharding import PartitionSpec as P

HEAD_DIM = 64
RANK = 16
ADAPT_DEV = 2
CAP = 64
SEQ_G = 4
SPAN = ADAPT_DEV * RANK
PAD = 8
NORM_EPS = 1e-05
BF = jnp.bfloat16
F32 = jnp.float32
VMEM_LIMIT = 56 * 1024 * 1024


def dot(a, b):
    return lax.dot_general(a, b, (((1,), (0,)), ((), ())), preferred_element_type=F32)


def dot_t(a, b):
    return lax.dot_general(a, b, (((1,), (1,)), ((), ())), preferred_element_type=F32)


def layer_norm(values, gain, shift):
    mean = jnp.mean(values, axis=-1, keepdims=True)
    centred = values - mean
    variance = jnp.mean(centred * centred, axis=-1, keepdims=True)
    return centred * lax.rsqrt(variance + NORM_EPS) * gain + shift


def split_low(low, sel):
    low = low * sel
    high = low.astype(BF).astype(F32)
    return jnp.concatenate([high, low - high], axis=1).astype(BF)


def pack_kernel(n_y, lengths_in, ids_in, slots, tok, out, owners, lengths, ids, sems):
    copies = [
        pltpu.make_async_copy(lengths_in, lengths, sems.at[0]),
        pltpu.make_async_copy(ids_in, ids, sems.at[1]),
    ]
    for c in copies:
        c.start()
    blocks = tok.shape[0]
    if out.shape[0] > blocks:
        out[...] = jnp.zeros(out.shape, out.dtype)
    width = out.shape[3]
    pos = lax.broadcasted_iota(jnp.int32, (PAD, width), 1) % CAP
    for c in copies:
        c.wait()
    for g in range(blocks):
        slot = [slots[ids[g, k]] for k in range(SEQ_G)]
        owner = slot[0] // ADAPT_DEV
        owners[g] = owner
        code = jnp.full((PAD, width), 1 + slot[0] % ADAPT_DEV, jnp.int32)
        end = jnp.int32(0)
        for k in range(1, SEQ_G):
            end = end + lengths[g, k - 1]
            code = jnp.where(pos >= end, 1 + k * ADAPT_DEV + slot[k] % ADAPT_DEV, code)
        code = code.astype(F32).astype(BF)
        for y in range(n_y):
            out[owner, y, :CAP, :] = tok[g]
            out[owner, y, CAP:, :] = code


def attn_kernel(n_y, me, mine, other, w, down, up, att, sel_out, x_full, up_all):
    blocks = mine.shape[0]
    width = mine.shape[3]
    rows = blocks * CAP
    core = me[0] % 2
    for y in range(n_y):
        for piece, c in ((mine, core), (other, 1 - core)):
            start = pl.multiple_of((2 * y + c) * width, width)
            x_full[:, pl.ds(start, width)] = piece[:, y, :CAP, :].reshape(rows, width)
    up_all[...] = jnp.zeros(up_all.shape, BF)
    for k in range(3):
        for part in range(2):
            first_row = (3 * part + k) * SPAN
            up_all[first_row : first_row + SPAN, k * width : (k + 1) * width] = up[k]
    downs = jnp.concatenate([down[0], down[1], down[2]], axis=1)
    pair_lane = lax.broadcasted_iota(jnp.int32, (2 * CAP, 2 * CAP), 1)
    pair_row = lax.broadcasted_iota(jnp.int32, (2 * CAP, 2 * CAP), 0)
    eye = pair_lane == pair_row
    lane_sel = ((pair_lane // RANK) % ADAPT_DEV).astype(F32)
    first = pair_lane < HEAD_DIM
    zero = jnp.zeros((), BF)
    tile = min(4, blocks)
    for t in range(blocks // tile):
        base = t * tile * CAP
        masks, sels = [], []
        for p in range(t * tile // 2, (t + 1) * tile // 2):
            c0 = mine[2 * p, 0, CAP : CAP + 1, : 2 * CAP].astype(F32)
            c1 = mine[2 * p + 1, 0, CAP : CAP + 1, : 2 * CAP].astype(F32) + 64.0
            idr = jnp.where(pair_lane < CAP, c0, c1)
            idc = jnp.sum(jnp.where(eye, idr, 0.0), axis=1, keepdims=True)
            masks.append(idr == idc)
            pick = idc - 1.0
            pick = pick - 2.0 * jnp.floor(pick * 0.5)
            sels.append((lane_sel == pick).astype(F32))
        sel = jnp.concatenate(sels, axis=0)
        rs = slice(base, base + tile * CAP)
        sel_out[rs] = sel.astype(BF)
        x = x_full[rs]
        low = split_low(dot(x, downs), sel[:, : 3 * SPAN])
        q, k_, v = [
            dot(x, w[k]) + dot(low, up_all[:, k * width : (k + 1) * width]) for k in range(3)
        ]
        q = (q.astype(BF).astype(F32) * HEAD_DIM**-0.5).astype(BF)
        k_, v = k_.astype(BF), v.astype(BF)
        for p in range(tile // 2):
            prs = slice(p * 2 * CAP, (p + 1) * 2 * CAP)
            out_rows = slice(base + p * 2 * CAP, base + (p + 1) * 2 * CAP)
            for h in range(width // (2 * HEAD_DIM)):
                cs = slice(h * 2 * HEAD_DIM, (h + 1) * 2 * HEAD_DIM)
                both = []
                for half in (first, ~first):
                    s = dot_t(jnp.where(half, q[prs, cs], zero), k_[prs, cs])
                    s = jnp.where(masks[p], s, -1e30)
                    e = jnp.exp(s - jnp.max(s, axis=-1, keepdims=True))
                    inv = 1.0 / jnp.sum(e, axis=-1, keepdims=True)
                    both.append(dot((e * inv).astype(BF), v[prs, cs]))
                att[out_rows, cs] = jnp.where(first, *both).astype(BF)


def ffn_kernel(n_tp, me, *refs):
    atts, wouts, odowns = refs[:n_tp], refs[n_tp : 2 * n_tp], refs[2 * n_tp : 3 * n_tp]
    (x, sel_in, oup, w1, d1, u1, w2, d2, u2, g1, b1, even, odd, h_own, h_scr) = refs[3 * n_tp :]
    rows, feat = x.shape
    blocks = rows // CAP
    share = CAP // n_tp
    tp = me[0]
    step = min(rows, 256)
    ups = [jnp.concatenate([u[...], u[...]], axis=0) for u in (oup, u1, u2)]
    for r0 in range(0, rows, step):
        rs = slice(r0, r0 + step)
        nb = step // CAP
        sel = sel_in[rs].astype(F32)[:, :SPAN]
        total = x[rs].astype(F32)
        low = None
        for r in range(n_tp):
            a = atts[r][rs]
            total = total + dot(a, wouts[r][...])
            part = dot(a, odowns[r][...])
            low = part if low is None else low + part
        total = total + dot(split_low(low, sel), ups[0])
        h1 = layer_norm(total, g1[...], b1[...]).astype(BF)
        h_scr[r0 // CAP : r0 // CAP + nb] = h1.reshape(nb, n_tp, share, feat)
        gate = dot(h1, w1[...]) + dot(split_low(dot(h1, d1[...]), sel), ups[1])
        hidden = (0.5 * gate * (1.0 + lax.erf(gate * 0.7071067811865476))).astype(BF)
        term = dot(hidden, w2[...]) + dot(split_low(dot(hidden, d2[...]), sel), ups[2])
        term = term.reshape(nb, n_tp, share, feat)
        own_rows = slice(r0 // n_tp, (r0 + step) // n_tp)
        for j in range(n_tp):
            rel = tp ^ j
            piece = term[:, j].reshape(nb * share, feat)

            @pl.when(rel % 2 == 0)
            def _():
                even[rel // 2, own_rows, :] = piece

            @pl.when(rel % 2 == 1)
            def _():
                odd[rel // 2, own_rows, :] = piece.astype(BF)

    h_own[...] = h_scr[:, tp].reshape(blocks * share, feat)


def last_kernel(n_tp, even, got, *refs):
    arrived, (h_own, g2, b2, out) = refs[: n_tp // 2 - 1], refs[n_tp // 2 - 1 :]
    total = h_own[...].astype(F32) + (even[0] + got[0].astype(F32))
    for a in arrived:
        total = total + a[...].astype(F32)
    done = layer_norm(total, g2[...], b2[...]).astype(BF)
    n, _, share, width = out.shape
    for f in range(n_tp):
        out[:, f] = done[:, f * width : (f + 1) * width].reshape(n, share, width)


def unpack_kernel(owners, arrived, out, sems):
    copies = [
        pltpu.make_async_copy(arrived.at[owners[g]], out.at[g], sems.at[g])
        for g in range(out.shape[0])
    ]
    for c in copies:
        c.start()
    for c in copies:
        c.wait()


def whole(shape):
    zeros = (0,) * len(shape)
    return pl.BlockSpec(tuple(shape), lambda *_: zeros)


vm = pl.BlockSpec(memory_space=pltpu.VMEM)
ANY = pl.BlockSpec(memory_space=pl.ANY)
SMEM = pl.BlockSpec(memory_space=pltpu.SMEM)


def params():
    return pltpu.CompilerParams(vmem_limit_bytes=VMEM_LIMIT)


def body(
    tokens,
    prompt_lengths,
    adapter_ids,
    adapter_slot,
    w_qkv,
    w_out,
    w_fc1,
    w_fc2,
    qkv_down,
    qkv_up,
    out_down,
    out_up,
    fc1_down,
    fc1_up,
    fc2_down,
    fc2_up,
    norm1_gain,
    norm1_bias,
    norm2_gain,
    norm2_bias,
):
    n_req = lax.axis_size("req")
    n_tp = lax.axis_size("tp")
    feat = w_qkv.shape[1]
    width = tokens.shape[1]
    blocks = tokens.shape[0] // CAP
    share = CAP // n_tp
    half = n_tp // 2
    me = jnp.reshape(lax.axis_index("tp"), (1,)).astype(jnp.int32)

    def swap(value, r):
        return lax.ppermute(value, "tp", [(i, i ^ r) for i in range(n_tp)])

    def gather(value):
        far = [value] + [swap(value, 2 * y) for y in range(1, n_tp // 2)]
        found = []
        for piece in far:
            found += [piece, swap(piece, 1)]
        return found

    groups = [
        [(r * half + y) * 2 + c for r in range(n_req) for y in range(half)] for c in range(2)
    ]
    packed, owners = pl.pallas_call(
        functools.partial(pack_kernel, half),
        out_shape=(
            jax.ShapeDtypeStruct((n_req, half, CAP + PAD, width), BF),
            jax.ShapeDtypeStruct((blocks,), jnp.int32),
        ),
        in_specs=[ANY, ANY, SMEM, vm],
        out_specs=(vm, SMEM),
        scratch_shapes=[
            pltpu.SMEM(prompt_lengths.shape, jnp.int32),
            pltpu.SMEM(adapter_ids.shape, jnp.int32),
            pltpu.SemaphoreType.DMA((2,)),
        ],
        name="pack",
    )(prompt_lengths, adapter_ids, adapter_slot, tokens.reshape(blocks, CAP, width))
    mine = lax.all_to_all(
        packed.reshape(n_req * half, CAP + PAD, width),
        ("req", "tp"),
        split_axis=0,
        concat_axis=0,
        tiled=True,
        axis_index_groups=groups,
    ).reshape(n_req, half, CAP + PAD, width)
    other = swap(mine, 1)
    wouts = gather(w_out)
    odowns = gather(out_down)

    step_blocks = min(n_req, 8)
    steps = n_req // step_blocks
    step_rows = step_blocks * CAP
    rows = n_req * CAP

    def by_rows(cols):
        return pl.BlockSpec((step_rows, cols), lambda i: (i, 0))

    by_block = pl.BlockSpec((step_blocks, half, CAP + PAD, width), lambda i: (i, 0, 0, 0))
    attended, sel, x_full = pl.pallas_call(
        functools.partial(attn_kernel, half),
        grid=(steps,),
        out_shape=(
            jax.ShapeDtypeStruct((rows, width), BF),
            jax.ShapeDtypeStruct((rows, 4 * SPAN), BF),
            jax.ShapeDtypeStruct((rows, feat), BF),
        ),
        in_specs=[SMEM, by_block, by_block]
        + [whole(w_qkv.shape), whole(qkv_down.shape), whole(qkv_up.shape)],
        out_specs=(by_rows(width), by_rows(4 * SPAN), by_rows(feat)),
        scratch_shapes=[pltpu.VMEM((6 * SPAN, 3 * width), BF)],
        compiler_params=params(),
        name="attend",
    )(me, mine, other, w_qkv, qkv_down, qkv_up)

    atts = gather(attended)
    g1, b1 = norm1_gain[None], norm1_bias[None]
    own = rows // n_tp
    step_own = step_rows // n_tp
    consts = [out_up, w_fc1, fc1_down, fc1_up, w_fc2, fc2_down, fc2_up, g1, b1]
    even, odd, h_own = pl.pallas_call(
        functools.partial(ffn_kernel, n_tp),
        grid=(steps,),
        out_shape=(
            jax.ShapeDtypeStruct((half, own, feat), F32),
            jax.ShapeDtypeStruct((half, own, feat), BF),
            jax.ShapeDtypeStruct((own, feat), BF),
        ),
        in_specs=[SMEM]
        + [by_rows(width)] * n_tp
        + [whole(w.shape) for w in wouts + odowns]
        + [by_rows(feat), by_rows(4 * SPAN)]
        + [whole(c.shape) for c in consts],
        out_specs=(
            pl.BlockSpec((half, step_own, feat), lambda i: (0, i, 0)),
            pl.BlockSpec((half, step_own, feat), lambda i: (0, i, 0)),
            pl.BlockSpec((step_own, feat), lambda i: (i, 0)),
        ),
        scratch_shapes=[pltpu.VMEM((step_blocks, n_tp, share, feat), BF)],
        compiler_params=params(),
        name="feed",
    )(me, *atts, *wouts, *odowns, x_full, sel, *consts)

    got = swap(odd, 1)
    sums = [
        swap((even[y] + got[y].astype(F32)).astype(BF), 2 * y) for y in range(1, half)
    ]
    done = pl.pallas_call(
        functools.partial(last_kernel, n_tp),
        out_shape=jax.ShapeDtypeStruct((n_req, n_tp, share, width), BF),
        grid=(1,),
        in_specs=[whole((1, own, feat)), whole((1, own, feat))]
        + [whole((own, feat))] * (1 + len(sums))
        + [whole((1, feat))] * 2,
        out_specs=whole((n_req, n_tp, share, width)),
        compiler_params=params(),
        name="finish",
    )(even, got, *sums, h_own, norm2_gain[None], norm2_bias[None])
    back = lax.all_to_all(
        done.reshape(n_req * n_tp, share, width),
        ("req", "tp"),
        split_axis=0,
        concat_axis=0,
        tiled=True,
    )
    result = pl.pallas_call(
        unpack_kernel,
        out_shape=jax.ShapeDtypeStruct((blocks, CAP, width), BF),
        in_specs=[SMEM, ANY],
        out_specs=ANY,
        scratch_shapes=[pltpu.SemaphoreType.DMA((blocks,))],
        name="unpack",
    )(owners, back.reshape(n_req, CAP, width))
    return result.reshape(blocks * CAP, width)


def solution(mesh):
    placed = (
        P("req", "tp"),
        P("req", None),
        P("req", None),
        P(),
        P(None, None, "tp"),
        P("tp", None),
        P(None, "tp"),
        P("tp", None),
        P(None, None, "req"),
        P(None, "req", "tp"),
        P("tp", "req"),
        P("req", None),
        P(None, "req"),
        P("req", "tp"),
        P("tp", "req"),
        P("req", None),
        P(),
        P(),
        P(),
        P(),
    )
    return jax.shard_map(
        body, mesh=mesh, in_specs=placed, out_specs=P("req", "tp"), check_vma=False
    )
```

time: 102 us -> 125 us (1.23)
  waiting for transfers between devices: 23.2 us -> 34.7 us
  Pallas kernels: 27.2 us -> 36.1 us
  blocking collectives: 31.5 us -> 39.7 us
  other arithmetic: 5.64 us -> 1.28 us
  starting transfers between devices: 7.5 us -> 3.34 us
  local copies, waits for them, and re-layouts: 6.73 us -> 9.22 us
    ppermute x14 -> x12, waiting for transfers between devices: 23.2 us -> 34.7 us  [swap(): return lax.ppermute(value, 'tp', [(i, i ^ r) for i in range(n_tp)])]
    all_to_all x1, blocking collectives: 17.6 us -> 25.8 us  [body(): lax.all_to_all(packed.reshape(n_req * half, CAP + PAD, width), ('req', 't...]
    pallas_call x1, Pallas kernels: 1.71 us -> 9.78 us  [body(): pl.pallas_call(unpack_kernel, out_shape=jax.ShapeDtypeStruct((blocks, CAP...]
    concatenate x6 -> x0, other arithmetic: 4.36 us -> none  [twice(): return jnp.concatenate([value, value], axis=axis)]
    ppermute x14 -> x12, starting transfers between devices: 7.5 us -> 3.34 us  [swap(): return lax.ppermute(value, 'tp', [(i, i ^ r) for i in range(n_tp)])]
    unnamed x53 -> x40, local copies, waits for them, and re-layouts: 5.74 us -> 9.22 us
  transfers between devices with their start and end apart: 14 -> 12, of which waited for: 6 -> 6; matrix products, arithmetic and copies ran while one was open for 6% -> 3% of each run, Pallas kernels for 9% -> 7%
where the time goes in v2:
time: 125 us
  blocking collectives  39.7 us (32%)
  Pallas kernels  36.1 us (29%)
  waiting for transfers between devices  34.7 us (28%)
  local copies, waits for them, and re-layouts  9.22 us (7%)
  starting transfers between devices  3.34 us (3%)
  other arithmetic  1.28 us (1%)
    ppermute x12, waiting for transfers between devices, swap(): return lax.ppermute(value, 'tp', [(i, i ^ r) for i in range(n_tp)])  34.7 us
    all_to_all x1, blocking collectives, body(): lax.all_to_all(packed.reshape(n_req * half, CAP + PAD, width), ('req', 't...  25.8 us
    all_to_all x1, blocking collectives, body(): lax.all_to_all(done.reshape(n_req * n_tp, share, width), ('req', 'tp'), s...  13.9 us
    pallas_call x1, Pallas kernels, body(): pl.pallas_call(functools.partial(ffn_kernel, n_tp), grid=(steps,), out_sh...  12.2 us
    pallas_call x1, Pallas kernels, body(): pl.pallas_call(unpack_kernel, out_shape=jax.ShapeDtypeStruct((blocks, CAP...  9.78 us
    unnamed x40, local copies, waits for them, and re-layouts  9.22 us
    pallas_call x1, Pallas kernels, body(): pl.pallas_call(functools.partial(attn_kernel, half), grid=(steps,), out_s...  9.14 us
    ppermute x12, starting transfers between devices, swap(): return lax.ppermute(value, 'tp', [(i, i ^ r) for i in range(n_tp)])  3.34 us
  transfers between devices with their start and end apart: 12, of which 6 were waited for; matrix products, arithmetic and copies ran while one was open for 3% of the time, Pallas kernels for 7%

profile of v2, /device:TPU:0, one launch (start us, length us, event | category | flops | bytes accessed | tf_op | source)
XLA Modules:
  0.0 124.5 jit_solution(14645381078385922051)
XLA Ops:
  0.0 1.3 %copy.21.lengths_in = s32[8,4]{1,0:T(8,128)} copy(s32[8,4]{0,1:T(4,128)} %param.21) | data formatting | bytes 256 | tf_op args[1]
  1.3 1.3 %copy.22.ids_in = s32[8,4]{1,0:T(8,128)} copy(s32[8,4]{0,1:T(4,128)} %param.22) | data formatting | bytes 256 | tf_op args[2]
  2.7 2.7 %pack.1 = (bf16[8,2,72,256]{3,2,1,0:T(8,128)(2,1)}, s32[8]{0:T(128)}) custom-call(s32[8,4]{1,0:T(8,128)} %copy.21.lengths_in, s32[8,4]{1,0:T(8,128)} %copy.22.ids_in, s32[16]{0:T(128)} %slots.1, bf16[8,64,256]{2,1,0:T(8,128)(2,1)} %bitcast.18), custom_call_target="tpu_custom_call" | custom-call | tf_op jit(solution)/shard_map/pack/pallas_call | solution.py:255
  5.4 25.8 %all_to_all.10 = bf16[16,72,256]{2,1,0:T(8,128)(2,1)S(1)} all-to-all(bf16[16,72,256]{2,1,0:T(8,128)(2,1)} %bitcast.17), channel_id=1, replica_groups={{0,2,4,6,8,10,12,14,16,18,20,22,24,26,28,30},{1,3,5,7,9,11,13,15,17,19,..., dimensions={0} | all-to-all | bytes 1179648 | tf_op jit(solution)/shard_map/all_to_all | solution.py:270
  31.2 0.0 collective-permute-start
  31.2 0.6 collective-permute-start.5
  31.8 0.2 collective-permute-start.4
  32.0 2.1 %copy.23.down = bf16[3,1024,32]{2,1,0:T(8,128)(2,1)} copy(bf16[3,1024,32]{1,2,0:T(8,128)(2,1)} %param.28) | data formatting | bytes 393216 | tf_op args[8]
  34.1 11.6 %collective-permute-done.5.refs_6_ = bf16[256,1024]{1,0:T(8,128)(2,1)S(1)} collective-permute-done((bf16[256,1024]{1,0:T(8,128)(2,1)}, bf16[256,1024]{1,0:T(8,128)(2,1)S(1)}, u32[]{:S(2)}, u32[]{:S(2)}) %collective-permute-start.5) | collective-permute-done | bytes 524320 | tf_op jit(solution)/shard_map/ppermute | solution.py:243
  45.8 0.0 collective-permute-start.6
  45.8 0.0 collective-permute-done.other
  45.8 0.0 copy-start.2
  45.8 0.8 copy-done.2
  46.6 9.1 %attend.1 = (bf16[512,256]{1,0:T(8,128)(2,1)}, bf16[512,128]{1,0:T(8,128)(2,1)}, bf16[512,1024]{1,0:T(8,128)(2,1)}) custom-call(s32[1]{0:T(128)} %bitcast.1.me, bf16[8,2,72,256]{3,2,1,0:T(8,128)(2,1)} %bitcast.14, bf16[8,2,72,256]{3,2,1,0:T(8,128)(2,1)} %copy-done.2, bf16[3,1024,256]{2,1,0:T(8,128)(2,1)} %w.1, bf16[3,1024,32]{2,1,0:T(8,128)(2,1)} %copy.23.down, ...), custom_call_target="tpu_custom_call" | custom-call | tf_op jit(solution)/shard_map/attend/pallas_call | solution.py:291
  55.8 0.6 collective-permute-start.2
  56.3 0.2 collective-permute-start.1
  56.5 8.1 %collective-permute-done.2.refs_2_ = bf16[512,256]{1,0:T(8,128)(2,1)S(1)} collective-permute-done((bf16[512,256]{1,0:T(8,128)(2,1)}, bf16[512,256]{1,0:T(8,128)(2,1)S(1)}, u32[]{:S(2)}, u32[]{:S(2)}) %collective-permute-start.2) | collective-permute-done | bytes 262176 | tf_op jit(solution)/shard_map/ppermute | solution.py:243
  64.7 0.0 collective-permute-start.3
  64.7 0.1 copy.26.refs_8_
  64.8 0.6 collective-permute-start.8
  65.4 3.9 %collective-permute-done.8.refs_10_ = bf16[256,32]{1,0:T(8,128)(2,1)S(1)} collective-permute-done((bf16[256,32]{1,0:T(8,128)(2,1)S(1)}, bf16[256,32]{1,0:T(8,128)(2,1)S(1)}, u32[]{:S(2)}, u32[]{:S(2)}) %collective-permute-start.8) | collective-permute-done | bytes 16416 | tf_op jit(solution)/shard_map/ppermute | solution.py:243
  69.4 0.0 collective-permute-start.7
  69.4 1.3 %collective-permute-done.7.refs_9_ = bf16[256,32]{1,0:T(8,128)(2,1)S(1)} collective-permute-done((bf16[256,32]{1,0:T(8,128)(2,1)S(1)}, bf16[256,32]{1,0:T(8,128)(2,1)S(1)}, u32[]{:S(2)}, u32[]{:S(2)}) %collective-permute-start.7) | collective-permute-done | bytes 16416 | tf_op jit(solution)/shard_map/ppermute | solution.py:243
  70.6 0.2 collective-permute-start.9
  70.8 0.8 copy.27.refs_16_
  71.6 0.8 copy.28.refs_19_
  72.5 0.0 collective-permute-done.9.refs_11_
  72.5 0.0 collective-permute-done.4.refs_5_
  72.5 0.0 collective-permute-done.6.refs_7_
  72.5 0.0 copy-start.5
  72.5 0.0 collective-permute-done.1.refs_1_
  72.5 0.0 collective-permute-done.3.refs_3_
  72.6 0.5 copy-done.13
  73.1 0.2 copy-done.4
  73.3 0.2 copy-done.5
  73.5 0.1 copy-done.8
  73.6 0.1 copy-done.9
  73.6 12.2 %feed.1 = (f32[2,128,1024]{2,1,0:T(8,128)}, bf16[2,128,1024]{2,1,0:T(8,128)(2,1)}, bf16[128,1024]{1,0:T(8,128)(2,1)}) custom-call(s32[1]{0:T(128)} %bitcast.1.me, bf16[512,256]{1,0:T(8,128)(2,1)} %get-tuple-element.15.refs_0_, bf16[512,256]{1,0:T(8,128)(2,1)} %copy-done.8, bf16[512,256]{1,0:T(8,128)(2,1)} %copy-done.7, bf16[512,256]{1,0:T(8,128)(2,1)} %copy-done.9, ...), custom_call_target="tpu_custom_call" | custom-call | tf_op jit(solution)/shard_map/feed/pallas_call | solution.py:312
  85.8 0.4 collective-permute-start.10
  86.2 1.8 %collective-permute-done.10.got = bf16[2,128,1024]{2,1,0:T(8,128)(2,1)S(1)} collective-permute-done((bf16[2,128,1024]{2,1,0:T(8,128)(2,1)}, bf16[2,128,1024]{2,1,0:T(8,128)(2,1)S(1)}, u32[]{:S(2)}, u32[]{:S(2)}) %collective-permute-start.10) | collective-permute-done | bytes 524320 | tf_op jit(solution)/shard_map/ppermute | solution.py:243
  88.0 1.3 %fusion = bf16[128,1024]{1,0:T(8,128)(2,1)S(1)} fusion(f32[2,128,1024]{2,1,0:T(8,128)} %get-tuple-element.18.even, bf16[2,128,1024]{2,1,0:T(8,128)(2,1)S(1)} %collective-permute-done.10.got), kind=kLoop, calls=%fused_computation.1 | loop fusion | flops 393216 | bytes 1048576 | tf_op jit(solution)/shard_map/convert_element_type | solution.py:337
  89.3 0.6 collective-permute-start.11
  89.9 8.0 %collective-permute-done.11.refs_0_ = bf16[128,1024]{1,0:T(8,128)(2,1)S(1)} collective-permute-done((bf16[128,1024]{1,0:T(8,128)(2,1)S(1)}, bf16[128,1024]{1,0:T(8,128)(2,1)S(1)}, u32[]{:S(2)}, u32[]{:S(2)}) %collective-permute-start.11) | collective-permute-done | bytes 262176 | tf_op jit(solution)/shard_map/ppermute | solution.py:243
  97.9 0.0 copy-done.1
  97.9 0.7 copy-done.10
  98.6 2.3 %finish.1 = bf16[8,4,16,256]{3,2,1,0:T(8,128)(2,1)} custom-call(f32[2,128,1024]{2,1,0:T(8,128)} %get-tuple-element.18.even, bf16[2,128,1024]{2,1,0:T(8,128)(2,1)} %copy-done.1, bf16[128,1024]{1,0:T(8,128)(2,1)} %copy-done.10, bf16[128,1024]{1,0:T(8,128)(2,1)} %get-tuple-element.20.refs_1_, f32[1,1024]{1,0:T(1,128)} %bitcast.21, f32[1,1024]{1,0:T(1,128)} %bitcast.22), custom_call_target="tpu_custom_call" | custom-call | tf_op jit(solution)/shard_map/finish/pallas_call | solution.py:339
  100.9 13.9 %all_to_all.11 = bf16[32,16,256]{2,1,0:T(8,128)(2,1)} all-to-all(bf16[32,16,256]{2,1,0:T(8,128)(2,1)} %bitcast.15), channel_id=1, replica_groups=mesh['req'=8,'tp'=4] {'req','tp'}, dimensions={0} | all-to-all | bytes 524288 | tf_op jit(solution)/shard_map/all_to_all | solution.py:350
  114.7 9.8 %unpack.1 = bf16[8,64,256]{2,1,0:T(8,128)(2,1)} custom-call(s32[8]{0:T(128)} %get-tuple-element.13.owners, bf16[8,64,256]{2,1,0:T(8,128)(2,1)} %bitcast.16), custom_call_target="tpu_custom_call" | custom-call | tf_op jit(solution)/shard_map/unpack/pallas_call | solution.py:357
  (24 shorter events, 0.0 us)
Async XLA Ops:
  31.2 14.6 %copy-start = (bf16[16,72,256]{2,1,0:T(8,128)(2,1)}, bf16[16,72,256]{2,1,0:T(8,128)(2,1)S(1)}, u32[]{:S(2)}) copy-start(bf16[16,72,256]{2,1,0:T(8,128)(2,1)S(1)} %all_to_all.10) | copy-start | bytes 1769476
  31.2 14.6 %collective-permute-start = (bf16[8,2,72,256]{3,2,1,0:T(8,128)(2,1)S(1)}, bf16[8,2,72,256]{3,2,1,0:T(8,128)(2,1)S(1)}, u32[]{:S(2)}, u32[]{:S(2)}) collective-permute-start(bf16[8,2,72,256]{3,2,1,0:T(8,128)(2,1)S(1)} %bitcast.13), channel_id=1, source_target_pairs={{0,1},{1,0},{2,3},{3,2},{4,5},{5,4},{6,7},{7,6},{8,9},{9,8},{10,11... | collective-permute-start | bytes 1769480 | tf_op jit(solution)/shard_map/ppermute | solution.py:243
  31.2 14.5 %collective-permute-start.5 = (bf16[256,1024]{1,0:T(8,128)(2,1)}, bf16[256,1024]{1,0:T(8,128)(2,1)S(1)}, u32[]{:S(2)}, u32[]{:S(2)}) collective-permute-start(bf16[256,1024]{1,0:T(8,128)(2,1)} %refs_4_.1), channel_id=1, source_target_pairs={{0,2},{1,3},{2,0},{3,1},{4,6},{5,7},{6,4},{7,5},{8,10},{9,11},{10,... | collective-permute-start | bytes 1572872 | tf_op jit(solution)/shard_map/ppermute | solution.py:243
  31.8 40.7 %collective-permute-start.4 = (bf16[256,1024]{1,0:T(8,128)(2,1)}, bf16[256,1024]{1,0:T(8,128)(2,1)S(1)}, u32[]{:S(2)}, u32[]{:S(2)}) collective-permute-start(bf16[256,1024]{1,0:T(8,128)(2,1)} %refs_4_.1), channel_id=1, source_target_pairs={{0,1},{1,0},{2,3},{3,2},{4,5},{5,4},{6,7},{7,6},{8,9},{9,8},{10,11... | collective-permute-start | bytes 1572872 | tf_op jit(solution)/shard_map/ppermute | solution.py:243
  32.0 32.7 %copy-start.16 = (bf16[256,32]{0,1:T(8,128)(2,1)S(1)}, bf16[256,32]{0,1:T(8,128)(2,1)}, u32[]{:S(2)}) copy-start(bf16[256,32]{0,1:T(8,128)(2,1)} %param.30) | copy-start | bytes 49156
  32.0 38.8 %copy-start.14 = (bf16[1024,32]{0,1:T(8,128)(2,1)S(1)}, bf16[1024,32]{0,1:T(8,128)(2,1)}, u32[]{:S(2)}) copy-start(bf16[1024,32]{0,1:T(8,128)(2,1)} %param.32) | copy-start | bytes 196612
  34.1 37.5 %copy-start.15 = (bf16[1024,32]{0,1:T(8,128)(2,1)S(1)}, bf16[1024,32]{0,1:T(8,128)(2,1)}, u32[]{:S(2)}) copy-start(bf16[1024,32]{0,1:T(8,128)(2,1)} %param.34) | copy-start | bytes 196612
  45.8 26.8 %copy-start.3 = (bf16[256,1024]{1,0:T(8,128)(2,1)}, bf16[256,1024]{1,0:T(8,128)(2,1)S(1)}, u32[]{:S(2)}) copy-start(bf16[256,1024]{1,0:T(8,128)(2,1)S(1)} %collective-permute-done.5.refs_6_) | copy-start | bytes 1572868
  45.8 26.7 %collective-permute-start.6 = (bf16[256,1024]{1,0:T(8,128)(2,1)S(1)}, bf16[256,1024]{1,0:T(8,128)(2,1)S(1)}, u32[]{:S(2)}, u32[]{:S(2)}) collective-permute-start(bf16[256,1024]{1,0:T(8,128)(2,1)S(1)} %collective-permute-done.5.refs_6_), channel_id=1, source_target_pairs={{0,1},{1,0},{2,3},{3,2},{4,5},{5,4},{6,7},{7,6},{8,9},{9,8},{10,11... | collective-permute-start | bytes 1572872 | tf_op jit(solution)/shard_map/ppermute | solution.py:243
  45.8 0.8 copy-start.2
  55.8 8.9 %collective-permute-start.2 = (bf16[512,256]{1,0:T(8,128)(2,1)}, bf16[512,256]{1,0:T(8,128)(2,1)S(1)}, u32[]{:S(2)}, u32[]{:S(2)}) collective-permute-start(bf16[512,256]{1,0:T(8,128)(2,1)} %get-tuple-element.15.refs_0_), channel_id=1, source_target_pairs={{0,2},{1,3},{2,0},{3,1},{4,6},{5,7},{6,4},{7,5},{8,10},{9,11},{10,... | collective-permute-start | bytes 786440 | tf_op jit(solution)/shard_map/ppermute | solution.py:243
  56.3 16.2 %collective-permute-start.1 = (bf16[512,256]{1,0:T(8,128)(2,1)}, bf16[512,256]{1,0:T(8,128)(2,1)S(1)}, u32[]{:S(2)}, u32[]{:S(2)}) collective-permute-start(bf16[512,256]{1,0:T(8,128)(2,1)} %get-tuple-element.15.refs_0_), channel_id=1, source_target_pairs={{0,1},{1,0},{2,3},{3,2},{4,5},{5,4},{6,7},{7,6},{8,9},{9,8},{10,11... | collective-permute-start | bytes 786440 | tf_op jit(solution)/shard_map/ppermute | solution.py:243
  64.7 7.9 %copy-start.7 = (bf16[512,256]{1,0:T(8,128)(2,1)}, bf16[512,256]{1,0:T(8,128)(2,1)S(1)}, u32[]{:S(2)}) copy-start(bf16[512,256]{1,0:T(8,128)(2,1)S(1)} %collective-permute-done.2.refs_2_) | copy-start | bytes 786436
  64.7 7.9 %collective-permute-start.3 = (bf16[512,256]{1,0:T(8,128)(2,1)S(1)}, bf16[512,256]{1,0:T(8,128)(2,1)S(1)}, u32[]{:S(2)}, u32[]{:S(2)}) collective-permute-start(bf16[512,256]{1,0:T(8,128)(2,1)S(1)} %collective-permute-done.2.refs_2_), channel_id=1, source_target_pairs={{0,1},{1,0},{2,3},{3,2},{4,5},{5,4},{6,7},{7,6},{8,9},{9,8},{10,11... | collective-permute-start | bytes 786440 | tf_op jit(solution)/shard_map/ppermute | solution.py:243
  64.8 7.8 %copy-start.6 = (bf16[256,32]{1,0:T(8,128)(2,1)}, bf16[256,32]{1,0:T(8,128)(2,1)S(1)}, u32[]{:S(2)}) copy-start(bf16[256,32]{1,0:T(8,128)(2,1)S(1)} %copy.26.refs_8_) | copy-start | bytes 49156
  64.8 4.6 %collective-permute-start.8 = (bf16[256,32]{1,0:T(8,128)(2,1)S(1)}, bf16[256,32]{1,0:T(8,128)(2,1)S(1)}, u32[]{:S(2)}, u32[]{:S(2)}) collective-permute-start(bf16[256,32]{1,0:T(8,128)(2,1)S(1)} %copy.26.refs_8_), channel_id=1, source_target_pairs={{0,2},{1,3},{2,0},{3,1},{4,6},{5,7},{6,4},{7,5},{8,10},{9,11},{10,... | collective-permute-start | bytes 49160 | tf_op jit(solution)/shard_map/ppermute | solution.py:243
  69.4 3.2 %copy-start.11 = (bf16[256,32]{1,0:T(8,128)(2,1)}, bf16[256,32]{1,0:T(8,128)(2,1)S(1)}, u32[]{:S(2)}) copy-start(bf16[256,32]{1,0:T(8,128)(2,1)S(1)} %collective-permute-done.8.refs_10_) | copy-start | bytes 49156
  69.4 1.3 %collective-permute-start.7 = (bf16[256,32]{1,0:T(8,128)(2,1)S(1)}, bf16[256,32]{1,0:T(8,128)(2,1)S(1)}, u32[]{:S(2)}, u32[]{:S(2)}) collective-permute-start(bf16[256,32]{1,0:T(8,128)(2,1)S(1)} %copy.26.refs_8_), channel_id=1, source_target_pairs={{0,1},{1,0},{2,3},{3,2},{4,5},{5,4},{6,7},{7,6},{8,9},{9,8},{10,11... | collective-permute-start | bytes 49160 | tf_op jit(solution)/shard_map/ppermute | solution.py:243
  70.6 2.0 %copy-start.12 = (bf16[256,32]{1,0:T(8,128)(2,1)}, bf16[256,32]{1,0:T(8,128)(2,1)S(1)}, u32[]{:S(2)}) copy-start(bf16[256,32]{1,0:T(8,128)(2,1)S(1)} %collective-permute-done.7.refs_9_) | copy-start | bytes 49156
  70.6 1.8 %collective-permute-start.9 = (bf16[256,32]{1,0:T(8,128)(2,1)S(1)}, bf16[256,32]{1,0:T(8,128)(2,1)S(1)}, u32[]{:S(2)}, u32[]{:S(2)}) collective-permute-start(bf16[256,32]{1,0:T(8,128)(2,1)S(1)} %collective-permute-done.8.refs_10_), channel_id=1, source_target_pairs={{0,1},{1,0},{2,3},{3,2},{4,5},{5,4},{6,7},{7,6},{8,9},{9,8},{10,11... | collective-permute-start | bytes 49160 | tf_op jit(solution)/shard_map/ppermute | solution.py:243
  72.5 0.6 copy-start.13
  72.5 0.8 copy-start.4
  72.5 1.0 copy-start.5
  72.5 1.1 copy-start.8
  72.5 1.1 copy-start.9
  85.8 2.1 %collective-permute-start.10 = (bf16[2,128,1024]{2,1,0:T(8,128)(2,1)}, bf16[2,128,1024]{2,1,0:T(8,128)(2,1)S(1)}, u32[]{:S(2)}, u32[]{:S(2)}) collective-permute-start(bf16[2,128,1024]{2,1,0:T(8,128)(2,1)} %get-tuple-element.19), channel_id=1, source_target_pairs={{0,1},{1,0},{2,3},{3,2},{4,5},{5,4},{6,7},{7,6},{8,9},{9,8},{10,11... | collective-permute-start | bytes 1572872 | tf_op jit(solution)/shard_map/ppermute | solution.py:243
  88.0 9.9 %copy-start.1 = (bf16[2,128,1024]{2,1,0:T(8,128)(2,1)}, bf16[2,128,1024]{2,1,0:T(8,128)(2,1)S(1)}, u32[]{:S(2)}) copy-start(bf16[2,128,1024]{2,1,0:T(8,128)(2,1)S(1)} %collective-permute-done.10.got) | copy-start | bytes 1572868
  89.3 8.6 %collective-permute-start.11 = (bf16[128,1024]{1,0:T(8,128)(2,1)S(1)}, bf16[128,1024]{1,0:T(8,128)(2,1)S(1)}, u32[]{:S(2)}, u32[]{:S(2)}) collective-permute-start(bf16[128,1024]{1,0:T(8,128)(2,1)S(1)} %fusion), channel_id=1, source_target_pairs={{0,2},{1,3},{2,0},{3,1},{4,6},{5,7},{6,4},{7,5},{8,10},{9,11},{10,... | collective-permute-start | bytes 786440 | tf_op jit(solution)/shard_map/ppermute | solution.py:243
  97.9 0.7 copy-start.10

commit v3 on v2

v3 whole, which is shorter than its diff:
```python
import functools

import jax
import jax.numpy as jnp
from jax import lax
from jax.experimental import pallas as pl
from jax.experimental.pallas import tpu as pltpu
from jax.sharding import PartitionSpec as P

HEAD_DIM = 64
RANK = 16
ADAPT_DEV = 2
CAP = 64
SEQ_G = 4
SPAN = ADAPT_DEV * RANK
PAD = 8
NORM_EPS = 1e-05
BF = jnp.bfloat16
F32 = jnp.float32


def dot(a, b):
    return lax.dot_general(a, b, (((1,), (0,)), ((), ())), preferred_element_type=F32)


def dot_t(a, b):
    return lax.dot_general(a, b, (((1,), (1,)), ((), ())), preferred_element_type=F32)


def layer_norm(values, gain, shift):
    mean = jnp.mean(values, axis=-1, keepdims=True)
    centred = values - mean
    variance = jnp.mean(centred * centred, axis=-1, keepdims=True)
    return centred * lax.rsqrt(variance + NORM_EPS) * gain + shift


def split_low(low, sel):
    low = low * sel
    high = low.astype(BF).astype(F32)
    return jnp.concatenate([high, low - high], axis=1).astype(BF)


def pack_kernel(lengths_in, ids_in, slots, tok, out, owners, lengths, ids, sems):
    copies = [
        pltpu.make_async_copy(lengths_in, lengths, sems.at[0]),
        pltpu.make_async_copy(ids_in, ids, sems.at[1]),
    ]
    for c in copies:
        c.start()
    blocks = tok.shape[0]
    if out.shape[0] > blocks:
        out[...] = jnp.zeros(out.shape, out.dtype)
    width = out.shape[2]
    pos = lax.broadcasted_iota(jnp.int32, (PAD, width), 1) % CAP
    for c in copies:
        c.wait()
    for g in range(blocks):
        slot = [slots[ids[k, g]] for k in range(SEQ_G)]
        owner = slot[0] // ADAPT_DEV
        owners[g] = owner
        code = jnp.full((PAD, width), 1 + slot[0] % ADAPT_DEV, jnp.int32)
        end = jnp.int32(0)
        for k in range(1, SEQ_G):
            end = end + lengths[k - 1, g]
            code = jnp.where(pos >= end, 1 + k * ADAPT_DEV + slot[k] % ADAPT_DEV, code)
        out[owner, :CAP, :] = tok[g]
        out[owner, CAP:, :] = code.astype(F32).astype(BF)


def tiles(count, step):
    if count <= 2:
        for t in range(count):
            step(t)
    else:
        lax.fori_loop(0, count, lambda t, c: (step(t), c)[1], 0)


def span(start, size):
    return pl.ds(start if isinstance(start, int) else pl.multiple_of(start, size), size)


def attn_kernel(n_tp, me, *refs):
    parts, (w, down, up, att, sel_out, x_full, up_all) = refs[:n_tp], refs[n_tp:]
    blocks = parts[0].shape[0]
    width = parts[0].shape[2]
    rows = blocks * CAP
    tp = me[0]
    for r in range(n_tp):
        x_full[:, span((tp ^ r) * width, width)] = parts[r][:, :CAP, :].reshape(rows, width)
    up_all[...] = jnp.zeros(up_all.shape, BF)
    for k in range(3):
        for part in range(2):
            first_row = (3 * part + k) * SPAN
            up_all[first_row : first_row + SPAN, k * width : (k + 1) * width] = up[k]
    pair_lane = lax.broadcasted_iota(jnp.int32, (2 * CAP, 2 * CAP), 1)
    pair_row = lax.broadcasted_iota(jnp.int32, (2 * CAP, 2 * CAP), 0)
    eye = pair_lane == pair_row
    lane_sel = ((pair_lane // RANK) % ADAPT_DEV).astype(F32)
    first = pair_lane < HEAD_DIM
    zero = jnp.zeros((), BF)
    tile = min(4, blocks)

    def step(t):
        rs = span(t * (tile * CAP), tile * CAP)
        masks, sels = [], []
        for p in range(tile // 2):
            b0 = t * tile + 2 * p
            c0 = parts[0][b0, CAP : CAP + 1, : 2 * CAP].astype(F32)
            c1 = parts[0][b0 + 1, CAP : CAP + 1, : 2 * CAP].astype(F32) + 64.0
            idr = jnp.where(pair_lane < CAP, c0, c1)
            idc = jnp.sum(jnp.where(eye, idr, 0.0), axis=1, keepdims=True)
            masks.append(idr == idc)
            pick = idc - 1.0
            pick = pick - 2.0 * jnp.floor(pick * 0.5)
            sels.append((lane_sel == pick).astype(F32))
        sel = jnp.concatenate(sels, axis=0)
        sel_out[rs] = sel.astype(BF)
        x = x_full[rs]
        low = split_low(dot_t(x, down[...]), sel[:, : 3 * SPAN])
        q, k_, v = [
            dot(x, w[k]) + dot(low, up_all[:, k * width : (k + 1) * width]) for k in range(3)
        ]
        q = (q.astype(BF).astype(F32) * HEAD_DIM**-0.5).astype(BF)
        k_, v = k_.astype(BF), v.astype(BF)
        for p in range(tile // 2):
            prs = slice(p * 2 * CAP, (p + 1) * 2 * CAP)
            out_rows = span(t * (tile * CAP) + p * 2 * CAP, 2 * CAP)
            for h in range(width // (2 * HEAD_DIM)):
                cs = slice(h * 2 * HEAD_DIM, (h + 1) * 2 * HEAD_DIM)
                both = []
                for half in (first, ~first):
                    s = dot_t(jnp.where(half, q[prs, cs], zero), k_[prs, cs])
                    s = jnp.where(masks[p], s, -1e30)
                    e = jnp.exp(s - jnp.max(s, axis=-1, keepdims=True))
                    inv = 1.0 / jnp.sum(e, axis=-1, keepdims=True)
                    both.append(dot((e * inv).astype(BF), v[prs, cs]))
                att[out_rows, cs] = jnp.where(first, *both).astype(BF)

    tiles(blocks // tile, step)


def ffn_kernel(n_tp, me, *refs):
    atts, wouts, odowns = refs[:n_tp], refs[n_tp : 2 * n_tp], refs[2 * n_tp : 3 * n_tp]
    (x, sel_in, oup, w1, d1, u1, w2, d2, u2, g1, b1, even, odd, h_own, h_scr) = refs[3 * n_tp :]
    rows, feat = x.shape
    blocks = rows // CAP
    share = CAP // n_tp
    tp = me[0]
    size = min(rows, 256)
    nb = size // CAP
    ups = [jnp.concatenate([u[...], u[...]], axis=0) for u in (oup, u1, u2)]

    def step(t):
        rs = span(t * size, size)
        sel = sel_in[rs].astype(F32)[:, :SPAN]
        total = x[rs].astype(F32)
        low = None
        for r in range(n_tp):
            a = atts[r][rs]
            total = total + dot(a, wouts[r][...])
            part = dot_t(a, odowns[r][...])
            low = part if low is None else low + part
        total = total + dot(split_low(low, sel), ups[0])
        h1 = layer_norm(total, g1[...], b1[...]).astype(BF)
        h_scr[span(t * nb, nb)] = h1.reshape(nb, n_tp, share, feat)
        gate = dot(h1, w1[...]) + dot(split_low(dot_t(h1, d1[...]), sel), ups[1])
        hidden = (0.5 * gate * (1.0 + lax.erf(gate * 0.7071067811865476))).astype(BF)
        term = dot(hidden, w2[...]) + dot(split_low(dot_t(hidden, d2[...]), sel), ups[2])
        term = term.reshape(nb, n_tp, share, feat)
        own_rows = span(t * (size // n_tp), size // n_tp)
        for j in range(n_tp):
            rel = tp ^ j
            piece = term[:, j].reshape(nb * share, feat)

            @pl.when(rel % 2 == 0)
            def _():
                even[rel // 2, own_rows, :] = piece

            @pl.when(rel % 2 == 1)
            def _():
                odd[rel // 2, own_rows, :] = piece.astype(BF)

    tiles(rows // size, step)
    h_own[...] = h_scr[:, tp].reshape(blocks * share, feat)


def last_kernel(n_tp, even, got, *refs):
    arrived, (h_own, g2, b2, out) = refs[: n_tp // 2 - 1], refs[n_tp // 2 - 1 :]
    total = h_own[...].astype(F32) + (even[0] + got[0].astype(F32))
    for a in arrived:
        total = total + a[...].astype(F32)
    done = layer_norm(total, g2[...], b2[...]).astype(BF)
    n, _, share, width = out.shape
    for f in range(n_tp):
        out[:, f] = done[:, f * width : (f + 1) * width].reshape(n, share, width)


def unpack_kernel(owners, arrived, out):
    for g in range(out.shape[0]):
        out[g] = arrived[owners[g]]


VM = pl.BlockSpec(memory_space=pltpu.VMEM)
ANY = pl.BlockSpec(memory_space=pl.ANY)
SMEM = pl.BlockSpec(memory_space=pltpu.SMEM)


def near(*arrays):
    return [pltpu.with_memory_space_constraint(a, pltpu.VMEM) for a in arrays]


def params(mib=20):
    return pltpu.CompilerParams(vmem_limit_bytes=mib * 1024 * 1024)


def body(
    tokens,
    prompt_lengths,
    adapter_ids,
    adapter_slot,
    w_qkv,
    w_out,
    w_fc1,
    w_fc2,
    qkv_down,
    qkv_up,
    out_down,
    out_up,
    fc1_down,
    fc1_up,
    fc2_down,
    fc2_up,
    norm1_gain,
    norm1_bias,
    norm2_gain,
    norm2_bias,
):
    n_req = lax.axis_size("req")
    n_tp = lax.axis_size("tp")
    feat = w_qkv.shape[1]
    width = tokens.shape[1]
    blocks = tokens.shape[0] // CAP
    share = CAP // n_tp
    half = n_tp // 2
    me = jnp.reshape(lax.axis_index("tp"), (1,)).astype(jnp.int32)

    def swap(value, r):
        return lax.ppermute(value, "tp", [(i, i ^ r) for i in range(n_tp)])

    def gather(value):
        far = [value] + [swap(value, 2 * y) for y in range(1, n_tp // 2)]
        found = []
        for piece in far:
            found += [piece, swap(piece, 1)]
        return found

    packed, owners = pl.pallas_call(
        pack_kernel,
        out_shape=(
            pltpu.VMEM((n_req, CAP + PAD, width), BF),
            jax.ShapeDtypeStruct((blocks,), jnp.int32),
        ),
        in_specs=[ANY, ANY, SMEM, VM],
        out_specs=(VM, SMEM),
        scratch_shapes=[
            pltpu.SMEM((SEQ_G, blocks), jnp.int32),
            pltpu.SMEM((SEQ_G, blocks), jnp.int32),
            pltpu.SemaphoreType.DMA((2,)),
        ],
        compiler_params=params(4),
        name="pack",
    )(prompt_lengths.T, adapter_ids.T, adapter_slot, tokens.reshape(blocks, CAP, width))
    arrived = lax.all_to_all(packed, "req", split_axis=0, concat_axis=0, tiled=True)
    w_far = [swap(w_out, 2 * y) for y in range(1, half)]
    o_own = out_down.T
    o_far = [swap(o_own, 2 * y) for y in range(1, half)]
    arrived, w_far, o_far = lax.optimization_barrier((arrived, w_far, o_far))
    parts = gather(arrived)

    rows = n_req * CAP
    attended, sel, x_full = pl.pallas_call(
        functools.partial(attn_kernel, n_tp),
        out_shape=(
            pltpu.VMEM((rows, width), BF),
            pltpu.VMEM((rows, 4 * SPAN), BF),
            pltpu.VMEM((rows, feat), BF),
        ),
        in_specs=[SMEM] + [VM] * (n_tp + 3),
        out_specs=(VM,) * 3,
        scratch_shapes=[pltpu.VMEM((6 * SPAN, 3 * width), BF)],
        compiler_params=params(),
        name="attend",
    )(
        me,
        *near(
            *parts,
            w_qkv,
            jnp.swapaxes(qkv_down, 1, 2).reshape(3 * SPAN, feat),
            qkv_up,
        ),
    )

    atts = gather(attended)
    wouts, odowns = [], []
    for w_piece, o_piece in zip([w_out] + w_far, [o_own] + o_far):
        wouts += [w_piece, swap(w_piece, 1)]
        odowns += [o_piece, swap(o_piece, 1)]
    own = rows // n_tp
    consts = [out_up, w_fc1, fc1_down.T, fc1_up, w_fc2, fc2_down.T, fc2_up]
    consts += [norm1_gain[None], norm1_bias[None]]
    even, odd, h_own = pl.pallas_call(
        functools.partial(ffn_kernel, n_tp),
        out_shape=(
            pltpu.VMEM((half, own, feat), F32),
            pltpu.VMEM((half, own, feat), BF),
            pltpu.VMEM((own, feat), BF),
        ),
        in_specs=[SMEM] + [VM] * (3 * n_tp + 2 + len(consts)),
        out_specs=(VM,) * 3,
        scratch_shapes=[pltpu.VMEM((n_req, n_tp, share, feat), BF)],
        compiler_params=params(),
        name="feed",
    )(me, *near(*atts, *wouts, *odowns, x_full, sel, *consts))

    got = swap(odd, 1)
    sums = [
        swap((even[y] + got[y].astype(F32)).astype(BF), 2 * y) for y in range(1, half)
    ]
    done = pl.pallas_call(
        functools.partial(last_kernel, n_tp),
        out_shape=pltpu.VMEM((n_req, n_tp, share, width), BF),
        in_specs=[VM] * (5 + len(sums)),
        out_specs=VM,
        compiler_params=params(),
        name="finish",
    )(*near(even, got, *sums, h_own, norm2_gain[None], norm2_bias[None]))
    back = lax.all_to_all(
        done.reshape(n_req * n_tp, share, width),
        ("req", "tp"),
        split_axis=0,
        concat_axis=0,
        tiled=True,
    )
    result = pl.pallas_call(
        unpack_kernel,
        out_shape=jax.ShapeDtypeStruct((blocks, CAP, width), BF),
        in_specs=[SMEM, VM],
        out_specs=VM,
        compiler_params=params(4),
        name="unpack",
    )(owners, *near(back.reshape(n_req, CAP, width)))
    return result.reshape(blocks * CAP, width)


def solution(mesh):
    placed = (
        P("req", "tp"),
        P("req", None),
        P("req", None),
        P(),
        P(None, None, "tp"),
        P("tp", None),
        P(None, "tp"),
        P("tp", None),
        P(None, None, "req"),
        P(None, "req", "tp"),
        P("tp", "req"),
        P("req", None),
        P(None, "req"),
        P("req", "tp"),
        P("tp", "req"),
        P("req", None),
        P(),
        P(),
        P(),
        P(),
    )
    return jax.shard_map(
        body, mesh=mesh, in_specs=placed, out_specs=P("req", "tp"), check_vma=False
    )
```

time: 125 us -> 92.8 us (0.74)
  blocking collectives: 39.7 us -> 14.8 us
  Pallas kernels: 36.1 us -> 21.1 us
  starting transfers between devices: 3.34 us -> 12.8 us
  local copies, waits for them, and re-layouts: 9.22 us -> 7.74 us
    all_to_all x1 -> x0, blocking collectives: 25.8 us -> none  [body(): lax.all_to_all(packed.reshape(n_req * half, CAP + PAD, width), ('req', 't...]
    pallas_call x1, Pallas kernels: 9.78 us -> 1.26 us  [body(): pl.pallas_call(unpack_kernel, out_shape=jax.ShapeDtypeStruct((blocks, CAP...]
    pallas_call x4, Pallas kernels: 26.3 us -> 19.8 us  [the longest x1 10.1 us: body(): pl.pallas_call(functools.partial(ffn_kernel, n_tp), out_shape=(pltpu.VMEM...]
    all_to_all x0 -> x1, starting transfers between devices: none -> 5.82 us  [body(): lax.all_to_all(packed, 'req', split_axis=0, concat_axis=0, tiled=True)]
    all_to_all x0 -> x1, waiting for transfers between devices: none -> 5.34 us  [body(): lax.all_to_all(packed, 'req', split_axis=0, concat_axis=0, tiled=True)]
    ppermute x12 -> x14, waiting for transfers between devices: 34.7 us -> 30.3 us  [swap(): return lax.ppermute(value, 'tp', [(i, i ^ r) for i in range(n_tp)])]
    ppermute x12 -> x14, starting transfers between devices: 3.34 us -> 6.99 us  [swap(): return lax.ppermute(value, 'tp', [(i, i ^ r) for i in range(n_tp)])]
    unnamed x40, local copies, waits for them, and re-layouts: 9.22 us -> 7.74 us
  transfers between devices with their start and end apart: 12 -> 15, of which waited for: 6 -> 9; matrix products, arithmetic and copies ran while one was open for 3% -> 0% of each run, Pallas kernels for 7% -> 10%
where the time goes in v3:
time: 92.8 us; the launch traced here: 92.3 us
  waiting for transfers between devices  35.7 us (38%)
  Pallas kernels  21.1 us (23%)
  blocking collectives  14.8 us (16%)
  starting transfers between devices  12.8 us (14%)
  local copies, waits for them, and re-layouts  7.74 us (8%)
    ppermute x14, waiting for transfers between devices, swap(): return lax.ppermute(value, 'tp', [(i, i ^ r) for i in range(n_tp)])  30.3 us
    all_to_all x1, blocking collectives, body(): lax.all_to_all(done.reshape(n_req * n_tp, share, width), ('req', 'tp'), s...  14.8 us
    pallas_call x1, Pallas kernels, body(): pl.pallas_call(functools.partial(ffn_kernel, n_tp), out_shape=(pltpu.VMEM...  10.1 us
    unnamed x40, local copies, waits for them, and re-layouts  7.74 us
    pallas_call x1, Pallas kernels, body(): pl.pallas_call(functools.partial(attn_kernel, n_tp), out_shape=(pltpu.VME...  7.34 us
    ppermute x14, starting transfers between devices, swap(): return lax.ppermute(value, 'tp', [(i, i ^ r) for i in range(n_tp)])  6.99 us
    all_to_all x1, starting transfers between devices, body(): lax.all_to_all(packed, 'req', split_axis=0, concat_axis=0, tiled=True)  5.82 us
    all_to_all x1, waiting for transfers between devices, body(): lax.all_to_all(packed, 'req', split_axis=0, concat_axis=0, tiled=True)  5.34 us
  transfers between devices with their start and end apart: 15, of which 9 were waited for; matrix products, arithmetic and copies ran while one was open for 0% of the time, Pallas kernels for 10%

profile of v3, /device:TPU:0, one launch (start us, length us, event | category | flops | bytes accessed | tf_op | source)
XLA Modules:
  0.0 92.3 jit_solution(16539838509341974758)
XLA Ops:
  0.0 3.0 %collective-permute-start = (bf16[256,1024]{1,0:T(8,128)(2,1)}, bf16[256,1024]{1,0:T(8,128)(2,1)S(1)}, u32[]{:S(2)}, u32[]{:S(2)}) collective-permute-start(bf16[256,1024]{1,0:T(8,128)(2,1)} %refs_4_.3), channel_id=1, source_target_pairs={{0,2},{1,3},{2,0},{3,1},{4,6},{5,7},{6,4},{7,5},{8,10},{9,11},{10,... | collective-permute-start | bytes 1572872 | tf_op jit(solution)/shard_map/ppermute | solution.py:248
  3.0 0.9 %copy-done.4 = bf16[512,256]{1,0:T(8,128)(2,1)S(1)} copy-done((bf16[512,256]{1,0:T(8,128)(2,1)S(1)}, bf16[512,256]{1,0:T(8,128)(2,1)}, u32[]{:S(2)}) %copy-start.4) | copy-done | bytes 262168
  3.9 0.7 copy-done.17
  4.6 0.7 copy-done.18
  5.3 0.7 copy-done.19
  5.9 2.0 %pack.1 = (bf16[8,72,256]{2,1,0:T(8,128)(2,1)}, s32[8]{0:T(128)S(1)}) custom-call(s32[4,8]{1,0:T(4,128)S(1)} %bitcast.32, s32[4,8]{1,0:T(4,128)S(1)} %bitcast.33, s32[16]{0:T(128)S(1)} %copy-done.19, bf16[8,64,256]{2,1,0:T(8,128)(2,1)S(1)} %bitcast.21), custom_call_target="tpu_custom_call" | custom-call | tf_op jit(solution)/shard_map/pack/pallas_call | solution.py:257
  8.0 5.8 %all-to-all-start = ((bf16[8,72,256]{2,1,0:T(8,128)(2,1)}), bf16[8,72,256]{2,1,0:T(8,128)(2,1)S(1)}, u32[]{:S(2)}, u32[]{:S(2)}) async-start(bf16[8,72,256]{2,1,0:T(8,128)(2,1)} %get-tuple-element.17), calls=%async_computation | async-start | bytes 589824 | tf_op jit(solution)/shard_map/all_to_all | solution.py:273
  13.8 0.6 collective-permute-start.1
  14.4 3.3 %collective-permute-done.1.refs_10_ = bf16[32,256]{1,0:T(8,128)(2,1)S(1)} collective-permute-done((bf16[32,256]{1,0:T(8,128)(2,1)}, bf16[32,256]{1,0:T(8,128)(2,1)S(1)}, u32[]{:S(2)}, u32[]{:S(2)}) %collective-permute-start.1) | collective-permute-done | bytes 16416 | tf_op jit(solution)/shard_map/ppermute | solution.py:248
  17.7 5.3 %all-to-all-done.refs_0_ = bf16[8,72,256]{2,1,0:T(8,128)(2,1)S(1)} async-done(((bf16[8,72,256]{2,1,0:T(8,128)(2,1)}), bf16[8,72,256]{2,1,0:T(8,128)(2,1)S(1)}, u32[]{:S(2)}, u32[]{:S(2)}) %all-to-all-start) | async-done | bytes 294944 | tf_op jit(solution)/shard_map/all_to_all | solution.py:273
  23.1 0.0 collective-permute-done.refs_6_
  23.1 0.6 collective-permute-start.3
  23.7 0.0 collective-permute-start.2
  23.7 6.2 %collective-permute-done.3.refs_2_ = bf16[8,72,256]{2,1,0:T(8,128)(2,1)} collective-permute-done((bf16[8,72,256]{2,1,0:T(8,128)(2,1)S(1)}, bf16[8,72,256]{2,1,0:T(8,128)(2,1)}, u32[]{:S(2)}, u32[]{:S(2)}) %collective-permute-start.3) | collective-permute-done | bytes 294944 | tf_op jit(solution)/shard_map/ppermute | solution.py:248
  29.9 0.0 collective-permute-start.4
  29.9 0.5 collective-permute-start.8
  30.4 0.0 collective-permute-start.9
  30.4 0.0 collective-permute-done.2.refs_1_
  30.4 1.5 %collective-permute-done.4.refs_3_ = bf16[8,72,256]{2,1,0:T(8,128)(2,1)} collective-permute-done((bf16[8,72,256]{2,1,0:T(8,128)(2,1)}, bf16[8,72,256]{2,1,0:T(8,128)(2,1)}, u32[]{:S(2)}, u32[]{:S(2)}) %collective-permute-start.4) | collective-permute-done | bytes 294944 | tf_op jit(solution)/shard_map/ppermute | solution.py:248
  31.9 1.4 %copy-done.2 = bf16[3,1024,256]{2,1,0:T(8,128)(2,1)S(1)} copy-done((bf16[3,1024,256]{2,1,0:T(8,128)(2,1)S(1)}, bf16[3,1024,256]{2,1,0:T(8,128)(2,1)}, u32[]{:S(2)}) %copy-start.2) | copy-done | bytes 1572888
  33.3 0.9 %copy-done.5 = bf16[3,1024,32]{1,2,0:T(8,128)(2,1)S(1)} copy-done((bf16[3,1024,32]{1,2,0:T(8,128)(2,1)S(1)}, bf16[3,1024,32]{1,2,0:T(8,128)(2,1)}, u32[]{:S(2)}) %copy-start.5) | copy-done | bytes 196632
  34.2 0.8 copy-done.11
  35.0 0.0 copy-start.8
  35.1 0.0 copy-start.9
  35.1 0.0 copy-start.10
  35.1 0.0 copy-start.13
  35.1 0.0 copy-start.14
  35.1 7.3 %attend.1 = (bf16[512,256]{1,0:T(8,128)(2,1)S(1)}, bf16[512,128]{1,0:T(8,128)(2,1)S(1)}, bf16[512,1024]{1,0:T(8,128)(2,1)S(1)}) custom-call(s32[1]{0:T(128)} %bitcast.3.me, bf16[8,72,256]{2,1,0:T(8,128)(2,1)S(1)} %all-to-all-done.refs_0_, bf16[8,72,256]{2,1,0:T(8,128)(2,1)} %collective-permute-done.2.refs_1_, ...), custom_call_target="tpu_custom_call" | custom-call | tf_op jit(solution)/shard_map/attend/pallas_call | solution.py:281
  42.4 0.7 collective-permute-start.6
  43.1 0.0 collective-permute-start.5
  43.1 7.7 %collective-permute-done.6.refs_2_ = bf16[512,256]{1,0:T(8,128)(2,1)S(1)} collective-permute-done((bf16[512,256]{1,0:T(8,128)(2,1)S(1)}, bf16[512,256]{1,0:T(8,128)(2,1)S(1)}, u32[]{:S(2)}, u32[]{:S(2)}) %collective-permute-start.6) | collective-permute-done | bytes 262176 | tf_op jit(solution)/shard_map/ppermute | solution.py:248
  50.9 0.0 collective-permute-start.7
  50.9 0.5 collective-permute-start.10
  51.4 1.0 %collective-permute-done.10.refs_9_ = bf16[32,256]{1,0:T(8,128)(2,1)S(1)} collective-permute-done((bf16[32,256]{1,0:T(8,128)(2,1)S(1)}, bf16[32,256]{1,0:T(8,128)(2,1)S(1)}, u32[]{:S(2)}, u32[]{:S(2)}) %collective-permute-start.10) | collective-permute-done | bytes 16416 | tf_op jit(solution)/shard_map/ppermute | solution.py:248
  52.4 0.1 collective-permute-start.11
  52.6 0.0 collective-permute-done.8.refs_5_
  52.6 1.0 %collective-permute-done.11.refs_11_ = bf16[32,256]{1,0:T(8,128)(2,1)S(1)} collective-permute-done((bf16[32,256]{1,0:T(8,128)(2,1)S(1)}, bf16[32,256]{1,0:T(8,128)(2,1)S(1)}, u32[]{:S(2)}, u32[]{:S(2)}) %collective-permute-start.11) | collective-permute-done | bytes 16416 | tf_op jit(solution)/shard_map/ppermute | solution.py:248
  53.7 0.0 copy-start.1
  53.7 1.6 %copy-done.1 = bf16[1024,1024]{1,0:T(8,128)(2,1)S(1)} copy-done((bf16[1024,1024]{1,0:T(8,128)(2,1)S(1)}, bf16[1024,1024]{1,0:T(8,128)(2,1)}, u32[]{:S(2)}) %copy-start.1) | copy-done | bytes 2097176
  55.3 10.1 %feed.1 = (f32[2,128,1024]{2,1,0:T(8,128)S(1)}, bf16[2,128,1024]{2,1,0:T(8,128)(2,1)S(1)}, bf16[128,1024]{1,0:T(8,128)(2,1)S(1)}) custom-call(s32[1]{0:T(128)} %bitcast.3.me, bf16[512,256]{1,0:T(8,128)(2,1)S(1)} %get-tuple-element.19.refs_0_, bf16[512,256]{1,0:T(8,128)(2,1)S(1)} %collective-permute-done.5.refs_1_, ...), custom_call_target="tpu_custom_call" | custom-call | tf_op jit(solution)/shard_map/feed/pallas_call | solution.py:311
  65.4 0.2 collective-permute-start.12
  65.7 1.7 %collective-permute-done.12.got = bf16[2,128,1024]{2,1,0:T(8,128)(2,1)S(1)} collective-permute-done((bf16[2,128,1024]{2,1,0:T(8,128)(2,1)S(1)}, bf16[2,128,1024]{2,1,0:T(8,128)(2,1)S(1)}, u32[]{:S(2)}, u32[]{:S(2)}) %collective-permute-start.12) | collective-permute-done | bytes 524320 | tf_op jit(solution)/shard_map/ppermute | solution.py:248
  67.4 0.1 fusion
  67.5 0.7 collective-permute-start.13
  68.2 7.8 %collective-permute-done.13.refs_0_ = bf16[128,1024]{1,0:T(8,128)(2,1)S(1)} collective-permute-done((bf16[128,1024]{1,0:T(8,128)(2,1)S(1)}, bf16[128,1024]{1,0:T(8,128)(2,1)S(1)}, u32[]{:S(2)}, u32[]{:S(2)}) %collective-permute-start.13) | collective-permute-done | bytes 262176 | tf_op jit(solution)/shard_map/ppermute | solution.py:248
  75.9 0.3 finish.1
  76.2 14.8 %all_to_all.10 = bf16[32,16,256]{2,1,0:T(8,128)(2,1)S(1)} all-to-all(bf16[32,16,256]{2,1,0:T(8,128)(2,1)S(1)} %bitcast.19), channel_id=1, replica_groups=mesh['req'=8,'tp'=4] {'req','tp'}, dimensions={0} | all-to-all | bytes 524288 | tf_op jit(solution)/shard_map/all_to_all | solution.py:337
  91.1 1.3 %unpack.1 = bf16[8,64,256]{2,1,0:T(8,128)(2,1)} custom-call(s32[8]{0:T(128)S(1)} %get-tuple-element.16.owners, bf16[8,64,256]{2,1,0:T(8,128)(2,1)S(1)} %bitcast.20), custom_call_target="tpu_custom_call" | custom-call | tf_op jit(solution)/shard_map/unpack/pallas_call | solution.py:344
  (29 shorter events, 0.1 us)
Async XLA Ops:
  0.0 53.6 %copy-start = (bf16[1024,1024]{1,0:T(8,128)(2,1)S(1)}, bf16[1024,1024]{1,0:T(8,128)(2,1)}, u32[]{:S(2)}) copy-start(bf16[1024,1024]{1,0:T(8,128)(2,1)} %refs_15_.1) | copy-start | bytes 6291460
  0.0 23.1 %collective-permute-start = (bf16[256,1024]{1,0:T(8,128)(2,1)}, bf16[256,1024]{1,0:T(8,128)(2,1)S(1)}, u32[]{:S(2)}, u32[]{:S(2)}) collective-permute-start(bf16[256,1024]{1,0:T(8,128)(2,1)} %refs_4_.3), channel_id=1, source_target_pairs={{0,2},{1,3},{2,0},{3,1},{4,6},{5,7},{6,4},{7,5},{8,10},{9,11},{10,... | collective-permute-start | bytes 1572872 | tf_op jit(solution)/shard_map/ppermute | solution.py:248
  3.0 0.9 %copy-start.4 = (bf16[512,256]{1,0:T(8,128)(2,1)S(1)}, bf16[512,256]{1,0:T(8,128)(2,1)}, u32[]{:S(2)}) copy-start(bf16[512,256]{1,0:T(8,128)(2,1)} %param.20) | copy-start | bytes 786436
  3.9 0.7 copy-start.17
  4.6 0.7 copy-start.18
  5.3 0.7 copy-start.19
  8.0 15.1 %all-to-all-start = ((bf16[8,72,256]{2,1,0:T(8,128)(2,1)}), bf16[8,72,256]{2,1,0:T(8,128)(2,1)S(1)}, u32[]{:S(2)}, u32[]{:S(2)}) async-start(bf16[8,72,256]{2,1,0:T(8,128)(2,1)} %get-tuple-element.17), calls=%async_computation | async-start | bytes 589824 | tf_op jit(solution)/shard_map/all_to_all | solution.py:273
  13.8 3.9 %collective-permute-start.1 = (bf16[32,256]{1,0:T(8,128)(2,1)}, bf16[32,256]{1,0:T(8,128)(2,1)S(1)}, u32[]{:S(2)}, u32[]{:S(2)}) collective-permute-start(bf16[32,256]{1,0:T(8,128)(2,1)} %bitcast.25), channel_id=1, source_target_pairs={{0,2},{1,3},{2,0},{3,1},{4,6},{5,7},{6,4},{7,5},{8,10},{9,11},{10,... | collective-permute-start | bytes 49160 | tf_op jit(solution)/shard_map/ppermute | solution.py:248
  23.1 6.8 %collective-permute-start.3 = (bf16[8,72,256]{2,1,0:T(8,128)(2,1)S(1)}, bf16[8,72,256]{2,1,0:T(8,128)(2,1)}, u32[]{:S(2)}, u32[]{:S(2)}) collective-permute-start(bf16[8,72,256]{2,1,0:T(8,128)(2,1)S(1)} %all-to-all-done.refs_0_), channel_id=1, source_target_pairs={{0,2},{1,3},{2,0},{3,1},{4,6},{5,7},{6,4},{7,5},{8,10},{9,11},{10,... | collective-permute-start | bytes 884744 | tf_op jit(solution)/shard_map/ppermute | solution.py:248
  23.7 6.7 %collective-permute-start.2 = (bf16[8,72,256]{2,1,0:T(8,128)(2,1)S(1)}, bf16[8,72,256]{2,1,0:T(8,128)(2,1)}, u32[]{:S(2)}, u32[]{:S(2)}) collective-permute-start(bf16[8,72,256]{2,1,0:T(8,128)(2,1)S(1)} %all-to-all-done.refs_0_), channel_id=1, source_target_pairs={{0,1},{1,0},{2,3},{3,2},{4,5},{5,4},{6,7},{7,6},{8,9},{9,8},{10,11... | collective-permute-start | bytes 884744 | tf_op jit(solution)/shard_map/ppermute | solution.py:248
  29.9 2.0 %collective-permute-start.4 = (bf16[8,72,256]{2,1,0:T(8,128)(2,1)}, bf16[8,72,256]{2,1,0:T(8,128)(2,1)}, u32[]{:S(2)}, u32[]{:S(2)}) collective-permute-start(bf16[8,72,256]{2,1,0:T(8,128)(2,1)} %collective-permute-done.3.refs_2_), channel_id=1, source_target_pairs={{0,1},{1,0},{2,3},{3,2},{4,5},{5,4},{6,7},{7,6},{8,9},{9,8},{10,11... | collective-permute-start | bytes 884744 | tf_op jit(solution)/shard_map/ppermute | solution.py:248
  29.9 22.6 %collective-permute-start.8 = (bf16[256,1024]{1,0:T(8,128)(2,1)}, bf16[256,1024]{1,0:T(8,128)(2,1)S(1)}, u32[]{:S(2)}, u32[]{:S(2)}) collective-permute-start(bf16[256,1024]{1,0:T(8,128)(2,1)} %refs_4_.3), channel_id=1, source_target_pairs={{0,1},{1,0},{2,3},{3,2},{4,5},{5,4},{6,7},{7,6},{8,9},{9,8},{10,11... | collective-permute-start | bytes 1572872 | tf_op jit(solution)/shard_map/ppermute | solution.py:248
  30.4 23.2 %collective-permute-start.9 = (bf16[256,1024]{1,0:T(8,128)(2,1)S(1)}, bf16[256,1024]{1,0:T(8,128)(2,1)S(1)}, u32[]{:S(2)}, u32[]{:S(2)}) collective-permute-start(bf16[256,1024]{1,0:T(8,128)(2,1)S(1)} %collective-permute-done.refs_6_), channel_id=1, source_target_pairs={{0,1},{1,0},{2,3},{3,2},{4,5},{5,4},{6,7},{7,6},{8,9},{9,8},{10,11... | collective-permute-start | bytes 1572872 | tf_op jit(solution)/shard_map/ppermute | solution.py:248
  31.9 1.4 %copy-start.2 = (bf16[3,1024,256]{2,1,0:T(8,128)(2,1)S(1)}, bf16[3,1024,256]{2,1,0:T(8,128)(2,1)}, u32[]{:S(2)}) copy-start(bf16[3,1024,256]{2,1,0:T(8,128)(2,1)} %refs_4_.2) | copy-start | bytes 4718596
  33.3 0.9 %copy-start.5 = (bf16[3,1024,32]{1,2,0:T(8,128)(2,1)S(1)}, bf16[3,1024,32]{1,2,0:T(8,128)(2,1)}, u32[]{:S(2)}) copy-start(bf16[3,1024,32]{1,2,0:T(8,128)(2,1)} %param.28) | copy-start | bytes 589828
  34.2 0.8 copy-start.11
  35.0 15.8 %copy-start.12 = (bf16[256,32]{0,1:T(8,128)(2,1)S(1)}, bf16[256,32]{0,1:T(8,128)(2,1)}, u32[]{:S(2)}) copy-start(bf16[256,32]{0,1:T(8,128)(2,1)} %param.30) | copy-start | bytes 49156
  35.0 18.6 %copy-start.3 = (bf16[256,1024]{1,0:T(8,128)(2,1)S(1)}, bf16[256,1024]{1,0:T(8,128)(2,1)}, u32[]{:S(2)}) copy-start(bf16[256,1024]{1,0:T(8,128)(2,1)} %refs_4_.3) | copy-start | bytes 1572868
  35.0 18.6 %copy-start.6 = (bf16[32,1024]{1,0:T(8,128)(2,1)S(1)}, bf16[32,1024]{1,0:T(8,128)(2,1)}, u32[]{:S(2)}) copy-start(bf16[32,1024]{1,0:T(8,128)(2,1)} %refs_14_.1) | copy-start | bytes 196612
  35.0 18.6 %copy-start.7 = (bf16[1024,32]{0,1:T(8,128)(2,1)S(1)}, bf16[1024,32]{0,1:T(8,128)(2,1)}, u32[]{:S(2)}) copy-start(bf16[1024,32]{0,1:T(8,128)(2,1)} %param.32) | copy-start | bytes 196612
  35.0 18.6 %copy-start.8 = (bf16[32,1024]{1,0:T(8,128)(2,1)S(1)}, bf16[32,1024]{1,0:T(8,128)(2,1)}, u32[]{:S(2)}) copy-start(bf16[32,1024]{1,0:T(8,128)(2,1)} %refs_17_.1) | copy-start | bytes 196612
  35.1 18.6 %copy-start.9 = (bf16[1024,32]{0,1:T(8,128)(2,1)S(1)}, bf16[1024,32]{0,1:T(8,128)(2,1)}, u32[]{:S(2)}) copy-start(bf16[1024,32]{0,1:T(8,128)(2,1)} %param.34) | copy-start | bytes 196612
  35.1 18.6 %copy-start.10 = (bf16[32,1024]{1,0:T(8,128)(2,1)S(1)}, bf16[32,1024]{1,0:T(8,128)(2,1)}, u32[]{:S(2)}) copy-start(bf16[32,1024]{1,0:T(8,128)(2,1)} %refs_20_.1) | copy-start | bytes 196612
  35.1 18.6 %copy-start.13 = (f32[1024]{0:T(1024)S(1)}, f32[1024]{0:T(1024)}, u32[]{:S(2)}) copy-start(f32[1024]{0:T(1024)} %param.36) | copy-start | bytes 12292
  35.1 18.6 %copy-start.14 = (f32[1024]{0:T(1024)S(1)}, f32[1024]{0:T(1024)}, u32[]{:S(2)}) copy-start(f32[1024]{0:T(1024)} %param.37) | copy-start | bytes 12292
  42.4 8.4 %collective-permute-start.6 = (bf16[512,256]{1,0:T(8,128)(2,1)S(1)}, bf16[512,256]{1,0:T(8,128)(2,1)S(1)}, u32[]{:S(2)}, u32[]{:S(2)}) collective-permute-start(bf16[512,256]{1,0:T(8,128)(2,1)S(1)} %get-tuple-element.19.refs_0_), channel_id=1, source_target_pairs={{0,2},{1,3},{2,0},{3,1},{4,6},{5,7},{6,4},{7,5},{8,10},{9,11},{10,... | collective-permute-start | bytes 786440 | tf_op jit(solution)/shard_map/ppermute | solution.py:248
  43.1 10.5 %collective-permute-start.5 = (bf16[512,256]{1,0:T(8,128)(2,1)S(1)}, bf16[512,256]{1,0:T(8,128)(2,1)S(1)}, u32[]{:S(2)}, u32[]{:S(2)}) collective-permute-start(bf16[512,256]{1,0:T(8,128)(2,1)S(1)} %get-tuple-element.19.refs_0_), channel_id=1, source_target_pairs={{0,1},{1,0},{2,3},{3,2},{4,5},{5,4},{6,7},{7,6},{8,9},{9,8},{10,11... | collective-permute-start | bytes 786440 | tf_op jit(solution)/shard_map/ppermute | solution.py:248
  50.9 2.8 %collective-permute-start.7 = (bf16[512,256]{1,0:T(8,128)(2,1)S(1)}, bf16[512,256]{1,0:T(8,128)(2,1)S(1)}, u32[]{:S(2)}, u32[]{:S(2)}) collective-permute-start(bf16[512,256]{1,0:T(8,128)(2,1)S(1)} %collective-permute-done.6.refs_2_), channel_id=1, source_target_pairs={{0,1},{1,0},{2,3},{3,2},{4,5},{5,4},{6,7},{7,6},{8,9},{9,8},{10,11... | collective-permute-start | bytes 786440 | tf_op jit(solution)/shard_map/ppermute | solution.py:248
  50.9 1.6 %collective-permute-start.10 = (bf16[32,256]{1,0:T(8,128)(2,1)S(1)}, bf16[32,256]{1,0:T(8,128)(2,1)S(1)}, u32[]{:S(2)}, u32[]{:S(2)}) collective-permute-start(bf16[32,256]{1,0:T(8,128)(2,1)S(1)} %bitcast.26), channel_id=1, source_target_pairs={{0,1},{1,0},{2,3},{3,2},{4,5},{5,4},{6,7},{7,6},{8,9},{9,8},{10,11... | collective-permute-start | bytes 49160 | tf_op jit(solution)/shard_map/ppermute | solution.py:248
  52.4 1.2 %collective-permute-start.11 = (bf16[32,256]{1,0:T(8,128)(2,1)S(1)}, bf16[32,256]{1,0:T(8,128)(2,1)S(1)}, u32[]{:S(2)}, u32[]{:S(2)}) collective-permute-start(bf16[32,256]{1,0:T(8,128)(2,1)S(1)} %collective-permute-done.1.refs_10_), channel_id=1, source_target_pairs={{0,1},{1,0},{2,3},{3,2},{4,5},{5,4},{6,7},{7,6},{8,9},{9,8},{10,11... | collective-permute-start | bytes 49160 | tf_op jit(solution)/shard_map/ppermute | solution.py:248
  53.7 1.6 %copy-start.1 = (bf16[1024,1024]{1,0:T(8,128)(2,1)S(1)}, bf16[1024,1024]{1,0:T(8,128)(2,1)}, u32[]{:S(2)}) copy-start(bf16[1024,1024]{1,0:T(8,128)(2,1)} %refs_18_.1) | copy-start | bytes 6291460
  55.3 20.6 %copy-start.15 = (f32[1024]{0:T(1024)S(1)}, f32[1024]{0:T(1024)}, u32[]{:S(2)}) copy-start(f32[1024]{0:T(1024)} %param.38) | copy-start | bytes 12292
  55.3 20.6 %copy-start.16 = (f32[1024]{0:T(1024)S(1)}, f32[1024]{0:T(1024)}, u32[]{:S(2)}) copy-start(f32[1024]{0:T(1024)} %param.39) | copy-start | bytes 12292
  65.4 2.0 %collective-permute-start.12 = (bf16[2,128,1024]{2,1,0:T(8,128)(2,1)S(1)}, bf16[2,128,1024]{2,1,0:T(8,128)(2,1)S(1)}, u32[]{:S(2)}, u32[]{:S(2)}) collective-permute-start(bf16[2,128,1024]{2,1,0:T(8,128)(2,1)S(1)} %get-tuple-element.25), channel_id=1, source_target_pairs={{0,1},{1,0},{2,3},{3,2},{4,5},{5,4},{6,7},{7,6},{8,9},{9,8},{10,11... | collective-permute-start | bytes 1572872 | tf_op jit(solution)/shard_map/ppermute | solution.py:248
  67.5 8.4 %collective-permute-start.13 = (bf16[128,1024]{1,0:T(8,128)(2,1)S(1)}, bf16[128,1024]{1,0:T(8,128)(2,1)S(1)}, u32[]{:S(2)}, u32[]{:S(2)}) collective-permute-start(bf16[128,1024]{1,0:T(8,128)(2,1)S(1)} %fusion), channel_id=1, source_target_pairs={{0,2},{1,3},{2,0},{3,1},{4,6},{5,7},{6,4},{7,5},{8,10},{9,11},{10,... | collective-permute-start | bytes 786440 | tf_op jit(solution)/shard_map/ppermute | solution.py:248

commit v4 on v3

--- a/solution.py
+++ b/solution.py
@@ -40,13 +40,21 @@
     return jnp.concatenate([high, low - high], axis=1).astype(BF)
 
 
-def pack_kernel(lengths_in, ids_in, slots, tok, out, owners, lengths, ids, sems):
+def fetch(pairs, sems):
     copies = [
-        pltpu.make_async_copy(lengths_in, lengths, sems.at[0]),
-        pltpu.make_async_copy(ids_in, ids, sems.at[1]),
+        pltpu.make_async_copy(src, dst, sems.at[i]) for i, (src, dst) in enumerate(pairs)
     ]
     for c in copies:
         c.start()
+    return copies
+
+
+def pack_kernel(
+    lengths_in, ids_in, slots_in, tok_in, out, owners, lengths, ids, slots, tok, sems
+):
+    copies = fetch(
+        [(lengths_in, lengths), (ids_in, ids), (slots_in, slots), (tok_in, tok)], sems
+    )
     blocks = tok.shape[0]
     if out.shape[0] > blocks:
         out[...] = jnp.zeros(out.shape, out.dtype)
@@ -68,11 +76,11 @@
 
 
 def tiles(count, step):
-    if count <= 2:
-        for t in range(count):
-            step(t)
-    else:
-        lax.fori_loop(0, count, lambda t, c: (step(t), c)[1], 0)
+    step(0)
+    if count == 2:
+        step(1)
+    elif count > 2:
+        lax.fori_loop(1, count, lambda t, c: (step(t), c)[1], 0)
 
 
 def span(start, size):
@@ -80,7 +88,11 @@
 
 
 def attn_kernel(n_tp, me, *refs):
-    parts, (w, down, up, att, sel_out, x_full, up_all) = refs[:n_tp], refs[n_tp:]
+    parts = refs[:n_tp]
+    w_in, down_in, up_in, att, sel_out, x_full, up_all, w, down, up, sems = refs[n_tp:]
+    copies = fetch(
+        [(down_in, down), (up_in, up)] + [(w_in.at[k], w.at[k]) for k in range(3)], sems
+    )
     blocks = parts[0].shape[0]
     width = parts[0].shape[2]
     rows = blocks * CAP
@@ -88,6 +100,8 @@
     for r in range(n_tp):
         x_full[:, span((tp ^ r) * width, width)] = parts[r][:, :CAP, :].reshape(rows, width)
     up_all[...] = jnp.zeros(up_all.shape, BF)
+    copies[0].wait()
+    copies[1].wait()
     for k in range(3):
         for part in range(2):
             first_row = (3 * part + k) * SPAN
@@ -117,9 +131,12 @@
         sel_out[rs] = sel.astype(BF)
         x = x_full[rs]
         low = split_low(dot_t(x, down[...]), sel[:, : 3 * SPAN])
-        q, k_, v = [
-            dot(x, w[k]) + dot(low, up_all[:, k * width : (k + 1) * width]) for k in range(3)
-        ]
+        qkv = []
+        for k in range(3):
+            if isinstance(t, int) and t == 0:
+                copies[2 + k].wait()
+            qkv.append(dot(x, w[k]) + dot(low, up_all[:, k * width : (k + 1) * width]))
+        q, k_, v = qkv
         q = (q.astype(BF).astype(F32) * HEAD_DIM**-0.5).astype(BF)
         k_, v = k_.astype(BF), v.astype(BF)
         for p in range(tile // 2):
@@ -141,7 +158,9 @@
 
 def ffn_kernel(n_tp, me, *refs):
     atts, wouts, odowns = refs[:n_tp], refs[n_tp : 2 * n_tp], refs[2 * n_tp : 3 * n_tp]
-    (x, sel_in, oup, w1, d1, u1, w2, d2, u2, g1, b1, even, odd, h_own, h_scr) = refs[3 * n_tp :]
+    (x, sel_in, w1_in, w2_in, oup, d1, u1, d2, u2, g1, b1) = refs[3 * n_tp : 3 * n_tp + 11]
+    even, odd, h_own, h_scr, w1, w2, sems = refs[3 * n_tp + 11 :]
+    copies = fetch([(w1_in, w1), (w2_in, w2)], sems)
     rows, feat = x.shape
     blocks = rows // CAP
     share = CAP // n_tp
@@ -163,8 +182,12 @@
         total = total + dot(split_low(low, sel), ups[0])
         h1 = layer_norm(total, g1[...], b1[...]).astype(BF)
         h_scr[span(t * nb, nb)] = h1.reshape(nb, n_tp, share, feat)
+        if isinstance(t, int) and t == 0:
+            copies[0].wait()
         gate = dot(h1, w1[...]) + dot(split_low(dot_t(h1, d1[...]), sel), ups[1])
         hidden = (0.5 * gate * (1.0 + lax.erf(gate * 0.7071067811865476))).astype(BF)
+        if isinstance(t, int) and t == 0:
+            copies[1].wait()
         term = dot(hidden, w2[...]) + dot(split_low(dot_t(hidden, d2[...]), sel), ups[2])
         term = term.reshape(nb, n_tp, share, feat)
         own_rows = span(t * (size // n_tp), size // n_tp)
@@ -201,12 +224,16 @@
 
 
 VM = pl.BlockSpec(memory_space=pltpu.VMEM)
-ANY = pl.BlockSpec(memory_space=pl.ANY)
+HBM = pl.BlockSpec(memory_space=pltpu.HBM)
 SMEM = pl.BlockSpec(memory_space=pltpu.SMEM)
 
 
 def near(*arrays):
     return [pltpu.with_memory_space_constraint(a, pltpu.VMEM) for a in arrays]
+
+
+def far(*arrays):
+    return [pltpu.with_memory_space_constraint(a, pltpu.HBM) for a in arrays]
 
 
 def params(mib=20):
@@ -260,22 +287,36 @@
             pltpu.VMEM((n_req, CAP + PAD, width), BF),
             jax.ShapeDtypeStruct((blocks,), jnp.int32),
         ),
-        in_specs=[ANY, ANY, SMEM, VM],
+        in_specs=[HBM] * 4,
         out_specs=(VM, SMEM),
         scratch_shapes=[
             pltpu.SMEM((SEQ_G, blocks), jnp.int32),
             pltpu.SMEM((SEQ_G, blocks), jnp.int32),
-            pltpu.SemaphoreType.DMA((2,)),
+            pltpu.SMEM(adapter_slot.shape, jnp.int32),
+            pltpu.VMEM((blocks, CAP, width), BF),
+            pltpu.SemaphoreType.DMA((4,)),
         ],
         compiler_params=params(4),
         name="pack",
-    )(prompt_lengths.T, adapter_ids.T, adapter_slot, tokens.reshape(blocks, CAP, width))
+    )(
+        *far(
+            prompt_lengths.T,
+            adapter_ids.T,
+            adapter_slot,
+            tokens.reshape(blocks, CAP, width),
+        )
+    )
     arrived = lax.all_to_all(packed, "req", split_axis=0, concat_axis=0, tiled=True)
     w_far = [swap(w_out, 2 * y) for y in range(1, half)]
     o_own = out_down.T
     o_far = [swap(o_own, 2 * y) for y in range(1, half)]
     arrived, w_far, o_far = lax.optimization_barrier((arrived, w_far, o_far))
     parts = gather(arrived)
+    wouts, odowns = [], []
+    for w_piece, o_piece in zip([w_out] + w_far, [o_own] + o_far):
+        wouts += [w_piece, swap(w_piece, 1)]
+        odowns += [o_piece, swap(o_piece, 1)]
+    parts, wouts, odowns = lax.optimization_barrier((parts, wouts, odowns))
 
     rows = n_req * CAP
     attended, sel, x_full = pl.pallas_call(
@@ -285,15 +326,21 @@
             pltpu.VMEM((rows, 4 * SPAN), BF),
             pltpu.VMEM((rows, feat), BF),
         ),
-        in_specs=[SMEM] + [VM] * (n_tp + 3),
+        in_specs=[SMEM] + [VM] * n_tp + [HBM] * 3,
         out_specs=(VM,) * 3,
-        scratch_shapes=[pltpu.VMEM((6 * SPAN, 3 * width), BF)],
+        scratch_shapes=[
+            pltpu.VMEM((6 * SPAN, 3 * width), BF),
+            pltpu.VMEM((3, feat, width), BF),
+            pltpu.VMEM((3 * SPAN, feat), BF),
+            pltpu.VMEM((3, SPAN, width), BF),
+            pltpu.SemaphoreType.DMA((5,)),
+        ],
         compiler_params=params(),
         name="attend",
     )(
         me,
-        *near(
-            *parts,
+        *near(*parts),
+        *far(
             w_qkv,
             jnp.swapaxes(qkv_down, 1, 2).reshape(3 * SPAN, feat),
             qkv_up,
@@ -301,12 +348,8 @@
     )
 
     atts = gather(attended)
-    wouts, odowns = [], []
-    for w_piece, o_piece in zip([w_out] + w_far, [o_own] + o_far):
-        wouts += [w_piece, swap(w_piece, 1)]
-        odowns += [o_piece, swap(o_piece, 1)]
     own = rows // n_tp
-    consts = [out_up, w_fc1, fc1_down.T, fc1_up, w_fc2, fc2_down.T, fc2_up]
+    consts = [out_up, fc1_down.T, fc1_up, fc2_down.T, fc2_up]
     consts += [norm1_gain[None], norm1_bias[None]]
     even, odd, h_own = pl.pallas_call(
         functools.partial(ffn_kernel, n_tp),
@@ -315,12 +358,25 @@
             pltpu.VMEM((half, own, feat), BF),
             pltpu.VMEM((own, feat), BF),
         ),
-        in_specs=[SMEM] + [VM] * (3 * n_tp + 2 + len(consts)),
+        in_specs=[SMEM]
+        + [VM] * (3 * n_tp + 2)
+        + [HBM] * 2
+        + [VM] * len(consts),
         out_specs=(VM,) * 3,
-        scratch_shapes=[pltpu.VMEM((n_req, n_tp, share, feat), BF)],
+        scratch_shapes=[
+            pltpu.VMEM((n_req, n_tp, share, feat), BF),
+            pltpu.VMEM(w_fc1.shape, BF),
+            pltpu.VMEM(w_fc2.shape, BF),
+            pltpu.SemaphoreType.DMA((2,)),
+        ],
         compiler_params=params(),
         name="feed",
-    )(me, *near(*atts, *wouts, *odowns, x_full, sel, *consts))
+    )(
+        me,
+        *near(*atts, *wouts, *odowns, x_full, sel),
+        *far(w_fc1, w_fc2),
+        *near(*consts),
+    )
 
     got = swap(odd, 1)
     sums = [

time: 92.8 us -> 88.2 us (0.950)
  local copies, waits for them, and re-layouts: 7.74 us -> 1.22 us
  Pallas kernels: 21.1 us -> 23.2 us
    unnamed x40 -> x30, local copies, waits for them, and re-layouts: 7.74 us -> 1.22 us
    pallas_call x1, Pallas kernels: 10.1 us -> 12.2 us  [body(): pl.pallas_call(functools.partial(ffn_kernel, n_tp), out_shape=(pltpu.VMEM...]
  transfers between devices with their start and end apart: 15 -> 15, of which waited for: 9 -> 9; matrix products, arithmetic and copies ran while one was open for 0% -> 0% of each run, Pallas kernels for 10% -> 2%
where the time goes in v4:
time: 88.2 us; the launch traced here: 87.9 us
  waiting for transfers between devices  35.8 us (41%)
  Pallas kernels  23.2 us (26%)
  blocking collectives  14.8 us (17%)
  starting transfers between devices  12.6 us (14%)
  local copies, waits for them, and re-layouts  1.22 us (1%)
    ppermute x14, waiting for transfers between devices, swap(): return lax.ppermute(value, 'tp', [(i, i ^ r) for i in range(n_tp)])  30.9 us
    all_to_all x1, blocking collectives, body(): lax.all_to_all(done.reshape(n_req * n_tp, share, width), ('req', 'tp'), s...  14.8 us
    pallas_call x1, Pallas kernels, body(): pl.pallas_call(functools.partial(ffn_kernel, n_tp), out_shape=(pltpu.VMEM...  12.2 us
    pallas_call x1, Pallas kernels, body(): pl.pallas_call(functools.partial(attn_kernel, n_tp), out_shape=(pltpu.VME...  7.61 us
    ppermute x14, starting transfers between devices, swap(): return lax.ppermute(value, 'tp', [(i, i ^ r) for i in range(n_tp)])  6.84 us
    all_to_all x1, starting transfers between devices, body(): lax.all_to_all(packed, 'req', split_axis=0, concat_axis=0, tiled=True)  5.81 us
    all_to_all x1, waiting for transfers between devices, body(): lax.all_to_all(packed, 'req', split_axis=0, concat_axis=0, tiled=True)  4.92 us
    pallas_call x1, Pallas kernels, body(): pl.pallas_call(pack_kernel, out_shape=(pltpu.VMEM((n_req, CAP + PAD, widt...  1.84 us
  transfers between devices with their start and end apart: 15, of which 9 were waited for; matrix products, arithmetic and copies ran while one was open for 0% of the time, Pallas kernels for 2%

profile of v4, /device:TPU:0, one launch (start us, length us, event | category | flops | bytes accessed | tf_op | source)
XLA Modules:
  0.0 87.9 jit_solution(1275958422726831854)
XLA Ops:
  0.0 3.0 %collective-permute-start = (bf16[256,1024]{1,0:T(8,128)(2,1)}, bf16[256,1024]{1,0:T(8,128)(2,1)S(1)}, u32[]{:S(2)}, u32[]{:S(2)}) collective-permute-start(bf16[256,1024]{1,0:T(8,128)(2,1)} %refs_4_.2), channel_id=1, source_target_pairs={{0,2},{1,3},{2,0},{3,1},{4,6},{5,7},{6,4},{7,5},{8,10},{9,11},{10,... | collective-permute-start | bytes 1572872 | tf_op jit(solution)/shard_map/ppermute | solution.py:275
  3.1 1.8 %pack.1 = (bf16[8,72,256]{2,1,0:T(8,128)(2,1)}, s32[8]{0:T(128)S(1)}) custom-call(s32[4,8]{1,0:T(4,128)} %bitcast.32, s32[4,8]{1,0:T(4,128)} %bitcast.33, s32[16]{0:T(128)} %slots_in.1, bf16[8,64,256]{2,1,0:T(8,128)(2,1)} %bitcast.30), custom_call_target="tpu_custom_call" | custom-call | tf_op jit(solution)/shard_map/pack/pallas_call | solution.py:284
  4.9 0.6 copy-done.13
  5.5 5.8 %all-to-all-start = ((bf16[8,72,256]{2,1,0:T(8,128)(2,1)}), bf16[8,72,256]{2,1,0:T(8,128)(2,1)S(1)}, u32[]{:S(2)}, u32[]{:S(2)}) async-start(bf16[8,72,256]{2,1,0:T(8,128)(2,1)} %get-tuple-element.29), calls=%async_computation | async-start | bytes 589824 | tf_op jit(solution)/shard_map/all_to_all | solution.py:309
  11.3 0.5 collective-permute-start.1
  11.8 3.9 %collective-permute-done.1.refs_10_ = bf16[32,256]{1,0:T(8,128)(2,1)} collective-permute-done((bf16[32,256]{1,0:T(8,128)(2,1)}, bf16[32,256]{1,0:T(8,128)(2,1)}, u32[]{:S(2)}, u32[]{:S(2)}) %collective-permute-start.1) | collective-permute-done | bytes 16416 | tf_op jit(solution)/shard_map/ppermute | solution.py:275
  15.7 4.9 %all-to-all-done.refs_0_ = bf16[8,72,256]{2,1,0:T(8,128)(2,1)S(1)} async-done(((bf16[8,72,256]{2,1,0:T(8,128)(2,1)}), bf16[8,72,256]{2,1,0:T(8,128)(2,1)S(1)}, u32[]{:S(2)}, u32[]{:S(2)}) %all-to-all-start) | async-done | bytes 294944 | tf_op jit(solution)/shard_map/all_to_all | solution.py:309
  20.6 0.0 collective-permute-done.refs_6_
  20.6 0.5 collective-permute-start.3
  21.1 0.0 collective-permute-start.5
  21.1 0.5 collective-permute-start.6
  21.6 0.0 collective-permute-start.2
  21.6 5.7 %collective-permute-done.3.refs_2_ = bf16[8,72,256]{2,1,0:T(8,128)(2,1)S(1)} collective-permute-done((bf16[8,72,256]{2,1,0:T(8,128)(2,1)S(1)}, bf16[8,72,256]{2,1,0:T(8,128)(2,1)S(1)}, u32[]{:S(2)}, u32[]{:S(2)}) %collective-permute-start.3) | collective-permute-done | bytes 294944 | tf_op jit(solution)/shard_map/ppermute | solution.py:275
  27.3 0.0 collective-permute-start.4
  27.3 0.5 collective-permute-start.7
  27.8 1.0 %collective-permute-done.7.refs_9_ = bf16[32,256]{1,0:T(8,128)(2,1)S(1)} collective-permute-done((bf16[32,256]{1,0:T(8,128)(2,1)}, bf16[32,256]{1,0:T(8,128)(2,1)S(1)}, u32[]{:S(2)}, u32[]{:S(2)}) %collective-permute-start.7) | collective-permute-done | bytes 16416 | tf_op jit(solution)/shard_map/ppermute | solution.py:275
  28.9 0.6 copy-done.7
  29.5 0.3 collective-permute-start.8
  29.8 0.0 collective-permute-done.5.refs_5_
  29.8 1.2 %collective-permute-done.8.refs_11_ = bf16[32,256]{1,0:T(8,128)(2,1)} collective-permute-done((bf16[32,256]{1,0:T(8,128)(2,1)}, bf16[32,256]{1,0:T(8,128)(2,1)}, u32[]{:S(2)}, u32[]{:S(2)}) %collective-permute-start.8) | collective-permute-done | bytes 16416 | tf_op jit(solution)/shard_map/ppermute | solution.py:275
  31.0 0.0 collective-permute-done.2.refs_1_
  31.0 0.0 collective-permute-done.6.refs_7_
  31.0 0.0 collective-permute-done.4.refs_3_
  31.0 7.6 %attend.1 = (bf16[512,256]{1,0:T(8,128)(2,1)S(1)}, bf16[512,128]{1,0:T(8,128)(2,1)S(1)}, bf16[512,1024]{1,0:T(8,128)(2,1)S(1)}) custom-call(s32[1]{0:T(128)} %bitcast.3.me, bf16[8,72,256]{2,1,0:T(8,128)(2,1)S(1)} %all-to-all-done.refs_0_, bf16[8,72,256]{2,1,0:T(8,128)(2,1)S(1)} %collective-permute-done.2.refs_1_, ...), custom_call_target="tpu_custom_call" | custom-call | tf_op jit(solution)/shard_map/attend/pallas_call | solution.py:322
  38.6 0.6 collective-permute-start.10
  39.2 0.1 collective-permute-start.9
  39.3 8.0 %collective-permute-done.10.refs_2_ = bf16[512,256]{1,0:T(8,128)(2,1)S(1)} collective-permute-done((bf16[512,256]{1,0:T(8,128)(2,1)S(1)}, bf16[512,256]{1,0:T(8,128)(2,1)S(1)}, u32[]{:S(2)}, u32[]{:S(2)}) %collective-permute-start.10) | collective-permute-done | bytes 262176 | tf_op jit(solution)/shard_map/ppermute | solution.py:275
  47.3 0.0 collective-permute-start.11
  47.3 0.0 collective-permute-done.9.refs_1_
  47.3 1.5 %collective-permute-done.11.refs_3_ = bf16[512,256]{1,0:T(8,128)(2,1)S(1)} collective-permute-done((bf16[512,256]{1,0:T(8,128)(2,1)S(1)}, bf16[512,256]{1,0:T(8,128)(2,1)S(1)}, u32[]{:S(2)}, u32[]{:S(2)}) %collective-permute-start.11) | collective-permute-done | bytes 262176 | tf_op jit(solution)/shard_map/ppermute | solution.py:275
  48.8 0.0 copy-done.4
  48.8 0.0 copy-done.3
  48.8 0.0 copy-done.2
  48.8 0.0 copy-done.1
  48.8 0.0 copy-done.5
  48.8 0.0 copy-done.8
  48.9 0.0 copy-done.9
  48.9 0.0 copy-start.11
  48.9 0.0 copy-start.12
  48.9 12.2 %feed.1 = (f32[2,128,1024]{2,1,0:T(8,128)S(1)}, bf16[2,128,1024]{2,1,0:T(8,128)(2,1)S(1)}, bf16[128,1024]{1,0:T(8,128)(2,1)S(1)}) custom-call(s32[1]{0:T(128)} %bitcast.3.me, bf16[512,256]{1,0:T(8,128)(2,1)S(1)} %get-tuple-element.37.refs_0_, bf16[512,256]{1,0:T(8,128)(2,1)S(1)} %collective-permute-done.9.refs_1_, ...), custom_call_target="tpu_custom_call" | custom-call | tf_op jit(solution)/shard_map/feed/pallas_call | solution.py:354
  61.1 0.2 collective-permute-start.12
  61.3 1.8 %collective-permute-done.12.got = bf16[2,128,1024]{2,1,0:T(8,128)(2,1)S(1)} collective-permute-done((bf16[2,128,1024]{2,1,0:T(8,128)(2,1)S(1)}, bf16[2,128,1024]{2,1,0:T(8,128)(2,1)S(1)}, u32[]{:S(2)}, u32[]{:S(2)}) %collective-permute-start.12) | collective-permute-done | bytes 524320 | tf_op jit(solution)/shard_map/ppermute | solution.py:275
  63.1 0.1 fusion
  63.2 0.6 collective-permute-start.13
  63.7 7.8 %collective-permute-done.13.refs_0_ = bf16[128,1024]{1,0:T(8,128)(2,1)S(1)} collective-permute-done((bf16[128,1024]{1,0:T(8,128)(2,1)S(1)}, bf16[128,1024]{1,0:T(8,128)(2,1)S(1)}, u32[]{:S(2)}, u32[]{:S(2)}) %collective-permute-start.13) | collective-permute-done | bytes 262176 | tf_op jit(solution)/shard_map/ppermute | solution.py:275
  71.6 0.3 finish.1
  71.9 14.8 %all_to_all.10 = bf16[32,16,256]{2,1,0:T(8,128)(2,1)S(1)} all-to-all(bf16[32,16,256]{2,1,0:T(8,128)(2,1)S(1)} %bitcast.19), channel_id=1, replica_groups=mesh['req'=8,'tp'=4] {'req','tp'}, dimensions={0} | all-to-all | bytes 524288 | tf_op jit(solution)/shard_map/all_to_all | solution.py:393
  86.6 1.3 %unpack.1 = bf16[8,64,256]{2,1,0:T(8,128)(2,1)} custom-call(s32[8]{0:T(128)S(1)} %copy-done.14, bf16[8,64,256]{2,1,0:T(8,128)(2,1)S(1)} %bitcast.20), custom_call_target="tpu_custom_call" | custom-call | tf_op jit(solution)/shard_map/unpack/pallas_call | solution.py:400
  (19 shorter events, 0.0 us)
Async XLA Ops:
  0.0 48.8 %copy-start = (bf16[256,1024]{1,0:T(8,128)(2,1)S(1)}, bf16[256,1024]{1,0:T(8,128)(2,1)}, u32[]{:S(2)}) copy-start(bf16[256,1024]{1,0:T(8,128)(2,1)} %refs_4_.2) | copy-start | bytes 1572868
  0.0 48.8 %copy-start.6 = (bf16[256,32]{0,1:T(8,128)(2,1)S(1)}, bf16[256,32]{0,1:T(8,128)(2,1)}, u32[]{:S(2)}) copy-start(bf16[256,32]{0,1:T(8,128)(2,1)} %param.30) | copy-start | bytes 49156
  0.0 48.8 %copy-start.4 = (bf16[1024,32]{0,1:T(8,128)(2,1)S(1)}, bf16[1024,32]{0,1:T(8,128)(2,1)}, u32[]{:S(2)}) copy-start(bf16[1024,32]{0,1:T(8,128)(2,1)} %param.34) | copy-start | bytes 196612
  0.0 48.8 %copy-start.3 = (bf16[32,1024]{1,0:T(8,128)(2,1)S(1)}, bf16[32,1024]{1,0:T(8,128)(2,1)}, u32[]{:S(2)}) copy-start(bf16[32,1024]{1,0:T(8,128)(2,1)} %refs_18_.1) | copy-start | bytes 196612
  0.0 48.8 %copy-start.2 = (bf16[1024,32]{0,1:T(8,128)(2,1)S(1)}, bf16[1024,32]{0,1:T(8,128)(2,1)}, u32[]{:S(2)}) copy-start(bf16[1024,32]{0,1:T(8,128)(2,1)} %param.32) | copy-start | bytes 196612
  0.0 48.8 %copy-start.1 = (bf16[32,1024]{1,0:T(8,128)(2,1)S(1)}, bf16[32,1024]{1,0:T(8,128)(2,1)}, u32[]{:S(2)}) copy-start(bf16[32,1024]{1,0:T(8,128)(2,1)} %refs_16_.1) | copy-start | bytes 196612
  0.0 20.6 %collective-permute-start = (bf16[256,1024]{1,0:T(8,128)(2,1)}, bf16[256,1024]{1,0:T(8,128)(2,1)S(1)}, u32[]{:S(2)}, u32[]{:S(2)}) collective-permute-start(bf16[256,1024]{1,0:T(8,128)(2,1)} %refs_4_.2), channel_id=1, source_target_pairs={{0,2},{1,3},{2,0},{3,1},{4,6},{5,7},{6,4},{7,5},{8,10},{9,11},{10,... | collective-permute-start | bytes 1572872 | tf_op jit(solution)/shard_map/ppermute | solution.py:275
  4.9 0.6 copy-start.13
  5.5 15.1 %all-to-all-start = ((bf16[8,72,256]{2,1,0:T(8,128)(2,1)}), bf16[8,72,256]{2,1,0:T(8,128)(2,1)S(1)}, u32[]{:S(2)}, u32[]{:S(2)}) async-start(bf16[8,72,256]{2,1,0:T(8,128)(2,1)} %get-tuple-element.29), calls=%async_computation | async-start | bytes 589824 | tf_op jit(solution)/shard_map/all_to_all | solution.py:309
  11.3 4.4 %collective-permute-start.1 = (bf16[32,256]{1,0:T(8,128)(2,1)}, bf16[32,256]{1,0:T(8,128)(2,1)}, u32[]{:S(2)}, u32[]{:S(2)}) collective-permute-start(bf16[32,256]{1,0:T(8,128)(2,1)} %bitcast.23), channel_id=1, source_target_pairs={{0,2},{1,3},{2,0},{3,1},{4,6},{5,7},{6,4},{7,5},{8,10},{9,11},{10,... | collective-permute-start | bytes 49160 | tf_op jit(solution)/shard_map/ppermute | solution.py:275
  20.6 6.7 %collective-permute-start.3 = (bf16[8,72,256]{2,1,0:T(8,128)(2,1)S(1)}, bf16[8,72,256]{2,1,0:T(8,128)(2,1)S(1)}, u32[]{:S(2)}, u32[]{:S(2)}) collective-permute-start(bf16[8,72,256]{2,1,0:T(8,128)(2,1)S(1)} %all-to-all-done.refs_0_), channel_id=1, source_target_pairs={{0,2},{1,3},{2,0},{3,1},{4,6},{5,7},{6,4},{7,5},{8,10},{9,11},{10,... | collective-permute-start | bytes 884744 | tf_op jit(solution)/shard_map/ppermute | solution.py:275
  21.1 8.7 %collective-permute-start.5 = (bf16[256,1024]{1,0:T(8,128)(2,1)}, bf16[256,1024]{1,0:T(8,128)(2,1)S(1)}, u32[]{:S(2)}, u32[]{:S(2)}) collective-permute-start(bf16[256,1024]{1,0:T(8,128)(2,1)} %refs_4_.2), channel_id=1, source_target_pairs={{0,1},{1,0},{2,3},{3,2},{4,5},{5,4},{6,7},{7,6},{8,9},{9,8},{10,11... | collective-permute-start | bytes 1572872 | tf_op jit(solution)/shard_map/ppermute | solution.py:275
  21.1 9.9 %collective-permute-start.6 = (bf16[256,1024]{1,0:T(8,128)(2,1)S(1)}, bf16[256,1024]{1,0:T(8,128)(2,1)S(1)}, u32[]{:S(2)}, u32[]{:S(2)}) collective-permute-start(bf16[256,1024]{1,0:T(8,128)(2,1)S(1)} %collective-permute-done.refs_6_), channel_id=1, source_target_pairs={{0,1},{1,0},{2,3},{3,2},{4,5},{5,4},{6,7},{7,6},{8,9},{9,8},{10,11... | collective-permute-start | bytes 1572872 | tf_op jit(solution)/shard_map/ppermute | solution.py:275
  21.6 9.4 %collective-permute-start.2 = (bf16[8,72,256]{2,1,0:T(8,128)(2,1)S(1)}, bf16[8,72,256]{2,1,0:T(8,128)(2,1)S(1)}, u32[]{:S(2)}, u32[]{:S(2)}) collective-permute-start(bf16[8,72,256]{2,1,0:T(8,128)(2,1)S(1)} %all-to-all-done.refs_0_), channel_id=1, source_target_pairs={{0,1},{1,0},{2,3},{3,2},{4,5},{5,4},{6,7},{7,6},{8,9},{9,8},{10,11... | collective-permute-start | bytes 884744 | tf_op jit(solution)/shard_map/ppermute | solution.py:275
  27.3 3.7 %collective-permute-start.4 = (bf16[8,72,256]{2,1,0:T(8,128)(2,1)S(1)}, bf16[8,72,256]{2,1,0:T(8,128)(2,1)S(1)}, u32[]{:S(2)}, u32[]{:S(2)}) collective-permute-start(bf16[8,72,256]{2,1,0:T(8,128)(2,1)S(1)} %collective-permute-done.3.refs_2_), channel_id=1, source_target_pairs={{0,1},{1,0},{2,3},{3,2},{4,5},{5,4},{6,7},{7,6},{8,9},{9,8},{10,11... | collective-permute-start | bytes 884744 | tf_op jit(solution)/shard_map/ppermute | solution.py:275
  27.3 1.6 %collective-permute-start.7 = (bf16[32,256]{1,0:T(8,128)(2,1)}, bf16[32,256]{1,0:T(8,128)(2,1)S(1)}, u32[]{:S(2)}, u32[]{:S(2)}) collective-permute-start(bf16[32,256]{1,0:T(8,128)(2,1)} %bitcast.24), channel_id=1, source_target_pairs={{0,1},{1,0},{2,3},{3,2},{4,5},{5,4},{6,7},{7,6},{8,9},{9,8},{10,11... | collective-permute-start | bytes 49160 | tf_op jit(solution)/shard_map/ppermute | solution.py:275
  28.9 0.6 copy-start.7
  29.5 1.5 %collective-permute-start.8 = (bf16[32,256]{1,0:T(8,128)(2,1)}, bf16[32,256]{1,0:T(8,128)(2,1)}, u32[]{:S(2)}, u32[]{:S(2)}) collective-permute-start(bf16[32,256]{1,0:T(8,128)(2,1)} %collective-permute-done.1.refs_10_), channel_id=1, source_target_pairs={{0,1},{1,0},{2,3},{3,2},{4,5},{5,4},{6,7},{7,6},{8,9},{9,8},{10,11... | collective-permute-start | bytes 49160 | tf_op jit(solution)/shard_map/ppermute | solution.py:275
  29.8 19.0 %copy-start.5 = (bf16[32,1024]{1,0:T(8,128)(2,1)S(1)}, bf16[32,1024]{1,0:T(8,128)(2,1)}, u32[]{:S(2)}) copy-start(bf16[32,1024]{1,0:T(8,128)(2,1)} %refs_20_.1) | copy-start | bytes 196612
  29.8 19.0 %copy-start.8 = (bf16[32,256]{1,0:T(8,128)(2,1)S(1)}, bf16[32,256]{1,0:T(8,128)(2,1)}, u32[]{:S(2)}) copy-start(bf16[32,256]{1,0:T(8,128)(2,1)} %copy-done.7) | copy-start | bytes 49156
  29.8 19.0 %copy-start.9 = (f32[1024]{0:T(1024)S(1)}, f32[1024]{0:T(1024)}, u32[]{:S(2)}) copy-start(f32[1024]{0:T(1024)} %param.36) | copy-start | bytes 12292
  29.8 19.0 %copy-start.10 = (f32[1024]{0:T(1024)S(1)}, f32[1024]{0:T(1024)}, u32[]{:S(2)}) copy-start(f32[1024]{0:T(1024)} %param.37) | copy-start | bytes 12292
  38.6 8.6 %collective-permute-start.10 = (bf16[512,256]{1,0:T(8,128)(2,1)S(1)}, bf16[512,256]{1,0:T(8,128)(2,1)S(1)}, u32[]{:S(2)}, u32[]{:S(2)}) collective-permute-start(bf16[512,256]{1,0:T(8,128)(2,1)S(1)} %get-tuple-element.37.refs_0_), channel_id=1, source_target_pairs={{0,2},{1,3},{2,0},{3,1},{4,6},{5,7},{6,4},{7,5},{8,10},{9,11},{10,... | collective-permute-start | bytes 786440 | tf_op jit(solution)/shard_map/ppermute | solution.py:275
  39.2 8.1 %collective-permute-start.9 = (bf16[512,256]{1,0:T(8,128)(2,1)S(1)}, bf16[512,256]{1,0:T(8,128)(2,1)S(1)}, u32[]{:S(2)}, u32[]{:S(2)}) collective-permute-start(bf16[512,256]{1,0:T(8,128)(2,1)S(1)} %get-tuple-element.37.refs_0_), channel_id=1, source_target_pairs={{0,1},{1,0},{2,3},{3,2},{4,5},{5,4},{6,7},{7,6},{8,9},{9,8},{10,11... | collective-permute-start | bytes 786440 | tf_op jit(solution)/shard_map/ppermute | solution.py:275
  47.3 1.5 %collective-permute-start.11 = (bf16[512,256]{1,0:T(8,128)(2,1)S(1)}, bf16[512,256]{1,0:T(8,128)(2,1)S(1)}, u32[]{:S(2)}, u32[]{:S(2)}) collective-permute-start(bf16[512,256]{1,0:T(8,128)(2,1)S(1)} %collective-permute-done.10.refs_2_), channel_id=1, source_target_pairs={{0,1},{1,0},{2,3},{3,2},{4,5},{5,4},{6,7},{7,6},{8,9},{9,8},{10,11... | collective-permute-start | bytes 786440 | tf_op jit(solution)/shard_map/ppermute | solution.py:275
  48.9 22.7 %copy-start.11 = (f32[1024]{0:T(1024)S(1)}, f32[1024]{0:T(1024)}, u32[]{:S(2)}) copy-start(f32[1024]{0:T(1024)} %param.38) | copy-start | bytes 12292
  48.9 22.7 %copy-start.12 = (f32[1024]{0:T(1024)S(1)}, f32[1024]{0:T(1024)}, u32[]{:S(2)}) copy-start(f32[1024]{0:T(1024)} %param.39) | copy-start | bytes 12292
  61.1 25.5 %copy-start.14 = (s32[8]{0:T(128)S(1)}, s32[8]{0:T(128)}, u32[]{:S(2)}) copy-start(s32[8]{0:T(128)} %copy-done.13) | copy-start | bytes 100
  61.1 2.0 %collective-permute-start.12 = (bf16[2,128,1024]{2,1,0:T(8,128)(2,1)S(1)}, bf16[2,128,1024]{2,1,0:T(8,128)(2,1)S(1)}, u32[]{:S(2)}, u32[]{:S(2)}) collective-permute-start(bf16[2,128,1024]{2,1,0:T(8,128)(2,1)S(1)} %get-tuple-element.49), channel_id=1, source_target_pairs={{0,1},{1,0},{2,3},{3,2},{4,5},{5,4},{6,7},{7,6},{8,9},{9,8},{10,11... | collective-permute-start | bytes 1572872 | tf_op jit(solution)/shard_map/ppermute | solution.py:275
  63.2 8.4 %collective-permute-start.13 = (bf16[128,1024]{1,0:T(8,128)(2,1)S(1)}, bf16[128,1024]{1,0:T(8,128)(2,1)S(1)}, u32[]{:S(2)}, u32[]{:S(2)}) collective-permute-start(bf16[128,1024]{1,0:T(8,128)(2,1)S(1)} %fusion), channel_id=1, source_target_pairs={{0,2},{1,3},{2,0},{3,1},{4,6},{5,7},{6,4},{7,5},{8,10},{9,11},{10,... | collective-permute-start | bytes 786440 | tf_op jit(solution)/shard_map/ppermute | solution.py:275

commit v5 on v4

--- a/solution.py
+++ b/solution.py
@@ -87,25 +87,33 @@
     return pl.ds(start if isinstance(start, int) else pl.multiple_of(start, size), size)
 
 
-def attn_kernel(n_tp, me, *refs):
+def attn_kernel(n_tp, chunk, me, *refs):
     parts = refs[:n_tp]
-    w_in, down_in, up_in, att, sel_out, x_full, up_all, w, down, up, sems = refs[n_tp:]
-    copies = fetch(
-        [(down_in, down), (up_in, up)] + [(w_in.at[k], w.at[k]) for k in range(3)], sems
-    )
-    blocks = parts[0].shape[0]
+    copies = None
+    if chunk == 0:
+        w_in, down_in, up_in, att, sel_out, x_full, w, down, up_all, up, sems = refs[n_tp:]
+        copies = fetch(
+            [(down_in, down), (up_in, up)] + [(w_in.at[k], w.at[k]) for k in range(3)], sems
+        )
+    else:
+        w, down, up_all, att, sel_out, x_full = refs[n_tp:]
+    blocks = att.shape[0] // CAP
     width = parts[0].shape[2]
     rows = blocks * CAP
     tp = me[0]
+    offsets = [chunk * blocks if part.shape[0] > blocks else 0 for part in parts]
     for r in range(n_tp):
-        x_full[:, span((tp ^ r) * width, width)] = parts[r][:, :CAP, :].reshape(rows, width)
-    up_all[...] = jnp.zeros(up_all.shape, BF)
-    copies[0].wait()
-    copies[1].wait()
-    for k in range(3):
-        for part in range(2):
-            first_row = (3 * part + k) * SPAN
-            up_all[first_row : first_row + SPAN, k * width : (k + 1) * width] = up[k]
+        x_full[:, span((tp ^ r) * width, width)] = parts[r][
+            offsets[r] : offsets[r] + blocks, :CAP, :
+        ].reshape(rows, width)
+    if chunk == 0:
+        up_all[...] = jnp.zeros(up_all.shape, BF)
+        copies[0].wait()
+        copies[1].wait()
+        for k in range(3):
+            for part in range(2):
+                first_row = (3 * part + k) * SPAN
+                up_all[first_row : first_row + SPAN, k * width : (k + 1) * width] = up[k]
     pair_lane = lax.broadcasted_iota(jnp.int32, (2 * CAP, 2 * CAP), 1)
     pair_row = lax.broadcasted_iota(jnp.int32, (2 * CAP, 2 * CAP), 0)
     eye = pair_lane == pair_row
@@ -118,7 +126,7 @@
         rs = span(t * (tile * CAP), tile * CAP)
         masks, sels = [], []
         for p in range(tile // 2):
-            b0 = t * tile + 2 * p
+            b0 = offsets[0] + t * tile + 2 * p
             c0 = parts[0][b0, CAP : CAP + 1, : 2 * CAP].astype(F32)
             c1 = parts[0][b0 + 1, CAP : CAP + 1, : 2 * CAP].astype(F32) + 64.0
             idr = jnp.where(pair_lane < CAP, c0, c1)
@@ -133,7 +141,7 @@
         low = split_low(dot_t(x, down[...]), sel[:, : 3 * SPAN])
         qkv = []
         for k in range(3):
-            if isinstance(t, int) and t == 0:
+            if copies and isinstance(t, int):
                 copies[2 + k].wait()
             qkv.append(dot(x, w[k]) + dot(low, up_all[:, k * width : (k + 1) * width]))
         q, k_, v = qkv
@@ -156,11 +164,15 @@
     tiles(blocks // tile, step)
 
 
-def ffn_kernel(n_tp, me, *refs):
+def ffn_kernel(n_tp, chunk, me, *refs):
     atts, wouts, odowns = refs[:n_tp], refs[n_tp : 2 * n_tp], refs[2 * n_tp : 3 * n_tp]
-    (x, sel_in, w1_in, w2_in, oup, d1, u1, d2, u2, g1, b1) = refs[3 * n_tp : 3 * n_tp + 11]
-    even, odd, h_own, h_scr, w1, w2, sems = refs[3 * n_tp + 11 :]
-    copies = fetch([(w1_in, w1), (w2_in, w2)], sems)
+    x, sel_in, oup, d1, u1, d2, u2, g1, b1 = refs[3 * n_tp : 3 * n_tp + 9]
+    copies = None
+    if chunk == 0:
+        w1_in, w2_in, even, odd, odds, h_own, w1, w2, h_scr, sems = refs[3 * n_tp + 9 :]
+        copies = fetch([(w1_in, w1), (w2_in, w2)], sems)
+    else:
+        w1, w2, even, odd, odds, h_own, h_scr = refs[3 * n_tp + 9 :]
     rows, feat = x.shape
     blocks = rows // CAP
     share = CAP // n_tp
@@ -182,11 +194,11 @@
         total = total + dot(split_low(low, sel), ups[0])
         h1 = layer_norm(total, g1[...], b1[...]).astype(BF)
         h_scr[span(t * nb, nb)] = h1.reshape(nb, n_tp, share, feat)
-        if isinstance(t, int) and t == 0:
+        if copies and isinstance(t, int):
             copies[0].wait()
         gate = dot(h1, w1[...]) + dot(split_low(dot_t(h1, d1[...]), sel), ups[1])
         hidden = (0.5 * gate * (1.0 + lax.erf(gate * 0.7071067811865476))).astype(BF)
-        if isinstance(t, int) and t == 0:
+        if copies and isinstance(t, int):
             copies[1].wait()
         term = dot(hidden, w2[...]) + dot(split_low(dot_t(hidden, d2[...]), sel), ups[2])
         term = term.reshape(nb, n_tp, share, feat)
@@ -199,23 +211,32 @@
             def _():
                 even[rel // 2, own_rows, :] = piece
 
-            @pl.when(rel % 2 == 1)
+            @pl.when(rel == 1)
             def _():
-                odd[rel // 2, own_rows, :] = piece.astype(BF)
+                odd[own_rows, :] = piece.astype(BF)
+
+            @pl.when((rel % 2 == 1) & (rel > 1))
+            def _():
+                odds[rel // 2 - 1, own_rows, :] = piece.astype(BF)
 
     tiles(rows // size, step)
     h_own[...] = h_scr[:, tp].reshape(blocks * share, feat)
 
 
-def last_kernel(n_tp, even, got, *refs):
-    arrived, (h_own, g2, b2, out) = refs[: n_tp // 2 - 1], refs[n_tp // 2 - 1 :]
-    total = h_own[...].astype(F32) + (even[0] + got[0].astype(F32))
-    for a in arrived:
-        total = total + a[...].astype(F32)
+def last_kernel(n_tp, earlier, *refs):
+    g2, b2, out = refs[-3:]
+    even, got, h_own = refs[earlier : earlier + 3]
+    _, share, width = out.shape[1:]
+    step = h_own.shape[0] // share
+    total = h_own[...].astype(F32) + (even[0] + got[...].astype(F32))
+    for arrived in refs[earlier + 3 : -3]:
+        total = total + arrived[...].astype(F32)
     done = layer_norm(total, g2[...], b2[...]).astype(BF)
-    n, _, share, width = out.shape
+    if earlier:
+        out[: refs[0].shape[0]] = refs[0][...]
     for f in range(n_tp):
-        out[:, f] = done[:, f * width : (f + 1) * width].reshape(n, share, width)
+        piece = done[:, f * width : (f + 1) * width].reshape(step, share, width)
+        out[out.shape[0] - step :, f] = piece
 
 
 def unpack_kernel(owners, arrived, out):
@@ -234,6 +255,10 @@
 
 def far(*arrays):
     return [pltpu.with_memory_space_constraint(a, pltpu.HBM) for a in arrays]
+
+
+def work(flops, rows):
+    return pl.CostEstimate(flops=5 * flops, transcendentals=rows * 1024, bytes_accessed=rows * 8192)
 
 
 def params(mib=20):
@@ -274,12 +299,8 @@
     def swap(value, r):
         return lax.ppermute(value, "tp", [(i, i ^ r) for i in range(n_tp)])
 
-    def gather(value):
-        far = [value] + [swap(value, 2 * y) for y in range(1, n_tp // 2)]
-        found = []
-        for piece in far:
-            found += [piece, swap(piece, 1)]
-        return found
+    def second_hop(pieces):
+        return [hop for piece in pieces for hop in (piece, swap(piece, 1))]
 
     packed, owners = pl.pallas_call(
         pack_kernel,
@@ -308,88 +329,120 @@
     )
     arrived = lax.all_to_all(packed, "req", split_axis=0, concat_axis=0, tiled=True)
     w_far = [swap(w_out, 2 * y) for y in range(1, half)]
-    o_own = out_down.T
-    o_far = [swap(o_own, 2 * y) for y in range(1, half)]
-    arrived, w_far, o_far = lax.optimization_barrier((arrived, w_far, o_far))
-    parts = gather(arrived)
-    wouts, odowns = [], []
-    for w_piece, o_piece in zip([w_out] + w_far, [o_own] + o_far):
-        wouts += [w_piece, swap(w_piece, 1)]
-        odowns += [o_piece, swap(o_piece, 1)]
-    parts, wouts, odowns = lax.optimization_barrier((parts, wouts, odowns))
-
-    rows = n_req * CAP
-    attended, sel, x_full = pl.pallas_call(
-        functools.partial(attn_kernel, n_tp),
-        out_shape=(
-            pltpu.VMEM((rows, width), BF),
-            pltpu.VMEM((rows, 4 * SPAN), BF),
-            pltpu.VMEM((rows, feat), BF),
-        ),
-        in_specs=[SMEM] + [VM] * n_tp + [HBM] * 3,
-        out_specs=(VM,) * 3,
-        scratch_shapes=[
-            pltpu.VMEM((6 * SPAN, 3 * width), BF),
+    w_near = swap(w_out, 1)
+    odowns = [out_down.T] + [swap(out_down.T, r) for r in range(1, n_tp)]
+    arrived, w_far, w_near, odowns = lax.optimization_barrier((arrived, w_far, w_near, odowns))
+    count = 2
+    step_blocks = n_req // count
+    rows = step_blocks * CAP
+    own = rows // n_tp
+    beside = swap(arrived, 1)
+    x_far = []
+    for c in range(count):
+        piece = arrived[c * step_blocks : (c + 1) * step_blocks]
+        x_far.append([swap(piece, 2 * y) for y in range(1, half)])
+    wouts = [w_out, w_near] + second_hop(w_far)
+    x_far[0] = second_hop(x_far[0])
+    x_far[0], wouts = lax.optimization_barrier((x_far[0], wouts))
+
+    qkv_weights = far(
+        w_qkv, jnp.swapaxes(qkv_down, 1, 2).reshape(3 * SPAN, feat), qkv_up
+    )
+    ffn_weights = far(w_fc1, w_fc2)
+    consts = near(
+        out_up, fc1_down.T, fc1_up, fc2_down.T, fc2_up, norm1_gain[None], norm1_bias[None]
+    )
+    steps = []
+    for c in range(count):
+        if c:
+            x_far[c], steps[0][0] = lax.optimization_barrier((x_far[c], steps[0][0]))
+            x_far[c] = second_hop(x_far[c])
+        keep = [] if c else [
             pltpu.VMEM((3, feat, width), BF),
             pltpu.VMEM((3 * SPAN, feat), BF),
-            pltpu.VMEM((3, SPAN, width), BF),
-            pltpu.SemaphoreType.DMA((5,)),
-        ],
-        compiler_params=params(),
-        name="attend",
-    )(
-        me,
-        *near(*parts),
-        *far(
-            w_qkv,
-            jnp.swapaxes(qkv_down, 1, 2).reshape(3 * SPAN, feat),
-            qkv_up,
-        ),
-    )
-
-    atts = gather(attended)
-    own = rows // n_tp
-    consts = [out_up, fc1_down.T, fc1_up, fc2_down.T, fc2_up]
-    consts += [norm1_gain[None], norm1_bias[None]]
-    even, odd, h_own = pl.pallas_call(
-        functools.partial(ffn_kernel, n_tp),
-        out_shape=(
-            pltpu.VMEM((half, own, feat), F32),
-            pltpu.VMEM((half, own, feat), BF),
-            pltpu.VMEM((own, feat), BF),
-        ),
-        in_specs=[SMEM]
-        + [VM] * (3 * n_tp + 2)
-        + [HBM] * 2
-        + [VM] * len(consts),
-        out_specs=(VM,) * 3,
-        scratch_shapes=[
-            pltpu.VMEM((n_req, n_tp, share, feat), BF),
-            pltpu.VMEM(w_fc1.shape, BF),
-            pltpu.VMEM(w_fc2.shape, BF),
-            pltpu.SemaphoreType.DMA((2,)),
-        ],
-        compiler_params=params(),
-        name="feed",
-    )(
-        me,
-        *near(*atts, *wouts, *odowns, x_full, sel),
-        *far(w_fc1, w_fc2),
-        *near(*consts),
-    )
-
-    got = swap(odd, 1)
-    sums = [
-        swap((even[y] + got[y].astype(F32)).astype(BF), 2 * y) for y in range(1, half)
-    ]
-    done = pl.pallas_call(
-        functools.partial(last_kernel, n_tp),
-        out_shape=pltpu.VMEM((n_req, n_tp, share, width), BF),
-        in_specs=[VM] * (5 + len(sums)),
-        out_specs=VM,
-        compiler_params=params(),
-        name="finish",
-    )(*near(even, got, *sums, h_own, norm2_gain[None], norm2_bias[None]))
+            pltpu.VMEM((6 * SPAN, 3 * width), BF),
+        ]
+        attended, sel, x_full, *kept = pl.pallas_call(
+            functools.partial(attn_kernel, n_tp, c),
+            out_shape=[
+                pltpu.VMEM((rows, width), BF),
+                pltpu.VMEM((rows, 4 * SPAN), BF),
+                pltpu.VMEM((rows, feat), BF),
+            ]
+            + keep,
+            in_specs=[SMEM] + [VM] * n_tp + [VM if c else HBM] * 3,
+            out_specs=[VM] * (3 + len(keep)),
+            scratch_shapes=[] if c else [
+                pltpu.VMEM((3, SPAN, width), BF),
+                pltpu.SemaphoreType.DMA((5,)),
+            ],
+            compiler_params=params(12),
+            cost_estimate=work(2 * rows * feat * 3 * width + 4 * rows * width * 2 * CAP, rows),
+            name="attend",
+        )(me, *near(arrived, beside, *x_far[c]), *qkv_weights)
+        if c == 0:
+            qkv_weights = near(*kept)
+        y_got = [swap(attended, 2 * y) for y in range(1, half)]
+        if c:
+            steps[0][1], attended = lax.optimization_barrier((steps[0][1], attended))
+        steps.append([attended, y_got, sel, x_full])
+
+    def finish(earlier, *values):
+        blocks_done = step_blocks + sum(e.shape[0] for e in earlier)
+        values = near(*earlier, *values, norm2_gain[None], norm2_bias[None])
+        return pl.pallas_call(
+            functools.partial(last_kernel, n_tp, len(earlier)),
+            out_shape=pltpu.VMEM((blocks_done, n_tp, share, width), BF),
+            in_specs=[VM] * len(values),
+            out_specs=VM,
+            compiler_params=params(8),
+            name="finish",
+        )(*values)
+
+    for c in range(count):
+        attended, y_got, sel, x_full = steps[c]
+        atts = second_hop([attended] + y_got)
+        if c:
+            atts, firsts = lax.optimization_barrier((atts, firsts))
+            firsts = [swap(piece, 2 * (y + 1)) for y, piece in enumerate(firsts)]
+        keep = [] if c else [pltpu.VMEM(w_fc1.shape, BF), pltpu.VMEM(w_fc2.shape, BF)]
+        even, odd, odds, h_own, *kept = pl.pallas_call(
+            functools.partial(ffn_kernel, n_tp, c),
+            out_shape=[
+                pltpu.VMEM((half, own, feat), F32),
+                pltpu.VMEM((own, feat), BF),
+                pltpu.VMEM((half - 1, own, feat), BF),
+                pltpu.VMEM((own, feat), BF),
+            ]
+            + keep,
+            in_specs=[SMEM]
+            + [VM] * (3 * n_tp + 2 + len(consts))
+            + [VM if c else HBM] * 2,
+            out_specs=[VM] * (4 + len(keep)),
+            scratch_shapes=[pltpu.VMEM((step_blocks, n_tp, share, feat), BF)]
+            + ([] if c else [pltpu.SemaphoreType.DMA((2,))]),
+            compiler_params=params(16),
+            cost_estimate=work(2 * rows * feat * (2 * w_fc1.shape[1] + feat), rows),
+            name="feed",
+        )(
+            me,
+            *near(*atts, *wouts, *odowns, x_full, sel),
+            *consts,
+            *ffn_weights,
+        )
+        if c == 0:
+            ffn_weights = near(*kept)
+        gots = swap(odds, 1)
+        if c:
+            earlier = finish([], *first_ends, *firsts)
+            gots, earlier = lax.optimization_barrier((gots, earlier))
+        sends = [(even[y] + gots[y - 1].astype(F32)).astype(BF) for y in range(1, half)]
+        ends = [even, swap(odd, 1), h_own]
+        if c == 0:
+            firsts, first_ends = sends, ends
+        else:
+            sends = [swap(piece, 2 * (y + 1)) for y, piece in enumerate(sends)]
+            done = finish([earlier], *ends, *sends)
     back = lax.all_to_all(
         done.reshape(n_req * n_tp, share, width),
         ("req", "tp"),

time: 88.2 us -> 77.9 us (0.88)
  waiting for transfers between devices: 35.8 us -> 23.5 us
  starting transfers between devices: 12.6 us -> 17 us
  local copies, waits for them, and re-layouts: 1.22 us -> 0.08 us
  blocking collectives: 14.8 us -> 13.8 us
    ppermute x14 -> x23, waiting for transfers between devices: 30.9 us -> 18.3 us  [swap(): return lax.ppermute(value, 'tp', [(i, i ^ r) for i in range(n_tp)])]
    ppermute x14 -> x23, starting transfers between devices: 6.84 us -> 11.2 us  [swap(): return lax.ppermute(value, 'tp', [(i, i ^ r) for i in range(n_tp)])]
    unnamed x30 -> x22, local copies, waits for them, and re-layouts: 1.22 us -> 0.05 us
    all_to_all x1, blocking collectives: 14.8 us -> 13.8 us  [body(): lax.all_to_all(done.reshape(n_req * n_tp, share, width), ('req', 'tp'), s...]
    pallas_call x3 -> x6, Pallas kernels: 20.1 us -> 19.7 us  [the longest x2 11.5 us: body(): pl.pallas_call(functools.partial(ffn_kernel, n_tp, c), out_shape=[pltpu.V...]
  transfers between devices with their start and end apart: 15 -> 24, of which waited for: 9 -> 13; matrix products, arithmetic and copies ran while one was open for 0% -> 0% of each run, Pallas kernels for 2% -> 28%
where the time goes in v5:
time: 77.9 us; the launch traced here: 77.6 us
  waiting for transfers between devices  23.5 us (30%)
  Pallas kernels  22.8 us (29%)
  starting transfers between devices  17 us (22%)
  blocking collectives  13.8 us (18%)
    ppermute x23, waiting for transfers between devices, swap(): return lax.ppermute(value, 'tp', [(i, i ^ r) for i in range(n_tp)])  18.3 us
    all_to_all x1, blocking collectives, body(): lax.all_to_all(done.reshape(n_req * n_tp, share, width), ('req', 'tp'), s...  13.8 us
    pallas_call x2, Pallas kernels, body(): pl.pallas_call(functools.partial(ffn_kernel, n_tp, c), out_shape=[pltpu.V...  11.5 us
    ppermute x23, starting transfers between devices, swap(): return lax.ppermute(value, 'tp', [(i, i ^ r) for i in range(n_tp)])  11.2 us
    pallas_call x2, Pallas kernels, body(): pl.pallas_call(functools.partial(attn_kernel, n_tp, c), out_shape=[pltpu....  7.81 us
    all_to_all x1, starting transfers between devices, body(): lax.all_to_all(packed, 'req', split_axis=0, concat_axis=0, tiled=True)  5.82 us
    all_to_all x1, waiting for transfers between devices, body(): lax.all_to_all(packed, 'req', split_axis=0, concat_axis=0, tiled=True)  5.25 us
    pallas_call x1, Pallas kernels, body(): pl.pallas_call(pack_kernel, out_shape=(pltpu.VMEM((n_req, CAP + PAD, widt...  1.84 us
  transfers between devices with their start and end apart: 24, of which 13 were waited for; matrix products, arithmetic and copies ran while one was open for 0% of the time, Pallas kernels for 28%

profile of v5, /device:TPU:0, one launch (start us, length us, event | category | flops | bytes accessed | tf_op | source)
XLA Modules:
  0.0 77.6 jit_solution(12505206093621701112)
XLA Ops:
  0.0 3.0 %collective-permute-start = (bf16[256,1024]{1,0:T(8,128)(2,1)}, bf16[256,1024]{1,0:T(8,128)(2,1)S(1)}, u32[]{:S(2)}, u32[]{:S(2)}) collective-permute-start(bf16[256,1024]{1,0:T(8,128)(2,1)} %refs_4_.3), channel_id=1, source_target_pairs={{0,2},{1,3},{2,0},{3,1},{4,6},{5,7},{6,4},{7,5},{8,10},{9,11},{10,... | collective-permute-start | bytes 1572872 | tf_op jit(solution)/shard_map/ppermute | solution.py:300
  3.0 1.8 %pack.1 = (bf16[8,72,256]{2,1,0:T(8,128)(2,1)}, s32[8]{0:T(128)S(1)}) custom-call(s32[4,8]{1,0:T(4,128)} %bitcast.41, s32[4,8]{1,0:T(4,128)} %bitcast.42, s32[16]{0:T(128)} %slots_in.1, bf16[8,64,256]{2,1,0:T(8,128)(2,1)} %bitcast.40), custom_call_target="tpu_custom_call" | custom-call | tf_op jit(solution)/shard_map/pack/pallas_call | solution.py:305
  4.8 5.8 %all-to-all-start = ((bf16[8,72,256]{2,1,0:T(8,128)(2,1)}), bf16[8,72,256]{2,1,0:T(8,128)(2,1)S(1)}, u32[]{:S(2)}, u32[]{:S(2)}) async-start(bf16[8,72,256]{2,1,0:T(8,128)(2,1)} %get-tuple-element.51), calls=%async_computation | async-start | bytes 589824 | tf_op jit(solution)/shard_map/all_to_all | solution.py:330
  10.6 0.2 collective-permute-start.2
  10.9 0.5 collective-permute-start.3
  11.4 1.1 %collective-permute-start.4 = (bf16[32,256]{1,0:T(8,128)(2,1)}, bf16[32,256]{1,0:T(8,128)(2,1)S(1)}, u32[]{:S(2)}, u32[]{:S(2)}) collective-permute-start(bf16[32,256]{1,0:T(8,128)(2,1)} %bitcast.33), channel_id=1, source_target_pairs={{0,3},{1,2},{2,1},{3,0},{4,7},{5,6},{6,5},{7,4},{8,11},{9,10},{10,... | collective-permute-start | bytes 49160 | tf_op jit(solution)/shard_map/ppermute | solution.py:300
  12.5 0.0 collective-permute-done.2.refs_9_
  12.5 3.1 %collective-permute-done.3.refs_10_ = bf16[32,256]{1,0:T(8,128)(2,1)S(1)} collective-permute-done((bf16[32,256]{1,0:T(8,128)(2,1)}, bf16[32,256]{1,0:T(8,128)(2,1)S(1)}, u32[]{:S(2)}, u32[]{:S(2)}) %collective-permute-start.3) | collective-permute-done | bytes 16416 | tf_op jit(solution)/shard_map/ppermute | solution.py:300
  15.6 5.3 %all-to-all-done.refs_0_ = bf16[8,72,256]{2,1,0:T(8,128)(2,1)S(1)} async-done(((bf16[8,72,256]{2,1,0:T(8,128)(2,1)}), bf16[8,72,256]{2,1,0:T(8,128)(2,1)S(1)}, u32[]{:S(2)}, u32[]{:S(2)}) %all-to-all-start) | async-done | bytes 294944 | tf_op jit(solution)/shard_map/all_to_all | solution.py:330
  20.9 0.6 collective-permute-start.6
  21.5 0.2 collective-permute-start.5
  21.7 5.5 %collective-permute-done.6.refs_2_ = bf16[4,72,256]{2,1,0:T(8,128)(2,1)S(1)} collective-permute-done((bf16[4,72,256]{2,1,0:T(8,128)(2,1)S(1)}, bf16[4,72,256]{2,1,0:T(8,128)(2,1)S(1)}, u32[]{:S(2)}, u32[]{:S(2)}) %collective-permute-start.6) | collective-permute-done | bytes 147488 | tf_op jit(solution)/shard_map/ppermute | solution.py:300
  27.2 0.5 collective-permute-start.10
  27.8 0.9 %collective-permute-done.7.refs_3_ = bf16[4,72,256]{2,1,0:T(8,128)(2,1)S(1)} collective-permute-done((bf16[4,72,256]{2,1,0:T(8,128)(2,1)S(1)}, bf16[4,72,256]{2,1,0:T(8,128)(2,1)S(1)}, u32[]{:S(2)}, u32[]{:S(2)}) %collective-permute-start.7) | collective-permute-done | bytes 147488 | tf_op jit(solution)/shard_map/ppermute | solution.py:300
  28.6 4.7 %attend.2 = (bf16[256,256]{1,0:T(8,128)(2,1)S(1)}, bf16[256,128]{1,0:T(8,128)(2,1)S(1)}, bf16[256,1024]{1,0:T(8,128)(2,1)S(1)}, bf16[3,1024,256]{2,1,0:T(8,128)(...) custom-call(s32[1]{0:T(128)} %bitcast.3.me, bf16[8,72,256]{2,1,0:T(8,128)(2,1)S(1)} %all-to-all-done.refs_0_, ...), custom_call_target="tpu_custom_call" | custom-call | flops 2181038080 | bytes 2097152 | tf_op jit(solution)/shard_map/attend/pallas_call | solution.py:365
  33.3 0.2 collective-permute-done.10.refs_2_
  33.5 0.0 collective-permute-start.11
  33.5 0.7 collective-permute-start.9
  34.3 0.0 collective-permute-start.15
  34.3 0.6 collective-permute-done.11.refs_3_
  34.9 0.0 copy-start.6
  34.9 0.0 copy-start.7
  34.9 0.0 copy-start.8
  34.9 0.0 copy-start.9
  34.9 0.0 copy-start.10
  34.9 3.1 %attend.3 = (bf16[256,256]{1,0:T(8,128)(2,1)S(1)}, bf16[256,128]{1,0:T(8,128)(2,1)S(1)}, bf16[256,1024]{1,0:T(8,128)(2,1)S(1)}) custom-call(s32[1]{0:T(128)} %bitcast.3.me, bf16[8,72,256]{2,1,0:T(8,128)(2,1)S(1)} %all-to-all-done.refs_0_, bf16[8,72,256]{2,1,0:T(8,128)(2,1)S(1)} %collective-permute-done.5.refs_1_, ...), custom_call_target="tpu_custom_call" | custom-call | flops 2181038080 | bytes 2097152 | tf_op jit(solution)/shard_map/attend/pallas_call | solution.py:365
  38.1 1.3 %collective-permute-done.9.refs_2_ = bf16[256,256]{1,0:T(8,128)(2,1)S(1)} collective-permute-done((bf16[256,256]{1,0:T(8,128)(2,1)S(1)}, bf16[256,256]{1,0:T(8,128)(2,1)S(1)}, u32[]{:S(2)}, u32[]{:S(2)}) %collective-permute-start.9) | collective-permute-done | bytes 131104 | tf_op jit(solution)/shard_map/ppermute | solution.py:300
  39.4 0.5 collective-permute-start.13
  40.0 0.8 %collective-permute-done.16.refs_3_ = bf16[256,256]{1,0:T(8,128)(2,1)S(1)} collective-permute-done((bf16[256,256]{1,0:T(8,128)(2,1)S(1)}, bf16[256,256]{1,0:T(8,128)(2,1)S(1)}, u32[]{:S(2)}, u32[]{:S(2)}) %collective-permute-start.16) | collective-permute-done | bytes 131104 | tf_op jit(solution)/shard_map/ppermute | solution.py:300
  40.8 6.3 %feed.2 = (f32[2,64,1024]{2,1,0:T(8,128)S(1)}, bf16[64,1024]{1,0:T(8,128)(2,1)S(1)}, bf16[1,64,1024]{2,1,0:T(8,128)(2,1)S(1)}, bf16[64,1024]{1,0:T(8,128)(2,1)S(...) custom-call(s32[1]{0:T(128)} %bitcast.3.me, bf16[256,256]{1,0:T(8,128)(2,1)S(1)} %get-tuple-element.64.refs_0_, ...), custom_call_target="tpu_custom_call" | custom-call | flops 8053063680 | bytes 2097152 | tf_op jit(solution)/shard_map/feed/pallas_call | solution.py:409
  47.2 0.2 collective-permute-start.17
  47.4 0.4 collective-permute-start.12
  47.8 0.1 collective-permute-start.19
  47.9 0.4 collective-permute-start.14
  48.3 0.3 collective-permute-done.17
  48.6 0.2 collective-permute-done.12.refs_1_
  48.8 0.5 collective-permute-done.14.refs_3_
  49.3 0.7 collective-permute-start.20
  50.0 5.1 %feed.3 = (f32[2,64,1024]{2,1,0:T(8,128)S(1)}, bf16[64,1024]{1,0:T(8,128)(2,1)S(1)}, bf16[1,64,1024]{2,1,0:T(8,128)(2,1)S(1)}, bf16[64,1024]{1,0:T(8,128)(2,1)S(1)}) custom-call(s32[1]{0:T(128)} %bitcast.3.me, bf16[256,256]{1,0:T(8,128)(2,1)S(1)} %get-tuple-element.78.refs_0_, bf16[256,256]{1,0:T(8,128)(2,1)S(1)} %collective-permute-done.12.refs_1_, ...), custom_call_target="tpu_custom_call" | custom-call | flops 8053063680 | bytes 2097152 | tf_op jit(solution)/shard_map/feed/pallas_call | solution.py:409
  55.2 0.1 collective-permute-start.18
  55.2 0.5 collective-permute-start.21
  55.8 0.2 finish.2.refs_0_
  56.0 0.6 collective-permute-done.18
  56.6 1.4 %collective-permute-start.22 = (bf16[64,1024]{1,0:T(8,128)(2,1)S(1)}, bf16[64,1024]{1,0:T(8,128)(2,1)S(1)}, u32[]{:S(2)}, u32[]{:S(2)}) collective-permute-start(bf16[64,1024]{1,0:T(8,128)(2,1)S(1)} %fusion.1), channel_id=1, source_target_pairs={{0,2},{1,3},{2,0},{3,1},{4,6},{5,7},{6,4},{7,5},{8,10},{9,11},{10,... | collective-permute-start | bytes 393224 | tf_op jit(solution)/shard_map/ppermute | solution.py:300
  58.0 4.3 %collective-permute-done.22.refs_4_ = bf16[64,1024]{1,0:T(8,128)(2,1)S(1)} collective-permute-done((bf16[64,1024]{1,0:T(8,128)(2,1)S(1)}, bf16[64,1024]{1,0:T(8,128)(2,1)S(1)}, u32[]{:S(2)}, u32[]{:S(2)}) %collective-permute-start.22) | collective-permute-done | bytes 131104 | tf_op jit(solution)/shard_map/ppermute | solution.py:300
  62.2 0.2 finish.3
  62.5 13.8 %all_to_all.10 = bf16[32,16,256]{2,1,0:T(8,128)(2,1)S(1)} all-to-all(bf16[32,16,256]{2,1,0:T(8,128)(2,1)S(1)} %bitcast.21), channel_id=1, replica_groups=mesh['req'=8,'tp'=4] {'req','tp'}, dimensions={0} | all-to-all | bytes 524288 | tf_op jit(solution)/shard_map/all_to_all | solution.py:446
  76.3 1.3 %unpack.1 = bf16[8,64,256]{2,1,0:T(8,128)(2,1)} custom-call(s32[8]{0:T(128)S(1)} %get-tuple-element.50.owners, bf16[8,64,256]{2,1,0:T(8,128)(2,1)S(1)} %bitcast.22), custom_call_target="tpu_custom_call" | custom-call | tf_op jit(solution)/shard_map/unpack/pallas_call | solution.py:453
  (34 shorter events, 0.2 us)
Async XLA Ops:
  0.0 20.9 %collective-permute-start = (bf16[256,1024]{1,0:T(8,128)(2,1)}, bf16[256,1024]{1,0:T(8,128)(2,1)S(1)}, u32[]{:S(2)}, u32[]{:S(2)}) collective-permute-start(bf16[256,1024]{1,0:T(8,128)(2,1)} %refs_4_.3), channel_id=1, source_target_pairs={{0,2},{1,3},{2,0},{3,1},{4,6},{5,7},{6,4},{7,5},{8,10},{9,11},{10,... | collective-permute-start | bytes 1572872 | tf_op jit(solution)/shard_map/ppermute | solution.py:300
  3.0 17.9 %collective-permute-start.1 = (bf16[256,1024]{1,0:T(8,128)(2,1)}, bf16[256,1024]{1,0:T(8,128)(2,1)S(1)}, u32[]{:S(2)}, u32[]{:S(2)}) collective-permute-start(bf16[256,1024]{1,0:T(8,128)(2,1)} %refs_4_.3), channel_id=1, source_target_pairs={{0,1},{1,0},{2,3},{3,2},{4,5},{5,4},{6,7},{7,6},{8,9},{9,8},{10,11... | collective-permute-start | bytes 1572872 | tf_op jit(solution)/shard_map/ppermute | solution.py:300
  4.8 16.1 %all-to-all-start = ((bf16[8,72,256]{2,1,0:T(8,128)(2,1)}), bf16[8,72,256]{2,1,0:T(8,128)(2,1)S(1)}, u32[]{:S(2)}, u32[]{:S(2)}) async-start(bf16[8,72,256]{2,1,0:T(8,128)(2,1)} %get-tuple-element.51), calls=%async_computation | async-start | bytes 589824 | tf_op jit(solution)/shard_map/all_to_all | solution.py:330
  10.6 1.9 %collective-permute-start.2 = (bf16[32,256]{1,0:T(8,128)(2,1)}, bf16[32,256]{1,0:T(8,128)(2,1)S(1)}, u32[]{:S(2)}, u32[]{:S(2)}) collective-permute-start(bf16[32,256]{1,0:T(8,128)(2,1)} %bitcast.31), channel_id=1, source_target_pairs={{0,1},{1,0},{2,3},{3,2},{4,5},{5,4},{6,7},{7,6},{8,9},{9,8},{10,11... | collective-permute-start | bytes 49160 | tf_op jit(solution)/shard_map/ppermute | solution.py:300
  10.9 4.8 %collective-permute-start.3 = (bf16[32,256]{1,0:T(8,128)(2,1)}, bf16[32,256]{1,0:T(8,128)(2,1)S(1)}, u32[]{:S(2)}, u32[]{:S(2)}) collective-permute-start(bf16[32,256]{1,0:T(8,128)(2,1)} %bitcast.32), channel_id=1, source_target_pairs={{0,2},{1,3},{2,0},{3,1},{4,6},{5,7},{6,4},{7,5},{8,10},{9,11},{10,... | collective-permute-start | bytes 49160 | tf_op jit(solution)/shard_map/ppermute | solution.py:300
  11.4 4.3 %collective-permute-start.4 = (bf16[32,256]{1,0:T(8,128)(2,1)}, bf16[32,256]{1,0:T(8,128)(2,1)S(1)}, u32[]{:S(2)}, u32[]{:S(2)}) collective-permute-start(bf16[32,256]{1,0:T(8,128)(2,1)} %bitcast.33), channel_id=1, source_target_pairs={{0,3},{1,2},{2,1},{3,0},{4,7},{5,6},{6,5},{7,4},{8,11},{9,10},{10,... | collective-permute-start | bytes 49160 | tf_op jit(solution)/shard_map/ppermute | solution.py:300
  20.9 7.7 %collective-permute-start.8 = (bf16[256,1024]{1,0:T(8,128)(2,1)S(1)}, bf16[256,1024]{1,0:T(8,128)(2,1)S(1)}, u32[]{:S(2)}, u32[]{:S(2)}) collective-permute-start(bf16[256,1024]{1,0:T(8,128)(2,1)S(1)} %collective-permute-done.refs_6_), channel_id=1, source_target_pairs={{0,1},{1,0},{2,3},{3,2},{4,5},{5,4},{6,7},{7,6},{8,9},{9,8},{10,11... | collective-permute-start | bytes 1572872 | tf_op jit(solution)/shard_map/ppermute | solution.py:300
  20.9 6.3 %collective-permute-start.6 = (bf16[4,72,256]{2,1,0:T(8,128)(2,1)S(1)}, bf16[4,72,256]{2,1,0:T(8,128)(2,1)S(1)}, u32[]{:S(2)}, u32[]{:S(2)}) collective-permute-start(bf16[4,72,256]{2,1,0:T(8,128)(2,1)S(1)} %get-tuple-element.96), channel_id=1, source_target_pairs={{0,2},{1,3},{2,0},{3,1},{4,6},{5,7},{6,4},{7,5},{8,10},{9,11},{10,... | collective-permute-start | bytes 442376 | tf_op jit(solution)/shard_map/ppermute | solution.py:300
  21.5 7.1 %collective-permute-start.5 = (bf16[8,72,256]{2,1,0:T(8,128)(2,1)S(1)}, bf16[8,72,256]{2,1,0:T(8,128)(2,1)S(1)}, u32[]{:S(2)}, u32[]{:S(2)}) collective-permute-start(bf16[8,72,256]{2,1,0:T(8,128)(2,1)S(1)} %all-to-all-done.refs_0_), channel_id=1, source_target_pairs={{0,1},{1,0},{2,3},{3,2},{4,5},{5,4},{6,7},{7,6},{8,9},{9,8},{10,11... | collective-permute-start | bytes 884744 | tf_op jit(solution)/shard_map/ppermute | solution.py:300
  27.2 1.4 %collective-permute-start.7 = (bf16[4,72,256]{2,1,0:T(8,128)(2,1)S(1)}, bf16[4,72,256]{2,1,0:T(8,128)(2,1)S(1)}, u32[]{:S(2)}, u32[]{:S(2)}) collective-permute-start(bf16[4,72,256]{2,1,0:T(8,128)(2,1)S(1)} %collective-permute-done.6.refs_2_), channel_id=1, source_target_pairs={{0,1},{1,0},{2,3},{3,2},{4,5},{5,4},{6,7},{7,6},{8,9},{9,8},{10,11... | collective-permute-start | bytes 442376 | tf_op jit(solution)/shard_map/ppermute | solution.py:300
  27.2 6.3 %collective-permute-start.10 = (bf16[4,72,256]{2,1,0:T(8,128)(2,1)S(1)}, bf16[4,72,256]{2,1,0:T(8,128)(2,1)S(1)}, u32[]{:S(2)}, u32[]{:S(2)}) collective-permute-start(bf16[4,72,256]{2,1,0:T(8,128)(2,1)S(1)} %get-tuple-element.95), channel_id=1, source_target_pairs={{0,2},{1,3},{2,0},{3,1},{4,6},{5,7},{6,4},{7,5},{8,10},{9,11},{10,... | collective-permute-start | bytes 442376 | tf_op jit(solution)/shard_map/ppermute | solution.py:300
  33.5 1.4 %collective-permute-start.11 = (bf16[4,72,256]{2,1,0:T(8,128)(2,1)S(1)}, bf16[4,72,256]{2,1,0:T(8,128)(2,1)S(1)}, u32[]{:S(2)}, u32[]{:S(2)}) collective-permute-start(bf16[4,72,256]{2,1,0:T(8,128)(2,1)S(1)} %collective-permute-done.10.refs_2_), channel_id=1, source_target_pairs={{0,1},{1,0},{2,3},{3,2},{4,5},{5,4},{6,7},{7,6},{8,9},{9,8},{10,11... | collective-permute-start | bytes 442376 | tf_op jit(solution)/shard_map/ppermute | solution.py:300
  33.5 5.9 %collective-permute-start.9 = (bf16[256,256]{1,0:T(8,128)(2,1)S(1)}, bf16[256,256]{1,0:T(8,128)(2,1)S(1)}, u32[]{:S(2)}, u32[]{:S(2)}) collective-permute-start(bf16[256,256]{1,0:T(8,128)(2,1)S(1)} %get-tuple-element.64.refs_0_), channel_id=1, source_target_pairs={{0,2},{1,3},{2,0},{3,1},{4,6},{5,7},{6,4},{7,5},{8,10},{9,11},{10,... | collective-permute-start | bytes 393224 | tf_op jit(solution)/shard_map/ppermute | solution.py:300
  34.3 5.7 %collective-permute-start.15 = (bf16[256,256]{1,0:T(8,128)(2,1)S(1)}, bf16[256,256]{1,0:T(8,128)(2,1)S(1)}, u32[]{:S(2)}, u32[]{:S(2)}) collective-permute-start(bf16[256,256]{1,0:T(8,128)(2,1)S(1)} %get-tuple-element.64.refs_0_), channel_id=1, source_target_pairs={{0,1},{1,0},{2,3},{3,2},{4,5},{5,4},{6,7},{7,6},{8,9},{9,8},{10,11... | collective-permute-start | bytes 393224 | tf_op jit(solution)/shard_map/ppermute | solution.py:300
  34.9 5.9 %copy-start.2 = (bf16[256,1024]{1,0:T(8,128)(2,1)S(1)}, bf16[256,1024]{1,0:T(8,128)(2,1)}, u32[]{:S(2)}) copy-start(bf16[256,1024]{1,0:T(8,128)(2,1)} %refs_4_.3) | copy-start | bytes 1572868
  34.9 5.9 %copy-start.3 = (bf16[32,1024]{1,0:T(8,128)(2,1)S(1)}, bf16[32,1024]{1,0:T(8,128)(2,1)}, u32[]{:S(2)}) copy-start(bf16[32,1024]{1,0:T(8,128)(2,1)} %refs_14_.3) | copy-start | bytes 196612
  34.9 5.9 %copy-start.4 = (bf16[1024,32]{0,1:T(8,128)(2,1)S(1)}, bf16[1024,32]{0,1:T(8,128)(2,1)}, u32[]{:S(2)}) copy-start(bf16[1024,32]{0,1:T(8,128)(2,1)} %param.32) | copy-start | bytes 196612
  34.9 5.9 %copy-start.5 = (bf16[32,1024]{1,0:T(8,128)(2,1)S(1)}, bf16[32,1024]{1,0:T(8,128)(2,1)}, u32[]{:S(2)}) copy-start(bf16[32,1024]{1,0:T(8,128)(2,1)} %refs_16_.3) | copy-start | bytes 196612
  34.9 5.9 %copy-start.6 = (bf16[1024,32]{0,1:T(8,128)(2,1)S(1)}, bf16[1024,32]{0,1:T(8,128)(2,1)}, u32[]{:S(2)}) copy-start(bf16[1024,32]{0,1:T(8,128)(2,1)} %param.34) | copy-start | bytes 196612
  34.9 5.9 %copy-start.7 = (bf16[32,1024]{1,0:T(8,128)(2,1)S(1)}, bf16[32,1024]{1,0:T(8,128)(2,1)}, u32[]{:S(2)}) copy-start(bf16[32,1024]{1,0:T(8,128)(2,1)} %refs_18_.3) | copy-start | bytes 196612
  34.9 5.9 %copy-start.8 = (bf16[256,32]{0,1:T(8,128)(2,1)S(1)}, bf16[256,32]{0,1:T(8,128)(2,1)}, u32[]{:S(2)}) copy-start(bf16[256,32]{0,1:T(8,128)(2,1)} %param.30) | copy-start | bytes 49156
  34.9 5.9 %copy-start.9 = (f32[1024]{0:T(1024)S(1)}, f32[1024]{0:T(1024)}, u32[]{:S(2)}) copy-start(f32[1024]{0:T(1024)} %param.36) | copy-start | bytes 12292
  34.9 5.9 %copy-start.10 = (f32[1024]{0:T(1024)S(1)}, f32[1024]{0:T(1024)}, u32[]{:S(2)}) copy-start(f32[1024]{0:T(1024)} %param.37) | copy-start | bytes 12292
  39.4 1.3 %collective-permute-start.16 = (bf16[256,256]{1,0:T(8,128)(2,1)S(1)}, bf16[256,256]{1,0:T(8,128)(2,1)S(1)}, u32[]{:S(2)}, u32[]{:S(2)}) collective-permute-start(bf16[256,256]{1,0:T(8,128)(2,1)S(1)} %collective-permute-done.9.refs_2_), channel_id=1, source_target_pairs={{0,1},{1,0},{2,3},{3,2},{4,5},{5,4},{6,7},{7,6},{8,9},{9,8},{10,11... | collective-permute-start | bytes 393224 | tf_op jit(solution)/shard_map/ppermute | solution.py:300
  39.4 8.5 %collective-permute-start.13 = (bf16[256,256]{1,0:T(8,128)(2,1)S(1)}, bf16[256,256]{1,0:T(8,128)(2,1)S(1)}, u32[]{:S(2)}, u32[]{:S(2)}) collective-permute-start(bf16[256,256]{1,0:T(8,128)(2,1)S(1)} %get-tuple-element.78.refs_0_), channel_id=1, source_target_pairs={{0,2},{1,3},{2,0},{3,1},{4,6},{5,7},{6,4},{7,5},{8,10},{9,11},{10,... | collective-permute-start | bytes 393224 | tf_op jit(solution)/shard_map/ppermute | solution.py:300
  47.2 1.4 %collective-permute-start.17 = (bf16[1,64,1024]{2,1,0:T(8,128)(2,1)S(1)}, bf16[1,64,1024]{2,1,0:T(8,128)(2,1)S(1)}, u32[]{:S(2)}, u32[]{:S(2)}) collective-permute-start(bf16[1,64,1024]{2,1,0:T(8,128)(2,1)S(1)} %get-tuple-element.77), channel_id=1, source_target_pairs={{0,1},{1,0},{2,3},{3,2},{4,5},{5,4},{6,7},{7,6},{8,9},{9,8},{10,11... | collective-permute-start | bytes 393224 | tf_op jit(solution)/shard_map/ppermute | solution.py:300
  47.4 1.4 %collective-permute-start.12 = (bf16[256,256]{1,0:T(8,128)(2,1)S(1)}, bf16[256,256]{1,0:T(8,128)(2,1)S(1)}, u32[]{:S(2)}, u32[]{:S(2)}) collective-permute-start(bf16[256,256]{1,0:T(8,128)(2,1)S(1)} %get-tuple-element.78.refs_0_), channel_id=1, source_target_pairs={{0,1},{1,0},{2,3},{3,2},{4,5},{5,4},{6,7},{7,6},{8,9},{9,8},{10,11... | collective-permute-start | bytes 393224 | tf_op jit(solution)/shard_map/ppermute | solution.py:300
  47.8 8.0 %collective-permute-start.19 = (bf16[64,1024]{1,0:T(8,128)(2,1)S(1)}, bf16[64,1024]{1,0:T(8,128)(2,1)S(1)}, u32[]{:S(2)}, u32[]{:S(2)}) collective-permute-start(bf16[64,1024]{1,0:T(8,128)(2,1)S(1)} %get-tuple-element.87), channel_id=1, source_target_pairs={{0,1},{1,0},{2,3},{3,2},{4,5},{5,4},{6,7},{7,6},{8,9},{9,8},{10,11... | collective-permute-start | bytes 393224 | tf_op jit(solution)/shard_map/ppermute | solution.py:300
  47.9 1.4 %collective-permute-start.14 = (bf16[256,256]{1,0:T(8,128)(2,1)S(1)}, bf16[256,256]{1,0:T(8,128)(2,1)S(1)}, u32[]{:S(2)}, u32[]{:S(2)}) collective-permute-start(bf16[256,256]{1,0:T(8,128)(2,1)S(1)} %collective-permute-done.13.refs_2_), channel_id=1, source_target_pairs={{0,1},{1,0},{2,3},{3,2},{4,5},{5,4},{6,7},{7,6},{8,9},{9,8},{10,11... | collective-permute-start | bytes 393224 | tf_op jit(solution)/shard_map/ppermute | solution.py:300
  49.3 6.4 %collective-permute-start.20 = (bf16[64,1024]{1,0:T(8,128)(2,1)S(1)}, bf16[64,1024]{1,0:T(8,128)(2,1)S(1)}, u32[]{:S(2)}, u32[]{:S(2)}) collective-permute-start(bf16[64,1024]{1,0:T(8,128)(2,1)S(1)} %fusion), channel_id=1, source_target_pairs={{0,2},{1,3},{2,0},{3,1},{4,6},{5,7},{6,4},{7,5},{8,10},{9,11},{10,... | collective-permute-start | bytes 393224 | tf_op jit(solution)/shard_map/ppermute | solution.py:300
  50.0 5.7 %copy-start = (f32[1024]{0:T(1024)S(1)}, f32[1024]{0:T(1024)}, u32[]{:S(2)}) copy-start(f32[1024]{0:T(1024)} %param.38) | copy-start | bytes 12292
  50.0 5.7 %copy-start.1 = (f32[1024]{0:T(1024)S(1)}, f32[1024]{0:T(1024)}, u32[]{:S(2)}) copy-start(f32[1024]{0:T(1024)} %param.39) | copy-start | bytes 12292
  55.2 1.4 %collective-permute-start.18 = (bf16[1,64,1024]{2,1,0:T(8,128)(2,1)S(1)}, bf16[1,64,1024]{2,1,0:T(8,128)(2,1)S(1)}, u32[]{:S(2)}, u32[]{:S(2)}) collective-permute-start(bf16[1,64,1024]{2,1,0:T(8,128)(2,1)S(1)} %get-tuple-element.86), channel_id=1, source_target_pairs={{0,1},{1,0},{2,3},{3,2},{4,5},{5,4},{6,7},{7,6},{8,9},{9,8},{10,11... | collective-permute-start | bytes 393224 | tf_op jit(solution)/shard_map/ppermute | solution.py:300
  55.2 2.7 %collective-permute-start.21 = (bf16[64,1024]{1,0:T(8,128)(2,1)S(1)}, bf16[64,1024]{1,0:T(8,128)(2,1)S(1)}, u32[]{:S(2)}, u32[]{:S(2)}) collective-permute-start(bf16[64,1024]{1,0:T(8,128)(2,1)S(1)} %get-tuple-element.92), channel_id=1, source_target_pairs={{0,1},{1,0},{2,3},{3,2},{4,5},{5,4},{6,7},{7,6},{8,9},{9,8},{10,11... | collective-permute-start | bytes 393224 | tf_op jit(solution)/shard_map/ppermute | solution.py:300
  56.6 5.6 %collective-permute-start.22 = (bf16[64,1024]{1,0:T(8,128)(2,1)S(1)}, bf16[64,1024]{1,0:T(8,128)(2,1)S(1)}, u32[]{:S(2)}, u32[]{:S(2)}) collective-permute-start(bf16[64,1024]{1,0:T(8,128)(2,1)S(1)} %fusion.1), channel_id=1, source_target_pairs={{0,2},{1,3},{2,0},{3,1},{4,6},{5,7},{6,4},{7,5},{8,10},{9,11},{10,... | collective-permute-start | bytes 393224 | tf_op jit(solution)/shard_map/ppermute | solution.py:300

commit v6 on v5

--- a/solution.py
+++ b/solution.py
@@ -87,75 +87,99 @@
     return pl.ds(start if isinstance(start, int) else pl.multiple_of(start, size), size)
 
 
+def begin_kernel(
+    me, own, beside, w_in, w1_in, w2_in, down_in, up_in, *refs
+):
+    acc, low, sel_out, bias_out, w, w1, w2, down, up_all, up, sems = refs
+    pairs = [(up_in, up), (down_in, down)] + [(w_in.at[k], w.at[k]) for k in range(3)]
+    for src, dst in ((w1_in, w1), (w2_in, w2)):
+        half = src.shape[0] // 2
+        pairs += [(src.at[:half], dst.at[:half]), (src.at[half:], dst.at[half:])]
+    copies = fetch(pairs, sems)
+    up_all[...] = jnp.zeros(up_all.shape, BF)
+    copies[0].wait()
+    for k in range(3):
+        for part in range(2):
+            first_row = (3 * part + k) * SPAN
+            up_all[first_row : first_row + SPAN, k * up.shape[2] : (k + 1) * up.shape[2]] = up[k]
+    for c in copies[1:5]:
+        c.wait()
+    blocks = own.shape[0]
+    width = own.shape[2]
+    tp = me[0]
+    spans = [span(tp * width, width), span((tp ^ 1) * width, width)]
+    pair_lane = lax.broadcasted_iota(jnp.int32, (2 * CAP, 2 * CAP), 1)
+    pair_row = lax.broadcasted_iota(jnp.int32, (2 * CAP, 2 * CAP), 0)
+    eye = pair_lane == pair_row
+    lane_sel = ((pair_lane // RANK) % ADAPT_DEV).astype(F32)
+    tile = min(4, blocks)
+
+    def step(t):
+        rs = span(t * (tile * CAP), tile * CAP)
+        bs = pl.ds(t * tile, tile)
+        xs = [part[bs, :CAP, :].reshape(tile * CAP, width) for part in (own, beside)]
+        for k in range(3):
+            acc[k, rs] = dot(xs[0], w[k, spans[0]]) + dot(xs[1], w[k, spans[1]])
+        low[rs] = dot_t(xs[0], down[:, spans[0]]) + dot_t(xs[1], down[:, spans[1]])
+        for p in range(tile // 2):
+            b0 = t * tile + 2 * p
+            c0 = own[b0, CAP : CAP + 1, : 2 * CAP].astype(F32)
+            c1 = own[b0 + 1, CAP : CAP + 1, : 2 * CAP].astype(F32) + 64.0
+            idr = jnp.where(pair_lane < CAP, c0, c1)
+            idc = jnp.sum(jnp.where(eye, idr, 0.0), axis=1, keepdims=True)
+            ps = span(t * (tile * CAP) + p * 2 * CAP, 2 * CAP)
+            bias_out[ps] = jnp.where(idr == idc, 0.0, -1e30)
+            pick = idc - 1.0
+            pick = pick - 2.0 * jnp.floor(pick * 0.5)
+            sel_out[ps] = (lane_sel == pick).astype(BF)
+
+    tiles(blocks // tile, step)
+    for c in copies[5:]:
+        c.wait()
+
+
 def attn_kernel(n_tp, chunk, me, *refs):
     parts = refs[:n_tp]
-    copies = None
-    if chunk == 0:
-        w_in, down_in, up_in, att, sel_out, x_full, w, down, up_all, up, sems = refs[n_tp:]
-        copies = fetch(
-            [(down_in, down), (up_in, up)] + [(w_in.at[k], w.at[k]) for k in range(3)], sems
-        )
-    else:
-        w, down, up_all, att, sel_out, x_full = refs[n_tp:]
+    acc, low_in, sel_in, bias, w, down, up_all, att, x_full = refs[n_tp:]
     blocks = att.shape[0] // CAP
     width = parts[0].shape[2]
     rows = blocks * CAP
     tp = me[0]
-    offsets = [chunk * blocks if part.shape[0] > blocks else 0 for part in parts]
+    spans = [span((tp ^ r) * width, width) for r in range(n_tp)]
     for r in range(n_tp):
-        x_full[:, span((tp ^ r) * width, width)] = parts[r][
-            offsets[r] : offsets[r] + blocks, :CAP, :
-        ].reshape(rows, width)
-    if chunk == 0:
-        up_all[...] = jnp.zeros(up_all.shape, BF)
-        copies[0].wait()
-        copies[1].wait()
-        for k in range(3):
-            for part in range(2):
-                first_row = (3 * part + k) * SPAN
-                up_all[first_row : first_row + SPAN, k * width : (k + 1) * width] = up[k]
-    pair_lane = lax.broadcasted_iota(jnp.int32, (2 * CAP, 2 * CAP), 1)
-    pair_row = lax.broadcasted_iota(jnp.int32, (2 * CAP, 2 * CAP), 0)
-    eye = pair_lane == pair_row
-    lane_sel = ((pair_lane // RANK) % ADAPT_DEV).astype(F32)
-    first = pair_lane < HEAD_DIM
+        offset = chunk * blocks if part_of(parts[r], blocks) else 0
+        x_full[:, spans[r]] = parts[r][offset : offset + blocks, :CAP, :].reshape(rows, width)
+    first = lax.broadcasted_iota(jnp.int32, (2 * CAP, 2 * CAP), 1) < HEAD_DIM
     zero = jnp.zeros((), BF)
     tile = min(4, blocks)
 
     def step(t):
-        rs = span(t * (tile * CAP), tile * CAP)
-        masks, sels = [], []
-        for p in range(tile // 2):
-            b0 = offsets[0] + t * tile + 2 * p
-            c0 = parts[0][b0, CAP : CAP + 1, : 2 * CAP].astype(F32)
-            c1 = parts[0][b0 + 1, CAP : CAP + 1, : 2 * CAP].astype(F32) + 64.0
-            idr = jnp.where(pair_lane < CAP, c0, c1)
-            idc = jnp.sum(jnp.where(eye, idr, 0.0), axis=1, keepdims=True)
-            masks.append(idr == idc)
-            pick = idc - 1.0
-            pick = pick - 2.0 * jnp.floor(pick * 0.5)
-            sels.append((lane_sel == pick).astype(F32))
-        sel = jnp.concatenate(sels, axis=0)
-        sel_out[rs] = sel.astype(BF)
-        x = x_full[rs]
-        low = split_low(dot_t(x, down[...]), sel[:, : 3 * SPAN])
+        start = t * (tile * CAP)
+        rs = span(start, tile * CAP)
+        whole = span(chunk * rows + start, tile * CAP)
+        bs = pl.ds(t * tile, tile)
+        xs = [parts[r][bs, :CAP, :].reshape(tile * CAP, width) for r in range(2, n_tp)]
+        low = low_in[whole]
+        for r in range(2, n_tp):
+            low = low + dot_t(xs[r - 2], down[:, spans[r]])
+        low = split_low(low, sel_in[whole].astype(F32)[:, : 3 * SPAN])
         qkv = []
         for k in range(3):
-            if copies and isinstance(t, int):
-                copies[2 + k].wait()
-            qkv.append(dot(x, w[k]) + dot(low, up_all[:, k * width : (k + 1) * width]))
+            total = acc[k, whole] + dot(low, up_all[:, k * width : (k + 1) * width])
+            for r in range(2, n_tp):
+                total = total + dot(xs[r - 2], w[k, spans[r]])
+            qkv.append(total.astype(BF))
         q, k_, v = qkv
-        q = (q.astype(BF).astype(F32) * HEAD_DIM**-0.5).astype(BF)
-        k_, v = k_.astype(BF), v.astype(BF)
+        q = (q.astype(F32) * HEAD_DIM**-0.5).astype(BF)
         for p in range(tile // 2):
             prs = slice(p * 2 * CAP, (p + 1) * 2 * CAP)
-            out_rows = span(t * (tile * CAP) + p * 2 * CAP, 2 * CAP)
+            out_rows = span(start + p * 2 * CAP, 2 * CAP)
+            mask = bias[span(chunk * rows + start + p * 2 * CAP, 2 * CAP)]
             for h in range(width // (2 * HEAD_DIM)):
                 cs = slice(h * 2 * HEAD_DIM, (h + 1) * 2 * HEAD_DIM)
                 both = []
                 for half in (first, ~first):
-                    s = dot_t(jnp.where(half, q[prs, cs], zero), k_[prs, cs])
-                    s = jnp.where(masks[p], s, -1e30)
+                    s = dot_t(jnp.where(half, q[prs, cs], zero), k_[prs, cs]) + mask
                     e = jnp.exp(s - jnp.max(s, axis=-1, keepdims=True))
                     inv = 1.0 / jnp.sum(e, axis=-1, keepdims=True)
                     both.append(dot((e * inv).astype(BF), v[prs, cs]))
@@ -164,15 +188,14 @@
     tiles(blocks // tile, step)
 
 
+def part_of(array, blocks):
+    return array.shape[0] > blocks
+
+
 def ffn_kernel(n_tp, chunk, me, *refs):
     atts, wouts, odowns = refs[:n_tp], refs[n_tp : 2 * n_tp], refs[2 * n_tp : 3 * n_tp]
-    x, sel_in, oup, d1, u1, d2, u2, g1, b1 = refs[3 * n_tp : 3 * n_tp + 9]
-    copies = None
-    if chunk == 0:
-        w1_in, w2_in, even, odd, odds, h_own, w1, w2, h_scr, sems = refs[3 * n_tp + 9 :]
-        copies = fetch([(w1_in, w1), (w2_in, w2)], sems)
-    else:
-        w1, w2, even, odd, odds, h_own, h_scr = refs[3 * n_tp + 9 :]
+    x, sel_in, oup, d1, u1, d2, u2, g1, b1, w1, w2 = refs[3 * n_tp : 3 * n_tp + 11]
+    even, odd, odds, h_own, h_scr = refs[3 * n_tp + 11 :]
     rows, feat = x.shape
     blocks = rows // CAP
     share = CAP // n_tp
@@ -183,7 +206,7 @@
 
     def step(t):
         rs = span(t * size, size)
-        sel = sel_in[rs].astype(F32)[:, :SPAN]
+        sel = sel_in[span(chunk * rows + t * size, size)].astype(F32)[:, :SPAN]
         total = x[rs].astype(F32)
         low = None
         for r in range(n_tp):
@@ -194,12 +217,8 @@
         total = total + dot(split_low(low, sel), ups[0])
         h1 = layer_norm(total, g1[...], b1[...]).astype(BF)
         h_scr[span(t * nb, nb)] = h1.reshape(nb, n_tp, share, feat)
-        if copies and isinstance(t, int):
-            copies[0].wait()
         gate = dot(h1, w1[...]) + dot(split_low(dot_t(h1, d1[...]), sel), ups[1])
         hidden = (0.5 * gate * (1.0 + lax.erf(gate * 0.7071067811865476))).astype(BF)
-        if copies and isinstance(t, int):
-            copies[1].wait()
         term = dot(hidden, w2[...]) + dot(split_low(dot_t(hidden, d2[...]), sel), ups[2])
         term = term.reshape(nb, n_tp, share, feat)
         own_rows = span(t * (size // n_tp), size // n_tp)
@@ -327,10 +346,13 @@
             tokens.reshape(blocks, CAP, width),
         )
     )
+    packed, me, w_first, o_first = lax.optimization_barrier(
+        (packed, me, w_out, out_down.T)
+    )
     arrived = lax.all_to_all(packed, "req", split_axis=0, concat_axis=0, tiled=True)
-    w_far = [swap(w_out, 2 * y) for y in range(1, half)]
-    w_near = swap(w_out, 1)
-    odowns = [out_down.T] + [swap(out_down.T, r) for r in range(1, n_tp)]
+    w_far = [swap(w_first, 2 * y) for y in range(1, half)]
+    w_near = swap(w_first, 1)
+    odowns = [out_down.T] + [swap(o_first, r) for r in range(1, n_tp)]
     arrived, w_far, w_near, odowns = lax.optimization_barrier((arrived, w_far, w_near, odowns))
     count = 2
     step_blocks = n_req // count
@@ -341,51 +363,68 @@
     for c in range(count):
         piece = arrived[c * step_blocks : (c + 1) * step_blocks]
         x_far.append([swap(piece, 2 * y) for y in range(1, half)])
-    wouts = [w_out, w_near] + second_hop(w_far)
+    *begun, w_all, w1, w2, downs, up_all = pl.pallas_call(
+        begin_kernel,
+        out_shape=[
+            pltpu.VMEM((3, count * rows, width), F32),
+            pltpu.VMEM((count * rows, 3 * SPAN), F32),
+            pltpu.VMEM((count * rows, 4 * SPAN), BF),
+            pltpu.VMEM((count * rows, 2 * CAP), F32),
+            pltpu.VMEM((3, feat, width), BF),
+            pltpu.VMEM(w_fc1.shape, BF),
+            pltpu.VMEM(w_fc2.shape, BF),
+            pltpu.VMEM((3 * SPAN, feat), BF),
+            pltpu.VMEM((6 * SPAN, 3 * width), BF),
+        ],
+        in_specs=[SMEM] + [VM] * 2 + [HBM] * 5,
+        out_specs=[VM] * 9,
+        scratch_shapes=[
+            pltpu.VMEM((3, SPAN, width), BF),
+            pltpu.SemaphoreType.DMA((9,)),
+        ],
+        compiler_params=params(8),
+        cost_estimate=work(rows * feat * 3 * width, rows),
+        name="begin",
+    )(
+        me,
+        *near(arrived, beside),
+        *far(
+            w_qkv,
+            w_fc1,
+            w_fc2,
+            jnp.swapaxes(qkv_down, 1, 2).reshape(3 * SPAN, feat),
+            qkv_up,
+        ),
+    )
+    w_all, w1, w2, downs, up_all = near(w_all, w1, w2, downs, up_all)
+    x_far[0], begun = lax.optimization_barrier((x_far[0], begun))
     x_far[0] = second_hop(x_far[0])
-    x_far[0], wouts = lax.optimization_barrier((x_far[0], wouts))
-
-    qkv_weights = far(
-        w_qkv, jnp.swapaxes(qkv_down, 1, 2).reshape(3 * SPAN, feat), qkv_up
-    )
-    ffn_weights = far(w_fc1, w_fc2)
+
     consts = near(
         out_up, fc1_down.T, fc1_up, fc2_down.T, fc2_up, norm1_gain[None], norm1_bias[None]
     )
+    sel = begun[2]
     steps = []
     for c in range(count):
         if c:
-            x_far[c], steps[0][0] = lax.optimization_barrier((x_far[c], steps[0][0]))
+            x_far[c], w_far, steps[0][0] = lax.optimization_barrier(
+                (x_far[c], w_far, steps[0][0])
+            )
             x_far[c] = second_hop(x_far[c])
-        keep = [] if c else [
-            pltpu.VMEM((3, feat, width), BF),
-            pltpu.VMEM((3 * SPAN, feat), BF),
-            pltpu.VMEM((6 * SPAN, 3 * width), BF),
-        ]
-        attended, sel, x_full, *kept = pl.pallas_call(
+        attended, x_full = pl.pallas_call(
             functools.partial(attn_kernel, n_tp, c),
-            out_shape=[
-                pltpu.VMEM((rows, width), BF),
-                pltpu.VMEM((rows, 4 * SPAN), BF),
-                pltpu.VMEM((rows, feat), BF),
-            ]
-            + keep,
-            in_specs=[SMEM] + [VM] * n_tp + [VM if c else HBM] * 3,
-            out_specs=[VM] * (3 + len(keep)),
-            scratch_shapes=[] if c else [
-                pltpu.VMEM((3, SPAN, width), BF),
-                pltpu.SemaphoreType.DMA((5,)),
-            ],
+            out_shape=[pltpu.VMEM((rows, width), BF), pltpu.VMEM((rows, feat), BF)],
+            in_specs=[SMEM] + [VM] * (n_tp + 7),
+            out_specs=[VM] * 2,
             compiler_params=params(12),
             cost_estimate=work(2 * rows * feat * 3 * width + 4 * rows * width * 2 * CAP, rows),
             name="attend",
-        )(me, *near(arrived, beside, *x_far[c]), *qkv_weights)
-        if c == 0:
-            qkv_weights = near(*kept)
+        )(me, *near(arrived, beside, *x_far[c], *begun), w_all, downs, up_all)
         y_got = [swap(attended, 2 * y) for y in range(1, half)]
         if c:
             steps[0][1], attended = lax.optimization_barrier((steps[0][1], attended))
-        steps.append([attended, y_got, sel, x_full])
+        steps.append([attended, y_got, x_full])
+    wouts = [w_out, w_near] + second_hop(w_far)
 
     def finish(earlier, *values):
         blocks_done = step_blocks + sum(e.shape[0] for e in earlier)
@@ -400,38 +439,26 @@
         )(*values)
 
     for c in range(count):
-        attended, y_got, sel, x_full = steps[c]
+        attended, y_got, x_full = steps[c]
         atts = second_hop([attended] + y_got)
         if c:
             atts, firsts = lax.optimization_barrier((atts, firsts))
             firsts = [swap(piece, 2 * (y + 1)) for y, piece in enumerate(firsts)]
-        keep = [] if c else [pltpu.VMEM(w_fc1.shape, BF), pltpu.VMEM(w_fc2.shape, BF)]
-        even, odd, odds, h_own, *kept = pl.pallas_call(
+        even, odd, odds, h_own = pl.pallas_call(
             functools.partial(ffn_kernel, n_tp, c),
             out_shape=[
                 pltpu.VMEM((half, own, feat), F32),
                 pltpu.VMEM((own, feat), BF),
                 pltpu.VMEM((half - 1, own, feat), BF),
                 pltpu.VMEM((own, feat), BF),
-            ]
-            + keep,
-            in_specs=[SMEM]
-            + [VM] * (3 * n_tp + 2 + len(consts))
-            + [VM if c else HBM] * 2,
-            out_specs=[VM] * (4 + len(keep)),
-            scratch_shapes=[pltpu.VMEM((step_blocks, n_tp, share, feat), BF)]
-            + ([] if c else [pltpu.SemaphoreType.DMA((2,))]),
+            ],
+            in_specs=[SMEM] + [VM] * (3 * n_tp + 4 + len(consts)),
+            out_specs=[VM] * 4,
+            scratch_shapes=[pltpu.VMEM((step_blocks, n_tp, share, feat), BF)],
             compiler_params=params(16),
             cost_estimate=work(2 * rows * feat * (2 * w_fc1.shape[1] + feat), rows),
             name="feed",
-        )(
-            me,
-            *near(*atts, *wouts, *odowns, x_full, sel),
-            *consts,
-            *ffn_weights,
-        )
-        if c == 0:
-            ffn_weights = near(*kept)
+        )(me, *near(*atts, *wouts, *odowns, x_full, sel), *consts, w1, w2)
         gots = swap(odds, 1)
         if c:
             earlier = finish([], *first_ends, *firsts)

time: 77.9 us -> 76.7 us (0.985)
    pallas_call x0 -> x1, Pallas kernels: none -> 2.86 us  [body(): pl.pallas_call(begin_kernel, out_shape=[pltpu.VMEM((3, count * rows, widt...]
    pallas_call x2, Pallas kernels: 7.81 us -> 5.52 us  [body(): pl.pallas_call(functools.partial(attn_kernel, n_tp, c), out_shape=[pltpu....]
    all_to_all x1, waiting for transfers between devices: 5.25 us -> 3.39 us  [body(): lax.all_to_all(packed, 'req', split_axis=0, concat_axis=0, tiled=True)]
    ppermute x23, waiting for transfers between devices: 18.3 us -> 19.5 us  [swap(): return lax.ppermute(value, 'tp', [(i, i ^ r) for i in range(n_tp)])]
    pallas_call x2, Pallas kernels: 11.5 us -> 10.2 us  [body(): pl.pallas_call(functools.partial(ffn_kernel, n_tp, c), out_shape=[pltpu.V...]
  transfers between devices with their start and end apart: 24 -> 24, of which waited for: 13 -> 14; matrix products, arithmetic and copies ran while one was open for 0% -> 0% of each run, Pallas kernels for 28% -> 25%
where the time goes in v6:
time: 76.7 us; the launch traced here: 76.5 us
  waiting for transfers between devices  22.9 us (30%)
  Pallas kernels  22.2 us (29%)
  starting transfers between devices  17.1 us (22%)
  blocking collectives  13.9 us (18%)
    ppermute x23, waiting for transfers between devices, swap(): return lax.ppermute(value, 'tp', [(i, i ^ r) for i in range(n_tp)])  19.5 us
    all_to_all x1, blocking collectives, body(): lax.all_to_all(done.reshape(n_req * n_tp, share, width), ('req', 'tp'), s...  13.9 us
    ppermute x23, starting transfers between devices, swap(): return lax.ppermute(value, 'tp', [(i, i ^ r) for i in range(n_tp)])  11.3 us
    pallas_call x2, Pallas kernels, body(): pl.pallas_call(functools.partial(ffn_kernel, n_tp, c), out_shape=[pltpu.V...  10.2 us
    all_to_all x1, starting transfers between devices, body(): lax.all_to_all(packed, 'req', split_axis=0, concat_axis=0, tiled=True)  5.81 us
    pallas_call x2, Pallas kernels, body(): pl.pallas_call(functools.partial(attn_kernel, n_tp, c), out_shape=[pltpu....  5.52 us
    all_to_all x1, waiting for transfers between devices, body(): lax.all_to_all(packed, 'req', split_axis=0, concat_axis=0, tiled=True)  3.39 us
    pallas_call x1, Pallas kernels, body(): pl.pallas_call(begin_kernel, out_shape=[pltpu.VMEM((3, count * rows, widt...  2.86 us
  transfers between devices with their start and end apart: 24, of which 14 were waited for; matrix products, arithmetic and copies ran while one was open for 0% of the time, Pallas kernels for 25%

profile of v6, /device:TPU:0, one launch (start us, length us, event | category | flops | bytes accessed | tf_op | source)
XLA Modules:
  0.0 76.5 jit_solution(8421565319401306844)
XLA Ops:
  0.0 1.8 %pack.1 = (bf16[8,72,256]{2,1,0:T(8,128)(2,1)}, s32[8]{0:T(128)S(1)}) custom-call(s32[4,8]{1,0:T(4,128)} %bitcast.42, s32[4,8]{1,0:T(4,128)} %bitcast.43, s32[16]{0:T(128)} %slots_in.1, bf16[8,64,256]{2,1,0:T(8,128)(2,1)} %bitcast.40), custom_call_target="tpu_custom_call" | custom-call | tf_op jit(solution)/shard_map/pack/pallas_call | solution.py:324
  1.8 3.0 %collective-permute-start = (bf16[256,1024]{1,0:T(8,128)(2,1)}, bf16[256,1024]{1,0:T(8,128)(2,1)S(1)}, u32[]{:S(2)}, u32[]{:S(2)}) collective-permute-start(bf16[256,1024]{1,0:T(8,128)(2,1)} %refs_4_.3), channel_id=1, source_target_pairs={{0,2},{1,3},{2,0},{3,1},{4,6},{5,7},{6,4},{7,5},{8,10},{9,11},{10,... | collective-permute-start | bytes 1572872 | tf_op jit(solution)/shard_map/ppermute | solution.py:319
  4.9 5.8 %all-to-all-start = ((bf16[8,72,256]{2,1,0:T(8,128)(2,1)}), bf16[8,72,256]{2,1,0:T(8,128)(2,1)S(1)}, u32[]{:S(2)}, u32[]{:S(2)}) async-start(bf16[8,72,256]{2,1,0:T(8,128)(2,1)} %get-tuple-element.59), calls=%async_computation | async-start | bytes 589824 | tf_op jit(solution)/shard_map/all_to_all | solution.py:352
  10.7 0.2 collective-permute-start.2
  10.9 0.5 collective-permute-start.3
  11.4 1.1 %collective-permute-start.4 = (bf16[32,256]{1,0:T(8,128)(2,1)}, bf16[32,256]{1,0:T(8,128)(2,1)S(1)}, u32[]{:S(2)}, u32[]{:S(2)}) collective-permute-start(bf16[32,256]{1,0:T(8,128)(2,1)} %bitcast.33), channel_id=1, source_target_pairs={{0,3},{1,2},{2,1},{3,0},{4,7},{5,6},{6,5},{7,4},{8,11},{9,10},{10,... | collective-permute-start | bytes 49160 | tf_op jit(solution)/shard_map/ppermute | solution.py:319
  12.6 5.0 %collective-permute-done.3.refs_10_ = bf16[32,256]{1,0:T(8,128)(2,1)S(1)} collective-permute-done((bf16[32,256]{1,0:T(8,128)(2,1)}, bf16[32,256]{1,0:T(8,128)(2,1)S(1)}, u32[]{:S(2)}, u32[]{:S(2)}) %collective-permute-start.3) | collective-permute-done | bytes 16416 | tf_op jit(solution)/shard_map/ppermute | solution.py:319
  17.5 3.4 %all-to-all-done.own.refs_0_ = bf16[8,72,256]{2,1,0:T(8,128)(2,1)S(1)} async-done(((bf16[8,72,256]{2,1,0:T(8,128)(2,1)}), bf16[8,72,256]{2,1,0:T(8,128)(2,1)S(1)}, u32[]{:S(2)}, u32[]{:S(2)}) %all-to-all-start) | async-done | bytes 294944 | tf_op jit(solution)/shard_map/all_to_all | solution.py:352
  21.0 0.6 collective-permute-start.6
  21.5 1.0 %collective-permute-done.5.beside.refs_1_ = bf16[8,72,256]{2,1,0:T(8,128)(2,1)S(1)} collective-permute-done((bf16[8,72,256]{2,1,0:T(8,128)(2,1)S(1)}, bf16[8,72,256]{2,1,0:T(8,128)(2,1)S(1)}, u32[]{:S(2)}, u32[]{:S(2)}) %collective-permute-start.5) | collective-permute-done | bytes 294944 | tf_op jit(solution)/shard_map/ppermute | solution.py:319
  22.5 2.9 %begin.1 = (f32[3,512,256]{2,1,0:T(8,128)S(1)}, f32[512,96]{1,0:T(8,128)S(1)}, bf16[512,128]{1,0:T(8,128)(2,1)S(1)}, f32[512,128]{1,0:T(8,128)S(1)}, bf16[3,1024...) custom-call(s32[1]{0:T(128)} %bitcast.3.me, ...), custom_call_target="tpu_custom_call" | custom-call | flops 1006632960 | bytes 2097152 | tf_op jit(solution)/shard_map/begin/pallas_call | solution.py:366
  25.4 1.9 %collective-permute-done.6.refs_2_ = bf16[4,72,256]{2,1,0:T(8,128)(2,1)S(1)} collective-permute-done((bf16[4,72,256]{2,1,0:T(8,128)(2,1)S(1)}, bf16[4,72,256]{2,1,0:T(8,128)(2,1)S(1)}, u32[]{:S(2)}, u32[]{:S(2)}) %collective-permute-start.6) | collective-permute-done | bytes 147488 | tf_op jit(solution)/shard_map/ppermute | solution.py:319
  27.3 0.5 collective-permute-start.9
  27.8 0.9 %collective-permute-done.7.refs_3_ = bf16[4,72,256]{2,1,0:T(8,128)(2,1)S(1)} collective-permute-done((bf16[4,72,256]{2,1,0:T(8,128)(2,1)S(1)}, bf16[4,72,256]{2,1,0:T(8,128)(2,1)S(1)}, u32[]{:S(2)}, u32[]{:S(2)}) %collective-permute-start.7) | collective-permute-done | bytes 147488 | tf_op jit(solution)/shard_map/ppermute | solution.py:319
  28.7 2.8 %attend.2 = (bf16[256,256]{1,0:T(8,128)(2,1)S(1)}, bf16[256,1024]{1,0:T(8,128)(2,1)S(1)}) custom-call(s32[1]{0:T(128)} %bitcast.3.me, bf16[8,72,256]{2,1,0:T(8,128)(2,1)S(1)} %all-to-all-done.own.refs_0_, bf16[8,72,256]{2,1,0:T(8,128)(2,1)S(1)} %collective-permute-done.5.beside.refs_1_, bf16[4,72,256]{2,1,0:T(8,128)(2,1)S(1)} %collective-permute-done.6.refs_2_, ...), custom_call_target="tpu_custom_call" | custom-call | flops 2181038080 | bytes 2097152 | tf_op jit(solution)/shard_map/attend/pallas_call | solution.py:414
  31.4 2.1 %collective-permute-done.9.refs_2_ = bf16[4,72,256]{2,1,0:T(8,128)(2,1)S(1)} collective-permute-done((bf16[4,72,256]{2,1,0:T(8,128)(2,1)S(1)}, bf16[4,72,256]{2,1,0:T(8,128)(2,1)S(1)}, u32[]{:S(2)}, u32[]{:S(2)}) %collective-permute-start.9) | collective-permute-done | bytes 147488 | tf_op jit(solution)/shard_map/ppermute | solution.py:319
  33.6 0.0 copy-start.6
  33.6 0.0 copy-start.7
  33.6 0.0 copy-start.8
  33.6 0.0 copy-start.9
  33.6 0.0 copy-start.10
  33.6 0.1 collective-permute-start.16
  33.7 0.5 collective-permute-start.10
  34.2 0.5 collective-permute-start.8
  34.7 1.1 %collective-permute-done.10.refs_3_ = bf16[4,72,256]{2,1,0:T(8,128)(2,1)S(1)} collective-permute-done((bf16[4,72,256]{2,1,0:T(8,128)(2,1)S(1)}, bf16[4,72,256]{2,1,0:T(8,128)(2,1)S(1)}, u32[]{:S(2)}, u32[]{:S(2)}) %collective-permute-start.10) | collective-permute-done | bytes 147488 | tf_op jit(solution)/shard_map/ppermute | solution.py:319
  35.8 2.8 %attend.3 = (bf16[256,256]{1,0:T(8,128)(2,1)S(1)}, bf16[256,1024]{1,0:T(8,128)(2,1)S(1)}) custom-call(s32[1]{0:T(128)} %bitcast.3.me, bf16[8,72,256]{2,1,0:T(8,128)(2,1)S(1)} %all-to-all-done.own.refs_0_, bf16[8,72,256]{2,1,0:T(8,128)(2,1)S(1)} %collective-permute-done.5.beside.refs_1_, bf16[4,72,256]{2,1,0:T(8,128)(2,1)S(1)} %collective-permute-done.9.refs_2_, ...), custom_call_target="tpu_custom_call" | custom-call | flops 2181038080 | bytes 2097152 | tf_op jit(solution)/shard_map/attend/pallas_call | solution.py:414
  38.6 1.1 %collective-permute-done.8.refs_2_ = bf16[256,256]{1,0:T(8,128)(2,1)S(1)} collective-permute-done((bf16[256,256]{1,0:T(8,128)(2,1)S(1)}, bf16[256,256]{1,0:T(8,128)(2,1)S(1)}, u32[]{:S(2)}, u32[]{:S(2)}) %collective-permute-start.8) | collective-permute-done | bytes 131104 | tf_op jit(solution)/shard_map/ppermute | solution.py:319
  39.7 0.5 collective-permute-start.12
  40.2 0.8 %collective-permute-done.15.refs_3_ = bf16[256,256]{1,0:T(8,128)(2,1)S(1)} collective-permute-done((bf16[256,256]{1,0:T(8,128)(2,1)S(1)}, bf16[256,256]{1,0:T(8,128)(2,1)S(1)}, u32[]{:S(2)}, u32[]{:S(2)}) %collective-permute-start.15) | collective-permute-done | bytes 131104 | tf_op jit(solution)/shard_map/ppermute | solution.py:319
  41.1 5.1 %feed.2 = (f32[2,64,1024]{2,1,0:T(8,128)S(1)}, bf16[64,1024]{1,0:T(8,128)(2,1)S(1)}, bf16[1,64,1024]{2,1,0:T(8,128)(2,1)S(1)}, bf16[64,1024]{1,0:T(8,128)(2,1)S(1)}) custom-call(s32[1]{0:T(128)} %bitcast.3.me, bf16[256,256]{1,0:T(8,128)(2,1)S(1)} %get-tuple-element.80.refs_0_, bf16[256,256]{1,0:T(8,128)(2,1)S(1)} %collective-permute-done.14.refs_1_, ...), custom_call_target="tpu_custom_call" | custom-call | flops 8053063680 | bytes 2097152 | tf_op jit(solution)/shard_map/feed/pallas_call | solution.py:447
  46.3 0.2 collective-permute-start.17
  46.5 0.4 collective-permute-start.11
  46.8 0.1 collective-permute-start.13
  47.0 0.4 collective-permute-start.19
  47.3 0.3 collective-permute-done.17
  47.7 0.2 collective-permute-done.11.refs_1_
  47.9 0.3 collective-permute-done.13.refs_3_
  48.2 0.7 collective-permute-start.20
  48.9 5.1 %feed.3 = (f32[2,64,1024]{2,1,0:T(8,128)S(1)}, bf16[64,1024]{1,0:T(8,128)(2,1)S(1)}, bf16[1,64,1024]{2,1,0:T(8,128)(2,1)S(1)}, bf16[64,1024]{1,0:T(8,128)(2,1)S(1)}) custom-call(s32[1]{0:T(128)} %bitcast.3.me, bf16[256,256]{1,0:T(8,128)(2,1)S(1)} %get-tuple-element.93.refs_0_, bf16[256,256]{1,0:T(8,128)(2,1)S(1)} %collective-permute-done.11.refs_1_, ...), custom_call_target="tpu_custom_call" | custom-call | flops 8053063680 | bytes 2097152 | tf_op jit(solution)/shard_map/feed/pallas_call | solution.py:447
  54.0 0.1 collective-permute-start.18
  54.1 0.5 collective-permute-start.21
  54.6 0.2 finish.2.refs_0_
  54.9 0.6 collective-permute-done.18
  55.5 1.4 %collective-permute-start.22 = (bf16[64,1024]{1,0:T(8,128)(2,1)S(1)}, bf16[64,1024]{1,0:T(8,128)(2,1)S(1)}, u32[]{:S(2)}, u32[]{:S(2)}) collective-permute-start(bf16[64,1024]{1,0:T(8,128)(2,1)S(1)} %fusion.1), channel_id=1, source_target_pairs={{0,2},{1,3},{2,0},{3,1},{4,6},{5,7},{6,4},{7,5},{8,10},{9,11},{10,... | collective-permute-start | bytes 393224 | tf_op jit(solution)/shard_map/ppermute | solution.py:319
  56.9 4.2 %collective-permute-done.22.refs_4_ = bf16[64,1024]{1,0:T(8,128)(2,1)S(1)} collective-permute-done((bf16[64,1024]{1,0:T(8,128)(2,1)S(1)}, bf16[64,1024]{1,0:T(8,128)(2,1)S(1)}, u32[]{:S(2)}, u32[]{:S(2)}) %collective-permute-start.22) | collective-permute-done | bytes 131104 | tf_op jit(solution)/shard_map/ppermute | solution.py:319
  61.1 0.2 finish.3
  61.3 13.9 %all_to_all.10 = bf16[32,16,256]{2,1,0:T(8,128)(2,1)S(1)} all-to-all(bf16[32,16,256]{2,1,0:T(8,128)(2,1)S(1)} %bitcast.21), channel_id=1, replica_groups=mesh['req'=8,'tp'=4] {'req','tp'}, dimensions={0} | all-to-all | bytes 524288 | tf_op jit(solution)/shard_map/all_to_all | solution.py:473
  75.2 1.3 %unpack.1 = bf16[8,64,256]{2,1,0:T(8,128)(2,1)} custom-call(s32[8]{0:T(128)S(1)} %get-tuple-element.56.owners, bf16[8,64,256]{2,1,0:T(8,128)(2,1)S(1)} %bitcast.22), custom_call_target="tpu_custom_call" | custom-call | tf_op jit(solution)/shard_map/unpack/pallas_call | solution.py:480
  (35 shorter events, 0.2 us)
Async XLA Ops:
  1.8 19.1 %collective-permute-start = (bf16[256,1024]{1,0:T(8,128)(2,1)}, bf16[256,1024]{1,0:T(8,128)(2,1)S(1)}, u32[]{:S(2)}, u32[]{:S(2)}) collective-permute-start(bf16[256,1024]{1,0:T(8,128)(2,1)} %refs_4_.3), channel_id=1, source_target_pairs={{0,2},{1,3},{2,0},{3,1},{4,6},{5,7},{6,4},{7,5},{8,10},{9,11},{10,... | collective-permute-start | bytes 1572872 | tf_op jit(solution)/shard_map/ppermute | solution.py:319
  4.9 16.1 %collective-permute-start.1 = (bf16[256,1024]{1,0:T(8,128)(2,1)}, bf16[256,1024]{1,0:T(8,128)(2,1)S(1)}, u32[]{:S(2)}, u32[]{:S(2)}) collective-permute-start(bf16[256,1024]{1,0:T(8,128)(2,1)} %refs_4_.3), channel_id=1, source_target_pairs={{0,1},{1,0},{2,3},{3,2},{4,5},{5,4},{6,7},{7,6},{8,9},{9,8},{10,11... | collective-permute-start | bytes 1572872 | tf_op jit(solution)/shard_map/ppermute | solution.py:319
  4.9 16.0 %all-to-all-start = ((bf16[8,72,256]{2,1,0:T(8,128)(2,1)}), bf16[8,72,256]{2,1,0:T(8,128)(2,1)S(1)}, u32[]{:S(2)}, u32[]{:S(2)}) async-start(bf16[8,72,256]{2,1,0:T(8,128)(2,1)} %get-tuple-element.59), calls=%async_computation | async-start | bytes 589824 | tf_op jit(solution)/shard_map/all_to_all | solution.py:352
  10.7 1.9 %collective-permute-start.2 = (bf16[32,256]{1,0:T(8,128)(2,1)}, bf16[32,256]{1,0:T(8,128)(2,1)S(1)}, u32[]{:S(2)}, u32[]{:S(2)}) collective-permute-start(bf16[32,256]{1,0:T(8,128)(2,1)} %bitcast.31), channel_id=1, source_target_pairs={{0,1},{1,0},{2,3},{3,2},{4,5},{5,4},{6,7},{7,6},{8,9},{9,8},{10,11... | collective-permute-start | bytes 49160 | tf_op jit(solution)/shard_map/ppermute | solution.py:319
  10.9 6.6 %collective-permute-start.3 = (bf16[32,256]{1,0:T(8,128)(2,1)}, bf16[32,256]{1,0:T(8,128)(2,1)S(1)}, u32[]{:S(2)}, u32[]{:S(2)}) collective-permute-start(bf16[32,256]{1,0:T(8,128)(2,1)} %bitcast.32), channel_id=1, source_target_pairs={{0,2},{1,3},{2,0},{3,1},{4,6},{5,7},{6,4},{7,5},{8,10},{9,11},{10,... | collective-permute-start | bytes 49160 | tf_op jit(solution)/shard_map/ppermute | solution.py:319
  11.4 6.1 %collective-permute-start.4 = (bf16[32,256]{1,0:T(8,128)(2,1)}, bf16[32,256]{1,0:T(8,128)(2,1)S(1)}, u32[]{:S(2)}, u32[]{:S(2)}) collective-permute-start(bf16[32,256]{1,0:T(8,128)(2,1)} %bitcast.33), channel_id=1, source_target_pairs={{0,3},{1,2},{2,1},{3,0},{4,7},{5,6},{6,5},{7,4},{8,11},{9,10},{10,... | collective-permute-start | bytes 49160 | tf_op jit(solution)/shard_map/ppermute | solution.py:319
  20.9 1.6 %collective-permute-start.5 = (bf16[8,72,256]{2,1,0:T(8,128)(2,1)S(1)}, bf16[8,72,256]{2,1,0:T(8,128)(2,1)S(1)}, u32[]{:S(2)}, u32[]{:S(2)}) collective-permute-start(bf16[8,72,256]{2,1,0:T(8,128)(2,1)S(1)} %all-to-all-done.own.refs_0_), channel_id=1, source_target_pairs={{0,1},{1,0},{2,3},{3,2},{4,5},{5,4},{6,7},{7,6},{8,9},{9,8},{10,11... | collective-permute-start | bytes 884744 | tf_op jit(solution)/shard_map/ppermute | solution.py:319
  21.0 6.3 %collective-permute-start.6 = (bf16[4,72,256]{2,1,0:T(8,128)(2,1)S(1)}, bf16[4,72,256]{2,1,0:T(8,128)(2,1)S(1)}, u32[]{:S(2)}, u32[]{:S(2)}) collective-permute-start(bf16[4,72,256]{2,1,0:T(8,128)(2,1)S(1)} %get-tuple-element.108), channel_id=1, source_target_pairs={{0,2},{1,3},{2,0},{3,1},{4,6},{5,7},{6,4},{7,5},{8,10},{9,11},{10,... | collective-permute-start | bytes 442376 | tf_op jit(solution)/shard_map/ppermute | solution.py:319
  27.3 1.4 %collective-permute-start.7 = (bf16[4,72,256]{2,1,0:T(8,128)(2,1)S(1)}, bf16[4,72,256]{2,1,0:T(8,128)(2,1)S(1)}, u32[]{:S(2)}, u32[]{:S(2)}) collective-permute-start(bf16[4,72,256]{2,1,0:T(8,128)(2,1)S(1)} %collective-permute-done.6.refs_2_), channel_id=1, source_target_pairs={{0,1},{1,0},{2,3},{3,2},{4,5},{5,4},{6,7},{7,6},{8,9},{9,8},{10,11... | collective-permute-start | bytes 442376 | tf_op jit(solution)/shard_map/ppermute | solution.py:319
  27.3 6.3 %collective-permute-start.9 = (bf16[4,72,256]{2,1,0:T(8,128)(2,1)S(1)}, bf16[4,72,256]{2,1,0:T(8,128)(2,1)S(1)}, u32[]{:S(2)}, u32[]{:S(2)}) collective-permute-start(bf16[4,72,256]{2,1,0:T(8,128)(2,1)S(1)} %get-tuple-element.107), channel_id=1, source_target_pairs={{0,2},{1,3},{2,0},{3,1},{4,6},{5,7},{6,4},{7,5},{8,10},{9,11},{10,... | collective-permute-start | bytes 442376 | tf_op jit(solution)/shard_map/ppermute | solution.py:319
  33.6 7.5 %copy-start.2 = (bf16[256,1024]{1,0:T(8,128)(2,1)S(1)}, bf16[256,1024]{1,0:T(8,128)(2,1)}, u32[]{:S(2)}) copy-start(bf16[256,1024]{1,0:T(8,128)(2,1)} %refs_4_.3) | copy-start | bytes 1572868
  33.6 7.5 %copy-start.3 = (bf16[32,1024]{1,0:T(8,128)(2,1)S(1)}, bf16[32,1024]{1,0:T(8,128)(2,1)}, u32[]{:S(2)}) copy-start(bf16[32,1024]{1,0:T(8,128)(2,1)} %refs_14_.3) | copy-start | bytes 196612
  33.6 7.5 %copy-start.4 = (bf16[1024,32]{0,1:T(8,128)(2,1)S(1)}, bf16[1024,32]{0,1:T(8,128)(2,1)}, u32[]{:S(2)}) copy-start(bf16[1024,32]{0,1:T(8,128)(2,1)} %param.32) | copy-start | bytes 196612
  33.6 7.5 %copy-start.5 = (bf16[32,1024]{1,0:T(8,128)(2,1)S(1)}, bf16[32,1024]{1,0:T(8,128)(2,1)}, u32[]{:S(2)}) copy-start(bf16[32,1024]{1,0:T(8,128)(2,1)} %refs_16_.3) | copy-start | bytes 196612
  33.6 7.5 %copy-start.6 = (bf16[1024,32]{0,1:T(8,128)(2,1)S(1)}, bf16[1024,32]{0,1:T(8,128)(2,1)}, u32[]{:S(2)}) copy-start(bf16[1024,32]{0,1:T(8,128)(2,1)} %param.34) | copy-start | bytes 196612
  33.6 7.5 %copy-start.7 = (bf16[32,1024]{1,0:T(8,128)(2,1)S(1)}, bf16[32,1024]{1,0:T(8,128)(2,1)}, u32[]{:S(2)}) copy-start(bf16[32,1024]{1,0:T(8,128)(2,1)} %refs_18_.3) | copy-start | bytes 196612
  33.6 7.5 %copy-start.8 = (bf16[256,32]{0,1:T(8,128)(2,1)S(1)}, bf16[256,32]{0,1:T(8,128)(2,1)}, u32[]{:S(2)}) copy-start(bf16[256,32]{0,1:T(8,128)(2,1)} %param.30) | copy-start | bytes 49156
  33.6 7.5 %copy-start.9 = (f32[1024]{0:T(1024)S(1)}, f32[1024]{0:T(1024)}, u32[]{:S(2)}) copy-start(f32[1024]{0:T(1024)} %param.36) | copy-start | bytes 12292
  33.6 7.5 %copy-start.10 = (f32[1024]{0:T(1024)S(1)}, f32[1024]{0:T(1024)}, u32[]{:S(2)}) copy-start(f32[1024]{0:T(1024)} %param.37) | copy-start | bytes 12292
  33.6 7.4 %collective-permute-start.16 = (bf16[256,1024]{1,0:T(8,128)(2,1)S(1)}, bf16[256,1024]{1,0:T(8,128)(2,1)S(1)}, u32[]{:S(2)}, u32[]{:S(2)}) collective-permute-start(bf16[256,1024]{1,0:T(8,128)(2,1)S(1)} %collective-permute-done.refs_6_), channel_id=1, source_target_pairs={{0,1},{1,0},{2,3},{3,2},{4,5},{5,4},{6,7},{7,6},{8,9},{9,8},{10,11... | collective-permute-start | bytes 1572872 | tf_op jit(solution)/shard_map/ppermute | solution.py:319
  33.7 2.1 %collective-permute-start.10 = (bf16[4,72,256]{2,1,0:T(8,128)(2,1)S(1)}, bf16[4,72,256]{2,1,0:T(8,128)(2,1)S(1)}, u32[]{:S(2)}, u32[]{:S(2)}) collective-permute-start(bf16[4,72,256]{2,1,0:T(8,128)(2,1)S(1)} %collective-permute-done.9.refs_2_), channel_id=1, source_target_pairs={{0,1},{1,0},{2,3},{3,2},{4,5},{5,4},{6,7},{7,6},{8,9},{9,8},{10,11... | collective-permute-start | bytes 442376 | tf_op jit(solution)/shard_map/ppermute | solution.py:319
  34.2 5.5 %collective-permute-start.8 = (bf16[256,256]{1,0:T(8,128)(2,1)S(1)}, bf16[256,256]{1,0:T(8,128)(2,1)S(1)}, u32[]{:S(2)}, u32[]{:S(2)}) collective-permute-start(bf16[256,256]{1,0:T(8,128)(2,1)S(1)} %get-tuple-element.80.refs_0_), channel_id=1, source_target_pairs={{0,2},{1,3},{2,0},{3,1},{4,6},{5,7},{6,4},{7,5},{8,10},{9,11},{10,... | collective-permute-start | bytes 393224 | tf_op jit(solution)/shard_map/ppermute | solution.py:319
  34.7 5.5 %collective-permute-start.14 = (bf16[256,256]{1,0:T(8,128)(2,1)S(1)}, bf16[256,256]{1,0:T(8,128)(2,1)S(1)}, u32[]{:S(2)}, u32[]{:S(2)}) collective-permute-start(bf16[256,256]{1,0:T(8,128)(2,1)S(1)} %get-tuple-element.80.refs_0_), channel_id=1, source_target_pairs={{0,1},{1,0},{2,3},{3,2},{4,5},{5,4},{6,7},{7,6},{8,9},{9,8},{10,11... | collective-permute-start | bytes 393224 | tf_op jit(solution)/shard_map/ppermute | solution.py:319
  39.7 1.3 %collective-permute-start.15 = (bf16[256,256]{1,0:T(8,128)(2,1)S(1)}, bf16[256,256]{1,0:T(8,128)(2,1)S(1)}, u32[]{:S(2)}, u32[]{:S(2)}) collective-permute-start(bf16[256,256]{1,0:T(8,128)(2,1)S(1)} %collective-permute-done.8.refs_2_), channel_id=1, source_target_pairs={{0,1},{1,0},{2,3},{3,2},{4,5},{5,4},{6,7},{7,6},{8,9},{9,8},{10,11... | collective-permute-start | bytes 393224 | tf_op jit(solution)/shard_map/ppermute | solution.py:319
  39.7 7.1 %collective-permute-start.12 = (bf16[256,256]{1,0:T(8,128)(2,1)S(1)}, bf16[256,256]{1,0:T(8,128)(2,1)S(1)}, u32[]{:S(2)}, u32[]{:S(2)}) collective-permute-start(bf16[256,256]{1,0:T(8,128)(2,1)S(1)} %get-tuple-element.93.refs_0_), channel_id=1, source_target_pairs={{0,2},{1,3},{2,0},{3,1},{4,6},{5,7},{6,4},{7,5},{8,10},{9,11},{10,... | collective-permute-start | bytes 393224 | tf_op jit(solution)/shard_map/ppermute | solution.py:319
  46.3 1.4 %collective-permute-start.17 = (bf16[1,64,1024]{2,1,0:T(8,128)(2,1)S(1)}, bf16[1,64,1024]{2,1,0:T(8,128)(2,1)S(1)}, u32[]{:S(2)}, u32[]{:S(2)}) collective-permute-start(bf16[1,64,1024]{2,1,0:T(8,128)(2,1)S(1)} %get-tuple-element.92), channel_id=1, source_target_pairs={{0,1},{1,0},{2,3},{3,2},{4,5},{5,4},{6,7},{7,6},{8,9},{9,8},{10,11... | collective-permute-start | bytes 393224 | tf_op jit(solution)/shard_map/ppermute | solution.py:319
  46.5 1.4 %collective-permute-start.11 = (bf16[256,256]{1,0:T(8,128)(2,1)S(1)}, bf16[256,256]{1,0:T(8,128)(2,1)S(1)}, u32[]{:S(2)}, u32[]{:S(2)}) collective-permute-start(bf16[256,256]{1,0:T(8,128)(2,1)S(1)} %get-tuple-element.93.refs_0_), channel_id=1, source_target_pairs={{0,1},{1,0},{2,3},{3,2},{4,5},{5,4},{6,7},{7,6},{8,9},{9,8},{10,11... | collective-permute-start | bytes 393224 | tf_op jit(solution)/shard_map/ppermute | solution.py:319
  46.8 1.3 %collective-permute-start.13 = (bf16[256,256]{1,0:T(8,128)(2,1)S(1)}, bf16[256,256]{1,0:T(8,128)(2,1)S(1)}, u32[]{:S(2)}, u32[]{:S(2)}) collective-permute-start(bf16[256,256]{1,0:T(8,128)(2,1)S(1)} %collective-permute-done.12.refs_2_), channel_id=1, source_target_pairs={{0,1},{1,0},{2,3},{3,2},{4,5},{5,4},{6,7},{7,6},{8,9},{9,8},{10,11... | collective-permute-start | bytes 393224 | tf_op jit(solution)/shard_map/ppermute | solution.py:319
  47.0 7.6 %collective-permute-start.19 = (bf16[64,1024]{1,0:T(8,128)(2,1)S(1)}, bf16[64,1024]{1,0:T(8,128)(2,1)S(1)}, u32[]{:S(2)}, u32[]{:S(2)}) collective-permute-start(bf16[64,1024]{1,0:T(8,128)(2,1)S(1)} %get-tuple-element.99), channel_id=1, source_target_pairs={{0,1},{1,0},{2,3},{3,2},{4,5},{5,4},{6,7},{7,6},{8,9},{9,8},{10,11... | collective-permute-start | bytes 393224 | tf_op jit(solution)/shard_map/ppermute | solution.py:319
  48.2 6.4 %collective-permute-start.20 = (bf16[64,1024]{1,0:T(8,128)(2,1)S(1)}, bf16[64,1024]{1,0:T(8,128)(2,1)S(1)}, u32[]{:S(2)}, u32[]{:S(2)}) collective-permute-start(bf16[64,1024]{1,0:T(8,128)(2,1)S(1)} %fusion), channel_id=1, source_target_pairs={{0,2},{1,3},{2,0},{3,1},{4,6},{5,7},{6,4},{7,5},{8,10},{9,11},{10,... | collective-permute-start | bytes 393224 | tf_op jit(solution)/shard_map/ppermute | solution.py:319
  48.9 5.7 %copy-start = (f32[1024]{0:T(1024)S(1)}, f32[1024]{0:T(1024)}, u32[]{:S(2)}) copy-start(f32[1024]{0:T(1024)} %param.38) | copy-start | bytes 12292
  48.9 5.7 %copy-start.1 = (f32[1024]{0:T(1024)S(1)}, f32[1024]{0:T(1024)}, u32[]{:S(2)}) copy-start(f32[1024]{0:T(1024)} %param.39) | copy-start | bytes 12292
  54.0 1.4 %collective-permute-start.18 = (bf16[1,64,1024]{2,1,0:T(8,128)(2,1)S(1)}, bf16[1,64,1024]{2,1,0:T(8,128)(2,1)S(1)}, u32[]{:S(2)}, u32[]{:S(2)}) collective-permute-start(bf16[1,64,1024]{2,1,0:T(8,128)(2,1)S(1)} %get-tuple-element.98), channel_id=1, source_target_pairs={{0,1},{1,0},{2,3},{3,2},{4,5},{5,4},{6,7},{7,6},{8,9},{9,8},{10,11... | collective-permute-start | bytes 393224 | tf_op jit(solution)/shard_map/ppermute | solution.py:319
  54.1 2.8 %collective-permute-start.21 = (bf16[64,1024]{1,0:T(8,128)(2,1)S(1)}, bf16[64,1024]{1,0:T(8,128)(2,1)S(1)}, u32[]{:S(2)}, u32[]{:S(2)}) collective-permute-start(bf16[64,1024]{1,0:T(8,128)(2,1)S(1)} %get-tuple-element.104), channel_id=1, source_target_pairs={{0,1},{1,0},{2,3},{3,2},{4,5},{5,4},{6,7},{7,6},{8,9},{9,8},{10,11... | collective-permute-start | bytes 393224 | tf_op jit(solution)/shard_map/ppermute | solution.py:319
  55.5 5.6 %collective-permute-start.22 = (bf16[64,1024]{1,0:T(8,128)(2,1)S(1)}, bf16[64,1024]{1,0:T(8,128)(2,1)S(1)}, u32[]{:S(2)}, u32[]{:S(2)}) collective-permute-start(bf16[64,1024]{1,0:T(8,128)(2,1)S(1)} %fusion.1), channel_id=1, source_target_pairs={{0,2},{1,3},{2,0},{3,1},{4,6},{5,7},{6,4},{7,5},{8,10},{9,11},{10,... | collective-permute-start | bytes 393224 | tf_op jit(solution)/shard_map/ppermute | solution.py:319

commit v7 on v6

--- a/solution.py
+++ b/solution.py
@@ -147,8 +147,8 @@
     tp = me[0]
     spans = [span((tp ^ r) * width, width) for r in range(n_tp)]
     for r in range(n_tp):
-        offset = chunk * blocks if part_of(parts[r], blocks) else 0
-        x_full[:, spans[r]] = parts[r][offset : offset + blocks, :CAP, :].reshape(rows, width)
+        chunk_part = parts[r][chunk * blocks : (chunk + 1) * blocks, :CAP, :]
+        x_full[:, spans[r]] = chunk_part.reshape(rows, width)
     first = lax.broadcasted_iota(jnp.int32, (2 * CAP, 2 * CAP), 1) < HEAD_DIM
     zero = jnp.zeros((), BF)
     tile = min(4, blocks)
@@ -157,7 +157,7 @@
         start = t * (tile * CAP)
         rs = span(start, tile * CAP)
         whole = span(chunk * rows + start, tile * CAP)
-        bs = pl.ds(t * tile, tile)
+        bs = pl.ds(chunk * blocks + t * tile, tile)
         xs = [parts[r][bs, :CAP, :].reshape(tile * CAP, width) for r in range(2, n_tp)]
         low = low_in[whole]
         for r in range(2, n_tp):
@@ -186,10 +186,6 @@
                 att[out_rows, cs] = jnp.where(first, *both).astype(BF)
 
     tiles(blocks // tile, step)
-
-
-def part_of(array, blocks):
-    return array.shape[0] > blocks
 
 
 def ffn_kernel(n_tp, chunk, me, *refs):
@@ -359,10 +355,7 @@
     rows = step_blocks * CAP
     own = rows // n_tp
     beside = swap(arrived, 1)
-    x_far = []
-    for c in range(count):
-        piece = arrived[c * step_blocks : (c + 1) * step_blocks]
-        x_far.append([swap(piece, 2 * y) for y in range(1, half)])
+    x_far = [swap(arrived, 2 * y) for y in range(1, half)]
     *begun, w_all, w1, w2, downs, up_all = pl.pallas_call(
         begin_kernel,
         out_shape=[
@@ -397,8 +390,8 @@
         ),
     )
     w_all, w1, w2, downs, up_all = near(w_all, w1, w2, downs, up_all)
-    x_far[0], begun = lax.optimization_barrier((x_far[0], begun))
-    x_far[0] = second_hop(x_far[0])
+    x_far, begun = lax.optimization_barrier((x_far, begun))
+    x_far = second_hop(x_far)
 
     consts = near(
         out_up, fc1_down.T, fc1_up, fc2_down.T, fc2_up, norm1_gain[None], norm1_bias[None]
@@ -406,11 +399,6 @@
     sel = begun[2]
     steps = []
     for c in range(count):
-        if c:
-            x_far[c], w_far, steps[0][0] = lax.optimization_barrier(
-                (x_far[c], w_far, steps[0][0])
-            )
-            x_far[c] = second_hop(x_far[c])
         attended, x_full = pl.pallas_call(
             functools.partial(attn_kernel, n_tp, c),
             out_shape=[pltpu.VMEM((rows, width), BF), pltpu.VMEM((rows, feat), BF)],
@@ -419,10 +407,12 @@
             compiler_params=params(12),
             cost_estimate=work(2 * rows * feat * 3 * width + 4 * rows * width * 2 * CAP, rows),
             name="attend",
-        )(me, *near(arrived, beside, *x_far[c], *begun), w_all, downs, up_all)
+        )(me, *near(arrived, beside, *x_far, *begun), w_all, downs, up_all)
         y_got = [swap(attended, 2 * y) for y in range(1, half)]
         if c:
-            steps[0][1], attended = lax.optimization_barrier((steps[0][1], attended))
+            steps[0][1], attended, w_far = lax.optimization_barrier(
+                (steps[0][1], attended, w_far)
+            )
         steps.append([attended, y_got, x_full])
     wouts = [w_out, w_near] + second_hop(w_far)
 
@@ -464,6 +454,7 @@
             earlier = finish([], *first_ends, *firsts)
             gots, earlier = lax.optimization_barrier((gots, earlier))
         sends = [(even[y] + gots[y - 1].astype(F32)).astype(BF) for y in range(1, half)]
+        odd, sends = lax.optimization_barrier((odd, sends))
         ends = [even, swap(odd, 1), h_own]
         if c == 0:
             firsts, first_ends = sends, ends

time: 76.7 us -> 78.9 us (1.029)
  waiting for transfers between devices: 22.9 us -> 25.1 us
    ppermute x23 -> x21, waiting for transfers between devices: 19.5 us -> 22.8 us  [swap(): return lax.ppermute(value, 'tp', [(i, i ^ r) for i in range(n_tp)])]
    all_to_all x1, waiting for transfers between devices: 3.39 us -> 2.27 us  [body(): lax.all_to_all(packed, 'req', split_axis=0, concat_axis=0, tiled=True)]
    ppermute x23 -> x21, starting transfers between devices: 11.3 us -> 10.9 us  [swap(): return lax.ppermute(value, 'tp', [(i, i ^ r) for i in range(n_tp)])]
  transfers between devices with their start and end apart: 24 -> 22, of which waited for: 14 -> 13; matrix products, arithmetic and copies ran while one was open for 0% -> 0% of each run, Pallas kernels for 25% -> 20%
where the time goes in v7:
time: 78.9 us; the launch traced here: 78.7 us
  waiting for transfers between devices  25.1 us (32%)
  Pallas kernels  22.2 us (28%)
  starting transfers between devices  16.7 us (21%)
  blocking collectives  14.4 us (18%)
    ppermute x21, waiting for transfers between devices, swap(): return lax.ppermute(value, 'tp', [(i, i ^ r) for i in range(n_tp)])  22.8 us
    all_to_all x1, blocking collectives, body(): lax.all_to_all(done.reshape(n_req * n_tp, share, width), ('req', 'tp'), s...  14.4 us
    ppermute x21, starting transfers between devices, swap(): return lax.ppermute(value, 'tp', [(i, i ^ r) for i in range(n_tp)])  10.9 us
    pallas_call x2, Pallas kernels, body(): pl.pallas_call(functools.partial(ffn_kernel, n_tp, c), out_shape=[pltpu.V...  10.2 us
    all_to_all x1, starting transfers between devices, body(): lax.all_to_all(packed, 'req', split_axis=0, concat_axis=0, tiled=True)  5.81 us
    pallas_call x2, Pallas kernels, body(): pl.pallas_call(functools.partial(attn_kernel, n_tp, c), out_shape=[pltpu....  5.52 us
    pallas_call x1, Pallas kernels, body(): pl.pallas_call(begin_kernel, out_shape=[pltpu.VMEM((3, count * rows, widt...  2.86 us
    all_to_all x1, waiting for transfers between devices, body(): lax.all_to_all(packed, 'req', split_axis=0, concat_axis=0, tiled=True)  2.27 us
  transfers between devices with their start and end apart: 22, of which 13 were waited for; matrix products, arithmetic and copies ran while one was open for 0% of the time, Pallas kernels for 20%

profile of v7, /device:TPU:0, one launch (start us, length us, event | category | flops | bytes accessed | tf_op | source)
XLA Modules:
  0.0 78.7 jit_solution(7234607398390032991)
XLA Ops:
  0.0 1.8 %pack.1 = (bf16[8,72,256]{2,1,0:T(8,128)(2,1)}, s32[8]{0:T(128)S(1)}) custom-call(s32[4,8]{1,0:T(4,128)} %bitcast.42, s32[4,8]{1,0:T(4,128)} %bitcast.43, s32[16]{0:T(128)} %slots_in.1, bf16[8,64,256]{2,1,0:T(8,128)(2,1)} %bitcast.40), custom_call_target="tpu_custom_call" | custom-call | tf_op jit(solution)/shard_map/pack/pallas_call | solution.py:320
  1.9 0.5 collective-permute-start.1
  2.4 2.6 %collective-permute-start = (bf16[256,1024]{1,0:T(8,128)(2,1)}, bf16[256,1024]{1,0:T(8,128)(2,1)S(1)}, u32[]{:S(2)}, u32[]{:S(2)}) collective-permute-start(bf16[256,1024]{1,0:T(8,128)(2,1)} %refs_4_.3), channel_id=1, source_target_pairs={{0,2},{1,3},{2,0},{3,1},{4,6},{5,7},{6,4},{7,5},{8,10},{9,11},{10,... | collective-permute-start | bytes 1572872 | tf_op jit(solution)/shard_map/ppermute | solution.py:315
  5.0 5.8 %all-to-all-start = ((bf16[8,72,256]{2,1,0:T(8,128)(2,1)}), bf16[8,72,256]{2,1,0:T(8,128)(2,1)S(1)}, u32[]{:S(2)}, u32[]{:S(2)}) async-start(bf16[8,72,256]{2,1,0:T(8,128)(2,1)} %get-tuple-element.61), calls=%async_computation | async-start | bytes 589824 | tf_op jit(solution)/shard_map/all_to_all | solution.py:348
  10.8 1.5 %collective-permute-start.3 = (bf16[32,256]{1,0:T(8,128)(2,1)}, bf16[32,256]{1,0:T(8,128)(2,1)S(1)}, u32[]{:S(2)}, u32[]{:S(2)}) collective-permute-start(bf16[32,256]{1,0:T(8,128)(2,1)} %bitcast.32), channel_id=1, source_target_pairs={{0,2},{1,3},{2,0},{3,1},{4,6},{5,7},{6,4},{7,5},{8,10},{9,11},{10,... | collective-permute-start | bytes 49160 | tf_op jit(solution)/shard_map/ppermute | solution.py:315
  12.3 0.3 collective-permute-start.2
  12.6 5.1 %collective-permute-done.4.refs_11_ = bf16[32,256]{1,0:T(8,128)(2,1)S(1)} collective-permute-done((bf16[32,256]{1,0:T(8,128)(2,1)}, bf16[32,256]{1,0:T(8,128)(2,1)S(1)}, u32[]{:S(2)}, u32[]{:S(2)}) %collective-permute-start.4) | collective-permute-done | bytes 16416 | tf_op jit(solution)/shard_map/ppermute | solution.py:315
  17.8 0.6 collective-permute-done.3.refs_10_
  18.4 2.3 %all-to-all-done.own.refs_0_ = bf16[8,72,256]{2,1,0:T(8,128)(2,1)S(1)} async-done(((bf16[8,72,256]{2,1,0:T(8,128)(2,1)}), bf16[8,72,256]{2,1,0:T(8,128)(2,1)S(1)}, u32[]{:S(2)}, u32[]{:S(2)}) %all-to-all-start) | async-done | bytes 294944 | tf_op jit(solution)/shard_map/all_to_all | solution.py:348
  20.7 0.6 collective-permute-start.6
  21.3 1.0 %collective-permute-done.5.beside.refs_1_ = bf16[8,72,256]{2,1,0:T(8,128)(2,1)S(1)} collective-permute-done((bf16[8,72,256]{2,1,0:T(8,128)(2,1)S(1)}, bf16[8,72,256]{2,1,0:T(8,128)(2,1)S(1)}, u32[]{:S(2)}, u32[]{:S(2)}) %collective-permute-start.5) | collective-permute-done | bytes 294944 | tf_op jit(solution)/shard_map/ppermute | solution.py:315
  22.3 2.9 %begin.1 = (f32[3,512,256]{2,1,0:T(8,128)S(1)}, f32[512,96]{1,0:T(8,128)S(1)}, bf16[512,128]{1,0:T(8,128)(2,1)S(1)}, f32[512,128]{1,0:T(8,128)S(1)}, bf16[3,1024...) custom-call(s32[1]{0:T(128)} %bitcast.3.me, ...), custom_call_target="tpu_custom_call" | custom-call | flops 1006632960 | bytes 2097152 | tf_op jit(solution)/shard_map/begin/pallas_call | solution.py:359
  25.1 5.0 %collective-permute-done.6.refs_2_ = bf16[8,72,256]{2,1,0:T(8,128)(2,1)S(1)} collective-permute-done((bf16[8,72,256]{2,1,0:T(8,128)(2,1)S(1)}, bf16[8,72,256]{2,1,0:T(8,128)(2,1)S(1)}, u32[]{:S(2)}, u32[]{:S(2)}) %collective-permute-start.6) | collective-permute-done | bytes 294944 | tf_op jit(solution)/shard_map/ppermute | solution.py:315
  30.1 1.6 %collective-permute-done.7.refs_3_ = bf16[8,72,256]{2,1,0:T(8,128)(2,1)S(1)} collective-permute-done((bf16[8,72,256]{2,1,0:T(8,128)(2,1)S(1)}, bf16[8,72,256]{2,1,0:T(8,128)(2,1)S(1)}, u32[]{:S(2)}, u32[]{:S(2)}) %collective-permute-start.7) | collective-permute-done | bytes 294944 | tf_op jit(solution)/shard_map/ppermute | solution.py:315
  31.7 2.8 %attend.2 = (bf16[256,256]{1,0:T(8,128)(2,1)S(1)}, bf16[256,1024]{1,0:T(8,128)(2,1)S(1)}) custom-call(s32[1]{0:T(128)} %bitcast.3.me, bf16[8,72,256]{2,1,0:T(8,128)(2,1)S(1)} %all-to-all-done.own.refs_0_, bf16[8,72,256]{2,1,0:T(8,128)(2,1)S(1)} %collective-permute-done.5.beside.refs_1_, bf16[8,72,256]{2,1,0:T(8,128)(2,1)S(1)} %collective-permute-done.6.refs_2_, ...), custom_call_target="tpu_custom_call" | custom-call | flops 2181038080 | bytes 2097152 | tf_op jit(solution)/shard_map/attend/pallas_call | solution.py:402
  34.5 0.0 copy-start.2
  34.5 0.0 copy-start.3
  34.5 0.0 copy-start.4
  34.5 0.0 copy-start.5
  34.5 0.0 copy-start.6
  34.5 0.0 copy-start.7
  34.5 0.0 copy-start.8
  34.5 0.0 copy-start.9
  34.5 0.0 copy-start.10
  34.6 0.6 collective-permute-start.8
  35.1 2.8 %attend.3 = (bf16[256,256]{1,0:T(8,128)(2,1)S(1)}, bf16[256,1024]{1,0:T(8,128)(2,1)S(1)}) custom-call(s32[1]{0:T(128)} %bitcast.3.me, bf16[8,72,256]{2,1,0:T(8,128)(2,1)S(1)} %all-to-all-done.own.refs_0_, bf16[8,72,256]{2,1,0:T(8,128)(2,1)S(1)} %collective-permute-done.5.beside.refs_1_, bf16[8,72,256]{2,1,0:T(8,128)(2,1)S(1)} %collective-permute-done.6.refs_2_, ...), custom_call_target="tpu_custom_call" | custom-call | flops 2181038080 | bytes 2097152 | tf_op jit(solution)/shard_map/attend/pallas_call | solution.py:402
  37.9 2.3 %collective-permute-done.8.refs_2_ = bf16[256,256]{1,0:T(8,128)(2,1)S(1)} collective-permute-done((bf16[256,256]{1,0:T(8,128)(2,1)S(1)}, bf16[256,256]{1,0:T(8,128)(2,1)S(1)}, u32[]{:S(2)}, u32[]{:S(2)}) %collective-permute-start.8) | collective-permute-done | bytes 131104 | tf_op jit(solution)/shard_map/ppermute | solution.py:315
  40.2 0.5 collective-permute-start.12
  40.7 0.5 collective-permute-start.10
  41.2 1.1 %collective-permute-done.12.refs_1_ = bf16[256,256]{1,0:T(8,128)(2,1)S(1)} collective-permute-done((bf16[256,256]{1,0:T(8,128)(2,1)S(1)}, bf16[256,256]{1,0:T(8,128)(2,1)S(1)}, u32[]{:S(2)}, u32[]{:S(2)}) %collective-permute-start.12) | collective-permute-done | bytes 131104 | tf_op jit(solution)/shard_map/ppermute | solution.py:315
  42.3 0.2 collective-permute-done.13.refs_3_
  42.5 5.1 %feed.2 = (f32[2,64,1024]{2,1,0:T(8,128)S(1)}, bf16[64,1024]{1,0:T(8,128)(2,1)S(1)}, bf16[1,64,1024]{2,1,0:T(8,128)(2,1)S(1)}, bf16[64,1024]{1,0:T(8,128)(2,1)S(1)}) custom-call(s32[1]{0:T(128)} %bitcast.3.me, bf16[256,256]{1,0:T(8,128)(2,1)S(1)} %get-tuple-element.77.refs_0_, bf16[256,256]{1,0:T(8,128)(2,1)S(1)} %collective-permute-done.12.refs_1_, ...), custom_call_target="tpu_custom_call" | custom-call | flops 8053063680 | bytes 2097152 | tf_op jit(solution)/shard_map/feed/pallas_call | solution.py:437
  47.7 0.2 collective-permute-start.15
  47.9 0.4 collective-permute-start.9
  48.3 0.1 collective-permute-start.11
  48.4 0.7 collective-permute-done.15
  49.1 0.5 collective-permute-done.11.refs_3_
  49.6 0.5 collective-permute-start.18
  50.1 5.1 %feed.3 = (f32[2,64,1024]{2,1,0:T(8,128)S(1)}, bf16[64,1024]{1,0:T(8,128)(2,1)S(1)}, bf16[1,64,1024]{2,1,0:T(8,128)(2,1)S(1)}, bf16[64,1024]{1,0:T(8,128)(2,1)S(1)}) custom-call(s32[1]{0:T(128)} %bitcast.3.me, bf16[256,256]{1,0:T(8,128)(2,1)S(1)} %get-tuple-element.95.refs_0_, bf16[256,256]{1,0:T(8,128)(2,1)S(1)} %collective-permute-done.9.refs_1_, ...), custom_call_target="tpu_custom_call" | custom-call | flops 8053063680 | bytes 2097152 | tf_op jit(solution)/shard_map/feed/pallas_call | solution.py:437
  55.2 0.6 collective-permute-start.16
  55.8 0.2 finish.2.refs_0_
  56.1 0.7 collective-permute-done.16
  56.8 0.4 collective-permute-start.19
  57.3 1.5 %collective-permute-start.20 = (bf16[64,1024]{1,0:T(8,128)(2,1)S(1)}, bf16[64,1024]{1,0:T(8,128)(2,1)S(1)}, u32[]{:S(2)}, u32[]{:S(2)}) collective-permute-start(bf16[64,1024]{1,0:T(8,128)(2,1)S(1)} %fusion.1), channel_id=1, source_target_pairs={{0,2},{1,3},{2,0},{3,1},{4,6},{5,7},{6,4},{7,5},{8,10},{9,11},{10,... | collective-permute-start | bytes 393224 | tf_op jit(solution)/shard_map/ppermute | solution.py:315
  58.8 4.0 %collective-permute-done.20.refs_4_ = bf16[64,1024]{1,0:T(8,128)(2,1)S(1)} collective-permute-done((bf16[64,1024]{1,0:T(8,128)(2,1)S(1)}, bf16[64,1024]{1,0:T(8,128)(2,1)S(1)}, u32[]{:S(2)}, u32[]{:S(2)}) %collective-permute-start.20) | collective-permute-done | bytes 131104 | tf_op jit(solution)/shard_map/ppermute | solution.py:315
  62.8 0.2 finish.3
  63.1 14.4 %all_to_all.10 = bf16[32,16,256]{2,1,0:T(8,128)(2,1)S(1)} all-to-all(bf16[32,16,256]{2,1,0:T(8,128)(2,1)S(1)} %bitcast.21), channel_id=1, replica_groups=mesh['req'=8,'tp'=4] {'req','tp'}, dimensions={0} | all-to-all | bytes 524288 | tf_op jit(solution)/shard_map/all_to_all | solution.py:464
  77.4 1.3 %unpack.1 = bf16[8,64,256]{2,1,0:T(8,128)(2,1)} custom-call(s32[8]{0:T(128)S(1)} %get-tuple-element.58.owners, bf16[8,64,256]{2,1,0:T(8,128)(2,1)S(1)} %bitcast.22), custom_call_target="tpu_custom_call" | custom-call | tf_op jit(solution)/shard_map/unpack/pallas_call | solution.py:471
  (30 shorter events, 0.1 us)
Async XLA Ops:
  1.9 18.8 %collective-permute-start.1 = (bf16[256,1024]{1,0:T(8,128)(2,1)}, bf16[256,1024]{1,0:T(8,128)(2,1)S(1)}, u32[]{:S(2)}, u32[]{:S(2)}) collective-permute-start(bf16[256,1024]{1,0:T(8,128)(2,1)} %refs_4_.3), channel_id=1, source_target_pairs={{0,1},{1,0},{2,3},{3,2},{4,5},{5,4},{6,7},{7,6},{8,9},{9,8},{10,11... | collective-permute-start | bytes 1572872 | tf_op jit(solution)/shard_map/ppermute | solution.py:315
  2.4 18.3 %collective-permute-start = (bf16[256,1024]{1,0:T(8,128)(2,1)}, bf16[256,1024]{1,0:T(8,128)(2,1)S(1)}, u32[]{:S(2)}, u32[]{:S(2)}) collective-permute-start(bf16[256,1024]{1,0:T(8,128)(2,1)} %refs_4_.3), channel_id=1, source_target_pairs={{0,2},{1,3},{2,0},{3,1},{4,6},{5,7},{6,4},{7,5},{8,10},{9,11},{10,... | collective-permute-start | bytes 1572872 | tf_op jit(solution)/shard_map/ppermute | solution.py:315
  5.0 15.7 %all-to-all-start = ((bf16[8,72,256]{2,1,0:T(8,128)(2,1)}), bf16[8,72,256]{2,1,0:T(8,128)(2,1)S(1)}, u32[]{:S(2)}, u32[]{:S(2)}) async-start(bf16[8,72,256]{2,1,0:T(8,128)(2,1)} %get-tuple-element.61), calls=%async_computation | async-start | bytes 589824 | tf_op jit(solution)/shard_map/all_to_all | solution.py:348
  10.8 7.0 %collective-permute-start.4 = (bf16[32,256]{1,0:T(8,128)(2,1)}, bf16[32,256]{1,0:T(8,128)(2,1)S(1)}, u32[]{:S(2)}, u32[]{:S(2)}) collective-permute-start(bf16[32,256]{1,0:T(8,128)(2,1)} %bitcast.31), channel_id=1, source_target_pairs={{0,3},{1,2},{2,1},{3,0},{4,7},{5,6},{6,5},{7,4},{8,11},{9,10},{10,... | collective-permute-start | bytes 49160 | tf_op jit(solution)/shard_map/ppermute | solution.py:315
  10.8 7.6 %collective-permute-start.3 = (bf16[32,256]{1,0:T(8,128)(2,1)}, bf16[32,256]{1,0:T(8,128)(2,1)S(1)}, u32[]{:S(2)}, u32[]{:S(2)}) collective-permute-start(bf16[32,256]{1,0:T(8,128)(2,1)} %bitcast.32), channel_id=1, source_target_pairs={{0,2},{1,3},{2,0},{3,1},{4,6},{5,7},{6,4},{7,5},{8,10},{9,11},{10,... | collective-permute-start | bytes 49160 | tf_op jit(solution)/shard_map/ppermute | solution.py:315
  12.3 6.1 %collective-permute-start.2 = (bf16[32,256]{1,0:T(8,128)(2,1)}, bf16[32,256]{1,0:T(8,128)(2,1)S(1)}, u32[]{:S(2)}, u32[]{:S(2)}) collective-permute-start(bf16[32,256]{1,0:T(8,128)(2,1)} %bitcast.33), channel_id=1, source_target_pairs={{0,1},{1,0},{2,3},{3,2},{4,5},{5,4},{6,7},{7,6},{8,9},{9,8},{10,11... | collective-permute-start | bytes 49160 | tf_op jit(solution)/shard_map/ppermute | solution.py:315
  20.7 1.6 %collective-permute-start.5 = (bf16[8,72,256]{2,1,0:T(8,128)(2,1)S(1)}, bf16[8,72,256]{2,1,0:T(8,128)(2,1)S(1)}, u32[]{:S(2)}, u32[]{:S(2)}) collective-permute-start(bf16[8,72,256]{2,1,0:T(8,128)(2,1)S(1)} %all-to-all-done.own.refs_0_), channel_id=1, source_target_pairs={{0,1},{1,0},{2,3},{3,2},{4,5},{5,4},{6,7},{7,6},{8,9},{9,8},{10,11... | collective-permute-start | bytes 884744 | tf_op jit(solution)/shard_map/ppermute | solution.py:315
  20.7 9.4 %collective-permute-start.6 = (bf16[8,72,256]{2,1,0:T(8,128)(2,1)S(1)}, bf16[8,72,256]{2,1,0:T(8,128)(2,1)S(1)}, u32[]{:S(2)}, u32[]{:S(2)}) collective-permute-start(bf16[8,72,256]{2,1,0:T(8,128)(2,1)S(1)} %all-to-all-done.own.refs_0_), channel_id=1, source_target_pairs={{0,2},{1,3},{2,0},{3,1},{4,6},{5,7},{6,4},{7,5},{8,10},{9,11},{10,... | collective-permute-start | bytes 884744 | tf_op jit(solution)/shard_map/ppermute | solution.py:315
  30.1 1.6 %collective-permute-start.7 = (bf16[8,72,256]{2,1,0:T(8,128)(2,1)S(1)}, bf16[8,72,256]{2,1,0:T(8,128)(2,1)S(1)}, u32[]{:S(2)}, u32[]{:S(2)}) collective-permute-start(bf16[8,72,256]{2,1,0:T(8,128)(2,1)S(1)} %collective-permute-done.6.refs_2_), channel_id=1, source_target_pairs={{0,1},{1,0},{2,3},{3,2},{4,5},{5,4},{6,7},{7,6},{8,9},{9,8},{10,11... | collective-permute-start | bytes 884744 | tf_op jit(solution)/shard_map/ppermute | solution.py:315
  34.5 8.0 %copy-start.2 = (bf16[256,1024]{1,0:T(8,128)(2,1)S(1)}, bf16[256,1024]{1,0:T(8,128)(2,1)}, u32[]{:S(2)}) copy-start(bf16[256,1024]{1,0:T(8,128)(2,1)} %refs_4_.3) | copy-start | bytes 1572868
  34.5 8.0 %copy-start.3 = (bf16[32,1024]{1,0:T(8,128)(2,1)S(1)}, bf16[32,1024]{1,0:T(8,128)(2,1)}, u32[]{:S(2)}) copy-start(bf16[32,1024]{1,0:T(8,128)(2,1)} %refs_14_.3) | copy-start | bytes 196612
  34.5 8.0 %copy-start.4 = (bf16[1024,32]{0,1:T(8,128)(2,1)S(1)}, bf16[1024,32]{0,1:T(8,128)(2,1)}, u32[]{:S(2)}) copy-start(bf16[1024,32]{0,1:T(8,128)(2,1)} %param.32) | copy-start | bytes 196612
  34.5 8.0 %copy-start.5 = (bf16[32,1024]{1,0:T(8,128)(2,1)S(1)}, bf16[32,1024]{1,0:T(8,128)(2,1)}, u32[]{:S(2)}) copy-start(bf16[32,1024]{1,0:T(8,128)(2,1)} %refs_16_.3) | copy-start | bytes 196612
  34.5 8.0 %copy-start.6 = (bf16[1024,32]{0,1:T(8,128)(2,1)S(1)}, bf16[1024,32]{0,1:T(8,128)(2,1)}, u32[]{:S(2)}) copy-start(bf16[1024,32]{0,1:T(8,128)(2,1)} %param.34) | copy-start | bytes 196612
  34.5 8.0 %copy-start.7 = (bf16[32,1024]{1,0:T(8,128)(2,1)S(1)}, bf16[32,1024]{1,0:T(8,128)(2,1)}, u32[]{:S(2)}) copy-start(bf16[32,1024]{1,0:T(8,128)(2,1)} %refs_18_.3) | copy-start | bytes 196612
  34.5 8.0 %copy-start.8 = (bf16[256,32]{0,1:T(8,128)(2,1)S(1)}, bf16[256,32]{0,1:T(8,128)(2,1)}, u32[]{:S(2)}) copy-start(bf16[256,32]{0,1:T(8,128)(2,1)} %param.30) | copy-start | bytes 49156
  34.5 8.0 %copy-start.9 = (f32[1024]{0:T(1024)S(1)}, f32[1024]{0:T(1024)}, u32[]{:S(2)}) copy-start(f32[1024]{0:T(1024)} %param.36) | copy-start | bytes 12292
  34.5 8.0 %copy-start.10 = (f32[1024]{0:T(1024)S(1)}, f32[1024]{0:T(1024)}, u32[]{:S(2)}) copy-start(f32[1024]{0:T(1024)} %param.37) | copy-start | bytes 12292
  34.6 5.6 %collective-permute-start.8 = (bf16[256,256]{1,0:T(8,128)(2,1)S(1)}, bf16[256,256]{1,0:T(8,128)(2,1)S(1)}, u32[]{:S(2)}, u32[]{:S(2)}) collective-permute-start(bf16[256,256]{1,0:T(8,128)(2,1)S(1)} %get-tuple-element.77.refs_0_), channel_id=1, source_target_pairs={{0,2},{1,3},{2,0},{3,1},{4,6},{5,7},{6,4},{7,5},{8,10},{9,11},{10,... | collective-permute-start | bytes 393224 | tf_op jit(solution)/shard_map/ppermute | solution.py:315
  40.2 2.3 %collective-permute-start.14 = (bf16[256,1024]{1,0:T(8,128)(2,1)S(1)}, bf16[256,1024]{1,0:T(8,128)(2,1)S(1)}, u32[]{:S(2)}, u32[]{:S(2)}) collective-permute-start(bf16[256,1024]{1,0:T(8,128)(2,1)S(1)} %collective-permute-done.refs_6_), channel_id=1, source_target_pairs={{0,1},{1,0},{2,3},{3,2},{4,5},{5,4},{6,7},{7,6},{8,9},{9,8},{10,11... | collective-permute-start | bytes 1572872 | tf_op jit(solution)/shard_map/ppermute | solution.py:315
  40.2 2.1 %collective-permute-start.12 = (bf16[256,256]{1,0:T(8,128)(2,1)S(1)}, bf16[256,256]{1,0:T(8,128)(2,1)S(1)}, u32[]{:S(2)}, u32[]{:S(2)}) collective-permute-start(bf16[256,256]{1,0:T(8,128)(2,1)S(1)} %get-tuple-element.77.refs_0_), channel_id=1, source_target_pairs={{0,1},{1,0},{2,3},{3,2},{4,5},{5,4},{6,7},{7,6},{8,9},{9,8},{10,11... | collective-permute-start | bytes 393224 | tf_op jit(solution)/shard_map/ppermute | solution.py:315
  40.7 1.8 %collective-permute-start.13 = (bf16[256,256]{1,0:T(8,128)(2,1)S(1)}, bf16[256,256]{1,0:T(8,128)(2,1)S(1)}, u32[]{:S(2)}, u32[]{:S(2)}) collective-permute-start(bf16[256,256]{1,0:T(8,128)(2,1)S(1)} %collective-permute-done.8.refs_2_), channel_id=1, source_target_pairs={{0,1},{1,0},{2,3},{3,2},{4,5},{5,4},{6,7},{7,6},{8,9},{9,8},{10,11... | collective-permute-start | bytes 393224 | tf_op jit(solution)/shard_map/ppermute | solution.py:315
  40.7 7.6 %collective-permute-start.10 = (bf16[256,256]{1,0:T(8,128)(2,1)S(1)}, bf16[256,256]{1,0:T(8,128)(2,1)S(1)}, u32[]{:S(2)}, u32[]{:S(2)}) collective-permute-start(bf16[256,256]{1,0:T(8,128)(2,1)S(1)} %get-tuple-element.95.refs_0_), channel_id=1, source_target_pairs={{0,2},{1,3},{2,0},{3,1},{4,6},{5,7},{6,4},{7,5},{8,10},{9,11},{10,... | collective-permute-start | bytes 393224 | tf_op jit(solution)/shard_map/ppermute | solution.py:315
  47.7 1.4 %collective-permute-start.15 = (bf16[1,64,1024]{2,1,0:T(8,128)(2,1)S(1)}, bf16[1,64,1024]{2,1,0:T(8,128)(2,1)S(1)}, u32[]{:S(2)}, u32[]{:S(2)}) collective-permute-start(bf16[1,64,1024]{2,1,0:T(8,128)(2,1)S(1)} %get-tuple-element.93), channel_id=1, source_target_pairs={{0,1},{1,0},{2,3},{3,2},{4,5},{5,4},{6,7},{7,6},{8,9},{9,8},{10,11... | collective-permute-start | bytes 393224 | tf_op jit(solution)/shard_map/ppermute | solution.py:315
  47.9 1.7 %collective-permute-start.9 = (bf16[256,256]{1,0:T(8,128)(2,1)S(1)}, bf16[256,256]{1,0:T(8,128)(2,1)S(1)}, u32[]{:S(2)}, u32[]{:S(2)}) collective-permute-start(bf16[256,256]{1,0:T(8,128)(2,1)S(1)} %get-tuple-element.95.refs_0_), channel_id=1, source_target_pairs={{0,1},{1,0},{2,3},{3,2},{4,5},{5,4},{6,7},{7,6},{8,9},{9,8},{10,11... | collective-permute-start | bytes 393224 | tf_op jit(solution)/shard_map/ppermute | solution.py:315
  48.3 1.3 %collective-permute-start.11 = (bf16[256,256]{1,0:T(8,128)(2,1)S(1)}, bf16[256,256]{1,0:T(8,128)(2,1)S(1)}, u32[]{:S(2)}, u32[]{:S(2)}) collective-permute-start(bf16[256,256]{1,0:T(8,128)(2,1)S(1)} %collective-permute-done.10.refs_2_), channel_id=1, source_target_pairs={{0,1},{1,0},{2,3},{3,2},{4,5},{5,4},{6,7},{7,6},{8,9},{9,8},{10,11... | collective-permute-start | bytes 393224 | tf_op jit(solution)/shard_map/ppermute | solution.py:315
  49.6 6.2 %collective-permute-start.18 = (bf16[64,1024]{1,0:T(8,128)(2,1)S(1)}, bf16[64,1024]{1,0:T(8,128)(2,1)S(1)}, u32[]{:S(2)}, u32[]{:S(2)}) collective-permute-start(bf16[64,1024]{1,0:T(8,128)(2,1)S(1)} %fusion), channel_id=1, source_target_pairs={{0,2},{1,3},{2,0},{3,1},{4,6},{5,7},{6,4},{7,5},{8,10},{9,11},{10,... | collective-permute-start | bytes 393224 | tf_op jit(solution)/shard_map/ppermute | solution.py:315
  50.1 5.7 %collective-permute-start.17 = (bf16[64,1024]{1,0:T(8,128)(2,1)S(1)}, bf16[64,1024]{1,0:T(8,128)(2,1)S(1)}, u32[]{:S(2)}, u32[]{:S(2)}) collective-permute-start(bf16[64,1024]{1,0:T(8,128)(2,1)S(1)} %get-tuple-element.101), channel_id=1, source_target_pairs={{0,1},{1,0},{2,3},{3,2},{4,5},{5,4},{6,7},{7,6},{8,9},{9,8},{10,11... | collective-permute-start | bytes 393224 | tf_op jit(solution)/shard_map/ppermute | solution.py:315
  50.1 5.7 %copy-start = (f32[1024]{0:T(1024)S(1)}, f32[1024]{0:T(1024)}, u32[]{:S(2)}) copy-start(f32[1024]{0:T(1024)} %param.38) | copy-start | bytes 12292
  50.1 5.7 %copy-start.1 = (f32[1024]{0:T(1024)S(1)}, f32[1024]{0:T(1024)}, u32[]{:S(2)}) copy-start(f32[1024]{0:T(1024)} %param.39) | copy-start | bytes 12292
  55.2 1.6 %collective-permute-start.16 = (bf16[1,64,1024]{2,1,0:T(8,128)(2,1)S(1)}, bf16[1,64,1024]{2,1,0:T(8,128)(2,1)S(1)}, u32[]{:S(2)}, u32[]{:S(2)}) collective-permute-start(bf16[1,64,1024]{2,1,0:T(8,128)(2,1)S(1)} %get-tuple-element.100), channel_id=1, source_target_pairs={{0,1},{1,0},{2,3},{3,2},{4,5},{5,4},{6,7},{7,6},{8,9},{9,8},{10,11... | collective-permute-start | bytes 393224 | tf_op jit(solution)/shard_map/ppermute | solution.py:315
  56.8 1.9 %collective-permute-start.19 = (bf16[64,1024]{1,0:T(8,128)(2,1)S(1)}, bf16[64,1024]{1,0:T(8,128)(2,1)S(1)}, u32[]{:S(2)}, u32[]{:S(2)}) collective-permute-start(bf16[64,1024]{1,0:T(8,128)(2,1)S(1)} %get-tuple-element.108), channel_id=1, source_target_pairs={{0,1},{1,0},{2,3},{3,2},{4,5},{5,4},{6,7},{7,6},{8,9},{9,8},{10,11... | collective-permute-start | bytes 393224 | tf_op jit(solution)/shard_map/ppermute | solution.py:315
  57.3 5.5 %collective-permute-start.20 = (bf16[64,1024]{1,0:T(8,128)(2,1)S(1)}, bf16[64,1024]{1,0:T(8,128)(2,1)S(1)}, u32[]{:S(2)}, u32[]{:S(2)}) collective-permute-start(bf16[64,1024]{1,0:T(8,128)(2,1)S(1)} %fusion.1), channel_id=1, source_target_pairs={{0,2},{1,3},{2,0},{3,1},{4,6},{5,7},{6,4},{7,5},{8,10},{9,11},{10,... | collective-permute-start | bytes 393224 | tf_op jit(solution)/shard_map/ppermute | solution.py:315

commit v8 on v6

--- a/solution.py
+++ b/solution.py
@@ -47,6 +47,17 @@
     for c in copies:
         c.start()
     return copies
+
+
+def twice(ref):
+    return jnp.concatenate([ref[...], ref[...]], axis=0)
+
+
+def split_two(low, sel):
+    low = low * sel
+    high = low.astype(BF).astype(F32)
+    lane = lax.broadcasted_iota(jnp.int32, low.shape, 1)
+    return jnp.where(lane < low.shape[1] // 2, high, low - high).astype(BF)
 
 
 def pack_kernel(
@@ -206,20 +217,27 @@
 
     def step(t):
         rs = span(t * size, size)
-        sel = sel_in[span(chunk * rows + t * size, size)].astype(F32)[:, :SPAN]
-        total = x[rs].astype(F32)
+        sel = sel_in[span(chunk * rows + t * size, size)].astype(F32)[:, : 2 * SPAN]
         low = None
         for r in range(n_tp):
-            a = atts[r][rs]
-            total = total + dot(a, wouts[r][...])
-            part = dot_t(a, odowns[r][...])
+            part = dot_t(atts[r][rs], twice(odowns[r]))
             low = part if low is None else low + part
-        total = total + dot(split_low(low, sel), ups[0])
+        low = split_two(low, sel)
+        total = x[rs].astype(F32)
+        for r in range(n_tp):
+            total = total + dot(atts[r][rs], wouts[r][...])
+        total = total + dot(low, ups[0])
         h1 = layer_norm(total, g1[...], b1[...]).astype(BF)
         h_scr[span(t * nb, nb)] = h1.reshape(nb, n_tp, share, feat)
-        gate = dot(h1, w1[...]) + dot(split_low(dot_t(h1, d1[...]), sel), ups[1])
-        hidden = (0.5 * gate * (1.0 + lax.erf(gate * 0.7071067811865476))).astype(BF)
-        term = dot(hidden, w2[...]) + dot(split_low(dot_t(hidden, d2[...]), sel), ups[2])
+        low = split_two(dot_t(h1, twice(d1)), sel)
+        pieces = []
+        for n in range(4):
+            ns = slice(n * w1.shape[1] // 4, (n + 1) * w1.shape[1] // 4)
+            gate = dot(h1, w1[:, ns]) + dot(low, ups[1][:, ns])
+            pieces.append((0.5 * gate * (1.0 + lax.erf(gate * 0.7071067811865476))).astype(BF))
+        hidden = jnp.concatenate(pieces, axis=1)
+        low = split_two(dot_t(hidden, twice(d2)), sel)
+        term = dot(hidden, w2[...]) + dot(low, ups[2])
         term = term.reshape(nb, n_tp, share, feat)
         own_rows = span(t * (size // n_tp), size // n_tp)
         for j in range(n_tp):

time: 76.7 us -> 75.4 us (0.983)
  Pallas kernels: 22.2 us -> 20.9 us
    pallas_call x2, Pallas kernels: 10.2 us -> 8.93 us  [body(): pl.pallas_call(functools.partial(ffn_kernel, n_tp, c), out_shape=[pltpu.V...]
  transfers between devices with their start and end apart: 24 -> 24, of which waited for: 14 -> 14; matrix products, arithmetic and copies ran while one was open for 0% -> 0% of each run, Pallas kernels for 25% -> 23%
where the time goes in v8:
time: 75.4 us; the launch traced here: 75.2 us
  waiting for transfers between devices  22.9 us (30%)
  Pallas kernels  20.9 us (28%)
  starting transfers between devices  17.1 us (23%)
  blocking collectives  13.9 us (18%)
    ppermute x23, waiting for transfers between devices, swap(): return lax.ppermute(value, 'tp', [(i, i ^ r) for i in range(n_tp)])  19.5 us
    all_to_all x1, blocking collectives, body(): lax.all_to_all(done.reshape(n_req * n_tp, share, width), ('req', 'tp'), s...  13.9 us
    ppermute x23, starting transfers between devices, swap(): return lax.ppermute(value, 'tp', [(i, i ^ r) for i in range(n_tp)])  11.3 us
    pallas_call x2, Pallas kernels, body(): pl.pallas_call(functools.partial(ffn_kernel, n_tp, c), out_shape=[pltpu.V...  8.93 us
    all_to_all x1, starting transfers between devices, body(): lax.all_to_all(packed, 'req', split_axis=0, concat_axis=0, tiled=True)  5.81 us
    pallas_call x2, Pallas kernels, body(): pl.pallas_call(functools.partial(attn_kernel, n_tp, c), out_shape=[pltpu....  5.52 us
    all_to_all x1, waiting for transfers between devices, body(): lax.all_to_all(packed, 'req', split_axis=0, concat_axis=0, tiled=True)  3.39 us
    pallas_call x1, Pallas kernels, body(): pl.pallas_call(begin_kernel, out_shape=[pltpu.VMEM((3, count * rows, widt...  2.86 us
  transfers between devices with their start and end apart: 24, of which 14 were waited for; matrix products, arithmetic and copies ran while one was open for 0% of the time, Pallas kernels for 23%

profile of v8, /device:TPU:0, one launch (start us, length us, event | category | flops | bytes accessed | tf_op | source)
XLA Modules:
  0.0 75.2 jit_solution(11817332397354789782)
XLA Ops:
  0.0 1.8 %pack.1 = (bf16[8,72,256]{2,1,0:T(8,128)(2,1)}, s32[8]{0:T(128)S(1)}) custom-call(s32[4,8]{1,0:T(4,128)} %bitcast.42, s32[4,8]{1,0:T(4,128)} %bitcast.43, s32[16]{0:T(128)} %slots_in.1, bf16[8,64,256]{2,1,0:T(8,128)(2,1)} %bitcast.40), custom_call_target="tpu_custom_call" | custom-call | tf_op jit(solution)/shard_map/pack/pallas_call | solution.py:342
  1.8 3.0 %collective-permute-start = (bf16[256,1024]{1,0:T(8,128)(2,1)}, bf16[256,1024]{1,0:T(8,128)(2,1)S(1)}, u32[]{:S(2)}, u32[]{:S(2)}) collective-permute-start(bf16[256,1024]{1,0:T(8,128)(2,1)} %refs_4_.3), channel_id=1, source_target_pairs={{0,2},{1,3},{2,0},{3,1},{4,6},{5,7},{6,4},{7,5},{8,10},{9,11},{10,... | collective-permute-start | bytes 1572872 | tf_op jit(solution)/shard_map/ppermute | solution.py:337
  4.9 5.8 %all-to-all-start = ((bf16[8,72,256]{2,1,0:T(8,128)(2,1)}), bf16[8,72,256]{2,1,0:T(8,128)(2,1)S(1)}, u32[]{:S(2)}, u32[]{:S(2)}) async-start(bf16[8,72,256]{2,1,0:T(8,128)(2,1)} %get-tuple-element.59), calls=%async_computation | async-start | bytes 589824 | tf_op jit(solution)/shard_map/all_to_all | solution.py:370
  10.7 0.2 collective-permute-start.2
  10.9 0.5 collective-permute-start.3
  11.4 1.1 %collective-permute-start.4 = (bf16[32,256]{1,0:T(8,128)(2,1)}, bf16[32,256]{1,0:T(8,128)(2,1)S(1)}, u32[]{:S(2)}, u32[]{:S(2)}) collective-permute-start(bf16[32,256]{1,0:T(8,128)(2,1)} %bitcast.33), channel_id=1, source_target_pairs={{0,3},{1,2},{2,1},{3,0},{4,7},{5,6},{6,5},{7,4},{8,11},{9,10},{10,... | collective-permute-start | bytes 49160 | tf_op jit(solution)/shard_map/ppermute | solution.py:337
  12.6 5.0 %collective-permute-done.3.refs_10_ = bf16[32,256]{1,0:T(8,128)(2,1)S(1)} collective-permute-done((bf16[32,256]{1,0:T(8,128)(2,1)}, bf16[32,256]{1,0:T(8,128)(2,1)S(1)}, u32[]{:S(2)}, u32[]{:S(2)}) %collective-permute-start.3) | collective-permute-done | bytes 16416 | tf_op jit(solution)/shard_map/ppermute | solution.py:337
  17.5 3.4 %all-to-all-done.own.refs_0_ = bf16[8,72,256]{2,1,0:T(8,128)(2,1)S(1)} async-done(((bf16[8,72,256]{2,1,0:T(8,128)(2,1)}), bf16[8,72,256]{2,1,0:T(8,128)(2,1)S(1)}, u32[]{:S(2)}, u32[]{:S(2)}) %all-to-all-start) | async-done | bytes 294944 | tf_op jit(solution)/shard_map/all_to_all | solution.py:370
  21.0 0.6 collective-permute-start.6
  21.5 1.0 %collective-permute-done.5.beside.refs_1_ = bf16[8,72,256]{2,1,0:T(8,128)(2,1)S(1)} collective-permute-done((bf16[8,72,256]{2,1,0:T(8,128)(2,1)S(1)}, bf16[8,72,256]{2,1,0:T(8,128)(2,1)S(1)}, u32[]{:S(2)}, u32[]{:S(2)}) %collective-permute-start.5) | collective-permute-done | bytes 294944 | tf_op jit(solution)/shard_map/ppermute | solution.py:337
  22.5 2.9 %begin.1 = (f32[3,512,256]{2,1,0:T(8,128)S(1)}, f32[512,96]{1,0:T(8,128)S(1)}, bf16[512,128]{1,0:T(8,128)(2,1)S(1)}, f32[512,128]{1,0:T(8,128)S(1)}, bf16[3,1024...) custom-call(s32[1]{0:T(128)} %bitcast.3.me, ...), custom_call_target="tpu_custom_call" | custom-call | flops 1006632960 | bytes 2097152 | tf_op jit(solution)/shard_map/begin/pallas_call | solution.py:384
  25.4 1.9 %collective-permute-done.6.refs_2_ = bf16[4,72,256]{2,1,0:T(8,128)(2,1)S(1)} collective-permute-done((bf16[4,72,256]{2,1,0:T(8,128)(2,1)S(1)}, bf16[4,72,256]{2,1,0:T(8,128)(2,1)S(1)}, u32[]{:S(2)}, u32[]{:S(2)}) %collective-permute-start.6) | collective-permute-done | bytes 147488 | tf_op jit(solution)/shard_map/ppermute | solution.py:337
  27.3 0.5 collective-permute-start.9
  27.8 0.9 %collective-permute-done.7.refs_3_ = bf16[4,72,256]{2,1,0:T(8,128)(2,1)S(1)} collective-permute-done((bf16[4,72,256]{2,1,0:T(8,128)(2,1)S(1)}, bf16[4,72,256]{2,1,0:T(8,128)(2,1)S(1)}, u32[]{:S(2)}, u32[]{:S(2)}) %collective-permute-start.7) | collective-permute-done | bytes 147488 | tf_op jit(solution)/shard_map/ppermute | solution.py:337
  28.7 2.8 %attend.2 = (bf16[256,256]{1,0:T(8,128)(2,1)S(1)}, bf16[256,1024]{1,0:T(8,128)(2,1)S(1)}) custom-call(s32[1]{0:T(128)} %bitcast.3.me, bf16[8,72,256]{2,1,0:T(8,128)(2,1)S(1)} %all-to-all-done.own.refs_0_, bf16[8,72,256]{2,1,0:T(8,128)(2,1)S(1)} %collective-permute-done.5.beside.refs_1_, bf16[4,72,256]{2,1,0:T(8,128)(2,1)S(1)} %collective-permute-done.6.refs_2_, ...), custom_call_target="tpu_custom_call" | custom-call | flops 2181038080 | bytes 2097152 | tf_op jit(solution)/shard_map/attend/pallas_call | solution.py:432
  31.4 2.1 %collective-permute-done.9.refs_2_ = bf16[4,72,256]{2,1,0:T(8,128)(2,1)S(1)} collective-permute-done((bf16[4,72,256]{2,1,0:T(8,128)(2,1)S(1)}, bf16[4,72,256]{2,1,0:T(8,128)(2,1)S(1)}, u32[]{:S(2)}, u32[]{:S(2)}) %collective-permute-start.9) | collective-permute-done | bytes 147488 | tf_op jit(solution)/shard_map/ppermute | solution.py:337
  33.6 0.0 copy-start.6
  33.6 0.0 copy-start.7
  33.6 0.0 copy-start.8
  33.6 0.0 copy-start.9
  33.6 0.0 copy-start.10
  33.6 0.1 collective-permute-start.16
  33.7 0.5 collective-permute-start.10
  34.2 0.5 collective-permute-start.8
  34.7 1.1 %collective-permute-done.10.refs_3_ = bf16[4,72,256]{2,1,0:T(8,128)(2,1)S(1)} collective-permute-done((bf16[4,72,256]{2,1,0:T(8,128)(2,1)S(1)}, bf16[4,72,256]{2,1,0:T(8,128)(2,1)S(1)}, u32[]{:S(2)}, u32[]{:S(2)}) %collective-permute-start.10) | collective-permute-done | bytes 147488 | tf_op jit(solution)/shard_map/ppermute | solution.py:337
  35.8 2.8 %attend.3 = (bf16[256,256]{1,0:T(8,128)(2,1)S(1)}, bf16[256,1024]{1,0:T(8,128)(2,1)S(1)}) custom-call(s32[1]{0:T(128)} %bitcast.3.me, bf16[8,72,256]{2,1,0:T(8,128)(2,1)S(1)} %all-to-all-done.own.refs_0_, bf16[8,72,256]{2,1,0:T(8,128)(2,1)S(1)} %collective-permute-done.5.beside.refs_1_, bf16[4,72,256]{2,1,0:T(8,128)(2,1)S(1)} %collective-permute-done.9.refs_2_, ...), custom_call_target="tpu_custom_call" | custom-call | flops 2181038080 | bytes 2097152 | tf_op jit(solution)/shard_map/attend/pallas_call | solution.py:432
  38.6 1.1 %collective-permute-done.8.refs_2_ = bf16[256,256]{1,0:T(8,128)(2,1)S(1)} collective-permute-done((bf16[256,256]{1,0:T(8,128)(2,1)S(1)}, bf16[256,256]{1,0:T(8,128)(2,1)S(1)}, u32[]{:S(2)}, u32[]{:S(2)}) %collective-permute-start.8) | collective-permute-done | bytes 131104 | tf_op jit(solution)/shard_map/ppermute | solution.py:337
  39.7 0.5 collective-permute-start.12
  40.2 0.8 %collective-permute-done.15.refs_3_ = bf16[256,256]{1,0:T(8,128)(2,1)S(1)} collective-permute-done((bf16[256,256]{1,0:T(8,128)(2,1)S(1)}, bf16[256,256]{1,0:T(8,128)(2,1)S(1)}, u32[]{:S(2)}, u32[]{:S(2)}) %collective-permute-start.15) | collective-permute-done | bytes 131104 | tf_op jit(solution)/shard_map/ppermute | solution.py:337
  41.1 4.5 %feed.2 = (f32[2,64,1024]{2,1,0:T(8,128)S(1)}, bf16[64,1024]{1,0:T(8,128)(2,1)S(1)}, bf16[1,64,1024]{2,1,0:T(8,128)(2,1)S(1)}, bf16[64,1024]{1,0:T(8,128)(2,1)S(1)}) custom-call(s32[1]{0:T(128)} %bitcast.3.me, bf16[256,256]{1,0:T(8,128)(2,1)S(1)} %get-tuple-element.80.refs_0_, bf16[256,256]{1,0:T(8,128)(2,1)S(1)} %collective-permute-done.14.refs_1_, ...), custom_call_target="tpu_custom_call" | custom-call | flops 8053063680 | bytes 2097152 | tf_op jit(solution)/shard_map/feed/pallas_call | solution.py:465
  45.6 0.2 collective-permute-start.17
  45.8 0.4 collective-permute-start.11
  46.2 0.1 collective-permute-start.13
  46.3 0.4 collective-permute-start.19
  46.7 0.3 collective-permute-done.17
  47.0 0.2 collective-permute-done.11.refs_1_
  47.2 0.3 collective-permute-done.13.refs_3_
  47.5 0.7 collective-permute-start.20
  48.2 4.5 %feed.3 = (f32[2,64,1024]{2,1,0:T(8,128)S(1)}, bf16[64,1024]{1,0:T(8,128)(2,1)S(1)}, bf16[1,64,1024]{2,1,0:T(8,128)(2,1)S(1)}, bf16[64,1024]{1,0:T(8,128)(2,1)S(1)}) custom-call(s32[1]{0:T(128)} %bitcast.3.me, bf16[256,256]{1,0:T(8,128)(2,1)S(1)} %get-tuple-element.93.refs_0_, bf16[256,256]{1,0:T(8,128)(2,1)S(1)} %collective-permute-done.11.refs_1_, ...), custom_call_target="tpu_custom_call" | custom-call | flops 8053063680 | bytes 2097152 | tf_op jit(solution)/shard_map/feed/pallas_call | solution.py:465
  52.7 0.1 collective-permute-start.18
  52.8 0.5 collective-permute-start.21
  53.3 0.2 finish.2.refs_0_
  53.5 0.6 collective-permute-done.18
  54.1 1.4 %collective-permute-start.22 = (bf16[64,1024]{1,0:T(8,128)(2,1)S(1)}, bf16[64,1024]{1,0:T(8,128)(2,1)S(1)}, u32[]{:S(2)}, u32[]{:S(2)}) collective-permute-start(bf16[64,1024]{1,0:T(8,128)(2,1)S(1)} %fusion.1), channel_id=1, source_target_pairs={{0,2},{1,3},{2,0},{3,1},{4,6},{5,7},{6,4},{7,5},{8,10},{9,11},{10,... | collective-permute-start | bytes 393224 | tf_op jit(solution)/shard_map/ppermute | solution.py:337
  55.5 4.2 %collective-permute-done.22.refs_4_ = bf16[64,1024]{1,0:T(8,128)(2,1)S(1)} collective-permute-done((bf16[64,1024]{1,0:T(8,128)(2,1)S(1)}, bf16[64,1024]{1,0:T(8,128)(2,1)S(1)}, u32[]{:S(2)}, u32[]{:S(2)}) %collective-permute-start.22) | collective-permute-done | bytes 131104 | tf_op jit(solution)/shard_map/ppermute | solution.py:337
  59.8 0.2 finish.3
  60.0 13.9 %all_to_all.10 = bf16[32,16,256]{2,1,0:T(8,128)(2,1)S(1)} all-to-all(bf16[32,16,256]{2,1,0:T(8,128)(2,1)S(1)} %bitcast.21), channel_id=1, replica_groups=mesh['req'=8,'tp'=4] {'req','tp'}, dimensions={0} | all-to-all | bytes 524288 | tf_op jit(solution)/shard_map/all_to_all | solution.py:491
  73.9 1.3 %unpack.1 = bf16[8,64,256]{2,1,0:T(8,128)(2,1)} custom-call(s32[8]{0:T(128)S(1)} %get-tuple-element.56.owners, bf16[8,64,256]{2,1,0:T(8,128)(2,1)S(1)} %bitcast.22), custom_call_target="tpu_custom_call" | custom-call | tf_op jit(solution)/shard_map/unpack/pallas_call | solution.py:498
  (35 shorter events, 0.2 us)
Async XLA Ops:
  1.8 19.1 %collective-permute-start = (bf16[256,1024]{1,0:T(8,128)(2,1)}, bf16[256,1024]{1,0:T(8,128)(2,1)S(1)}, u32[]{:S(2)}, u32[]{:S(2)}) collective-permute-start(bf16[256,1024]{1,0:T(8,128)(2,1)} %refs_4_.3), channel_id=1, source_target_pairs={{0,2},{1,3},{2,0},{3,1},{4,6},{5,7},{6,4},{7,5},{8,10},{9,11},{10,... | collective-permute-start | bytes 1572872 | tf_op jit(solution)/shard_map/ppermute | solution.py:337
  4.9 16.1 %collective-permute-start.1 = (bf16[256,1024]{1,0:T(8,128)(2,1)}, bf16[256,1024]{1,0:T(8,128)(2,1)S(1)}, u32[]{:S(2)}, u32[]{:S(2)}) collective-permute-start(bf16[256,1024]{1,0:T(8,128)(2,1)} %refs_4_.3), channel_id=1, source_target_pairs={{0,1},{1,0},{2,3},{3,2},{4,5},{5,4},{6,7},{7,6},{8,9},{9,8},{10,11... | collective-permute-start | bytes 1572872 | tf_op jit(solution)/shard_map/ppermute | solution.py:337
  4.9 16.0 %all-to-all-start = ((bf16[8,72,256]{2,1,0:T(8,128)(2,1)}), bf16[8,72,256]{2,1,0:T(8,128)(2,1)S(1)}, u32[]{:S(2)}, u32[]{:S(2)}) async-start(bf16[8,72,256]{2,1,0:T(8,128)(2,1)} %get-tuple-element.59), calls=%async_computation | async-start | bytes 589824 | tf_op jit(solution)/shard_map/all_to_all | solution.py:370
  10.7 1.9 %collective-permute-start.2 = (bf16[32,256]{1,0:T(8,128)(2,1)}, bf16[32,256]{1,0:T(8,128)(2,1)S(1)}, u32[]{:S(2)}, u32[]{:S(2)}) collective-permute-start(bf16[32,256]{1,0:T(8,128)(2,1)} %bitcast.31), channel_id=1, source_target_pairs={{0,1},{1,0},{2,3},{3,2},{4,5},{5,4},{6,7},{7,6},{8,9},{9,8},{10,11... | collective-permute-start | bytes 49160 | tf_op jit(solution)/shard_map/ppermute | solution.py:337
  10.9 6.6 %collective-permute-start.3 = (bf16[32,256]{1,0:T(8,128)(2,1)}, bf16[32,256]{1,0:T(8,128)(2,1)S(1)}, u32[]{:S(2)}, u32[]{:S(2)}) collective-permute-start(bf16[32,256]{1,0:T(8,128)(2,1)} %bitcast.32), channel_id=1, source_target_pairs={{0,2},{1,3},{2,0},{3,1},{4,6},{5,7},{6,4},{7,5},{8,10},{9,11},{10,... | collective-permute-start | bytes 49160 | tf_op jit(solution)/shard_map/ppermute | solution.py:337
  11.4 6.1 %collective-permute-start.4 = (bf16[32,256]{1,0:T(8,128)(2,1)}, bf16[32,256]{1,0:T(8,128)(2,1)S(1)}, u32[]{:S(2)}, u32[]{:S(2)}) collective-permute-start(bf16[32,256]{1,0:T(8,128)(2,1)} %bitcast.33), channel_id=1, source_target_pairs={{0,3},{1,2},{2,1},{3,0},{4,7},{5,6},{6,5},{7,4},{8,11},{9,10},{10,... | collective-permute-start | bytes 49160 | tf_op jit(solution)/shard_map/ppermute | solution.py:337
  20.9 1.6 %collective-permute-start.5 = (bf16[8,72,256]{2,1,0:T(8,128)(2,1)S(1)}, bf16[8,72,256]{2,1,0:T(8,128)(2,1)S(1)}, u32[]{:S(2)}, u32[]{:S(2)}) collective-permute-start(bf16[8,72,256]{2,1,0:T(8,128)(2,1)S(1)} %all-to-all-done.own.refs_0_), channel_id=1, source_target_pairs={{0,1},{1,0},{2,3},{3,2},{4,5},{5,4},{6,7},{7,6},{8,9},{9,8},{10,11... | collective-permute-start | bytes 884744 | tf_op jit(solution)/shard_map/ppermute | solution.py:337
  21.0 6.3 %collective-permute-start.6 = (bf16[4,72,256]{2,1,0:T(8,128)(2,1)S(1)}, bf16[4,72,256]{2,1,0:T(8,128)(2,1)S(1)}, u32[]{:S(2)}, u32[]{:S(2)}) collective-permute-start(bf16[4,72,256]{2,1,0:T(8,128)(2,1)S(1)} %get-tuple-element.108), channel_id=1, source_target_pairs={{0,2},{1,3},{2,0},{3,1},{4,6},{5,7},{6,4},{7,5},{8,10},{9,11},{10,... | collective-permute-start | bytes 442376 | tf_op jit(solution)/shard_map/ppermute | solution.py:337
  27.3 1.4 %collective-permute-start.7 = (bf16[4,72,256]{2,1,0:T(8,128)(2,1)S(1)}, bf16[4,72,256]{2,1,0:T(8,128)(2,1)S(1)}, u32[]{:S(2)}, u32[]{:S(2)}) collective-permute-start(bf16[4,72,256]{2,1,0:T(8,128)(2,1)S(1)} %collective-permute-done.6.refs_2_), channel_id=1, source_target_pairs={{0,1},{1,0},{2,3},{3,2},{4,5},{5,4},{6,7},{7,6},{8,9},{9,8},{10,11... | collective-permute-start | bytes 442376 | tf_op jit(solution)/shard_map/ppermute | solution.py:337
  27.3 6.3 %collective-permute-start.9 = (bf16[4,72,256]{2,1,0:T(8,128)(2,1)S(1)}, bf16[4,72,256]{2,1,0:T(8,128)(2,1)S(1)}, u32[]{:S(2)}, u32[]{:S(2)}) collective-permute-start(bf16[4,72,256]{2,1,0:T(8,128)(2,1)S(1)} %get-tuple-element.107), channel_id=1, source_target_pairs={{0,2},{1,3},{2,0},{3,1},{4,6},{5,7},{6,4},{7,5},{8,10},{9,11},{10,... | collective-permute-start | bytes 442376 | tf_op jit(solution)/shard_map/ppermute | solution.py:337
  33.6 7.5 %copy-start.2 = (bf16[256,1024]{1,0:T(8,128)(2,1)S(1)}, bf16[256,1024]{1,0:T(8,128)(2,1)}, u32[]{:S(2)}) copy-start(bf16[256,1024]{1,0:T(8,128)(2,1)} %refs_4_.3) | copy-start | bytes 1572868
  33.6 7.5 %copy-start.3 = (bf16[32,1024]{1,0:T(8,128)(2,1)S(1)}, bf16[32,1024]{1,0:T(8,128)(2,1)}, u32[]{:S(2)}) copy-start(bf16[32,1024]{1,0:T(8,128)(2,1)} %refs_14_.3) | copy-start | bytes 196612
  33.6 7.5 %copy-start.4 = (bf16[1024,32]{0,1:T(8,128)(2,1)S(1)}, bf16[1024,32]{0,1:T(8,128)(2,1)}, u32[]{:S(2)}) copy-start(bf16[1024,32]{0,1:T(8,128)(2,1)} %param.32) | copy-start | bytes 196612
  33.6 7.5 %copy-start.5 = (bf16[32,1024]{1,0:T(8,128)(2,1)S(1)}, bf16[32,1024]{1,0:T(8,128)(2,1)}, u32[]{:S(2)}) copy-start(bf16[32,1024]{1,0:T(8,128)(2,1)} %refs_16_.3) | copy-start | bytes 196612
  33.6 7.5 %copy-start.6 = (bf16[1024,32]{0,1:T(8,128)(2,1)S(1)}, bf16[1024,32]{0,1:T(8,128)(2,1)}, u32[]{:S(2)}) copy-start(bf16[1024,32]{0,1:T(8,128)(2,1)} %param.34) | copy-start | bytes 196612
  33.6 7.5 %copy-start.7 = (bf16[32,1024]{1,0:T(8,128)(2,1)S(1)}, bf16[32,1024]{1,0:T(8,128)(2,1)}, u32[]{:S(2)}) copy-start(bf16[32,1024]{1,0:T(8,128)(2,1)} %refs_18_.3) | copy-start | bytes 196612
  33.6 7.5 %copy-start.8 = (bf16[256,32]{0,1:T(8,128)(2,1)S(1)}, bf16[256,32]{0,1:T(8,128)(2,1)}, u32[]{:S(2)}) copy-start(bf16[256,32]{0,1:T(8,128)(2,1)} %param.30) | copy-start | bytes 49156
  33.6 7.5 %copy-start.9 = (f32[1024]{0:T(1024)S(1)}, f32[1024]{0:T(1024)}, u32[]{:S(2)}) copy-start(f32[1024]{0:T(1024)} %param.36) | copy-start | bytes 12292
  33.6 7.5 %copy-start.10 = (f32[1024]{0:T(1024)S(1)}, f32[1024]{0:T(1024)}, u32[]{:S(2)}) copy-start(f32[1024]{0:T(1024)} %param.37) | copy-start | bytes 12292
  33.6 7.4 %collective-permute-start.16 = (bf16[256,1024]{1,0:T(8,128)(2,1)S(1)}, bf16[256,1024]{1,0:T(8,128)(2,1)S(1)}, u32[]{:S(2)}, u32[]{:S(2)}) collective-permute-start(bf16[256,1024]{1,0:T(8,128)(2,1)S(1)} %collective-permute-done.refs_6_), channel_id=1, source_target_pairs={{0,1},{1,0},{2,3},{3,2},{4,5},{5,4},{6,7},{7,6},{8,9},{9,8},{10,11... | collective-permute-start | bytes 1572872 | tf_op jit(solution)/shard_map/ppermute | solution.py:337
  33.7 2.1 %collective-permute-start.10 = (bf16[4,72,256]{2,1,0:T(8,128)(2,1)S(1)}, bf16[4,72,256]{2,1,0:T(8,128)(2,1)S(1)}, u32[]{:S(2)}, u32[]{:S(2)}) collective-permute-start(bf16[4,72,256]{2,1,0:T(8,128)(2,1)S(1)} %collective-permute-done.9.refs_2_), channel_id=1, source_target_pairs={{0,1},{1,0},{2,3},{3,2},{4,5},{5,4},{6,7},{7,6},{8,9},{9,8},{10,11... | collective-permute-start | bytes 442376 | tf_op jit(solution)/shard_map/ppermute | solution.py:337
  34.2 5.5 %collective-permute-start.8 = (bf16[256,256]{1,0:T(8,128)(2,1)S(1)}, bf16[256,256]{1,0:T(8,128)(2,1)S(1)}, u32[]{:S(2)}, u32[]{:S(2)}) collective-permute-start(bf16[256,256]{1,0:T(8,128)(2,1)S(1)} %get-tuple-element.80.refs_0_), channel_id=1, source_target_pairs={{0,2},{1,3},{2,0},{3,1},{4,6},{5,7},{6,4},{7,5},{8,10},{9,11},{10,... | collective-permute-start | bytes 393224 | tf_op jit(solution)/shard_map/ppermute | solution.py:337
  34.7 5.5 %collective-permute-start.14 = (bf16[256,256]{1,0:T(8,128)(2,1)S(1)}, bf16[256,256]{1,0:T(8,128)(2,1)S(1)}, u32[]{:S(2)}, u32[]{:S(2)}) collective-permute-start(bf16[256,256]{1,0:T(8,128)(2,1)S(1)} %get-tuple-element.80.refs_0_), channel_id=1, source_target_pairs={{0,1},{1,0},{2,3},{3,2},{4,5},{5,4},{6,7},{7,6},{8,9},{9,8},{10,11... | collective-permute-start | bytes 393224 | tf_op jit(solution)/shard_map/ppermute | solution.py:337
  39.7 1.3 %collective-permute-start.15 = (bf16[256,256]{1,0:T(8,128)(2,1)S(1)}, bf16[256,256]{1,0:T(8,128)(2,1)S(1)}, u32[]{:S(2)}, u32[]{:S(2)}) collective-permute-start(bf16[256,256]{1,0:T(8,128)(2,1)S(1)} %collective-permute-done.8.refs_2_), channel_id=1, source_target_pairs={{0,1},{1,0},{2,3},{3,2},{4,5},{5,4},{6,7},{7,6},{8,9},{9,8},{10,11... | collective-permute-start | bytes 393224 | tf_op jit(solution)/shard_map/ppermute | solution.py:337
  39.7 6.5 %collective-permute-start.12 = (bf16[256,256]{1,0:T(8,128)(2,1)S(1)}, bf16[256,256]{1,0:T(8,128)(2,1)S(1)}, u32[]{:S(2)}, u32[]{:S(2)}) collective-permute-start(bf16[256,256]{1,0:T(8,128)(2,1)S(1)} %get-tuple-element.93.refs_0_), channel_id=1, source_target_pairs={{0,2},{1,3},{2,0},{3,1},{4,6},{5,7},{6,4},{7,5},{8,10},{9,11},{10,... | collective-permute-start | bytes 393224 | tf_op jit(solution)/shard_map/ppermute | solution.py:337
  45.6 1.4 %collective-permute-start.17 = (bf16[1,64,1024]{2,1,0:T(8,128)(2,1)S(1)}, bf16[1,64,1024]{2,1,0:T(8,128)(2,1)S(1)}, u32[]{:S(2)}, u32[]{:S(2)}) collective-permute-start(bf16[1,64,1024]{2,1,0:T(8,128)(2,1)S(1)} %get-tuple-element.92), channel_id=1, source_target_pairs={{0,1},{1,0},{2,3},{3,2},{4,5},{5,4},{6,7},{7,6},{8,9},{9,8},{10,11... | collective-permute-start | bytes 393224 | tf_op jit(solution)/shard_map/ppermute | solution.py:337
  45.8 1.4 %collective-permute-start.11 = (bf16[256,256]{1,0:T(8,128)(2,1)S(1)}, bf16[256,256]{1,0:T(8,128)(2,1)S(1)}, u32[]{:S(2)}, u32[]{:S(2)}) collective-permute-start(bf16[256,256]{1,0:T(8,128)(2,1)S(1)} %get-tuple-element.93.refs_0_), channel_id=1, source_target_pairs={{0,1},{1,0},{2,3},{3,2},{4,5},{5,4},{6,7},{7,6},{8,9},{9,8},{10,11... | collective-permute-start | bytes 393224 | tf_op jit(solution)/shard_map/ppermute | solution.py:337
  46.2 1.3 %collective-permute-start.13 = (bf16[256,256]{1,0:T(8,128)(2,1)S(1)}, bf16[256,256]{1,0:T(8,128)(2,1)S(1)}, u32[]{:S(2)}, u32[]{:S(2)}) collective-permute-start(bf16[256,256]{1,0:T(8,128)(2,1)S(1)} %collective-permute-done.12.refs_2_), channel_id=1, source_target_pairs={{0,1},{1,0},{2,3},{3,2},{4,5},{5,4},{6,7},{7,6},{8,9},{9,8},{10,11... | collective-permute-start | bytes 393224 | tf_op jit(solution)/shard_map/ppermute | solution.py:337
  46.3 7.0 %collective-permute-start.19 = (bf16[64,1024]{1,0:T(8,128)(2,1)S(1)}, bf16[64,1024]{1,0:T(8,128)(2,1)S(1)}, u32[]{:S(2)}, u32[]{:S(2)}) collective-permute-start(bf16[64,1024]{1,0:T(8,128)(2,1)S(1)} %get-tuple-element.99), channel_id=1, source_target_pairs={{0,1},{1,0},{2,3},{3,2},{4,5},{5,4},{6,7},{7,6},{8,9},{9,8},{10,11... | collective-permute-start | bytes 393224 | tf_op jit(solution)/shard_map/ppermute | solution.py:337
  47.5 5.8 %collective-permute-start.20 = (bf16[64,1024]{1,0:T(8,128)(2,1)S(1)}, bf16[64,1024]{1,0:T(8,128)(2,1)S(1)}, u32[]{:S(2)}, u32[]{:S(2)}) collective-permute-start(bf16[64,1024]{1,0:T(8,128)(2,1)S(1)} %fusion), channel_id=1, source_target_pairs={{0,2},{1,3},{2,0},{3,1},{4,6},{5,7},{6,4},{7,5},{8,10},{9,11},{10,... | collective-permute-start | bytes 393224 | tf_op jit(solution)/shard_map/ppermute | solution.py:337
  48.2 5.1 %copy-start = (f32[1024]{0:T(1024)S(1)}, f32[1024]{0:T(1024)}, u32[]{:S(2)}) copy-start(f32[1024]{0:T(1024)} %param.38) | copy-start | bytes 12292
  48.2 5.1 %copy-start.1 = (f32[1024]{0:T(1024)S(1)}, f32[1024]{0:T(1024)}, u32[]{:S(2)}) copy-start(f32[1024]{0:T(1024)} %param.39) | copy-start | bytes 12292
  52.7 1.4 %collective-permute-start.18 = (bf16[1,64,1024]{2,1,0:T(8,128)(2,1)S(1)}, bf16[1,64,1024]{2,1,0:T(8,128)(2,1)S(1)}, u32[]{:S(2)}, u32[]{:S(2)}) collective-permute-start(bf16[1,64,1024]{2,1,0:T(8,128)(2,1)S(1)} %get-tuple-element.98), channel_id=1, source_target_pairs={{0,1},{1,0},{2,3},{3,2},{4,5},{5,4},{6,7},{7,6},{8,9},{9,8},{10,11... | collective-permute-start | bytes 393224 | tf_op jit(solution)/shard_map/ppermute | solution.py:337
  52.8 2.8 %collective-permute-start.21 = (bf16[64,1024]{1,0:T(8,128)(2,1)S(1)}, bf16[64,1024]{1,0:T(8,128)(2,1)S(1)}, u32[]{:S(2)}, u32[]{:S(2)}) collective-permute-start(bf16[64,1024]{1,0:T(8,128)(2,1)S(1)} %get-tuple-element.104), channel_id=1, source_target_pairs={{0,1},{1,0},{2,3},{3,2},{4,5},{5,4},{6,7},{7,6},{8,9},{9,8},{10,11... | collective-permute-start | bytes 393224 | tf_op jit(solution)/shard_map/ppermute | solution.py:337
  54.1 5.6 %collective-permute-start.22 = (bf16[64,1024]{1,0:T(8,128)(2,1)S(1)}, bf16[64,1024]{1,0:T(8,128)(2,1)S(1)}, u32[]{:S(2)}, u32[]{:S(2)}) collective-permute-start(bf16[64,1024]{1,0:T(8,128)(2,1)S(1)} %fusion.1), channel_id=1, source_target_pairs={{0,2},{1,3},{2,0},{3,1},{4,6},{5,7},{6,4},{7,5},{8,10},{9,11},{10,... | collective-permute-start | bytes 393224 | tf_op jit(solution)/shard_map/ppermute | solution.py:337

commit v9 on v8

--- a/solution.py
+++ b/solution.py
@@ -276,9 +276,10 @@
         out[out.shape[0] - step :, f] = piece
 
 
-def unpack_kernel(owners, arrived, out):
-    for g in range(out.shape[0]):
-        out[g] = arrived[owners[g]]
+def unpack_kernel(owners, arrived, out, sems):
+    pairs = [(arrived.at[owners[g]], out.at[g]) for g in range(out.shape[0])]
+    for c in fetch(pairs, sems):
+        c.wait()
 
 
 VM = pl.BlockSpec(memory_space=pltpu.VMEM)
@@ -417,6 +418,8 @@
     w_all, w1, w2, downs, up_all = near(w_all, w1, w2, downs, up_all)
     x_far[0], begun = lax.optimization_barrier((x_far[0], begun))
     x_far[0] = second_hop(x_far[0])
+    x_far = lax.optimization_barrier(x_far)
+    x_far[1:] = [second_hop(pieces) for pieces in x_far[1:]]
 
     consts = near(
         out_up, fc1_down.T, fc1_up, fc2_down.T, fc2_up, norm1_gain[None], norm1_bias[None]
@@ -425,17 +428,14 @@
     steps = []
     for c in range(count):
         if c:
-            x_far[c], w_far, steps[0][0] = lax.optimization_barrier(
-                (x_far[c], w_far, steps[0][0])
-            )
-            x_far[c] = second_hop(x_far[c])
+            w_far, steps[0][0] = lax.optimization_barrier((w_far, steps[0][0]))
         attended, x_full = pl.pallas_call(
             functools.partial(attn_kernel, n_tp, c),
             out_shape=[pltpu.VMEM((rows, width), BF), pltpu.VMEM((rows, feat), BF)],
             in_specs=[SMEM] + [VM] * (n_tp + 7),
             out_specs=[VM] * 2,
             compiler_params=params(12),
-            cost_estimate=work(2 * rows * feat * 3 * width + 4 * rows * width * 2 * CAP, rows),
+            cost_estimate=work(8 * rows * feat * 3 * width + 16 * rows * width * 2 * CAP, rows),
             name="attend",
         )(me, *near(arrived, beside, *x_far[c], *begun), w_all, downs, up_all)
         y_got = [swap(attended, 2 * y) for y in range(1, half)]
@@ -499,7 +499,8 @@
         unpack_kernel,
         out_shape=jax.ShapeDtypeStruct((blocks, CAP, width), BF),
         in_specs=[SMEM, VM],
-        out_specs=VM,
+        out_specs=HBM,
+        scratch_shapes=[pltpu.SemaphoreType.DMA((blocks,))],
         compiler_params=params(4),
         name="unpack",
     )(owners, *near(back.reshape(n_req, CAP, width)))

time: 75.4 us -> 75.2 us (level)
  waiting for transfers between devices: 22.9 us -> 21.1 us
  starting transfers between devices: 17.1 us -> 18.2 us
    all_to_all x1, waiting for transfers between devices: 3.39 us -> 2.27 us  [body(): lax.all_to_all(packed, 'req', split_axis=0, concat_axis=0, tiled=True)]
    ppermute x23, starting transfers between devices: 11.3 us -> 12.4 us  [swap(): return lax.ppermute(value, 'tp', [(i, i ^ r) for i in range(n_tp)])]
  transfers between devices with their start and end apart: 24 -> 24, of which waited for: 14 -> 12; matrix products, arithmetic and copies ran while one was open for 0% -> 0% of each run, Pallas kernels for 23% -> 23%
where the time goes in v9:
time: 75.2 us; the launch traced here: 75 us
  waiting for transfers between devices  21.1 us (28%)
  Pallas kernels  20.9 us (28%)
  starting transfers between devices  18.2 us (24%)
  blocking collectives  14.3 us (19%)
    ppermute x23, waiting for transfers between devices, swap(): return lax.ppermute(value, 'tp', [(i, i ^ r) for i in range(n_tp)])  18.8 us
    all_to_all x1, blocking collectives, body(): lax.all_to_all(done.reshape(n_req * n_tp, share, width), ('req', 'tp'), s...  14.3 us
    ppermute x23, starting transfers between devices, swap(): return lax.ppermute(value, 'tp', [(i, i ^ r) for i in range(n_tp)])  12.4 us
    pallas_call x2, Pallas kernels, body(): pl.pallas_call(functools.partial(ffn_kernel, n_tp, c), out_shape=[pltpu.V...  8.94 us
    all_to_all x1, starting transfers between devices, body(): lax.all_to_all(packed, 'req', split_axis=0, concat_axis=0, tiled=True)  5.81 us
    pallas_call x2, Pallas kernels, body(): pl.pallas_call(functools.partial(attn_kernel, n_tp, c), out_shape=[pltpu....  5.52 us
    pallas_call x1, Pallas kernels, body(): pl.pallas_call(begin_kernel, out_shape=[pltpu.VMEM((3, count * rows, widt...  2.86 us
    all_to_all x1, waiting for transfers between devices, body(): lax.all_to_all(packed, 'req', split_axis=0, concat_axis=0, tiled=True)  2.27 us
  transfers between devices with their start and end apart: 24, of which 12 were waited for; matrix products, arithmetic and copies ran while one was open for 0% of the time, Pallas kernels for 23%

profile of v9, /device:TPU:0, one launch (start us, length us, event | category | flops | bytes accessed | tf_op | source)
XLA Modules:
  0.0 75.0 jit_solution(10427494499100398606)
XLA Ops:
  0.0 1.8 %pack.1 = (bf16[8,72,256]{2,1,0:T(8,128)(2,1)}, s32[8]{0:T(128)S(1)}) custom-call(s32[4,8]{1,0:T(4,128)} %bitcast.42, s32[4,8]{1,0:T(4,128)} %bitcast.43, s32[16]{0:T(128)} %slots_in.1, bf16[8,64,256]{2,1,0:T(8,128)(2,1)} %bitcast.40), custom_call_target="tpu_custom_call" | custom-call | tf_op jit(solution)/shard_map/pack/pallas_call | solution.py:343
  1.8 0.5 collective-permute-start.1
  2.4 2.6 %collective-permute-start = (bf16[256,1024]{1,0:T(8,128)(2,1)}, bf16[256,1024]{1,0:T(8,128)(2,1)S(1)}, u32[]{:S(2)}, u32[]{:S(2)}) collective-permute-start(bf16[256,1024]{1,0:T(8,128)(2,1)} %refs_4_.3), channel_id=1, source_target_pairs={{0,2},{1,3},{2,0},{3,1},{4,6},{5,7},{6,4},{7,5},{8,10},{9,11},{10,... | collective-permute-start | bytes 1572872 | tf_op jit(solution)/shard_map/ppermute | solution.py:338
  5.0 5.8 %all-to-all-start = ((bf16[8,72,256]{2,1,0:T(8,128)(2,1)}), bf16[8,72,256]{2,1,0:T(8,128)(2,1)S(1)}, u32[]{:S(2)}, u32[]{:S(2)}) async-start(bf16[8,72,256]{2,1,0:T(8,128)(2,1)} %get-tuple-element.61), calls=%async_computation | async-start | bytes 589824 | tf_op jit(solution)/shard_map/all_to_all | solution.py:371
  10.8 1.5 %collective-permute-start.3 = (bf16[32,256]{1,0:T(8,128)(2,1)}, bf16[32,256]{1,0:T(8,128)(2,1)S(1)}, u32[]{:S(2)}, u32[]{:S(2)}) collective-permute-start(bf16[32,256]{1,0:T(8,128)(2,1)} %bitcast.32), channel_id=1, source_target_pairs={{0,2},{1,3},{2,0},{3,1},{4,6},{5,7},{6,4},{7,5},{8,10},{9,11},{10,... | collective-permute-start | bytes 49160 | tf_op jit(solution)/shard_map/ppermute | solution.py:338
  12.3 0.3 collective-permute-start.2
  12.6 5.1 %collective-permute-done.4.refs_11_ = bf16[32,256]{1,0:T(8,128)(2,1)S(1)} collective-permute-done((bf16[32,256]{1,0:T(8,128)(2,1)}, bf16[32,256]{1,0:T(8,128)(2,1)S(1)}, u32[]{:S(2)}, u32[]{:S(2)}) %collective-permute-start.4) | collective-permute-done | bytes 16416 | tf_op jit(solution)/shard_map/ppermute | solution.py:338
  17.8 0.6 collective-permute-done.3.refs_10_
  18.4 2.3 %all-to-all-done.own.refs_0_ = bf16[8,72,256]{2,1,0:T(8,128)(2,1)S(1)} async-done(((bf16[8,72,256]{2,1,0:T(8,128)(2,1)}), bf16[8,72,256]{2,1,0:T(8,128)(2,1)S(1)}, u32[]{:S(2)}, u32[]{:S(2)}) %all-to-all-start) | async-done | bytes 294944 | tf_op jit(solution)/shard_map/all_to_all | solution.py:371
  20.7 0.6 collective-permute-start.6
  21.3 1.5 %collective-permute-start.8 = (bf16[4,72,256]{2,1,0:T(8,128)(2,1)S(1)}, bf16[4,72,256]{2,1,0:T(8,128)(2,1)S(1)}, u32[]{:S(2)}, u32[]{:S(2)}) collective-permute-start(bf16[4,72,256]{2,1,0:T(8,128)(2,1)S(1)} %get-tuple-element.111), channel_id=1, source_target_pairs={{0,2},{1,3},{2,0},{3,1},{4,6},{5,7},{6,4},{7,5},{8,10},{9,11},{10,... | collective-permute-start | bytes 442376 | tf_op jit(solution)/shard_map/ppermute | solution.py:338
  22.8 2.9 %begin.1 = (f32[3,512,256]{2,1,0:T(8,128)S(1)}, f32[512,96]{1,0:T(8,128)S(1)}, bf16[512,128]{1,0:T(8,128)(2,1)S(1)}, f32[512,128]{1,0:T(8,128)S(1)}, bf16[3,1024...) custom-call(s32[1]{0:T(128)} %bitcast.3.me, ...), custom_call_target="tpu_custom_call" | custom-call | flops 1006632960 | bytes 2097152 | tf_op jit(solution)/shard_map/begin/pallas_call | solution.py:385
  25.7 1.7 %collective-permute-done.6.refs_2_ = bf16[4,72,256]{2,1,0:T(8,128)(2,1)S(1)} collective-permute-done((bf16[4,72,256]{2,1,0:T(8,128)(2,1)S(1)}, bf16[4,72,256]{2,1,0:T(8,128)(2,1)S(1)}, u32[]{:S(2)}, u32[]{:S(2)}) %collective-permute-start.6) | collective-permute-done | bytes 147488 | tf_op jit(solution)/shard_map/ppermute | solution.py:338
  27.4 2.8 %collective-permute-done.8.refs_2_ = bf16[4,72,256]{2,1,0:T(8,128)(2,1)S(1)} collective-permute-done((bf16[4,72,256]{2,1,0:T(8,128)(2,1)S(1)}, bf16[4,72,256]{2,1,0:T(8,128)(2,1)S(1)}, u32[]{:S(2)}, u32[]{:S(2)}) %collective-permute-start.8) | collective-permute-done | bytes 147488 | tf_op jit(solution)/shard_map/ppermute | solution.py:338
  30.2 2.8 %attend.2 = (bf16[256,256]{1,0:T(8,128)(2,1)S(1)}, bf16[256,1024]{1,0:T(8,128)(2,1)S(1)}) custom-call(s32[1]{0:T(128)} %bitcast.3.me, bf16[8,72,256]{2,1,0:T(8,128)(2,1)S(1)} %all-to-all-done.own.refs_0_, bf16[8,72,256]{2,1,0:T(8,128)(2,1)S(1)} %collective-permute-done.5.beside.refs_1_, bf16[4,72,256]{2,1,0:T(8,128)(2,1)S(1)} %collective-permute-done.6.refs_2_, ...), custom_call_target="tpu_custom_call" | custom-call | flops 8724152320 | bytes 2097152 | tf_op jit(solution)/shard_map/attend/pallas_call | solution.py:432
  33.0 0.0 copy-start.2
  33.0 0.0 copy-start.3
  33.0 0.0 copy-start.4
  33.0 0.0 copy-start.5
  33.0 0.0 copy-start.6
  33.0 0.0 copy-start.9
  33.1 0.0 copy-start.10
  33.1 0.6 collective-permute-start.9
  33.6 0.2 collective-permute-start.14
  33.9 0.3 collective-permute-start.16
  34.2 2.8 %attend.3 = (bf16[256,256]{1,0:T(8,128)(2,1)S(1)}, bf16[256,1024]{1,0:T(8,128)(2,1)S(1)}) custom-call(s32[1]{0:T(128)} %bitcast.3.me, bf16[8,72,256]{2,1,0:T(8,128)(2,1)S(1)} %all-to-all-done.own.refs_0_, bf16[8,72,256]{2,1,0:T(8,128)(2,1)S(1)} %collective-permute-done.5.beside.refs_1_, bf16[4,72,256]{2,1,0:T(8,128)(2,1)S(1)} %collective-permute-done.8.refs_2_, ...), custom_call_target="tpu_custom_call" | custom-call | flops 8724152320 | bytes 2097152 | tf_op jit(solution)/shard_map/attend/pallas_call | solution.py:432
  36.9 2.1 %collective-permute-done.9.refs_2_ = bf16[256,256]{1,0:T(8,128)(2,1)S(1)} collective-permute-done((bf16[256,256]{1,0:T(8,128)(2,1)S(1)}, bf16[256,256]{1,0:T(8,128)(2,1)S(1)}, u32[]{:S(2)}, u32[]{:S(2)}) %collective-permute-start.9) | collective-permute-done | bytes 131104 | tf_op jit(solution)/shard_map/ppermute | solution.py:338
  39.1 0.5 collective-permute-start.12
  39.6 0.8 %collective-permute-done.15.refs_3_ = bf16[256,256]{1,0:T(8,128)(2,1)S(1)} collective-permute-done((bf16[256,256]{1,0:T(8,128)(2,1)S(1)}, bf16[256,256]{1,0:T(8,128)(2,1)S(1)}, u32[]{:S(2)}, u32[]{:S(2)}) %collective-permute-start.15) | collective-permute-done | bytes 131104 | tf_op jit(solution)/shard_map/ppermute | solution.py:338
  40.5 4.5 %feed.2 = (f32[2,64,1024]{2,1,0:T(8,128)S(1)}, bf16[64,1024]{1,0:T(8,128)(2,1)S(1)}, bf16[1,64,1024]{2,1,0:T(8,128)(2,1)S(1)}, bf16[64,1024]{1,0:T(8,128)(2,1)S(1)}) custom-call(s32[1]{0:T(128)} %bitcast.3.me, bf16[256,256]{1,0:T(8,128)(2,1)S(1)} %get-tuple-element.84.refs_0_, bf16[256,256]{1,0:T(8,128)(2,1)S(1)} %collective-permute-done.14.refs_1_, ...), custom_call_target="tpu_custom_call" | custom-call | flops 8053063680 | bytes 2097152 | tf_op jit(solution)/shard_map/feed/pallas_call | solution.py:465
  45.0 0.2 collective-permute-start.17
  45.2 0.4 collective-permute-start.11
  45.5 0.1 collective-permute-start.13
  45.7 0.4 collective-permute-start.19
  46.0 0.3 collective-permute-done.17
  46.4 0.2 collective-permute-done.11.refs_1_
  46.6 0.3 collective-permute-done.13.refs_3_
  46.9 0.7 collective-permute-start.20
  47.6 4.5 %feed.3 = (f32[2,64,1024]{2,1,0:T(8,128)S(1)}, bf16[64,1024]{1,0:T(8,128)(2,1)S(1)}, bf16[1,64,1024]{2,1,0:T(8,128)(2,1)S(1)}, bf16[64,1024]{1,0:T(8,128)(2,1)S(1)}) custom-call(s32[1]{0:T(128)} %bitcast.3.me, bf16[256,256]{1,0:T(8,128)(2,1)S(1)} %get-tuple-element.97.refs_0_, bf16[256,256]{1,0:T(8,128)(2,1)S(1)} %collective-permute-done.11.refs_1_, ...), custom_call_target="tpu_custom_call" | custom-call | flops 8053063680 | bytes 2097152 | tf_op jit(solution)/shard_map/feed/pallas_call | solution.py:465
  52.1 0.1 collective-permute-start.18
  52.2 0.5 collective-permute-start.21
  52.7 0.2 finish.2.refs_0_
  52.9 0.6 collective-permute-done.18
  53.5 1.4 %collective-permute-start.22 = (bf16[64,1024]{1,0:T(8,128)(2,1)S(1)}, bf16[64,1024]{1,0:T(8,128)(2,1)S(1)}, u32[]{:S(2)}, u32[]{:S(2)}) collective-permute-start(bf16[64,1024]{1,0:T(8,128)(2,1)S(1)} %fusion.1), channel_id=1, source_target_pairs={{0,2},{1,3},{2,0},{3,1},{4,6},{5,7},{6,4},{7,5},{8,10},{9,11},{10,... | collective-permute-start | bytes 393224 | tf_op jit(solution)/shard_map/ppermute | solution.py:338
  54.9 4.2 %collective-permute-done.22.refs_4_ = bf16[64,1024]{1,0:T(8,128)(2,1)S(1)} collective-permute-done((bf16[64,1024]{1,0:T(8,128)(2,1)S(1)}, bf16[64,1024]{1,0:T(8,128)(2,1)S(1)}, u32[]{:S(2)}, u32[]{:S(2)}) %collective-permute-start.22) | collective-permute-done | bytes 131104 | tf_op jit(solution)/shard_map/ppermute | solution.py:338
  59.1 0.2 finish.3
  59.4 14.3 %all_to_all.10 = bf16[32,16,256]{2,1,0:T(8,128)(2,1)S(1)} all-to-all(bf16[32,16,256]{2,1,0:T(8,128)(2,1)S(1)} %bitcast.21), channel_id=1, replica_groups=mesh['req'=8,'tp'=4] {'req','tp'}, dimensions={0} | all-to-all | bytes 524288 | tf_op jit(solution)/shard_map/all_to_all | solution.py:491
  73.7 1.3 %unpack.1 = bf16[8,64,256]{2,1,0:T(8,128)(2,1)} custom-call(s32[8]{0:T(128)S(1)} %get-tuple-element.58.owners, bf16[8,64,256]{2,1,0:T(8,128)(2,1)S(1)} %bitcast.22), custom_call_target="tpu_custom_call" | custom-call | tf_op jit(solution)/shard_map/unpack/pallas_call | solution.py:498
  (35 shorter events, 0.2 us)
Async XLA Ops:
  1.8 18.8 %collective-permute-start.1 = (bf16[256,1024]{1,0:T(8,128)(2,1)}, bf16[256,1024]{1,0:T(8,128)(2,1)S(1)}, u32[]{:S(2)}, u32[]{:S(2)}) collective-permute-start(bf16[256,1024]{1,0:T(8,128)(2,1)} %refs_4_.3), channel_id=1, source_target_pairs={{0,1},{1,0},{2,3},{3,2},{4,5},{5,4},{6,7},{7,6},{8,9},{9,8},{10,11... | collective-permute-start | bytes 1572872 | tf_op jit(solution)/shard_map/ppermute | solution.py:338
  2.4 18.3 %collective-permute-start = (bf16[256,1024]{1,0:T(8,128)(2,1)}, bf16[256,1024]{1,0:T(8,128)(2,1)S(1)}, u32[]{:S(2)}, u32[]{:S(2)}) collective-permute-start(bf16[256,1024]{1,0:T(8,128)(2,1)} %refs_4_.3), channel_id=1, source_target_pairs={{0,2},{1,3},{2,0},{3,1},{4,6},{5,7},{6,4},{7,5},{8,10},{9,11},{10,... | collective-permute-start | bytes 1572872 | tf_op jit(solution)/shard_map/ppermute | solution.py:338
  5.0 15.7 %all-to-all-start = ((bf16[8,72,256]{2,1,0:T(8,128)(2,1)}), bf16[8,72,256]{2,1,0:T(8,128)(2,1)S(1)}, u32[]{:S(2)}, u32[]{:S(2)}) async-start(bf16[8,72,256]{2,1,0:T(8,128)(2,1)} %get-tuple-element.61), calls=%async_computation | async-start | bytes 589824 | tf_op jit(solution)/shard_map/all_to_all | solution.py:371
  10.8 7.0 %collective-permute-start.4 = (bf16[32,256]{1,0:T(8,128)(2,1)}, bf16[32,256]{1,0:T(8,128)(2,1)S(1)}, u32[]{:S(2)}, u32[]{:S(2)}) collective-permute-start(bf16[32,256]{1,0:T(8,128)(2,1)} %bitcast.31), channel_id=1, source_target_pairs={{0,3},{1,2},{2,1},{3,0},{4,7},{5,6},{6,5},{7,4},{8,11},{9,10},{10,... | collective-permute-start | bytes 49160 | tf_op jit(solution)/shard_map/ppermute | solution.py:338
  10.8 7.6 %collective-permute-start.3 = (bf16[32,256]{1,0:T(8,128)(2,1)}, bf16[32,256]{1,0:T(8,128)(2,1)S(1)}, u32[]{:S(2)}, u32[]{:S(2)}) collective-permute-start(bf16[32,256]{1,0:T(8,128)(2,1)} %bitcast.32), channel_id=1, source_target_pairs={{0,2},{1,3},{2,0},{3,1},{4,6},{5,7},{6,4},{7,5},{8,10},{9,11},{10,... | collective-permute-start | bytes 49160 | tf_op jit(solution)/shard_map/ppermute | solution.py:338
  12.3 6.1 %collective-permute-start.2 = (bf16[32,256]{1,0:T(8,128)(2,1)}, bf16[32,256]{1,0:T(8,128)(2,1)S(1)}, u32[]{:S(2)}, u32[]{:S(2)}) collective-permute-start(bf16[32,256]{1,0:T(8,128)(2,1)} %bitcast.33), channel_id=1, source_target_pairs={{0,1},{1,0},{2,3},{3,2},{4,5},{5,4},{6,7},{7,6},{8,9},{9,8},{10,11... | collective-permute-start | bytes 49160 | tf_op jit(solution)/shard_map/ppermute | solution.py:338
  20.7 2.1 %collective-permute-start.5 = (bf16[8,72,256]{2,1,0:T(8,128)(2,1)S(1)}, bf16[8,72,256]{2,1,0:T(8,128)(2,1)S(1)}, u32[]{:S(2)}, u32[]{:S(2)}) collective-permute-start(bf16[8,72,256]{2,1,0:T(8,128)(2,1)S(1)} %all-to-all-done.own.refs_0_), channel_id=1, source_target_pairs={{0,1},{1,0},{2,3},{3,2},{4,5},{5,4},{6,7},{7,6},{8,9},{9,8},{10,11... | collective-permute-start | bytes 884744 | tf_op jit(solution)/shard_map/ppermute | solution.py:338
  20.7 6.7 %collective-permute-start.6 = (bf16[4,72,256]{2,1,0:T(8,128)(2,1)S(1)}, bf16[4,72,256]{2,1,0:T(8,128)(2,1)S(1)}, u32[]{:S(2)}, u32[]{:S(2)}) collective-permute-start(bf16[4,72,256]{2,1,0:T(8,128)(2,1)S(1)} %get-tuple-element.112), channel_id=1, source_target_pairs={{0,2},{1,3},{2,0},{3,1},{4,6},{5,7},{6,4},{7,5},{8,10},{9,11},{10,... | collective-permute-start | bytes 442376 | tf_op jit(solution)/shard_map/ppermute | solution.py:338
  21.3 8.9 %collective-permute-start.8 = (bf16[4,72,256]{2,1,0:T(8,128)(2,1)S(1)}, bf16[4,72,256]{2,1,0:T(8,128)(2,1)S(1)}, u32[]{:S(2)}, u32[]{:S(2)}) collective-permute-start(bf16[4,72,256]{2,1,0:T(8,128)(2,1)S(1)} %get-tuple-element.111), channel_id=1, source_target_pairs={{0,2},{1,3},{2,0},{3,1},{4,6},{5,7},{6,4},{7,5},{8,10},{9,11},{10,... | collective-permute-start | bytes 442376 | tf_op jit(solution)/shard_map/ppermute | solution.py:338
  27.4 2.8 %collective-permute-start.7 = (bf16[4,72,256]{2,1,0:T(8,128)(2,1)S(1)}, bf16[4,72,256]{2,1,0:T(8,128)(2,1)S(1)}, u32[]{:S(2)}, u32[]{:S(2)}) collective-permute-start(bf16[4,72,256]{2,1,0:T(8,128)(2,1)S(1)} %collective-permute-done.6.refs_2_), channel_id=1, source_target_pairs={{0,1},{1,0},{2,3},{3,2},{4,5},{5,4},{6,7},{7,6},{8,9},{9,8},{10,11... | collective-permute-start | bytes 442376 | tf_op jit(solution)/shard_map/ppermute | solution.py:338
  30.2 4.0 %collective-permute-start.10 = (bf16[4,72,256]{2,1,0:T(8,128)(2,1)S(1)}, bf16[4,72,256]{2,1,0:T(8,128)(2,1)S(1)}, u32[]{:S(2)}, u32[]{:S(2)}) collective-permute-start(bf16[4,72,256]{2,1,0:T(8,128)(2,1)S(1)} %collective-permute-done.8.refs_2_), channel_id=1, source_target_pairs={{0,1},{1,0},{2,3},{3,2},{4,5},{5,4},{6,7},{7,6},{8,9},{9,8},{10,11... | collective-permute-start | bytes 442376 | tf_op jit(solution)/shard_map/ppermute | solution.py:338
  33.0 7.4 %copy-start.2 = (bf16[256,1024]{1,0:T(8,128)(2,1)S(1)}, bf16[256,1024]{1,0:T(8,128)(2,1)}, u32[]{:S(2)}) copy-start(bf16[256,1024]{1,0:T(8,128)(2,1)} %refs_4_.3) | copy-start | bytes 1572868
  33.0 7.4 %copy-start.3 = (bf16[32,1024]{1,0:T(8,128)(2,1)S(1)}, bf16[32,1024]{1,0:T(8,128)(2,1)}, u32[]{:S(2)}) copy-start(bf16[32,1024]{1,0:T(8,128)(2,1)} %refs_14_.3) | copy-start | bytes 196612
  33.0 7.4 %copy-start.4 = (bf16[1024,32]{0,1:T(8,128)(2,1)S(1)}, bf16[1024,32]{0,1:T(8,128)(2,1)}, u32[]{:S(2)}) copy-start(bf16[1024,32]{0,1:T(8,128)(2,1)} %param.32) | copy-start | bytes 196612
  33.0 7.4 %copy-start.5 = (bf16[32,1024]{1,0:T(8,128)(2,1)S(1)}, bf16[32,1024]{1,0:T(8,128)(2,1)}, u32[]{:S(2)}) copy-start(bf16[32,1024]{1,0:T(8,128)(2,1)} %refs_16_.3) | copy-start | bytes 196612
  33.0 7.4 %copy-start.6 = (bf16[1024,32]{0,1:T(8,128)(2,1)S(1)}, bf16[1024,32]{0,1:T(8,128)(2,1)}, u32[]{:S(2)}) copy-start(bf16[1024,32]{0,1:T(8,128)(2,1)} %param.34) | copy-start | bytes 196612
  33.0 7.4 %copy-start.7 = (bf16[32,1024]{1,0:T(8,128)(2,1)S(1)}, bf16[32,1024]{1,0:T(8,128)(2,1)}, u32[]{:S(2)}) copy-start(bf16[32,1024]{1,0:T(8,128)(2,1)} %refs_18_.3) | copy-start | bytes 196612
  33.0 7.4 %copy-start.8 = (bf16[256,32]{0,1:T(8,128)(2,1)S(1)}, bf16[256,32]{0,1:T(8,128)(2,1)}, u32[]{:S(2)}) copy-start(bf16[256,32]{0,1:T(8,128)(2,1)} %param.30) | copy-start | bytes 49156
  33.0 7.4 %copy-start.9 = (f32[1024]{0:T(1024)S(1)}, f32[1024]{0:T(1024)}, u32[]{:S(2)}) copy-start(f32[1024]{0:T(1024)} %param.36) | copy-start | bytes 12292
  33.1 7.4 %copy-start.10 = (f32[1024]{0:T(1024)S(1)}, f32[1024]{0:T(1024)}, u32[]{:S(2)}) copy-start(f32[1024]{0:T(1024)} %param.37) | copy-start | bytes 12292
  33.1 6.0 %collective-permute-start.9 = (bf16[256,256]{1,0:T(8,128)(2,1)S(1)}, bf16[256,256]{1,0:T(8,128)(2,1)S(1)}, u32[]{:S(2)}, u32[]{:S(2)}) collective-permute-start(bf16[256,256]{1,0:T(8,128)(2,1)S(1)} %get-tuple-element.84.refs_0_), channel_id=1, source_target_pairs={{0,2},{1,3},{2,0},{3,1},{4,6},{5,7},{6,4},{7,5},{8,10},{9,11},{10,... | collective-permute-start | bytes 393224 | tf_op jit(solution)/shard_map/ppermute | solution.py:338
  33.6 5.9 %collective-permute-start.14 = (bf16[256,256]{1,0:T(8,128)(2,1)S(1)}, bf16[256,256]{1,0:T(8,128)(2,1)S(1)}, u32[]{:S(2)}, u32[]{:S(2)}) collective-permute-start(bf16[256,256]{1,0:T(8,128)(2,1)S(1)} %get-tuple-element.84.refs_0_), channel_id=1, source_target_pairs={{0,1},{1,0},{2,3},{3,2},{4,5},{5,4},{6,7},{7,6},{8,9},{9,8},{10,11... | collective-permute-start | bytes 393224 | tf_op jit(solution)/shard_map/ppermute | solution.py:338
  33.9 6.5 %collective-permute-start.16 = (bf16[256,1024]{1,0:T(8,128)(2,1)S(1)}, bf16[256,1024]{1,0:T(8,128)(2,1)S(1)}, u32[]{:S(2)}, u32[]{:S(2)}) collective-permute-start(bf16[256,1024]{1,0:T(8,128)(2,1)S(1)} %collective-permute-done.refs_6_), channel_id=1, source_target_pairs={{0,1},{1,0},{2,3},{3,2},{4,5},{5,4},{6,7},{7,6},{8,9},{9,8},{10,11... | collective-permute-start | bytes 1572872 | tf_op jit(solution)/shard_map/ppermute | solution.py:338
  39.0 1.3 %collective-permute-start.15 = (bf16[256,256]{1,0:T(8,128)(2,1)S(1)}, bf16[256,256]{1,0:T(8,128)(2,1)S(1)}, u32[]{:S(2)}, u32[]{:S(2)}) collective-permute-start(bf16[256,256]{1,0:T(8,128)(2,1)S(1)} %collective-permute-done.9.refs_2_), channel_id=1, source_target_pairs={{0,1},{1,0},{2,3},{3,2},{4,5},{5,4},{6,7},{7,6},{8,9},{9,8},{10,11... | collective-permute-start | bytes 393224 | tf_op jit(solution)/shard_map/ppermute | solution.py:338
  39.1 6.5 %collective-permute-start.12 = (bf16[256,256]{1,0:T(8,128)(2,1)S(1)}, bf16[256,256]{1,0:T(8,128)(2,1)S(1)}, u32[]{:S(2)}, u32[]{:S(2)}) collective-permute-start(bf16[256,256]{1,0:T(8,128)(2,1)S(1)} %get-tuple-element.97.refs_0_), channel_id=1, source_target_pairs={{0,2},{1,3},{2,0},{3,1},{4,6},{5,7},{6,4},{7,5},{8,10},{9,11},{10,... | collective-permute-start | bytes 393224 | tf_op jit(solution)/shard_map/ppermute | solution.py:338
  45.0 1.4 %collective-permute-start.17 = (bf16[1,64,1024]{2,1,0:T(8,128)(2,1)S(1)}, bf16[1,64,1024]{2,1,0:T(8,128)(2,1)S(1)}, u32[]{:S(2)}, u32[]{:S(2)}) collective-permute-start(bf16[1,64,1024]{2,1,0:T(8,128)(2,1)S(1)} %get-tuple-element.96), channel_id=1, source_target_pairs={{0,1},{1,0},{2,3},{3,2},{4,5},{5,4},{6,7},{7,6},{8,9},{9,8},{10,11... | collective-permute-start | bytes 393224 | tf_op jit(solution)/shard_map/ppermute | solution.py:338
  45.2 1.4 %collective-permute-start.11 = (bf16[256,256]{1,0:T(8,128)(2,1)S(1)}, bf16[256,256]{1,0:T(8,128)(2,1)S(1)}, u32[]{:S(2)}, u32[]{:S(2)}) collective-permute-start(bf16[256,256]{1,0:T(8,128)(2,1)S(1)} %get-tuple-element.97.refs_0_), channel_id=1, source_target_pairs={{0,1},{1,0},{2,3},{3,2},{4,5},{5,4},{6,7},{7,6},{8,9},{9,8},{10,11... | collective-permute-start | bytes 393224 | tf_op jit(solution)/shard_map/ppermute | solution.py:338
  45.5 1.3 %collective-permute-start.13 = (bf16[256,256]{1,0:T(8,128)(2,1)S(1)}, bf16[256,256]{1,0:T(8,128)(2,1)S(1)}, u32[]{:S(2)}, u32[]{:S(2)}) collective-permute-start(bf16[256,256]{1,0:T(8,128)(2,1)S(1)} %collective-permute-done.12.refs_2_), channel_id=1, source_target_pairs={{0,1},{1,0},{2,3},{3,2},{4,5},{5,4},{6,7},{7,6},{8,9},{9,8},{10,11... | collective-permute-start | bytes 393224 | tf_op jit(solution)/shard_map/ppermute | solution.py:338
  45.7 7.0 %collective-permute-start.19 = (bf16[64,1024]{1,0:T(8,128)(2,1)S(1)}, bf16[64,1024]{1,0:T(8,128)(2,1)S(1)}, u32[]{:S(2)}, u32[]{:S(2)}) collective-permute-start(bf16[64,1024]{1,0:T(8,128)(2,1)S(1)} %get-tuple-element.103), channel_id=1, source_target_pairs={{0,1},{1,0},{2,3},{3,2},{4,5},{5,4},{6,7},{7,6},{8,9},{9,8},{10,11... | collective-permute-start | bytes 393224 | tf_op jit(solution)/shard_map/ppermute | solution.py:338
  46.9 5.8 %collective-permute-start.20 = (bf16[64,1024]{1,0:T(8,128)(2,1)S(1)}, bf16[64,1024]{1,0:T(8,128)(2,1)S(1)}, u32[]{:S(2)}, u32[]{:S(2)}) collective-permute-start(bf16[64,1024]{1,0:T(8,128)(2,1)S(1)} %fusion), channel_id=1, source_target_pairs={{0,2},{1,3},{2,0},{3,1},{4,6},{5,7},{6,4},{7,5},{8,10},{9,11},{10,... | collective-permute-start | bytes 393224 | tf_op jit(solution)/shard_map/ppermute | solution.py:338
  47.6 5.1 %copy-start = (f32[1024]{0:T(1024)S(1)}, f32[1024]{0:T(1024)}, u32[]{:S(2)}) copy-start(f32[1024]{0:T(1024)} %param.38) | copy-start | bytes 12292
  47.6 5.1 %copy-start.1 = (f32[1024]{0:T(1024)S(1)}, f32[1024]{0:T(1024)}, u32[]{:S(2)}) copy-start(f32[1024]{0:T(1024)} %param.39) | copy-start | bytes 12292
  52.1 1.4 %collective-permute-start.18 = (bf16[1,64,1024]{2,1,0:T(8,128)(2,1)S(1)}, bf16[1,64,1024]{2,1,0:T(8,128)(2,1)S(1)}, u32[]{:S(2)}, u32[]{:S(2)}) collective-permute-start(bf16[1,64,1024]{2,1,0:T(8,128)(2,1)S(1)} %get-tuple-element.102), channel_id=1, source_target_pairs={{0,1},{1,0},{2,3},{3,2},{4,5},{5,4},{6,7},{7,6},{8,9},{9,8},{10,11... | collective-permute-start | bytes 393224 | tf_op jit(solution)/shard_map/ppermute | solution.py:338
  52.2 2.8 %collective-permute-start.21 = (bf16[64,1024]{1,0:T(8,128)(2,1)S(1)}, bf16[64,1024]{1,0:T(8,128)(2,1)S(1)}, u32[]{:S(2)}, u32[]{:S(2)}) collective-permute-start(bf16[64,1024]{1,0:T(8,128)(2,1)S(1)} %get-tuple-element.108), channel_id=1, source_target_pairs={{0,1},{1,0},{2,3},{3,2},{4,5},{5,4},{6,7},{7,6},{8,9},{9,8},{10,11... | collective-permute-start | bytes 393224 | tf_op jit(solution)/shard_map/ppermute | solution.py:338
  53.5 5.6 %collective-permute-start.22 = (bf16[64,1024]{1,0:T(8,128)(2,1)S(1)}, bf16[64,1024]{1,0:T(8,128)(2,1)S(1)}, u32[]{:S(2)}, u32[]{:S(2)}) collective-permute-start(bf16[64,1024]{1,0:T(8,128)(2,1)S(1)} %fusion.1), channel_id=1, source_target_pairs={{0,2},{1,3},{2,0},{3,1},{4,6},{5,7},{6,4},{7,5},{8,10},{9,11},{10,... | collective-permute-start | bytes 393224 | tf_op jit(solution)/shard_map/ppermute | solution.py:338

commit v10 on v8

--- a/solution.py
+++ b/solution.py
@@ -204,9 +204,13 @@
 
 
 def ffn_kernel(n_tp, chunk, me, *refs):
-    atts, wouts, odowns = refs[:n_tp], refs[n_tp : 2 * n_tp], refs[2 * n_tp : 3 * n_tp]
-    x, sel_in, oup, d1, u1, d2, u2, g1, b1, w1, w2 = refs[3 * n_tp : 3 * n_tp + 11]
-    even, odd, odds, h_own, h_scr = refs[3 * n_tp + 11 :]
+    n_w = 2 * n_tp - 2
+    atts, pieces, odowns = refs[:n_tp], refs[n_tp : n_tp + n_w], refs[n_tp + n_w : 2 * n_tp + n_w]
+    x, sel_in, oup, d1, u1, d2, u2, g1, b1, w1, w2 = refs[2 * n_tp + n_w : 2 * n_tp + n_w + 11]
+    even, odd, odds, h_own, h_scr = refs[2 * n_tp + n_w + 11 :]
+    wouts = [pieces[0][...], pieces[1][...]]
+    for r in range(2, n_w, 2):
+        wouts.append(jnp.concatenate([pieces[r][...], pieces[r + 1][...]], axis=0))
     rows, feat = x.shape
     blocks = rows // CAP
     share = CAP // n_tp
@@ -225,7 +229,7 @@
         low = split_two(low, sel)
         total = x[rs].astype(F32)
         for r in range(n_tp):
-            total = total + dot(atts[r][rs], wouts[r][...])
+            total = total + dot(atts[r][rs], wouts[r])
         total = total + dot(low, ups[0])
         h1 = layer_norm(total, g1[...], b1[...]).astype(BF)
         h_scr[span(t * nb, nb)] = h1.reshape(nb, n_tp, share, feat)
@@ -368,10 +372,12 @@
         (packed, me, w_out, out_down.T)
     )
     arrived = lax.all_to_all(packed, "req", split_axis=0, concat_axis=0, tiled=True)
-    w_far = [swap(w_first, 2 * y) for y in range(1, half)]
-    w_near = swap(w_first, 1)
+    w_half = w_out.shape[0] // 2
+    w_far = [
+        [swap(w_first[:w_half], 2 * y), swap(w_first[w_half:], 2 * y)] for y in range(1, half)
+    ]
     odowns = [out_down.T] + [swap(o_first, r) for r in range(1, n_tp)]
-    arrived, w_far, w_near, odowns = lax.optimization_barrier((arrived, w_far, w_near, odowns))
+    arrived, w_far, odowns = lax.optimization_barrier((arrived, w_far, odowns))
     count = 2
     step_blocks = n_req // count
     rows = step_blocks * CAP
@@ -417,6 +423,8 @@
     w_all, w1, w2, downs, up_all = near(w_all, w1, w2, downs, up_all)
     x_far[0], begun = lax.optimization_barrier((x_far[0], begun))
     x_far[0] = second_hop(x_far[0])
+    x_far = lax.optimization_barrier(x_far)
+    x_far[1:] = [second_hop(pieces) for pieces in x_far[1:]]
 
     consts = near(
         out_up, fc1_down.T, fc1_up, fc2_down.T, fc2_up, norm1_gain[None], norm1_bias[None]
@@ -425,24 +433,26 @@
     steps = []
     for c in range(count):
         if c:
-            x_far[c], w_far, steps[0][0] = lax.optimization_barrier(
-                (x_far[c], w_far, steps[0][0])
+            w_far, w_first, steps[0][0] = lax.optimization_barrier(
+                (w_far, w_first, steps[0][0])
             )
-            x_far[c] = second_hop(x_far[c])
         attended, x_full = pl.pallas_call(
             functools.partial(attn_kernel, n_tp, c),
             out_shape=[pltpu.VMEM((rows, width), BF), pltpu.VMEM((rows, feat), BF)],
             in_specs=[SMEM] + [VM] * (n_tp + 7),
             out_specs=[VM] * 2,
             compiler_params=params(12),
-            cost_estimate=work(2 * rows * feat * 3 * width + 4 * rows * width * 2 * CAP, rows),
+            cost_estimate=work(8 * rows * feat * 3 * width + 16 * rows * width * 2 * CAP, rows),
             name="attend",
         )(me, *near(arrived, beside, *x_far[c], *begun), w_all, downs, up_all)
         y_got = [swap(attended, 2 * y) for y in range(1, half)]
         if c:
             steps[0][1], attended = lax.optimization_barrier((steps[0][1], attended))
         steps.append([attended, y_got, x_full])
-    wouts = [w_out, w_near] + second_hop(w_far)
+    w_near = swap(w_first, 1)
+    wouts = [w_out, w_near]
+    for first_half, second_half in w_far:
+        wouts += [first_half, second_half, swap(first_half, 1), swap(second_half, 1)]
 
     def finish(earlier, *values):
         blocks_done = step_blocks + sum(e.shape[0] for e in earlier)
@@ -470,7 +480,7 @@
                 pltpu.VMEM((half - 1, own, feat), BF),
                 pltpu.VMEM((own, feat), BF),
             ],
-            in_specs=[SMEM] + [VM] * (3 * n_tp + 4 + len(consts)),
+            in_specs=[SMEM] + [VM] * (2 * n_tp + len(wouts) + 4 + len(consts)),
             out_specs=[VM] * 4,
             scratch_shapes=[pltpu.VMEM((step_blocks, n_tp, share, feat), BF)],
             compiler_params=params(16),

time: 75.4 us -> 80.8 us (1.072)
  starting transfers between devices: 17.1 us -> 21.3 us
  blocking collectives: 13.9 us -> 15.4 us
  waiting for transfers between devices: 22.9 us -> 21.5 us
  local copies, waits for them, and re-layouts: 0.08 us -> 1.15 us
    all_to_all x1, waiting for transfers between devices: 3.39 us -> 0.01 us  [body(): lax.all_to_all(packed, 'req', split_axis=0, concat_axis=0, tiled=True)]
    ppermute x23 -> x25, starting transfers between devices: 11.3 us -> 14 us  [swap(): return lax.ppermute(value, 'tp', [(i, i ^ r) for i in range(n_tp)])]
    ppermute x23 -> x25, waiting for transfers between devices: 19.5 us -> 21.5 us  [swap(): return lax.ppermute(value, 'tp', [(i, i ^ r) for i in range(n_tp)])]
    all_to_all x1, blocking collectives: 13.9 us -> 15.4 us  [body(): lax.all_to_all(done.reshape(n_req * n_tp, share, width), ('req', 'tp'), s...]
    all_to_all x1, starting transfers between devices: 5.81 us -> 7.26 us  [body(): lax.all_to_all(packed, 'req', split_axis=0, concat_axis=0, tiled=True)]
    slice x0 -> x1, local copies, waits for them, and re-layouts: none -> 1.06 us  [body(): w_first[w_half:]]
  transfers between devices with their start and end apart: 24 -> 26, of which waited for: 14 -> 10; matrix products, arithmetic and copies ran while one was open for 0% -> 1% of each run, Pallas kernels for 23% -> 22%
where the time goes in v10:
time: 80.8 us; the launch traced here: 80.6 us
  waiting for transfers between devices  21.5 us (27%)
  starting transfers between devices  21.3 us (26%)
  Pallas kernels  20.9 us (26%)
  blocking collectives  15.4 us (19%)
  local copies, waits for them, and re-layouts  1.15 us (1%)
    ppermute x25, waiting for transfers between devices, swap(): return lax.ppermute(value, 'tp', [(i, i ^ r) for i in range(n_tp)])  21.5 us
    all_to_all x1, blocking collectives, body(): lax.all_to_all(done.reshape(n_req * n_tp, share, width), ('req', 'tp'), s...  15.4 us
    ppermute x25, starting transfers between devices, swap(): return lax.ppermute(value, 'tp', [(i, i ^ r) for i in range(n_tp)])  14 us
    pallas_call x2, Pallas kernels, body(): pl.pallas_call(functools.partial(ffn_kernel, n_tp, c), out_shape=[pltpu.V...  8.94 us
    all_to_all x1, starting transfers between devices, body(): lax.all_to_all(packed, 'req', split_axis=0, concat_axis=0, tiled=True)  7.26 us
    pallas_call x2, Pallas kernels, body(): pl.pallas_call(functools.partial(attn_kernel, n_tp, c), out_shape=[pltpu....  5.53 us
    pallas_call x1, Pallas kernels, body(): pl.pallas_call(begin_kernel, out_shape=[pltpu.VMEM((3, count * rows, widt...  2.86 us
    pallas_call x1, Pallas kernels, body(): pl.pallas_call(pack_kernel, out_shape=(pltpu.VMEM((n_req, CAP + PAD, widt...  1.85 us
  transfers between devices with their start and end apart: 26, of which 10 were waited for; matrix products, arithmetic and copies ran while one was open for 1% of the time, Pallas kernels for 22%

profile of v10, /device:TPU:0, one launch (start us, length us, event | category | flops | bytes accessed | tf_op | source)
XLA Modules:
  0.0 80.6 jit_solution(16356917010439338789)
XLA Ops:
  0.0 1.9 %pack.1 = (bf16[8,72,256]{2,1,0:T(8,128)(2,1)}, s32[8]{0:T(128)S(1)}) custom-call(s32[4,8]{1,0:T(4,128)} %bitcast.42, s32[4,8]{1,0:T(4,128)} %bitcast.43, s32[16]{0:T(128)} %slots_in.1, bf16[8,64,256]{2,1,0:T(8,128)(2,1)} %bitcast.40), custom_call_target="tpu_custom_call" | custom-call | tf_op jit(solution)/shard_map/pack/pallas_call | solution.py:346
  1.9 7.3 %all-to-all-start = ((bf16[8,72,256]{2,1,0:T(8,128)(2,1)}), bf16[8,72,256]{2,1,0:T(8,128)(2,1)S(1)}, u32[]{:S(2)}, u32[]{:S(2)}) async-start(bf16[8,72,256]{2,1,0:T(8,128)(2,1)} %get-tuple-element.63), calls=%async_computation | async-start | bytes 589824 | tf_op jit(solution)/shard_map/all_to_all | solution.py:374
  9.1 1.1 %fusion.2 = (bf16[128,1024]{1,0:T(8,128)(2,1)S(1)}, bf16[128,1024]{1,0:T(8,128)(2,1)S(1)}) fusion(bf16[256,1024]{1,0:T(8,128)(2,1)} %refs_4_.3), kind=kLoop, calls=%fused_computation.4 | loop fusion | bytes 1048576 | tf_op jit(solution)/shard_map/slice | solution.py:377
  10.2 1.6 %collective-permute-start.1 = (bf16[128,1024]{1,0:T(8,128)(2,1)S(1)}, bf16[128,1024]{1,0:T(8,128)(2,1)S(1)}, u32[]{:S(2)}, u32[]{:S(2)}) collective-permute-start(bf16[128,1024]{1,0:T(8,128)(2,1)S(1)} %get-tuple-element.115), channel_id=1, source_target_pairs={{0,2},{1,3},{2,0},{3,1},{4,6},{5,7},{6,4},{7,5},{8,10},{9,11},{10,... | collective-permute-start | bytes 786440 | tf_op jit(solution)/shard_map/ppermute | solution.py:341
  11.8 0.5 collective-permute-start
  12.3 0.1 collective-permute-start.4
  12.4 1.4 %collective-permute-start.3 = (bf16[32,256]{1,0:T(8,128)(2,1)}, bf16[32,256]{1,0:T(8,128)(2,1)S(1)}, u32[]{:S(2)}, u32[]{:S(2)}) collective-permute-start(bf16[32,256]{1,0:T(8,128)(2,1)} %bitcast.32), channel_id=1, source_target_pairs={{0,2},{1,3},{2,0},{3,1},{4,6},{5,7},{6,4},{7,5},{8,10},{9,11},{10,... | collective-permute-start | bytes 49160 | tf_op jit(solution)/shard_map/ppermute | solution.py:341
  13.8 0.3 collective-permute-start.2
  14.1 9.1 %collective-permute-done.4.refs_13_ = bf16[32,256]{1,0:T(8,128)(2,1)S(1)} collective-permute-done((bf16[32,256]{1,0:T(8,128)(2,1)}, bf16[32,256]{1,0:T(8,128)(2,1)S(1)}, u32[]{:S(2)}, u32[]{:S(2)}) %collective-permute-start.4) | collective-permute-done | bytes 16416 | tf_op jit(solution)/shard_map/ppermute | solution.py:341
  23.2 1.1 %collective-permute-done.3.refs_12_ = bf16[32,256]{1,0:T(8,128)(2,1)S(1)} collective-permute-done((bf16[32,256]{1,0:T(8,128)(2,1)}, bf16[32,256]{1,0:T(8,128)(2,1)S(1)}, u32[]{:S(2)}, u32[]{:S(2)}) %collective-permute-start.3) | collective-permute-done | bytes 16416 | tf_op jit(solution)/shard_map/ppermute | solution.py:341
  24.4 0.1 collective-permute-start.5
  24.5 1.6 %collective-permute-start.6 = (bf16[4,72,256]{2,1,0:T(8,128)(2,1)S(1)}, bf16[4,72,256]{2,1,0:T(8,128)(2,1)S(1)}, u32[]{:S(2)}, u32[]{:S(2)}) collective-permute-start(bf16[4,72,256]{2,1,0:T(8,128)(2,1)S(1)} %get-tuple-element.118), channel_id=1, source_target_pairs={{0,2},{1,3},{2,0},{3,1},{4,6},{5,7},{6,4},{7,5},{8,10},{9,11},{10,... | collective-permute-start | bytes 442376 | tf_op jit(solution)/shard_map/ppermute | solution.py:341
  26.1 0.5 collective-permute-start.8
  26.6 2.9 %begin.1 = (f32[3,512,256]{2,1,0:T(8,128)S(1)}, f32[512,96]{1,0:T(8,128)S(1)}, bf16[512,128]{1,0:T(8,128)(2,1)S(1)}, f32[512,128]{1,0:T(8,128)S(1)}, bf16[3,1024...) custom-call(s32[1]{0:T(128)} %bitcast.3.me, ...), custom_call_target="tpu_custom_call" | custom-call | flops 1006632960 | bytes 2097152 | tf_op jit(solution)/shard_map/begin/pallas_call | solution.py:390
  29.4 1.7 %collective-permute-done.6.refs_2_ = bf16[4,72,256]{2,1,0:T(8,128)(2,1)S(1)} collective-permute-done((bf16[4,72,256]{2,1,0:T(8,128)(2,1)S(1)}, bf16[4,72,256]{2,1,0:T(8,128)(2,1)S(1)}, u32[]{:S(2)}, u32[]{:S(2)}) %collective-permute-start.6) | collective-permute-done | bytes 147488 | tf_op jit(solution)/shard_map/ppermute | solution.py:341
  31.2 2.8 %collective-permute-done.8.refs_2_ = bf16[4,72,256]{2,1,0:T(8,128)(2,1)S(1)} collective-permute-done((bf16[4,72,256]{2,1,0:T(8,128)(2,1)S(1)}, bf16[4,72,256]{2,1,0:T(8,128)(2,1)S(1)}, u32[]{:S(2)}, u32[]{:S(2)}) %collective-permute-start.8) | collective-permute-done | bytes 147488 | tf_op jit(solution)/shard_map/ppermute | solution.py:341
  34.0 2.8 %attend.2 = (bf16[256,256]{1,0:T(8,128)(2,1)S(1)}, bf16[256,1024]{1,0:T(8,128)(2,1)S(1)}) custom-call(s32[1]{0:T(128)} %bitcast.3.me, bf16[8,72,256]{2,1,0:T(8,128)(2,1)S(1)} %all-to-all-done.own.refs_0_, bf16[8,72,256]{2,1,0:T(8,128)(2,1)S(1)} %collective-permute-done.5.beside.refs_1_, bf16[4,72,256]{2,1,0:T(8,128)(2,1)S(1)} %collective-permute-done.6.refs_2_, ...), custom_call_target="tpu_custom_call" | custom-call | flops 8724152320 | bytes 2097152 | tf_op jit(solution)/shard_map/attend/pallas_call | solution.py:439
  36.7 0.0 copy-start.4
  36.8 0.0 copy-start.5
  36.8 0.0 copy-start.8
  36.8 0.0 copy-start.9
  36.8 1.6 %collective-permute-start.9 = (bf16[256,256]{1,0:T(8,128)(2,1)S(1)}, bf16[256,256]{1,0:T(8,128)(2,1)S(1)}, u32[]{:S(2)}, u32[]{:S(2)}) collective-permute-start(bf16[256,256]{1,0:T(8,128)(2,1)S(1)} %get-tuple-element.87.refs_0_), channel_id=1, source_target_pairs={{0,2},{1,3},{2,0},{3,1},{4,6},{5,7},{6,4},{7,5},{8,10},{9,11},{10,... | collective-permute-start | bytes 393224 | tf_op jit(solution)/shard_map/ppermute | solution.py:341
  38.4 0.2 collective-permute-start.14
  38.6 0.3 collective-permute-start.17
  38.9 0.2 collective-permute-start.18
  39.1 0.3 collective-permute-start.16
  39.4 2.8 %attend.3 = (bf16[256,256]{1,0:T(8,128)(2,1)S(1)}, bf16[256,1024]{1,0:T(8,128)(2,1)S(1)}) custom-call(s32[1]{0:T(128)} %bitcast.3.me, bf16[8,72,256]{2,1,0:T(8,128)(2,1)S(1)} %all-to-all-done.own.refs_0_, bf16[8,72,256]{2,1,0:T(8,128)(2,1)S(1)} %collective-permute-done.5.beside.refs_1_, bf16[4,72,256]{2,1,0:T(8,128)(2,1)S(1)} %collective-permute-done.8.refs_2_, ...), custom_call_target="tpu_custom_call" | custom-call | flops 8724152320 | bytes 2097152 | tf_op jit(solution)/shard_map/attend/pallas_call | solution.py:439
  42.2 0.6 collective-permute-done.9.refs_2_
  42.8 1.5 %collective-permute-start.12 = (bf16[256,256]{1,0:T(8,128)(2,1)S(1)}, bf16[256,256]{1,0:T(8,128)(2,1)S(1)}, u32[]{:S(2)}, u32[]{:S(2)}) collective-permute-start(bf16[256,256]{1,0:T(8,128)(2,1)S(1)} %get-tuple-element.101.refs_0_), channel_id=1, source_target_pairs={{0,2},{1,3},{2,0},{3,1},{4,6},{5,7},{6,4},{7,5},{8,10},{9,11},{10,... | collective-permute-start | bytes 393224 | tf_op jit(solution)/shard_map/ppermute | solution.py:341
  44.4 4.5 %feed.2 = (f32[2,64,1024]{2,1,0:T(8,128)S(1)}, bf16[64,1024]{1,0:T(8,128)(2,1)S(1)}, bf16[1,64,1024]{2,1,0:T(8,128)(2,1)S(1)}, bf16[64,1024]{1,0:T(8,128)(2,1)S(1)}) custom-call(s32[1]{0:T(128)} %bitcast.3.me, bf16[256,256]{1,0:T(8,128)(2,1)S(1)} %get-tuple-element.87.refs_0_, bf16[256,256]{1,0:T(8,128)(2,1)S(1)} %collective-permute-done.14.refs_1_, ...), custom_call_target="tpu_custom_call" | custom-call | flops 8053063680 | bytes 2097152 | tf_op jit(solution)/shard_map/feed/pallas_call | solution.py:475
  48.9 0.3 collective-permute-start.19
  49.2 0.3 collective-permute-start.11
  49.5 0.2 collective-permute-start.13
  49.7 0.3 collective-permute-start.21
  50.0 0.3 collective-permute-done.19
  50.4 0.2 collective-permute-done.11.refs_1_
  50.5 0.3 collective-permute-done.13.refs_3_
  50.8 1.3 %collective-permute-start.22 = (bf16[64,1024]{1,0:T(8,128)(2,1)S(1)}, bf16[64,1024]{1,0:T(8,128)(2,1)S(1)}, u32[]{:S(2)}, u32[]{:S(2)}) collective-permute-start(bf16[64,1024]{1,0:T(8,128)(2,1)S(1)} %fusion), channel_id=1, source_target_pairs={{0,2},{1,3},{2,0},{3,1},{4,6},{5,7},{6,4},{7,5},{8,10},{9,11},{10,... | collective-permute-start | bytes 393224 | tf_op jit(solution)/shard_map/ppermute | solution.py:341
  52.1 4.5 %feed.3 = (f32[2,64,1024]{2,1,0:T(8,128)S(1)}, bf16[64,1024]{1,0:T(8,128)(2,1)S(1)}, bf16[1,64,1024]{2,1,0:T(8,128)(2,1)S(1)}, bf16[64,1024]{1,0:T(8,128)(2,1)S(1)}) custom-call(s32[1]{0:T(128)} %bitcast.3.me, bf16[256,256]{1,0:T(8,128)(2,1)S(1)} %get-tuple-element.101.refs_0_, bf16[256,256]{1,0:T(8,128)(2,1)S(1)} %collective-permute-done.11.refs_1_, ...), custom_call_target="tpu_custom_call" | custom-call | flops 8053063680 | bytes 2097152 | tf_op jit(solution)/shard_map/feed/pallas_call | solution.py:475
  56.6 0.1 collective-permute-start.20
  56.7 0.5 collective-permute-start.23
  57.2 0.2 finish.2.refs_0_
  57.5 0.6 collective-permute-done.20
  58.1 0.8 collective-permute-start.24
  58.9 4.8 %collective-permute-done.24.refs_4_ = bf16[64,1024]{1,0:T(8,128)(2,1)S(1)} collective-permute-done((bf16[64,1024]{1,0:T(8,128)(2,1)S(1)}, bf16[64,1024]{1,0:T(8,128)(2,1)S(1)}, u32[]{:S(2)}, u32[]{:S(2)}) %collective-permute-start.24) | collective-permute-done | bytes 131104 | tf_op jit(solution)/shard_map/ppermute | solution.py:341
  63.7 0.2 finish.3
  63.9 15.4 %all_to_all.10 = bf16[32,16,256]{2,1,0:T(8,128)(2,1)S(1)} all-to-all(bf16[32,16,256]{2,1,0:T(8,128)(2,1)S(1)} %bitcast.21), channel_id=1, replica_groups=mesh['req'=8,'tp'=4] {'req','tp'}, dimensions={0} | all-to-all | bytes 524288 | tf_op jit(solution)/shard_map/all_to_all | solution.py:501
  79.3 1.3 %unpack.1 = bf16[8,64,256]{2,1,0:T(8,128)(2,1)} custom-call(s32[8]{0:T(128)S(1)} %get-tuple-element.60.owners, bf16[8,64,256]{2,1,0:T(8,128)(2,1)S(1)} %bitcast.22), custom_call_target="tpu_custom_call" | custom-call | tf_op jit(solution)/shard_map/unpack/pallas_call | solution.py:508
  (40 shorter events, 0.2 us)
Async XLA Ops:
  1.9 22.5 %all-to-all-start = ((bf16[8,72,256]{2,1,0:T(8,128)(2,1)}), bf16[8,72,256]{2,1,0:T(8,128)(2,1)S(1)}, u32[]{:S(2)}, u32[]{:S(2)}) async-start(bf16[8,72,256]{2,1,0:T(8,128)(2,1)} %get-tuple-element.63), calls=%async_computation | async-start | bytes 589824 | tf_op jit(solution)/shard_map/all_to_all | solution.py:374
  10.2 14.2 %collective-permute-start.1 = (bf16[128,1024]{1,0:T(8,128)(2,1)S(1)}, bf16[128,1024]{1,0:T(8,128)(2,1)S(1)}, u32[]{:S(2)}, u32[]{:S(2)}) collective-permute-start(bf16[128,1024]{1,0:T(8,128)(2,1)S(1)} %get-tuple-element.115), channel_id=1, source_target_pairs={{0,2},{1,3},{2,0},{3,1},{4,6},{5,7},{6,4},{7,5},{8,10},{9,11},{10,... | collective-permute-start | bytes 786440 | tf_op jit(solution)/shard_map/ppermute | solution.py:341
  11.8 12.6 %collective-permute-start = (bf16[128,1024]{1,0:T(8,128)(2,1)S(1)}, bf16[128,1024]{1,0:T(8,128)(2,1)S(1)}, u32[]{:S(2)}, u32[]{:S(2)}) collective-permute-start(bf16[128,1024]{1,0:T(8,128)(2,1)S(1)} %get-tuple-element.116), channel_id=1, source_target_pairs={{0,2},{1,3},{2,0},{3,1},{4,6},{5,7},{6,4},{7,5},{8,10},{9,11},{10,... | collective-permute-start | bytes 786440 | tf_op jit(solution)/shard_map/ppermute | solution.py:341
  12.3 10.9 %collective-permute-start.4 = (bf16[32,256]{1,0:T(8,128)(2,1)}, bf16[32,256]{1,0:T(8,128)(2,1)S(1)}, u32[]{:S(2)}, u32[]{:S(2)}) collective-permute-start(bf16[32,256]{1,0:T(8,128)(2,1)} %bitcast.31), channel_id=1, source_target_pairs={{0,3},{1,2},{2,1},{3,0},{4,7},{5,6},{6,5},{7,4},{8,11},{9,10},{10,... | collective-permute-start | bytes 49160 | tf_op jit(solution)/shard_map/ppermute | solution.py:341
  12.4 11.9 %collective-permute-start.3 = (bf16[32,256]{1,0:T(8,128)(2,1)}, bf16[32,256]{1,0:T(8,128)(2,1)S(1)}, u32[]{:S(2)}, u32[]{:S(2)}) collective-permute-start(bf16[32,256]{1,0:T(8,128)(2,1)} %bitcast.32), channel_id=1, source_target_pairs={{0,2},{1,3},{2,0},{3,1},{4,6},{5,7},{6,4},{7,5},{8,10},{9,11},{10,... | collective-permute-start | bytes 49160 | tf_op jit(solution)/shard_map/ppermute | solution.py:341
  13.8 10.5 %collective-permute-start.2 = (bf16[32,256]{1,0:T(8,128)(2,1)}, bf16[32,256]{1,0:T(8,128)(2,1)S(1)}, u32[]{:S(2)}, u32[]{:S(2)}) collective-permute-start(bf16[32,256]{1,0:T(8,128)(2,1)} %bitcast.33), channel_id=1, source_target_pairs={{0,1},{1,0},{2,3},{3,2},{4,5},{5,4},{6,7},{7,6},{8,9},{9,8},{10,11... | collective-permute-start | bytes 49160 | tf_op jit(solution)/shard_map/ppermute | solution.py:341
  24.4 2.2 %collective-permute-start.5 = (bf16[8,72,256]{2,1,0:T(8,128)(2,1)S(1)}, bf16[8,72,256]{2,1,0:T(8,128)(2,1)S(1)}, u32[]{:S(2)}, u32[]{:S(2)}) collective-permute-start(bf16[8,72,256]{2,1,0:T(8,128)(2,1)S(1)} %all-to-all-done.own.refs_0_), channel_id=1, source_target_pairs={{0,1},{1,0},{2,3},{3,2},{4,5},{5,4},{6,7},{7,6},{8,9},{9,8},{10,11... | collective-permute-start | bytes 884744 | tf_op jit(solution)/shard_map/ppermute | solution.py:341
  24.5 6.7 %collective-permute-start.6 = (bf16[4,72,256]{2,1,0:T(8,128)(2,1)S(1)}, bf16[4,72,256]{2,1,0:T(8,128)(2,1)S(1)}, u32[]{:S(2)}, u32[]{:S(2)}) collective-permute-start(bf16[4,72,256]{2,1,0:T(8,128)(2,1)S(1)} %get-tuple-element.118), channel_id=1, source_target_pairs={{0,2},{1,3},{2,0},{3,1},{4,6},{5,7},{6,4},{7,5},{8,10},{9,11},{10,... | collective-permute-start | bytes 442376 | tf_op jit(solution)/shard_map/ppermute | solution.py:341
  26.1 7.9 %collective-permute-start.8 = (bf16[4,72,256]{2,1,0:T(8,128)(2,1)S(1)}, bf16[4,72,256]{2,1,0:T(8,128)(2,1)S(1)}, u32[]{:S(2)}, u32[]{:S(2)}) collective-permute-start(bf16[4,72,256]{2,1,0:T(8,128)(2,1)S(1)} %get-tuple-element.117), channel_id=1, source_target_pairs={{0,2},{1,3},{2,0},{3,1},{4,6},{5,7},{6,4},{7,5},{8,10},{9,11},{10,... | collective-permute-start | bytes 442376 | tf_op jit(solution)/shard_map/ppermute | solution.py:341
  31.2 2.8 %collective-permute-start.7 = (bf16[4,72,256]{2,1,0:T(8,128)(2,1)S(1)}, bf16[4,72,256]{2,1,0:T(8,128)(2,1)S(1)}, u32[]{:S(2)}, u32[]{:S(2)}) collective-permute-start(bf16[4,72,256]{2,1,0:T(8,128)(2,1)S(1)} %collective-permute-done.6.refs_2_), channel_id=1, source_target_pairs={{0,1},{1,0},{2,3},{3,2},{4,5},{5,4},{6,7},{7,6},{8,9},{9,8},{10,11... | collective-permute-start | bytes 442376 | tf_op jit(solution)/shard_map/ppermute | solution.py:341
  33.9 5.2 %collective-permute-start.10 = (bf16[4,72,256]{2,1,0:T(8,128)(2,1)S(1)}, bf16[4,72,256]{2,1,0:T(8,128)(2,1)S(1)}, u32[]{:S(2)}, u32[]{:S(2)}) collective-permute-start(bf16[4,72,256]{2,1,0:T(8,128)(2,1)S(1)} %collective-permute-done.8.refs_2_), channel_id=1, source_target_pairs={{0,1},{1,0},{2,3},{3,2},{4,5},{5,4},{6,7},{7,6},{8,9},{9,8},{10,11... | collective-permute-start | bytes 442376 | tf_op jit(solution)/shard_map/ppermute | solution.py:341
  34.0 5.2 %copy-start = (bf16[256,1024]{1,0:T(8,128)(2,1)S(1)}, bf16[256,1024]{1,0:T(8,128)(2,1)}, u32[]{:S(2)}) copy-start(bf16[256,1024]{1,0:T(8,128)(2,1)} %refs_4_.3) | copy-start | bytes 1572868
  36.7 7.6 %copy-start.3 = (bf16[32,1024]{1,0:T(8,128)(2,1)S(1)}, bf16[32,1024]{1,0:T(8,128)(2,1)}, u32[]{:S(2)}) copy-start(bf16[32,1024]{1,0:T(8,128)(2,1)} %refs_16_.3) | copy-start | bytes 196612
  36.7 7.6 %copy-start.4 = (bf16[1024,32]{0,1:T(8,128)(2,1)S(1)}, bf16[1024,32]{0,1:T(8,128)(2,1)}, u32[]{:S(2)}) copy-start(bf16[1024,32]{0,1:T(8,128)(2,1)} %param.32) | copy-start | bytes 196612
  36.8 7.6 %copy-start.5 = (bf16[32,1024]{1,0:T(8,128)(2,1)S(1)}, bf16[32,1024]{1,0:T(8,128)(2,1)}, u32[]{:S(2)}) copy-start(bf16[32,1024]{1,0:T(8,128)(2,1)} %refs_18_.3) | copy-start | bytes 196612
  36.8 7.6 %copy-start.6 = (bf16[1024,32]{0,1:T(8,128)(2,1)S(1)}, bf16[1024,32]{0,1:T(8,128)(2,1)}, u32[]{:S(2)}) copy-start(bf16[1024,32]{0,1:T(8,128)(2,1)} %param.34) | copy-start | bytes 196612
  36.8 7.6 %copy-start.7 = (bf16[32,1024]{1,0:T(8,128)(2,1)S(1)}, bf16[32,1024]{1,0:T(8,128)(2,1)}, u32[]{:S(2)}) copy-start(bf16[32,1024]{1,0:T(8,128)(2,1)} %refs_20_.3) | copy-start | bytes 196612
  36.8 7.6 %copy-start.8 = (bf16[256,32]{0,1:T(8,128)(2,1)S(1)}, bf16[256,32]{0,1:T(8,128)(2,1)}, u32[]{:S(2)}) copy-start(bf16[256,32]{0,1:T(8,128)(2,1)} %param.30) | copy-start | bytes 49156
  36.8 7.6 %copy-start.9 = (f32[1024]{0:T(1024)S(1)}, f32[1024]{0:T(1024)}, u32[]{:S(2)}) copy-start(f32[1024]{0:T(1024)} %param.36) | copy-start | bytes 12292
  36.8 7.6 %copy-start.10 = (f32[1024]{0:T(1024)S(1)}, f32[1024]{0:T(1024)}, u32[]{:S(2)}) copy-start(f32[1024]{0:T(1024)} %param.37) | copy-start | bytes 12292
  36.8 6.0 %collective-permute-start.9 = (bf16[256,256]{1,0:T(8,128)(2,1)S(1)}, bf16[256,256]{1,0:T(8,128)(2,1)S(1)}, u32[]{:S(2)}, u32[]{:S(2)}) collective-permute-start(bf16[256,256]{1,0:T(8,128)(2,1)S(1)} %get-tuple-element.87.refs_0_), channel_id=1, source_target_pairs={{0,2},{1,3},{2,0},{3,1},{4,6},{5,7},{6,4},{7,5},{8,10},{9,11},{10,... | collective-permute-start | bytes 393224 | tf_op jit(solution)/shard_map/ppermute | solution.py:341
  38.4 4.4 %collective-permute-start.14 = (bf16[256,256]{1,0:T(8,128)(2,1)S(1)}, bf16[256,256]{1,0:T(8,128)(2,1)S(1)}, u32[]{:S(2)}, u32[]{:S(2)}) collective-permute-start(bf16[256,256]{1,0:T(8,128)(2,1)S(1)} %get-tuple-element.87.refs_0_), channel_id=1, source_target_pairs={{0,1},{1,0},{2,3},{3,2},{4,5},{5,4},{6,7},{7,6},{8,9},{9,8},{10,11... | collective-permute-start | bytes 393224 | tf_op jit(solution)/shard_map/ppermute | solution.py:341
  38.6 5.7 %collective-permute-start.17 = (bf16[128,1024]{1,0:T(8,128)(2,1)S(1)}, bf16[128,1024]{1,0:T(8,128)(2,1)S(1)}, u32[]{:S(2)}, u32[]{:S(2)}) collective-permute-start(bf16[128,1024]{1,0:T(8,128)(2,1)S(1)} %collective-permute-done.refs_6_), channel_id=1, source_target_pairs={{0,1},{1,0},{2,3},{3,2},{4,5},{5,4},{6,7},{7,6},{8,9},{9,8},{10,11... | collective-permute-start | bytes 786440 | tf_op jit(solution)/shard_map/ppermute | solution.py:341
  38.9 5.4 %collective-permute-start.18 = (bf16[128,1024]{1,0:T(8,128)(2,1)S(1)}, bf16[128,1024]{1,0:T(8,128)(2,1)S(1)}, u32[]{:S(2)}, u32[]{:S(2)}) collective-permute-start(bf16[128,1024]{1,0:T(8,128)(2,1)S(1)} %collective-permute-done.1.refs_7_), channel_id=1, source_target_pairs={{0,1},{1,0},{2,3},{3,2},{4,5},{5,4},{6,7},{7,6},{8,9},{9,8},{10,11... | collective-permute-start | bytes 786440 | tf_op jit(solution)/shard_map/ppermute | solution.py:341
  39.1 5.2 %collective-permute-start.16 = (bf16[256,1024]{1,0:T(8,128)(2,1)S(1)}, bf16[256,1024]{1,0:T(8,128)(2,1)S(1)}, u32[]{:S(2)}, u32[]{:S(2)}) collective-permute-start(bf16[256,1024]{1,0:T(8,128)(2,1)S(1)} %copy-done), channel_id=1, source_target_pairs={{0,1},{1,0},{2,3},{3,2},{4,5},{5,4},{6,7},{7,6},{8,9},{9,8},{10,11... | collective-permute-start | bytes 1572872 | tf_op jit(solution)/shard_map/ppermute | solution.py:341
  42.8 1.5 %collective-permute-start.15 = (bf16[256,256]{1,0:T(8,128)(2,1)S(1)}, bf16[256,256]{1,0:T(8,128)(2,1)S(1)}, u32[]{:S(2)}, u32[]{:S(2)}) collective-permute-start(bf16[256,256]{1,0:T(8,128)(2,1)S(1)} %collective-permute-done.9.refs_2_), channel_id=1, source_target_pairs={{0,1},{1,0},{2,3},{3,2},{4,5},{5,4},{6,7},{7,6},{8,9},{9,8},{10,11... | collective-permute-start | bytes 393224 | tf_op jit(solution)/shard_map/ppermute | solution.py:341
  42.8 6.7 %collective-permute-start.12 = (bf16[256,256]{1,0:T(8,128)(2,1)S(1)}, bf16[256,256]{1,0:T(8,128)(2,1)S(1)}, u32[]{:S(2)}, u32[]{:S(2)}) collective-permute-start(bf16[256,256]{1,0:T(8,128)(2,1)S(1)} %get-tuple-element.101.refs_0_), channel_id=1, source_target_pairs={{0,2},{1,3},{2,0},{3,1},{4,6},{5,7},{6,4},{7,5},{8,10},{9,11},{10,... | collective-permute-start | bytes 393224 | tf_op jit(solution)/shard_map/ppermute | solution.py:341
  48.9 1.4 %collective-permute-start.19 = (bf16[1,64,1024]{2,1,0:T(8,128)(2,1)S(1)}, bf16[1,64,1024]{2,1,0:T(8,128)(2,1)S(1)}, u32[]{:S(2)}, u32[]{:S(2)}) collective-permute-start(bf16[1,64,1024]{2,1,0:T(8,128)(2,1)S(1)} %get-tuple-element.100), channel_id=1, source_target_pairs={{0,1},{1,0},{2,3},{3,2},{4,5},{5,4},{6,7},{7,6},{8,9},{9,8},{10,11... | collective-permute-start | bytes 393224 | tf_op jit(solution)/shard_map/ppermute | solution.py:341
  49.2 1.3 %collective-permute-start.11 = (bf16[256,256]{1,0:T(8,128)(2,1)S(1)}, bf16[256,256]{1,0:T(8,128)(2,1)S(1)}, u32[]{:S(2)}, u32[]{:S(2)}) collective-permute-start(bf16[256,256]{1,0:T(8,128)(2,1)S(1)} %get-tuple-element.101.refs_0_), channel_id=1, source_target_pairs={{0,1},{1,0},{2,3},{3,2},{4,5},{5,4},{6,7},{7,6},{8,9},{9,8},{10,11... | collective-permute-start | bytes 393224 | tf_op jit(solution)/shard_map/ppermute | solution.py:341
  49.5 1.3 %collective-permute-start.13 = (bf16[256,256]{1,0:T(8,128)(2,1)S(1)}, bf16[256,256]{1,0:T(8,128)(2,1)S(1)}, u32[]{:S(2)}, u32[]{:S(2)}) collective-permute-start(bf16[256,256]{1,0:T(8,128)(2,1)S(1)} %collective-permute-done.12.refs_2_), channel_id=1, source_target_pairs={{0,1},{1,0},{2,3},{3,2},{4,5},{5,4},{6,7},{7,6},{8,9},{9,8},{10,11... | collective-permute-start | bytes 393224 | tf_op jit(solution)/shard_map/ppermute | solution.py:341
  49.7 7.5 %collective-permute-start.21 = (bf16[64,1024]{1,0:T(8,128)(2,1)S(1)}, bf16[64,1024]{1,0:T(8,128)(2,1)S(1)}, u32[]{:S(2)}, u32[]{:S(2)}) collective-permute-start(bf16[64,1024]{1,0:T(8,128)(2,1)S(1)} %get-tuple-element.107), channel_id=1, source_target_pairs={{0,1},{1,0},{2,3},{3,2},{4,5},{5,4},{6,7},{7,6},{8,9},{9,8},{10,11... | collective-permute-start | bytes 393224 | tf_op jit(solution)/shard_map/ppermute | solution.py:341
  50.8 6.4 %collective-permute-start.22 = (bf16[64,1024]{1,0:T(8,128)(2,1)S(1)}, bf16[64,1024]{1,0:T(8,128)(2,1)S(1)}, u32[]{:S(2)}, u32[]{:S(2)}) collective-permute-start(bf16[64,1024]{1,0:T(8,128)(2,1)S(1)} %fusion), channel_id=1, source_target_pairs={{0,2},{1,3},{2,0},{3,1},{4,6},{5,7},{6,4},{7,5},{8,10},{9,11},{10,... | collective-permute-start | bytes 393224 | tf_op jit(solution)/shard_map/ppermute | solution.py:341
  52.1 5.1 %copy-start.1 = (f32[1024]{0:T(1024)S(1)}, f32[1024]{0:T(1024)}, u32[]{:S(2)}) copy-start(f32[1024]{0:T(1024)} %param.38) | copy-start | bytes 12292
  52.1 5.1 %copy-start.2 = (f32[1024]{0:T(1024)S(1)}, f32[1024]{0:T(1024)}, u32[]{:S(2)}) copy-start(f32[1024]{0:T(1024)} %param.39) | copy-start | bytes 12292
  56.6 1.4 %collective-permute-start.20 = (bf16[1,64,1024]{2,1,0:T(8,128)(2,1)S(1)}, bf16[1,64,1024]{2,1,0:T(8,128)(2,1)S(1)}, u32[]{:S(2)}, u32[]{:S(2)}) collective-permute-start(bf16[1,64,1024]{2,1,0:T(8,128)(2,1)S(1)} %get-tuple-element.106), channel_id=1, source_target_pairs={{0,1},{1,0},{2,3},{3,2},{4,5},{5,4},{6,7},{7,6},{8,9},{9,8},{10,11... | collective-permute-start | bytes 393224 | tf_op jit(solution)/shard_map/ppermute | solution.py:341
  56.7 2.2 %collective-permute-start.23 = (bf16[64,1024]{1,0:T(8,128)(2,1)S(1)}, bf16[64,1024]{1,0:T(8,128)(2,1)S(1)}, u32[]{:S(2)}, u32[]{:S(2)}) collective-permute-start(bf16[64,1024]{1,0:T(8,128)(2,1)S(1)} %get-tuple-element.112), channel_id=1, source_target_pairs={{0,1},{1,0},{2,3},{3,2},{4,5},{5,4},{6,7},{7,6},{8,9},{9,8},{10,11... | collective-permute-start | bytes 393224 | tf_op jit(solution)/shard_map/ppermute | solution.py:341
  58.1 5.6 %collective-permute-start.24 = (bf16[64,1024]{1,0:T(8,128)(2,1)S(1)}, bf16[64,1024]{1,0:T(8,128)(2,1)S(1)}, u32[]{:S(2)}, u32[]{:S(2)}) collective-permute-start(bf16[64,1024]{1,0:T(8,128)(2,1)S(1)} %fusion.1), channel_id=1, source_target_pairs={{0,2},{1,3},{2,0},{3,1},{4,6},{5,7},{6,4},{7,5},{8,10},{9,11},{10,... | collective-permute-start | bytes 393224 | tf_op jit(solution)/shard_map/ppermute | solution.py:341

commit v11 on v10

--- a/solution.py
+++ b/solution.py
@@ -372,17 +372,19 @@
         (packed, me, w_out, out_down.T)
     )
     arrived = lax.all_to_all(packed, "req", split_axis=0, concat_axis=0, tiled=True)
-    w_half = w_out.shape[0] // 2
+    w_half = w_out.shape[0] * 3 // 8
     w_far = [
         [swap(w_first[:w_half], 2 * y), swap(w_first[w_half:], 2 * y)] for y in range(1, half)
     ]
     odowns = [out_down.T] + [swap(o_first, r) for r in range(1, n_tp)]
-    arrived, w_far, odowns = lax.optimization_barrier((arrived, w_far, odowns))
+    w_small, w_large = [pair[0] for pair in w_far], [pair[1] for pair in w_far]
+    arrived, w_small = lax.optimization_barrier((arrived, w_small))
     count = 2
     step_blocks = n_req // count
     rows = step_blocks * CAP
     own = rows // n_tp
-    beside = swap(arrived, 1)
+    beside, w_large = lax.optimization_barrier((swap(arrived, 1), w_large))
+    w_far = list(zip(w_small, w_large))
     x_far = []
     for c in range(count):
         piece = arrived[c * step_blocks : (c + 1) * step_blocks]
@@ -423,7 +425,7 @@
     w_all, w1, w2, downs, up_all = near(w_all, w1, w2, downs, up_all)
     x_far[0], begun = lax.optimization_barrier((x_far[0], begun))
     x_far[0] = second_hop(x_far[0])
-    x_far = lax.optimization_barrier(x_far)
+    x_far, odowns = lax.optimization_barrier((x_far, odowns))
     x_far[1:] = [second_hop(pieces) for pieces in x_far[1:]]
 
     consts = near(

time: 80.8 us -> 80.4 us (level)
  starting transfers between devices: 21.3 us -> 19.6 us
  local copies, waits for them, and re-layouts: 1.15 us -> 2.01 us
    ppermute x25, starting transfers between devices: 14 us -> 12.3 us  [swap(): return lax.ppermute(value, 'tp', [(i, i ^ r) for i in range(n_tp)])]
    ppermute x25, waiting for transfers between devices: 21.5 us -> 20.4 us  [swap(): return lax.ppermute(value, 'tp', [(i, i ^ r) for i in range(n_tp)])]
    slice x0 -> x1, local copies, waits for them, and re-layouts: none -> 0.94 us  [body(): w_first[:w_half]]
  transfers between devices with their start and end apart: 26 -> 26, of which waited for: 10 -> 13; matrix products, arithmetic and copies ran while one was open for 1% -> 3% of each run, Pallas kernels for 22% -> 22%
where the time goes in v11:
time: 80.4 us; the launch traced here: 80.1 us
  waiting for transfers between devices  21.2 us (26%)
  Pallas kernels  21 us (26%)
  starting transfers between devices  19.6 us (24%)
  blocking collectives  16.1 us (20%)
  local copies, waits for them, and re-layouts  2.01 us (2%)
    ppermute x25, waiting for transfers between devices, swap(): return lax.ppermute(value, 'tp', [(i, i ^ r) for i in range(n_tp)])  20.4 us
    all_to_all x1, blocking collectives, body(): lax.all_to_all(done.reshape(n_req * n_tp, share, width), ('req', 'tp'), s...  16.1 us
    ppermute x25, starting transfers between devices, swap(): return lax.ppermute(value, 'tp', [(i, i ^ r) for i in range(n_tp)])  12.3 us
    pallas_call x2, Pallas kernels, body(): pl.pallas_call(functools.partial(ffn_kernel, n_tp, c), out_shape=[pltpu.V...  8.94 us
    all_to_all x1, starting transfers between devices, body(): lax.all_to_all(packed, 'req', split_axis=0, concat_axis=0, tiled=True)  7.26 us
    pallas_call x2, Pallas kernels, body(): pl.pallas_call(functools.partial(attn_kernel, n_tp, c), out_shape=[pltpu....  5.53 us
    pallas_call x1, Pallas kernels, body(): pl.pallas_call(begin_kernel, out_shape=[pltpu.VMEM((3, count * rows, widt...  2.87 us
    pallas_call x1, Pallas kernels, body(): pl.pallas_call(pack_kernel, out_shape=(pltpu.VMEM((n_req, CAP + PAD, widt...  1.86 us
  transfers between devices with their start and end apart: 26, of which 13 were waited for; matrix products, arithmetic and copies ran while one was open for 3% of the time, Pallas kernels for 22%

profile of v11, /device:TPU:0, one launch (start us, length us, event | category | flops | bytes accessed | tf_op | source)
XLA Modules:
  0.0 80.1 jit_solution(16488009338499942608)
XLA Ops:
  0.0 1.9 %pack.1 = (bf16[8,72,256]{2,1,0:T(8,128)(2,1)}, s32[8]{0:T(128)S(1)}) custom-call(s32[4,8]{1,0:T(4,128)} %bitcast.42, s32[4,8]{1,0:T(4,128)} %bitcast.43, s32[16]{0:T(128)} %slots_in.1, bf16[8,64,256]{2,1,0:T(8,128)(2,1)} %bitcast.40), custom_call_target="tpu_custom_call" | custom-call | tf_op jit(solution)/shard_map/pack/pallas_call | solution.py:346
  1.9 7.3 %all-to-all-start = ((bf16[8,72,256]{2,1,0:T(8,128)(2,1)}), bf16[8,72,256]{2,1,0:T(8,128)(2,1)S(1)}, u32[]{:S(2)}, u32[]{:S(2)}) async-start(bf16[8,72,256]{2,1,0:T(8,128)(2,1)} %get-tuple-element.64), calls=%async_computation | async-start | bytes 589824 | tf_op jit(solution)/shard_map/all_to_all | solution.py:374
  9.1 0.9 %slice.18 = bf16[96,1024]{1,0:T(8,128)(2,1)S(1)} slice(bf16[256,1024]{1,0:T(8,128)(2,1)} %refs_4_.3), slice={[0:96], [0:1024]} | slice | bytes 393216 | tf_op jit(solution)/shard_map/slice | solution.py:377
  10.1 1.6 %collective-permute-start = (bf16[96,1024]{1,0:T(8,128)(2,1)S(1)}, bf16[96,1024]{1,0:T(8,128)(2,1)S(1)}, u32[]{:S(2)}, u32[]{:S(2)}) collective-permute-start(bf16[96,1024]{1,0:T(8,128)(2,1)S(1)} %slice.18), channel_id=1, source_target_pairs={{0,2},{1,3},{2,0},{3,1},{4,6},{5,7},{6,4},{7,5},{8,10},{9,11},{10,... | collective-permute-start | bytes 589832 | tf_op jit(solution)/shard_map/ppermute | solution.py:341
  11.7 1.0 %slice.19 = bf16[160,1024]{1,0:T(8,128)(2,1)S(1)} slice(bf16[256,1024]{1,0:T(8,128)(2,1)} %refs_4_.3), slice={[96:256], [0:1024]} | slice | bytes 655360 | tf_op jit(solution)/shard_map/slice | solution.py:377
  12.7 0.6 collective-permute-start.2
  13.2 4.7 %collective-permute-done.refs_6_ = bf16[96,1024]{1,0:T(8,128)(2,1)S(1)} collective-permute-done((bf16[96,1024]{1,0:T(8,128)(2,1)S(1)}, bf16[96,1024]{1,0:T(8,128)(2,1)S(1)}, u32[]{:S(2)}, u32[]{:S(2)}) %collective-permute-start) | collective-permute-done | bytes 196640 | tf_op jit(solution)/shard_map/ppermute | solution.py:341
  18.0 0.8 all-to-all-done.own.refs_0_
  18.8 1.6 %collective-permute-start.3 = (bf16[4,72,256]{2,1,0:T(8,128)(2,1)S(1)}, bf16[4,72,256]{2,1,0:T(8,128)(2,1)S(1)}, u32[]{:S(2)}, u32[]{:S(2)}) collective-permute-start(bf16[4,72,256]{2,1,0:T(8,128)(2,1)S(1)} %get-tuple-element.118), channel_id=1, source_target_pairs={{0,2},{1,3},{2,0},{3,1},{4,6},{5,7},{6,4},{7,5},{8,10},{9,11},{10,... | collective-permute-start | bytes 442376 | tf_op jit(solution)/shard_map/ppermute | solution.py:341
  20.4 0.5 collective-permute-start.5
  20.9 4.1 %collective-permute-done.2.refs_7_ = bf16[160,1024]{1,0:T(8,128)(2,1)S(1)} collective-permute-done((bf16[160,1024]{1,0:T(8,128)(2,1)S(1)}, bf16[160,1024]{1,0:T(8,128)(2,1)S(1)}, u32[]{:S(2)}, u32[]{:S(2)}) %collective-permute-start.2) | collective-permute-done | bytes 327712 | tf_op jit(solution)/shard_map/ppermute | solution.py:341
  25.0 2.9 %begin.1 = (f32[3,512,256]{2,1,0:T(8,128)S(1)}, f32[512,96]{1,0:T(8,128)S(1)}, bf16[512,128]{1,0:T(8,128)(2,1)S(1)}, f32[512,128]{1,0:T(8,128)S(1)}, bf16[3,1024...) custom-call(s32[1]{0:T(128)} %bitcast.3.me, ...), custom_call_target="tpu_custom_call" | custom-call | flops 1006632960 | bytes 2097152 | tf_op jit(solution)/shard_map/begin/pallas_call | solution.py:392
  27.9 0.3 collective-permute-done.3.refs_2_
  28.2 1.6 %collective-permute-start.8 = (bf16[32,256]{1,0:T(8,128)(2,1)S(1)}, bf16[32,256]{1,0:T(8,128)(2,1)S(1)}, u32[]{:S(2)}, u32[]{:S(2)}) collective-permute-start(bf16[32,256]{1,0:T(8,128)(2,1)S(1)} %bitcast.31), channel_id=1, source_target_pairs={{0,3},{1,2},{2,1},{3,0},{4,7},{5,6},{6,5},{7,4},{8,11},{9,10},{10,... | collective-permute-start | bytes 49160 | tf_op jit(solution)/shard_map/ppermute | solution.py:341
  29.8 0.5 collective-permute-start.7
  30.3 1.0 %collective-permute-done.8.refs_13_ = bf16[32,256]{1,0:T(8,128)(2,1)S(1)} collective-permute-done((bf16[32,256]{1,0:T(8,128)(2,1)S(1)}, bf16[32,256]{1,0:T(8,128)(2,1)S(1)}, u32[]{:S(2)}, u32[]{:S(2)}) %collective-permute-start.8) | collective-permute-done | bytes 16416 | tf_op jit(solution)/shard_map/ppermute | solution.py:341
  31.3 2.2 %collective-permute-done.7.refs_12_ = bf16[32,256]{1,0:T(8,128)(2,1)S(1)} collective-permute-done((bf16[32,256]{1,0:T(8,128)(2,1)S(1)}, bf16[32,256]{1,0:T(8,128)(2,1)S(1)}, u32[]{:S(2)}, u32[]{:S(2)}) %collective-permute-start.7) | collective-permute-done | bytes 16416 | tf_op jit(solution)/shard_map/ppermute | solution.py:341
  33.5 0.1 collective-permute-start.10
  33.6 0.0 copy-start
  33.6 2.8 %attend.2 = (bf16[256,256]{1,0:T(8,128)(2,1)S(1)}, bf16[256,1024]{1,0:T(8,128)(2,1)S(1)}) custom-call(s32[1]{0:T(128)} %bitcast.3.me, bf16[8,72,256]{2,1,0:T(8,128)(2,1)S(1)} %all-to-all-done.own.refs_0_, bf16[8,72,256]{2,1,0:T(8,128)(2,1)S(1)} %collective-permute-done.1.beside.refs_1_, bf16[4,72,256]{2,1,0:T(8,128)(2,1)S(1)} %collective-permute-done.3.refs_2_, ...), custom_call_target="tpu_custom_call" | custom-call | flops 8724152320 | bytes 2097152 | tf_op jit(solution)/shard_map/attend/pallas_call | solution.py:441
  36.5 0.6 collective-permute-start.9
  37.1 0.2 collective-permute-start.14
  37.3 0.3 collective-permute-start.17
  37.6 0.2 collective-permute-start.18
  37.8 0.3 collective-permute-start.16
  38.1 2.8 %attend.3 = (bf16[256,256]{1,0:T(8,128)(2,1)S(1)}, bf16[256,1024]{1,0:T(8,128)(2,1)S(1)}) custom-call(s32[1]{0:T(128)} %bitcast.3.me, bf16[8,72,256]{2,1,0:T(8,128)(2,1)S(1)} %all-to-all-done.own.refs_0_, bf16[8,72,256]{2,1,0:T(8,128)(2,1)S(1)} %collective-permute-done.1.beside.refs_1_, bf16[4,72,256]{2,1,0:T(8,128)(2,1)S(1)} %collective-permute-done.5.refs_2_, ...), custom_call_target="tpu_custom_call" | custom-call | flops 8724152320 | bytes 2097152 | tf_op jit(solution)/shard_map/attend/pallas_call | solution.py:441
  40.9 1.6 %collective-permute-done.9.refs_2_ = bf16[256,256]{1,0:T(8,128)(2,1)S(1)} collective-permute-done((bf16[256,256]{1,0:T(8,128)(2,1)S(1)}, bf16[256,256]{1,0:T(8,128)(2,1)S(1)}, u32[]{:S(2)}, u32[]{:S(2)}) %collective-permute-start.9) | collective-permute-done | bytes 131104 | tf_op jit(solution)/shard_map/ppermute | solution.py:341
  42.4 0.5 collective-permute-start.12
  43.0 0.8 %collective-permute-done.15.refs_3_ = bf16[256,256]{1,0:T(8,128)(2,1)S(1)} collective-permute-done((bf16[256,256]{1,0:T(8,128)(2,1)S(1)}, bf16[256,256]{1,0:T(8,128)(2,1)S(1)}, u32[]{:S(2)}, u32[]{:S(2)}) %collective-permute-start.15) | collective-permute-done | bytes 131104 | tf_op jit(solution)/shard_map/ppermute | solution.py:341
  43.9 4.5 %feed.2 = (f32[2,64,1024]{2,1,0:T(8,128)S(1)}, bf16[64,1024]{1,0:T(8,128)(2,1)S(1)}, bf16[1,64,1024]{2,1,0:T(8,128)(2,1)S(1)}, bf16[64,1024]{1,0:T(8,128)(2,1)S(1)}) custom-call(s32[1]{0:T(128)} %bitcast.3.me, bf16[256,256]{1,0:T(8,128)(2,1)S(1)} %get-tuple-element.89.refs_0_, bf16[256,256]{1,0:T(8,128)(2,1)S(1)} %collective-permute-done.14.refs_1_, ...), custom_call_target="tpu_custom_call" | custom-call | flops 8053063680 | bytes 2097152 | tf_op jit(solution)/shard_map/feed/pallas_call | solution.py:477
  48.3 0.2 collective-permute-start.19
  48.6 0.4 collective-permute-start.11
  48.9 0.1 collective-permute-start.13
  49.1 0.4 collective-permute-start.21
  49.4 0.3 collective-permute-done.19
  49.8 0.2 collective-permute-done.11.refs_1_
  49.9 0.3 collective-permute-done.13.refs_3_
  50.3 0.7 collective-permute-start.22
  51.0 4.5 %feed.3 = (f32[2,64,1024]{2,1,0:T(8,128)S(1)}, bf16[64,1024]{1,0:T(8,128)(2,1)S(1)}, bf16[1,64,1024]{2,1,0:T(8,128)(2,1)S(1)}, bf16[64,1024]{1,0:T(8,128)(2,1)S(1)}) custom-call(s32[1]{0:T(128)} %bitcast.3.me, bf16[256,256]{1,0:T(8,128)(2,1)S(1)} %get-tuple-element.103.refs_0_, bf16[256,256]{1,0:T(8,128)(2,1)S(1)} %collective-permute-done.11.refs_1_, ...), custom_call_target="tpu_custom_call" | custom-call | flops 8053063680 | bytes 2097152 | tf_op jit(solution)/shard_map/feed/pallas_call | solution.py:477
  55.4 0.1 collective-permute-start.20
  55.5 0.5 collective-permute-start.23
  56.0 0.2 finish.2.refs_0_
  56.3 0.6 collective-permute-done.20
  56.9 1.4 %collective-permute-start.24 = (bf16[64,1024]{1,0:T(8,128)(2,1)S(1)}, bf16[64,1024]{1,0:T(8,128)(2,1)S(1)}, u32[]{:S(2)}, u32[]{:S(2)}) collective-permute-start(bf16[64,1024]{1,0:T(8,128)(2,1)S(1)} %fusion.1), channel_id=1, source_target_pairs={{0,2},{1,3},{2,0},{3,1},{4,6},{5,7},{6,4},{7,5},{8,10},{9,11},{10,... | collective-permute-start | bytes 393224 | tf_op jit(solution)/shard_map/ppermute | solution.py:341
  58.3 4.2 %collective-permute-done.24.refs_4_ = bf16[64,1024]{1,0:T(8,128)(2,1)S(1)} collective-permute-done((bf16[64,1024]{1,0:T(8,128)(2,1)S(1)}, bf16[64,1024]{1,0:T(8,128)(2,1)S(1)}, u32[]{:S(2)}, u32[]{:S(2)}) %collective-permute-start.24) | collective-permute-done | bytes 131104 | tf_op jit(solution)/shard_map/ppermute | solution.py:341
  62.5 0.2 finish.3
  62.8 16.1 %all_to_all.10 = bf16[32,16,256]{2,1,0:T(8,128)(2,1)S(1)} all-to-all(bf16[32,16,256]{2,1,0:T(8,128)(2,1)S(1)} %bitcast.21), channel_id=1, replica_groups=mesh['req'=8,'tp'=4] {'req','tp'}, dimensions={0} | all-to-all | bytes 524288 | tf_op jit(solution)/shard_map/all_to_all | solution.py:503
  78.9 1.3 %unpack.1 = bf16[8,64,256]{2,1,0:T(8,128)(2,1)} custom-call(s32[8]{0:T(128)S(1)} %get-tuple-element.61.owners, bf16[8,64,256]{2,1,0:T(8,128)(2,1)S(1)} %bitcast.22), custom_call_target="tpu_custom_call" | custom-call | tf_op jit(solution)/shard_map/unpack/pallas_call | solution.py:510
  (41 shorter events, 0.2 us)
Async XLA Ops:
  1.9 16.9 %all-to-all-start = ((bf16[8,72,256]{2,1,0:T(8,128)(2,1)}), bf16[8,72,256]{2,1,0:T(8,128)(2,1)S(1)}, u32[]{:S(2)}, u32[]{:S(2)}) async-start(bf16[8,72,256]{2,1,0:T(8,128)(2,1)} %get-tuple-element.64), calls=%async_computation | async-start | bytes 589824 | tf_op jit(solution)/shard_map/all_to_all | solution.py:374
  10.1 7.9 %collective-permute-start = (bf16[96,1024]{1,0:T(8,128)(2,1)S(1)}, bf16[96,1024]{1,0:T(8,128)(2,1)S(1)}, u32[]{:S(2)}, u32[]{:S(2)}) collective-permute-start(bf16[96,1024]{1,0:T(8,128)(2,1)S(1)} %slice.18), channel_id=1, source_target_pairs={{0,2},{1,3},{2,0},{3,1},{4,6},{5,7},{6,4},{7,5},{8,10},{9,11},{10,... | collective-permute-start | bytes 589832 | tf_op jit(solution)/shard_map/ppermute | solution.py:341
  12.7 12.3 %collective-permute-start.2 = (bf16[160,1024]{1,0:T(8,128)(2,1)S(1)}, bf16[160,1024]{1,0:T(8,128)(2,1)S(1)}, u32[]{:S(2)}, u32[]{:S(2)}) collective-permute-start(bf16[160,1024]{1,0:T(8,128)(2,1)S(1)} %slice.19), channel_id=1, source_target_pairs={{0,2},{1,3},{2,0},{3,1},{4,6},{5,7},{6,4},{7,5},{8,10},{9,11},{10,... | collective-permute-start | bytes 983048 | tf_op jit(solution)/shard_map/ppermute | solution.py:341
  18.7 6.2 %collective-permute-start.1 = (bf16[8,72,256]{2,1,0:T(8,128)(2,1)S(1)}, bf16[8,72,256]{2,1,0:T(8,128)(2,1)S(1)}, u32[]{:S(2)}, u32[]{:S(2)}) collective-permute-start(bf16[8,72,256]{2,1,0:T(8,128)(2,1)S(1)} %all-to-all-done.own.refs_0_), channel_id=1, source_target_pairs={{0,1},{1,0},{2,3},{3,2},{4,5},{5,4},{6,7},{7,6},{8,9},{9,8},{10,11... | collective-permute-start | bytes 884744 | tf_op jit(solution)/shard_map/ppermute | solution.py:341
  18.8 9.4 %collective-permute-start.3 = (bf16[4,72,256]{2,1,0:T(8,128)(2,1)S(1)}, bf16[4,72,256]{2,1,0:T(8,128)(2,1)S(1)}, u32[]{:S(2)}, u32[]{:S(2)}) collective-permute-start(bf16[4,72,256]{2,1,0:T(8,128)(2,1)S(1)} %get-tuple-element.118), channel_id=1, source_target_pairs={{0,2},{1,3},{2,0},{3,1},{4,6},{5,7},{6,4},{7,5},{8,10},{9,11},{10,... | collective-permute-start | bytes 442376 | tf_op jit(solution)/shard_map/ppermute | solution.py:341
  20.4 13.2 %collective-permute-start.5 = (bf16[4,72,256]{2,1,0:T(8,128)(2,1)S(1)}, bf16[4,72,256]{2,1,0:T(8,128)(2,1)S(1)}, u32[]{:S(2)}, u32[]{:S(2)}) collective-permute-start(bf16[4,72,256]{2,1,0:T(8,128)(2,1)S(1)} %get-tuple-element.117), channel_id=1, source_target_pairs={{0,2},{1,3},{2,0},{3,1},{4,6},{5,7},{6,4},{7,5},{8,10},{9,11},{10,... | collective-permute-start | bytes 442376 | tf_op jit(solution)/shard_map/ppermute | solution.py:341
  25.0 3.2 %copy-start.8 = (bf16[256,32]{0,1:T(8,128)(2,1)S(1)}, bf16[256,32]{0,1:T(8,128)(2,1)}, u32[]{:S(2)}) copy-start(bf16[256,32]{0,1:T(8,128)(2,1)} %param.30) | copy-start | bytes 49156
  28.1 5.4 %collective-permute-start.4 = (bf16[4,72,256]{2,1,0:T(8,128)(2,1)S(1)}, bf16[4,72,256]{2,1,0:T(8,128)(2,1)S(1)}, u32[]{:S(2)}, u32[]{:S(2)}) collective-permute-start(bf16[4,72,256]{2,1,0:T(8,128)(2,1)S(1)} %collective-permute-done.3.refs_2_), channel_id=1, source_target_pairs={{0,1},{1,0},{2,3},{3,2},{4,5},{5,4},{6,7},{7,6},{8,9},{9,8},{10,11... | collective-permute-start | bytes 442376 | tf_op jit(solution)/shard_map/ppermute | solution.py:341
  28.2 3.2 %collective-permute-start.8 = (bf16[32,256]{1,0:T(8,128)(2,1)S(1)}, bf16[32,256]{1,0:T(8,128)(2,1)S(1)}, u32[]{:S(2)}, u32[]{:S(2)}) collective-permute-start(bf16[32,256]{1,0:T(8,128)(2,1)S(1)} %bitcast.31), channel_id=1, source_target_pairs={{0,3},{1,2},{2,1},{3,0},{4,7},{5,6},{6,5},{7,4},{8,11},{9,10},{10,... | collective-permute-start | bytes 49160 | tf_op jit(solution)/shard_map/ppermute | solution.py:341
  29.8 3.7 %collective-permute-start.7 = (bf16[32,256]{1,0:T(8,128)(2,1)S(1)}, bf16[32,256]{1,0:T(8,128)(2,1)S(1)}, u32[]{:S(2)}, u32[]{:S(2)}) collective-permute-start(bf16[32,256]{1,0:T(8,128)(2,1)S(1)} %bitcast.32), channel_id=1, source_target_pairs={{0,2},{1,3},{2,0},{3,1},{4,6},{5,7},{6,4},{7,5},{8,10},{9,11},{10,... | collective-permute-start | bytes 49160 | tf_op jit(solution)/shard_map/ppermute | solution.py:341
  30.3 3.2 %collective-permute-start.6 = (bf16[32,256]{1,0:T(8,128)(2,1)S(1)}, bf16[32,256]{1,0:T(8,128)(2,1)S(1)}, u32[]{:S(2)}, u32[]{:S(2)}) collective-permute-start(bf16[32,256]{1,0:T(8,128)(2,1)S(1)} %bitcast.33), channel_id=1, source_target_pairs={{0,1},{1,0},{2,3},{3,2},{4,5},{5,4},{6,7},{7,6},{8,9},{9,8},{10,11... | collective-permute-start | bytes 49160 | tf_op jit(solution)/shard_map/ppermute | solution.py:341
  33.5 4.2 %collective-permute-start.10 = (bf16[4,72,256]{2,1,0:T(8,128)(2,1)S(1)}, bf16[4,72,256]{2,1,0:T(8,128)(2,1)S(1)}, u32[]{:S(2)}, u32[]{:S(2)}) collective-permute-start(bf16[4,72,256]{2,1,0:T(8,128)(2,1)S(1)} %collective-permute-done.5.refs_2_), channel_id=1, source_target_pairs={{0,1},{1,0},{2,3},{3,2},{4,5},{5,4},{6,7},{7,6},{8,9},{9,8},{10,11... | collective-permute-start | bytes 442376 | tf_op jit(solution)/shard_map/ppermute | solution.py:341
  33.6 4.2 %copy-start = (bf16[256,1024]{1,0:T(8,128)(2,1)S(1)}, bf16[256,1024]{1,0:T(8,128)(2,1)}, u32[]{:S(2)}) copy-start(bf16[256,1024]{1,0:T(8,128)(2,1)} %refs_4_.3) | copy-start | bytes 1572868
  36.4 7.4 %copy-start.3 = (bf16[32,1024]{1,0:T(8,128)(2,1)S(1)}, bf16[32,1024]{1,0:T(8,128)(2,1)}, u32[]{:S(2)}) copy-start(bf16[32,1024]{1,0:T(8,128)(2,1)} %refs_16_.3) | copy-start | bytes 196612
  36.4 7.4 %copy-start.4 = (bf16[1024,32]{0,1:T(8,128)(2,1)S(1)}, bf16[1024,32]{0,1:T(8,128)(2,1)}, u32[]{:S(2)}) copy-start(bf16[1024,32]{0,1:T(8,128)(2,1)} %param.32) | copy-start | bytes 196612
  36.4 7.4 %copy-start.5 = (bf16[32,1024]{1,0:T(8,128)(2,1)S(1)}, bf16[32,1024]{1,0:T(8,128)(2,1)}, u32[]{:S(2)}) copy-start(bf16[32,1024]{1,0:T(8,128)(2,1)} %refs_18_.3) | copy-start | bytes 196612
  36.4 7.4 %copy-start.6 = (bf16[1024,32]{0,1:T(8,128)(2,1)S(1)}, bf16[1024,32]{0,1:T(8,128)(2,1)}, u32[]{:S(2)}) copy-start(bf16[1024,32]{0,1:T(8,128)(2,1)} %param.34) | copy-start | bytes 196612
  36.4 7.4 %copy-start.7 = (bf16[32,1024]{1,0:T(8,128)(2,1)S(1)}, bf16[32,1024]{1,0:T(8,128)(2,1)}, u32[]{:S(2)}) copy-start(bf16[32,1024]{1,0:T(8,128)(2,1)} %refs_20_.3) | copy-start | bytes 196612
  36.5 7.4 %copy-start.9 = (f32[1024]{0:T(1024)S(1)}, f32[1024]{0:T(1024)}, u32[]{:S(2)}) copy-start(f32[1024]{0:T(1024)} %param.36) | copy-start | bytes 12292
  36.5 7.4 %copy-start.10 = (f32[1024]{0:T(1024)S(1)}, f32[1024]{0:T(1024)}, u32[]{:S(2)}) copy-start(f32[1024]{0:T(1024)} %param.37) | copy-start | bytes 12292
  36.5 5.9 %collective-permute-start.9 = (bf16[256,256]{1,0:T(8,128)(2,1)S(1)}, bf16[256,256]{1,0:T(8,128)(2,1)S(1)}, u32[]{:S(2)}, u32[]{:S(2)}) collective-permute-start(bf16[256,256]{1,0:T(8,128)(2,1)S(1)} %get-tuple-element.89.refs_0_), channel_id=1, source_target_pairs={{0,2},{1,3},{2,0},{3,1},{4,6},{5,7},{6,4},{7,5},{8,10},{9,11},{10,... | collective-permute-start | bytes 393224 | tf_op jit(solution)/shard_map/ppermute | solution.py:341
  37.1 5.4 %collective-permute-start.14 = (bf16[256,256]{1,0:T(8,128)(2,1)S(1)}, bf16[256,256]{1,0:T(8,128)(2,1)S(1)}, u32[]{:S(2)}, u32[]{:S(2)}) collective-permute-start(bf16[256,256]{1,0:T(8,128)(2,1)S(1)} %get-tuple-element.89.refs_0_), channel_id=1, source_target_pairs={{0,1},{1,0},{2,3},{3,2},{4,5},{5,4},{6,7},{7,6},{8,9},{9,8},{10,11... | collective-permute-start | bytes 393224 | tf_op jit(solution)/shard_map/ppermute | solution.py:341
  37.3 5.7 %collective-permute-start.17 = (bf16[96,1024]{1,0:T(8,128)(2,1)S(1)}, bf16[96,1024]{1,0:T(8,128)(2,1)S(1)}, u32[]{:S(2)}, u32[]{:S(2)}) collective-permute-start(bf16[96,1024]{1,0:T(8,128)(2,1)S(1)} %collective-permute-done.refs_6_), channel_id=1, source_target_pairs={{0,1},{1,0},{2,3},{3,2},{4,5},{5,4},{6,7},{7,6},{8,9},{9,8},{10,11... | collective-permute-start | bytes 589832 | tf_op jit(solution)/shard_map/ppermute | solution.py:341
  37.6 6.2 %collective-permute-start.18 = (bf16[160,1024]{1,0:T(8,128)(2,1)S(1)}, bf16[160,1024]{1,0:T(8,128)(2,1)S(1)}, u32[]{:S(2)}, u32[]{:S(2)}) collective-permute-start(bf16[160,1024]{1,0:T(8,128)(2,1)S(1)} %collective-permute-done.2.refs_7_), channel_id=1, source_target_pairs={{0,1},{1,0},{2,3},{3,2},{4,5},{5,4},{6,7},{7,6},{8,9},{9,8},{10,11... | collective-permute-start | bytes 983048 | tf_op jit(solution)/shard_map/ppermute | solution.py:341
  37.8 6.0 %collective-permute-start.16 = (bf16[256,1024]{1,0:T(8,128)(2,1)S(1)}, bf16[256,1024]{1,0:T(8,128)(2,1)S(1)}, u32[]{:S(2)}, u32[]{:S(2)}) collective-permute-start(bf16[256,1024]{1,0:T(8,128)(2,1)S(1)} %copy-done), channel_id=1, source_target_pairs={{0,1},{1,0},{2,3},{3,2},{4,5},{5,4},{6,7},{7,6},{8,9},{9,8},{10,11... | collective-permute-start | bytes 1572872 | tf_op jit(solution)/shard_map/ppermute | solution.py:341
  42.4 1.3 %collective-permute-start.15 = (bf16[256,256]{1,0:T(8,128)(2,1)S(1)}, bf16[256,256]{1,0:T(8,128)(2,1)S(1)}, u32[]{:S(2)}, u32[]{:S(2)}) collective-permute-start(bf16[256,256]{1,0:T(8,128)(2,1)S(1)} %collective-permute-done.9.refs_2_), channel_id=1, source_target_pairs={{0,1},{1,0},{2,3},{3,2},{4,5},{5,4},{6,7},{7,6},{8,9},{9,8},{10,11... | collective-permute-start | bytes 393224 | tf_op jit(solution)/shard_map/ppermute | solution.py:341
  42.4 6.5 %collective-permute-start.12 = (bf16[256,256]{1,0:T(8,128)(2,1)S(1)}, bf16[256,256]{1,0:T(8,128)(2,1)S(1)}, u32[]{:S(2)}, u32[]{:S(2)}) collective-permute-start(bf16[256,256]{1,0:T(8,128)(2,1)S(1)} %get-tuple-element.103.refs_0_), channel_id=1, source_target_pairs={{0,2},{1,3},{2,0},{3,1},{4,6},{5,7},{6,4},{7,5},{8,10},{9,11},{10,... | collective-permute-start | bytes 393224 | tf_op jit(solution)/shard_map/ppermute | solution.py:341
  48.3 1.4 %collective-permute-start.19 = (bf16[1,64,1024]{2,1,0:T(8,128)(2,1)S(1)}, bf16[1,64,1024]{2,1,0:T(8,128)(2,1)S(1)}, u32[]{:S(2)}, u32[]{:S(2)}) collective-permute-start(bf16[1,64,1024]{2,1,0:T(8,128)(2,1)S(1)} %get-tuple-element.102), channel_id=1, source_target_pairs={{0,1},{1,0},{2,3},{3,2},{4,5},{5,4},{6,7},{7,6},{8,9},{9,8},{10,11... | collective-permute-start | bytes 393224 | tf_op jit(solution)/shard_map/ppermute | solution.py:341
  48.6 1.4 %collective-permute-start.11 = (bf16[256,256]{1,0:T(8,128)(2,1)S(1)}, bf16[256,256]{1,0:T(8,128)(2,1)S(1)}, u32[]{:S(2)}, u32[]{:S(2)}) collective-permute-start(bf16[256,256]{1,0:T(8,128)(2,1)S(1)} %get-tuple-element.103.refs_0_), channel_id=1, source_target_pairs={{0,1},{1,0},{2,3},{3,2},{4,5},{5,4},{6,7},{7,6},{8,9},{9,8},{10,11... | collective-permute-start | bytes 393224 | tf_op jit(solution)/shard_map/ppermute | solution.py:341
  48.9 1.3 %collective-permute-start.13 = (bf16[256,256]{1,0:T(8,128)(2,1)S(1)}, bf16[256,256]{1,0:T(8,128)(2,1)S(1)}, u32[]{:S(2)}, u32[]{:S(2)}) collective-permute-start(bf16[256,256]{1,0:T(8,128)(2,1)S(1)} %collective-permute-done.12.refs_2_), channel_id=1, source_target_pairs={{0,1},{1,0},{2,3},{3,2},{4,5},{5,4},{6,7},{7,6},{8,9},{9,8},{10,11... | collective-permute-start | bytes 393224 | tf_op jit(solution)/shard_map/ppermute | solution.py:341
  49.1 7.0 %collective-permute-start.21 = (bf16[64,1024]{1,0:T(8,128)(2,1)S(1)}, bf16[64,1024]{1,0:T(8,128)(2,1)S(1)}, u32[]{:S(2)}, u32[]{:S(2)}) collective-permute-start(bf16[64,1024]{1,0:T(8,128)(2,1)S(1)} %get-tuple-element.109), channel_id=1, source_target_pairs={{0,1},{1,0},{2,3},{3,2},{4,5},{5,4},{6,7},{7,6},{8,9},{9,8},{10,11... | collective-permute-start | bytes 393224 | tf_op jit(solution)/shard_map/ppermute | solution.py:341
  50.3 5.8 %collective-permute-start.22 = (bf16[64,1024]{1,0:T(8,128)(2,1)S(1)}, bf16[64,1024]{1,0:T(8,128)(2,1)S(1)}, u32[]{:S(2)}, u32[]{:S(2)}) collective-permute-start(bf16[64,1024]{1,0:T(8,128)(2,1)S(1)} %fusion), channel_id=1, source_target_pairs={{0,2},{1,3},{2,0},{3,1},{4,6},{5,7},{6,4},{7,5},{8,10},{9,11},{10,... | collective-permute-start | bytes 393224 | tf_op jit(solution)/shard_map/ppermute | solution.py:341
  51.0 5.1 %copy-start.1 = (f32[1024]{0:T(1024)S(1)}, f32[1024]{0:T(1024)}, u32[]{:S(2)}) copy-start(f32[1024]{0:T(1024)} %param.38) | copy-start | bytes 12292
  51.0 5.1 %copy-start.2 = (f32[1024]{0:T(1024)S(1)}, f32[1024]{0:T(1024)}, u32[]{:S(2)}) copy-start(f32[1024]{0:T(1024)} %param.39) | copy-start | bytes 12292
  55.4 1.4 %collective-permute-start.20 = (bf16[1,64,1024]{2,1,0:T(8,128)(2,1)S(1)}, bf16[1,64,1024]{2,1,0:T(8,128)(2,1)S(1)}, u32[]{:S(2)}, u32[]{:S(2)}) collective-permute-start(bf16[1,64,1024]{2,1,0:T(8,128)(2,1)S(1)} %get-tuple-element.108), channel_id=1, source_target_pairs={{0,1},{1,0},{2,3},{3,2},{4,5},{5,4},{6,7},{7,6},{8,9},{9,8},{10,11... | collective-permute-start | bytes 393224 | tf_op jit(solution)/shard_map/ppermute | solution.py:341
  55.5 2.8 %collective-permute-start.23 = (bf16[64,1024]{1,0:T(8,128)(2,1)S(1)}, bf16[64,1024]{1,0:T(8,128)(2,1)S(1)}, u32[]{:S(2)}, u32[]{:S(2)}) collective-permute-start(bf16[64,1024]{1,0:T(8,128)(2,1)S(1)} %get-tuple-element.114), channel_id=1, source_target_pairs={{0,1},{1,0},{2,3},{3,2},{4,5},{5,4},{6,7},{7,6},{8,9},{9,8},{10,11... | collective-permute-start | bytes 393224 | tf_op jit(solution)/shard_map/ppermute | solution.py:341
  56.9 5.6 %collective-permute-start.24 = (bf16[64,1024]{1,0:T(8,128)(2,1)S(1)}, bf16[64,1024]{1,0:T(8,128)(2,1)S(1)}, u32[]{:S(2)}, u32[]{:S(2)}) collective-permute-start(bf16[64,1024]{1,0:T(8,128)(2,1)S(1)} %fusion.1), channel_id=1, source_target_pairs={{0,2},{1,3},{2,0},{3,1},{4,6},{5,7},{6,4},{7,5},{8,10},{9,11},{10,... | collective-permute-start | bytes 393224 | tf_op jit(solution)/shard_map/ppermute | solution.py:341

commit v12 on v9

--- a/solution.py
+++ b/solution.py
@@ -32,12 +32,6 @@
     centred = values - mean
     variance = jnp.mean(centred * centred, axis=-1, keepdims=True)
     return centred * lax.rsqrt(variance + NORM_EPS) * gain + shift
-
-
-def split_low(low, sel):
-    low = low * sel
-    high = low.astype(BF).astype(F32)
-    return jnp.concatenate([high, low - high], axis=1).astype(BF)
 
 
 def fetch(pairs, sems):
@@ -102,7 +96,8 @@
     me, own, beside, w_in, w1_in, w2_in, down_in, up_in, *refs
 ):
     acc, low, sel_out, bias_out, w, w1, w2, down, up_all, up, sems = refs
-    pairs = [(up_in, up), (down_in, down)] + [(w_in.at[k], w.at[k]) for k in range(3)]
+    low_rows = down_in.shape[0]
+    pairs = [(up_in, up), (down_in, down.at[:low_rows]), (down_in, down.at[low_rows:])] + [(w_in.at[k], w.at[k]) for k in range(3)]
     for src, dst in ((w1_in, w1), (w2_in, w2)):
         half = src.shape[0] // 2
         pairs += [(src.at[:half], dst.at[:half]), (src.at[half:], dst.at[half:])]
@@ -113,7 +108,7 @@
         for part in range(2):
             first_row = (3 * part + k) * SPAN
             up_all[first_row : first_row + SPAN, k * up.shape[2] : (k + 1) * up.shape[2]] = up[k]
-    for c in copies[1:5]:
+    for c in copies[1:6]:
         c.wait()
     blocks = own.shape[0]
     width = own.shape[2]
@@ -145,7 +140,7 @@
             sel_out[ps] = (lane_sel == pick).astype(BF)
 
     tiles(blocks // tile, step)
-    for c in copies[5:]:
+    for c in copies[6:]:
         c.wait()
 
 
@@ -173,7 +168,8 @@
         low = low_in[whole]
         for r in range(2, n_tp):
             low = low + dot_t(xs[r - 2], down[:, spans[r]])
-        low = split_low(low, sel_in[whole].astype(F32)[:, : 3 * SPAN])
+        sel = sel_in[whole].astype(F32)
+        low = split_two(low, jnp.concatenate([sel, sel[:, : 2 * SPAN]], axis=1))
         qkv = []
         for k in range(3):
             total = acc[k, whole] + dot(low, up_all[:, k * width : (k + 1) * width])
@@ -386,20 +382,20 @@
         begin_kernel,
         out_shape=[
             pltpu.VMEM((3, count * rows, width), F32),
-            pltpu.VMEM((count * rows, 3 * SPAN), F32),
+            pltpu.VMEM((count * rows, 6 * SPAN), F32),
             pltpu.VMEM((count * rows, 4 * SPAN), BF),
             pltpu.VMEM((count * rows, 2 * CAP), F32),
             pltpu.VMEM((3, feat, width), BF),
             pltpu.VMEM(w_fc1.shape, BF),
             pltpu.VMEM(w_fc2.shape, BF),
-            pltpu.VMEM((3 * SPAN, feat), BF),
+            pltpu.VMEM((6 * SPAN, feat), BF),
             pltpu.VMEM((6 * SPAN, 3 * width), BF),
         ],
         in_specs=[SMEM] + [VM] * 2 + [HBM] * 5,
         out_specs=[VM] * 9,
         scratch_shapes=[
             pltpu.VMEM((3, SPAN, width), BF),
-            pltpu.SemaphoreType.DMA((9,)),
+            pltpu.SemaphoreType.DMA((10,)),
         ],
         compiler_params=params(8),
         cost_estimate=work(rows * feat * 3 * width, rows),

time: 75.2 us -> 75.5 us (level)
  Pallas kernels: 20.9 us -> 21.7 us
  transfers between devices with their start and end apart: 24 -> 24, of which waited for: 12 -> 12; matrix products, arithmetic and copies ran while one was open for 0% -> 0% of each run, Pallas kernels for 23% -> 24%
where the time goes in v12:
time: 75.5 us; the launch traced here: 75.3 us
  Pallas kernels  21.7 us (29%)
  waiting for transfers between devices  20.7 us (27%)
  starting transfers between devices  18.2 us (24%)
  blocking collectives  14.3 us (19%)
    ppermute x23, waiting for transfers between devices, swap(): return lax.ppermute(value, 'tp', [(i, i ^ r) for i in range(n_tp)])  18.4 us
    all_to_all x1, blocking collectives, body(): lax.all_to_all(done.reshape(n_req * n_tp, share, width), ('req', 'tp'), s...  14.3 us
    ppermute x23, starting transfers between devices, swap(): return lax.ppermute(value, 'tp', [(i, i ^ r) for i in range(n_tp)])  12.4 us
    pallas_call x2, Pallas kernels, body(): pl.pallas_call(functools.partial(ffn_kernel, n_tp, c), out_shape=[pltpu.V...  8.93 us
    pallas_call x2, Pallas kernels, body(): pl.pallas_call(functools.partial(attn_kernel, n_tp, c), out_shape=[pltpu....  6.14 us
    all_to_all x1, starting transfers between devices, body(): lax.all_to_all(packed, 'req', split_axis=0, concat_axis=0, tiled=True)  5.81 us
    pallas_call x1, Pallas kernels, body(): pl.pallas_call(begin_kernel, out_shape=[pltpu.VMEM((3, count * rows, widt...  2.96 us
    all_to_all x1, waiting for transfers between devices, body(): lax.all_to_all(packed, 'req', split_axis=0, concat_axis=0, tiled=True)  2.27 us
  transfers between devices with their start and end apart: 24, of which 12 were waited for; matrix products, arithmetic and copies ran while one was open for 0% of the time, Pallas kernels for 24%

profile of v12, /device:TPU:0, one launch (start us, length us, event | category | flops | bytes accessed | tf_op | source)
XLA Modules:
  0.0 75.3 jit_solution(10884161611570004326)
XLA Ops:
  0.0 1.8 %pack.1 = (bf16[8,72,256]{2,1,0:T(8,128)(2,1)}, s32[8]{0:T(128)S(1)}) custom-call(s32[4,8]{1,0:T(4,128)} %bitcast.42, s32[4,8]{1,0:T(4,128)} %bitcast.43, s32[16]{0:T(128)} %slots_in.1, bf16[8,64,256]{2,1,0:T(8,128)(2,1)} %bitcast.40), custom_call_target="tpu_custom_call" | custom-call | tf_op jit(solution)/shard_map/pack/pallas_call | solution.py:339
  1.8 0.5 collective-permute-start.1
  2.4 2.6 %collective-permute-start = (bf16[256,1024]{1,0:T(8,128)(2,1)}, bf16[256,1024]{1,0:T(8,128)(2,1)S(1)}, u32[]{:S(2)}, u32[]{:S(2)}) collective-permute-start(bf16[256,1024]{1,0:T(8,128)(2,1)} %refs_4_.3), channel_id=1, source_target_pairs={{0,2},{1,3},{2,0},{3,1},{4,6},{5,7},{6,4},{7,5},{8,10},{9,11},{10,... | collective-permute-start | bytes 1572872 | tf_op jit(solution)/shard_map/ppermute | solution.py:334
  5.0 5.8 %all-to-all-start = ((bf16[8,72,256]{2,1,0:T(8,128)(2,1)}), bf16[8,72,256]{2,1,0:T(8,128)(2,1)S(1)}, u32[]{:S(2)}, u32[]{:S(2)}) async-start(bf16[8,72,256]{2,1,0:T(8,128)(2,1)} %get-tuple-element.61), calls=%async_computation | async-start | bytes 589824 | tf_op jit(solution)/shard_map/all_to_all | solution.py:367
  10.8 1.5 %collective-permute-start.3 = (bf16[32,256]{1,0:T(8,128)(2,1)}, bf16[32,256]{1,0:T(8,128)(2,1)S(1)}, u32[]{:S(2)}, u32[]{:S(2)}) collective-permute-start(bf16[32,256]{1,0:T(8,128)(2,1)} %bitcast.32), channel_id=1, source_target_pairs={{0,2},{1,3},{2,0},{3,1},{4,6},{5,7},{6,4},{7,5},{8,10},{9,11},{10,... | collective-permute-start | bytes 49160 | tf_op jit(solution)/shard_map/ppermute | solution.py:334
  12.3 0.3 collective-permute-start.2
  12.6 5.1 %collective-permute-done.4.refs_11_ = bf16[32,256]{1,0:T(8,128)(2,1)S(1)} collective-permute-done((bf16[32,256]{1,0:T(8,128)(2,1)}, bf16[32,256]{1,0:T(8,128)(2,1)S(1)}, u32[]{:S(2)}, u32[]{:S(2)}) %collective-permute-start.4) | collective-permute-done | bytes 16416 | tf_op jit(solution)/shard_map/ppermute | solution.py:334
  17.8 0.6 collective-permute-done.3.refs_10_
  18.4 2.3 %all-to-all-done.own.refs_0_ = bf16[8,72,256]{2,1,0:T(8,128)(2,1)S(1)} async-done(((bf16[8,72,256]{2,1,0:T(8,128)(2,1)}), bf16[8,72,256]{2,1,0:T(8,128)(2,1)S(1)}, u32[]{:S(2)}, u32[]{:S(2)}) %all-to-all-start) | async-done | bytes 294944 | tf_op jit(solution)/shard_map/all_to_all | solution.py:367
  20.7 0.6 collective-permute-start.6
  21.3 1.5 %collective-permute-start.8 = (bf16[4,72,256]{2,1,0:T(8,128)(2,1)S(1)}, bf16[4,72,256]{2,1,0:T(8,128)(2,1)S(1)}, u32[]{:S(2)}, u32[]{:S(2)}) collective-permute-start(bf16[4,72,256]{2,1,0:T(8,128)(2,1)S(1)} %get-tuple-element.111), channel_id=1, source_target_pairs={{0,2},{1,3},{2,0},{3,1},{4,6},{5,7},{6,4},{7,5},{8,10},{9,11},{10,... | collective-permute-start | bytes 442376 | tf_op jit(solution)/shard_map/ppermute | solution.py:334
  22.8 3.0 %begin.1 = (f32[3,512,256]{2,1,0:T(8,128)S(1)}, f32[512,192]{1,0:T(8,128)S(1)}, bf16[512,128]{1,0:T(8,128)(2,1)S(1)}, f32[512,128]{1,0:T(8,128)S(1)}, bf16[3,102...) custom-call(s32[1]{0:T(128)} %bitcast.3.me, ...), custom_call_target="tpu_custom_call" | custom-call | flops 1006632960 | bytes 2097152 | tf_op jit(solution)/shard_map/begin/pallas_call | solution.py:381
  25.8 1.6 %collective-permute-done.6.refs_2_ = bf16[4,72,256]{2,1,0:T(8,128)(2,1)S(1)} collective-permute-done((bf16[4,72,256]{2,1,0:T(8,128)(2,1)S(1)}, bf16[4,72,256]{2,1,0:T(8,128)(2,1)S(1)}, u32[]{:S(2)}, u32[]{:S(2)}) %collective-permute-start.6) | collective-permute-done | bytes 147488 | tf_op jit(solution)/shard_map/ppermute | solution.py:334
  27.4 2.8 %collective-permute-done.8.refs_2_ = bf16[4,72,256]{2,1,0:T(8,128)(2,1)S(1)} collective-permute-done((bf16[4,72,256]{2,1,0:T(8,128)(2,1)S(1)}, bf16[4,72,256]{2,1,0:T(8,128)(2,1)S(1)}, u32[]{:S(2)}, u32[]{:S(2)}) %collective-permute-start.8) | collective-permute-done | bytes 147488 | tf_op jit(solution)/shard_map/ppermute | solution.py:334
  30.2 3.1 %attend.2 = (bf16[256,256]{1,0:T(8,128)(2,1)S(1)}, bf16[256,1024]{1,0:T(8,128)(2,1)S(1)}) custom-call(s32[1]{0:T(128)} %bitcast.3.me, bf16[8,72,256]{2,1,0:T(8,128)(2,1)S(1)} %all-to-all-done.own.refs_0_, bf16[8,72,256]{2,1,0:T(8,128)(2,1)S(1)} %collective-permute-done.5.beside.refs_1_, bf16[4,72,256]{2,1,0:T(8,128)(2,1)S(1)} %collective-permute-done.6.refs_2_, ...), custom_call_target="tpu_custom_call" | custom-call | flops 8724152320 | bytes 2097152 | tf_op jit(solution)/shard_map/attend/pallas_call | solution.py:428
  33.3 0.0 copy-start.2
  33.3 0.0 copy-start.3
  33.3 0.0 copy-start.4
  33.3 0.0 copy-start.5
  33.3 0.0 copy-start.7
  33.3 0.0 copy-start.8
  33.4 0.0 copy-start.10
  33.4 0.6 collective-permute-start.9
  34.0 0.2 collective-permute-start.14
  34.2 0.3 collective-permute-start.16
  34.5 3.1 %attend.3 = (bf16[256,256]{1,0:T(8,128)(2,1)S(1)}, bf16[256,1024]{1,0:T(8,128)(2,1)S(1)}) custom-call(s32[1]{0:T(128)} %bitcast.3.me, bf16[8,72,256]{2,1,0:T(8,128)(2,1)S(1)} %all-to-all-done.own.refs_0_, bf16[8,72,256]{2,1,0:T(8,128)(2,1)S(1)} %collective-permute-done.5.beside.refs_1_, bf16[4,72,256]{2,1,0:T(8,128)(2,1)S(1)} %collective-permute-done.8.refs_2_, ...), custom_call_target="tpu_custom_call" | custom-call | flops 8724152320 | bytes 2097152 | tf_op jit(solution)/shard_map/attend/pallas_call | solution.py:428
  37.5 1.8 %collective-permute-done.9.refs_2_ = bf16[256,256]{1,0:T(8,128)(2,1)S(1)} collective-permute-done((bf16[256,256]{1,0:T(8,128)(2,1)S(1)}, bf16[256,256]{1,0:T(8,128)(2,1)S(1)}, u32[]{:S(2)}, u32[]{:S(2)}) %collective-permute-start.9) | collective-permute-done | bytes 131104 | tf_op jit(solution)/shard_map/ppermute | solution.py:334
  39.4 0.5 collective-permute-start.12
  39.9 0.8 %collective-permute-done.15.refs_3_ = bf16[256,256]{1,0:T(8,128)(2,1)S(1)} collective-permute-done((bf16[256,256]{1,0:T(8,128)(2,1)S(1)}, bf16[256,256]{1,0:T(8,128)(2,1)S(1)}, u32[]{:S(2)}, u32[]{:S(2)}) %collective-permute-start.15) | collective-permute-done | bytes 131104 | tf_op jit(solution)/shard_map/ppermute | solution.py:334
  40.8 4.5 %feed.2 = (f32[2,64,1024]{2,1,0:T(8,128)S(1)}, bf16[64,1024]{1,0:T(8,128)(2,1)S(1)}, bf16[1,64,1024]{2,1,0:T(8,128)(2,1)S(1)}, bf16[64,1024]{1,0:T(8,128)(2,1)S(1)}) custom-call(s32[1]{0:T(128)} %bitcast.3.me, bf16[256,256]{1,0:T(8,128)(2,1)S(1)} %get-tuple-element.84.refs_0_, bf16[256,256]{1,0:T(8,128)(2,1)S(1)} %collective-permute-done.14.refs_1_, ...), custom_call_target="tpu_custom_call" | custom-call | flops 8053063680 | bytes 2097152 | tf_op jit(solution)/shard_map/feed/pallas_call | solution.py:461
  45.3 0.2 collective-permute-start.17
  45.5 0.4 collective-permute-start.11
  45.8 0.1 collective-permute-start.13
  46.0 0.4 collective-permute-start.19
  46.4 0.3 collective-permute-done.17
  46.7 0.2 collective-permute-done.11.refs_1_
  46.9 0.3 collective-permute-done.13.refs_3_
  47.2 0.7 collective-permute-start.20
  47.9 4.5 %feed.3 = (f32[2,64,1024]{2,1,0:T(8,128)S(1)}, bf16[64,1024]{1,0:T(8,128)(2,1)S(1)}, bf16[1,64,1024]{2,1,0:T(8,128)(2,1)S(1)}, bf16[64,1024]{1,0:T(8,128)(2,1)S(1)}) custom-call(s32[1]{0:T(128)} %bitcast.3.me, bf16[256,256]{1,0:T(8,128)(2,1)S(1)} %get-tuple-element.97.refs_0_, bf16[256,256]{1,0:T(8,128)(2,1)S(1)} %collective-permute-done.11.refs_1_, ...), custom_call_target="tpu_custom_call" | custom-call | flops 8053063680 | bytes 2097152 | tf_op jit(solution)/shard_map/feed/pallas_call | solution.py:461
  52.4 0.1 collective-permute-start.18
  52.4 0.5 collective-permute-start.21
  53.0 0.2 finish.2.refs_0_
  53.2 0.6 collective-permute-done.18
  53.8 1.4 %collective-permute-start.22 = (bf16[64,1024]{1,0:T(8,128)(2,1)S(1)}, bf16[64,1024]{1,0:T(8,128)(2,1)S(1)}, u32[]{:S(2)}, u32[]{:S(2)}) collective-permute-start(bf16[64,1024]{1,0:T(8,128)(2,1)S(1)} %fusion.1), channel_id=1, source_target_pairs={{0,2},{1,3},{2,0},{3,1},{4,6},{5,7},{6,4},{7,5},{8,10},{9,11},{10,... | collective-permute-start | bytes 393224 | tf_op jit(solution)/shard_map/ppermute | solution.py:334
  55.2 4.2 %collective-permute-done.22.refs_4_ = bf16[64,1024]{1,0:T(8,128)(2,1)S(1)} collective-permute-done((bf16[64,1024]{1,0:T(8,128)(2,1)S(1)}, bf16[64,1024]{1,0:T(8,128)(2,1)S(1)}, u32[]{:S(2)}, u32[]{:S(2)}) %collective-permute-start.22) | collective-permute-done | bytes 131104 | tf_op jit(solution)/shard_map/ppermute | solution.py:334
  59.4 0.2 finish.3
  59.7 14.3 %all_to_all.10 = bf16[32,16,256]{2,1,0:T(8,128)(2,1)S(1)} all-to-all(bf16[32,16,256]{2,1,0:T(8,128)(2,1)S(1)} %bitcast.21), channel_id=1, replica_groups=mesh['req'=8,'tp'=4] {'req','tp'}, dimensions={0} | all-to-all | bytes 524288 | tf_op jit(solution)/shard_map/all_to_all | solution.py:487
  74.0 1.3 %unpack.1 = bf16[8,64,256]{2,1,0:T(8,128)(2,1)} custom-call(s32[8]{0:T(128)S(1)} %get-tuple-element.58.owners, bf16[8,64,256]{2,1,0:T(8,128)(2,1)S(1)} %bitcast.22), custom_call_target="tpu_custom_call" | custom-call | tf_op jit(solution)/shard_map/unpack/pallas_call | solution.py:494
  (35 shorter events, 0.2 us)
Async XLA Ops:
  1.8 18.8 %collective-permute-start.1 = (bf16[256,1024]{1,0:T(8,128)(2,1)}, bf16[256,1024]{1,0:T(8,128)(2,1)S(1)}, u32[]{:S(2)}, u32[]{:S(2)}) collective-permute-start(bf16[256,1024]{1,0:T(8,128)(2,1)} %refs_4_.3), channel_id=1, source_target_pairs={{0,1},{1,0},{2,3},{3,2},{4,5},{5,4},{6,7},{7,6},{8,9},{9,8},{10,11... | collective-permute-start | bytes 1572872 | tf_op jit(solution)/shard_map/ppermute | solution.py:334
  2.4 18.3 %collective-permute-start = (bf16[256,1024]{1,0:T(8,128)(2,1)}, bf16[256,1024]{1,0:T(8,128)(2,1)S(1)}, u32[]{:S(2)}, u32[]{:S(2)}) collective-permute-start(bf16[256,1024]{1,0:T(8,128)(2,1)} %refs_4_.3), channel_id=1, source_target_pairs={{0,2},{1,3},{2,0},{3,1},{4,6},{5,7},{6,4},{7,5},{8,10},{9,11},{10,... | collective-permute-start | bytes 1572872 | tf_op jit(solution)/shard_map/ppermute | solution.py:334
  5.0 15.7 %all-to-all-start = ((bf16[8,72,256]{2,1,0:T(8,128)(2,1)}), bf16[8,72,256]{2,1,0:T(8,128)(2,1)S(1)}, u32[]{:S(2)}, u32[]{:S(2)}) async-start(bf16[8,72,256]{2,1,0:T(8,128)(2,1)} %get-tuple-element.61), calls=%async_computation | async-start | bytes 589824 | tf_op jit(solution)/shard_map/all_to_all | solution.py:367
  10.8 7.0 %collective-permute-start.4 = (bf16[32,256]{1,0:T(8,128)(2,1)}, bf16[32,256]{1,0:T(8,128)(2,1)S(1)}, u32[]{:S(2)}, u32[]{:S(2)}) collective-permute-start(bf16[32,256]{1,0:T(8,128)(2,1)} %bitcast.31), channel_id=1, source_target_pairs={{0,3},{1,2},{2,1},{3,0},{4,7},{5,6},{6,5},{7,4},{8,11},{9,10},{10,... | collective-permute-start | bytes 49160 | tf_op jit(solution)/shard_map/ppermute | solution.py:334
  10.8 7.6 %collective-permute-start.3 = (bf16[32,256]{1,0:T(8,128)(2,1)}, bf16[32,256]{1,0:T(8,128)(2,1)S(1)}, u32[]{:S(2)}, u32[]{:S(2)}) collective-permute-start(bf16[32,256]{1,0:T(8,128)(2,1)} %bitcast.32), channel_id=1, source_target_pairs={{0,2},{1,3},{2,0},{3,1},{4,6},{5,7},{6,4},{7,5},{8,10},{9,11},{10,... | collective-permute-start | bytes 49160 | tf_op jit(solution)/shard_map/ppermute | solution.py:334
  12.3 6.1 %collective-permute-start.2 = (bf16[32,256]{1,0:T(8,128)(2,1)}, bf16[32,256]{1,0:T(8,128)(2,1)S(1)}, u32[]{:S(2)}, u32[]{:S(2)}) collective-permute-start(bf16[32,256]{1,0:T(8,128)(2,1)} %bitcast.33), channel_id=1, source_target_pairs={{0,1},{1,0},{2,3},{3,2},{4,5},{5,4},{6,7},{7,6},{8,9},{9,8},{10,11... | collective-permute-start | bytes 49160 | tf_op jit(solution)/shard_map/ppermute | solution.py:334
  20.7 2.1 %collective-permute-start.5 = (bf16[8,72,256]{2,1,0:T(8,128)(2,1)S(1)}, bf16[8,72,256]{2,1,0:T(8,128)(2,1)S(1)}, u32[]{:S(2)}, u32[]{:S(2)}) collective-permute-start(bf16[8,72,256]{2,1,0:T(8,128)(2,1)S(1)} %all-to-all-done.own.refs_0_), channel_id=1, source_target_pairs={{0,1},{1,0},{2,3},{3,2},{4,5},{5,4},{6,7},{7,6},{8,9},{9,8},{10,11... | collective-permute-start | bytes 884744 | tf_op jit(solution)/shard_map/ppermute | solution.py:334
  20.7 6.7 %collective-permute-start.6 = (bf16[4,72,256]{2,1,0:T(8,128)(2,1)S(1)}, bf16[4,72,256]{2,1,0:T(8,128)(2,1)S(1)}, u32[]{:S(2)}, u32[]{:S(2)}) collective-permute-start(bf16[4,72,256]{2,1,0:T(8,128)(2,1)S(1)} %get-tuple-element.112), channel_id=1, source_target_pairs={{0,2},{1,3},{2,0},{3,1},{4,6},{5,7},{6,4},{7,5},{8,10},{9,11},{10,... | collective-permute-start | bytes 442376 | tf_op jit(solution)/shard_map/ppermute | solution.py:334
  21.3 8.9 %collective-permute-start.8 = (bf16[4,72,256]{2,1,0:T(8,128)(2,1)S(1)}, bf16[4,72,256]{2,1,0:T(8,128)(2,1)S(1)}, u32[]{:S(2)}, u32[]{:S(2)}) collective-permute-start(bf16[4,72,256]{2,1,0:T(8,128)(2,1)S(1)} %get-tuple-element.111), channel_id=1, source_target_pairs={{0,2},{1,3},{2,0},{3,1},{4,6},{5,7},{6,4},{7,5},{8,10},{9,11},{10,... | collective-permute-start | bytes 442376 | tf_op jit(solution)/shard_map/ppermute | solution.py:334
  27.4 2.8 %collective-permute-start.7 = (bf16[4,72,256]{2,1,0:T(8,128)(2,1)S(1)}, bf16[4,72,256]{2,1,0:T(8,128)(2,1)S(1)}, u32[]{:S(2)}, u32[]{:S(2)}) collective-permute-start(bf16[4,72,256]{2,1,0:T(8,128)(2,1)S(1)} %collective-permute-done.6.refs_2_), channel_id=1, source_target_pairs={{0,1},{1,0},{2,3},{3,2},{4,5},{5,4},{6,7},{7,6},{8,9},{9,8},{10,11... | collective-permute-start | bytes 442376 | tf_op jit(solution)/shard_map/ppermute | solution.py:334
  30.2 4.3 %collective-permute-start.10 = (bf16[4,72,256]{2,1,0:T(8,128)(2,1)S(1)}, bf16[4,72,256]{2,1,0:T(8,128)(2,1)S(1)}, u32[]{:S(2)}, u32[]{:S(2)}) collective-permute-start(bf16[4,72,256]{2,1,0:T(8,128)(2,1)S(1)} %collective-permute-done.8.refs_2_), channel_id=1, source_target_pairs={{0,1},{1,0},{2,3},{3,2},{4,5},{5,4},{6,7},{7,6},{8,9},{9,8},{10,11... | collective-permute-start | bytes 442376 | tf_op jit(solution)/shard_map/ppermute | solution.py:334
  33.3 7.4 %copy-start.2 = (bf16[256,1024]{1,0:T(8,128)(2,1)S(1)}, bf16[256,1024]{1,0:T(8,128)(2,1)}, u32[]{:S(2)}) copy-start(bf16[256,1024]{1,0:T(8,128)(2,1)} %refs_4_.3) | copy-start | bytes 1572868
  33.3 7.4 %copy-start.3 = (bf16[32,1024]{1,0:T(8,128)(2,1)S(1)}, bf16[32,1024]{1,0:T(8,128)(2,1)}, u32[]{:S(2)}) copy-start(bf16[32,1024]{1,0:T(8,128)(2,1)} %refs_14_.3) | copy-start | bytes 196612
  33.3 7.4 %copy-start.4 = (bf16[1024,32]{0,1:T(8,128)(2,1)S(1)}, bf16[1024,32]{0,1:T(8,128)(2,1)}, u32[]{:S(2)}) copy-start(bf16[1024,32]{0,1:T(8,128)(2,1)} %param.32) | copy-start | bytes 196612
  33.3 7.4 %copy-start.5 = (bf16[32,1024]{1,0:T(8,128)(2,1)S(1)}, bf16[32,1024]{1,0:T(8,128)(2,1)}, u32[]{:S(2)}) copy-start(bf16[32,1024]{1,0:T(8,128)(2,1)} %refs_16_.3) | copy-start | bytes 196612
  33.3 7.4 %copy-start.6 = (bf16[1024,32]{0,1:T(8,128)(2,1)S(1)}, bf16[1024,32]{0,1:T(8,128)(2,1)}, u32[]{:S(2)}) copy-start(bf16[1024,32]{0,1:T(8,128)(2,1)} %param.34) | copy-start | bytes 196612
  33.3 7.4 %copy-start.7 = (bf16[32,1024]{1,0:T(8,128)(2,1)S(1)}, bf16[32,1024]{1,0:T(8,128)(2,1)}, u32[]{:S(2)}) copy-start(bf16[32,1024]{1,0:T(8,128)(2,1)} %refs_18_.3) | copy-start | bytes 196612
  33.3 7.4 %copy-start.8 = (bf16[256,32]{0,1:T(8,128)(2,1)S(1)}, bf16[256,32]{0,1:T(8,128)(2,1)}, u32[]{:S(2)}) copy-start(bf16[256,32]{0,1:T(8,128)(2,1)} %param.30) | copy-start | bytes 49156
  33.4 7.4 %copy-start.9 = (f32[1024]{0:T(1024)S(1)}, f32[1024]{0:T(1024)}, u32[]{:S(2)}) copy-start(f32[1024]{0:T(1024)} %param.36) | copy-start | bytes 12292
  33.4 7.4 %copy-start.10 = (f32[1024]{0:T(1024)S(1)}, f32[1024]{0:T(1024)}, u32[]{:S(2)}) copy-start(f32[1024]{0:T(1024)} %param.37) | copy-start | bytes 12292
  33.4 6.0 %collective-permute-start.9 = (bf16[256,256]{1,0:T(8,128)(2,1)S(1)}, bf16[256,256]{1,0:T(8,128)(2,1)S(1)}, u32[]{:S(2)}, u32[]{:S(2)}) collective-permute-start(bf16[256,256]{1,0:T(8,128)(2,1)S(1)} %get-tuple-element.84.refs_0_), channel_id=1, source_target_pairs={{0,2},{1,3},{2,0},{3,1},{4,6},{5,7},{6,4},{7,5},{8,10},{9,11},{10,... | collective-permute-start | bytes 393224 | tf_op jit(solution)/shard_map/ppermute | solution.py:334
  34.0 5.9 %collective-permute-start.14 = (bf16[256,256]{1,0:T(8,128)(2,1)S(1)}, bf16[256,256]{1,0:T(8,128)(2,1)S(1)}, u32[]{:S(2)}, u32[]{:S(2)}) collective-permute-start(bf16[256,256]{1,0:T(8,128)(2,1)S(1)} %get-tuple-element.84.refs_0_), channel_id=1, source_target_pairs={{0,1},{1,0},{2,3},{3,2},{4,5},{5,4},{6,7},{7,6},{8,9},{9,8},{10,11... | collective-permute-start | bytes 393224 | tf_op jit(solution)/shard_map/ppermute | solution.py:334
  34.2 6.5 %collective-permute-start.16 = (bf16[256,1024]{1,0:T(8,128)(2,1)S(1)}, bf16[256,1024]{1,0:T(8,128)(2,1)S(1)}, u32[]{:S(2)}, u32[]{:S(2)}) collective-permute-start(bf16[256,1024]{1,0:T(8,128)(2,1)S(1)} %collective-permute-done.refs_6_), channel_id=1, source_target_pairs={{0,1},{1,0},{2,3},{3,2},{4,5},{5,4},{6,7},{7,6},{8,9},{9,8},{10,11... | collective-permute-start | bytes 1572872 | tf_op jit(solution)/shard_map/ppermute | solution.py:334
  39.4 1.3 %collective-permute-start.15 = (bf16[256,256]{1,0:T(8,128)(2,1)S(1)}, bf16[256,256]{1,0:T(8,128)(2,1)S(1)}, u32[]{:S(2)}, u32[]{:S(2)}) collective-permute-start(bf16[256,256]{1,0:T(8,128)(2,1)S(1)} %collective-permute-done.9.refs_2_), channel_id=1, source_target_pairs={{0,1},{1,0},{2,3},{3,2},{4,5},{5,4},{6,7},{7,6},{8,9},{9,8},{10,11... | collective-permute-start | bytes 393224 | tf_op jit(solution)/shard_map/ppermute | solution.py:334
  39.4 6.5 %collective-permute-start.12 = (bf16[256,256]{1,0:T(8,128)(2,1)S(1)}, bf16[256,256]{1,0:T(8,128)(2,1)S(1)}, u32[]{:S(2)}, u32[]{:S(2)}) collective-permute-start(bf16[256,256]{1,0:T(8,128)(2,1)S(1)} %get-tuple-element.97.refs_0_), channel_id=1, source_target_pairs={{0,2},{1,3},{2,0},{3,1},{4,6},{5,7},{6,4},{7,5},{8,10},{9,11},{10,... | collective-permute-start | bytes 393224 | tf_op jit(solution)/shard_map/ppermute | solution.py:334
  45.3 1.4 %collective-permute-start.17 = (bf16[1,64,1024]{2,1,0:T(8,128)(2,1)S(1)}, bf16[1,64,1024]{2,1,0:T(8,128)(2,1)S(1)}, u32[]{:S(2)}, u32[]{:S(2)}) collective-permute-start(bf16[1,64,1024]{2,1,0:T(8,128)(2,1)S(1)} %get-tuple-element.96), channel_id=1, source_target_pairs={{0,1},{1,0},{2,3},{3,2},{4,5},{5,4},{6,7},{7,6},{8,9},{9,8},{10,11... | collective-permute-start | bytes 393224 | tf_op jit(solution)/shard_map/ppermute | solution.py:334
  45.5 1.4 %collective-permute-start.11 = (bf16[256,256]{1,0:T(8,128)(2,1)S(1)}, bf16[256,256]{1,0:T(8,128)(2,1)S(1)}, u32[]{:S(2)}, u32[]{:S(2)}) collective-permute-start(bf16[256,256]{1,0:T(8,128)(2,1)S(1)} %get-tuple-element.97.refs_0_), channel_id=1, source_target_pairs={{0,1},{1,0},{2,3},{3,2},{4,5},{5,4},{6,7},{7,6},{8,9},{9,8},{10,11... | collective-permute-start | bytes 393224 | tf_op jit(solution)/shard_map/ppermute | solution.py:334
  45.8 1.3 %collective-permute-start.13 = (bf16[256,256]{1,0:T(8,128)(2,1)S(1)}, bf16[256,256]{1,0:T(8,128)(2,1)S(1)}, u32[]{:S(2)}, u32[]{:S(2)}) collective-permute-start(bf16[256,256]{1,0:T(8,128)(2,1)S(1)} %collective-permute-done.12.refs_2_), channel_id=1, source_target_pairs={{0,1},{1,0},{2,3},{3,2},{4,5},{5,4},{6,7},{7,6},{8,9},{9,8},{10,11... | collective-permute-start | bytes 393224 | tf_op jit(solution)/shard_map/ppermute | solution.py:334
  46.0 7.0 %collective-permute-start.19 = (bf16[64,1024]{1,0:T(8,128)(2,1)S(1)}, bf16[64,1024]{1,0:T(8,128)(2,1)S(1)}, u32[]{:S(2)}, u32[]{:S(2)}) collective-permute-start(bf16[64,1024]{1,0:T(8,128)(2,1)S(1)} %get-tuple-element.103), channel_id=1, source_target_pairs={{0,1},{1,0},{2,3},{3,2},{4,5},{5,4},{6,7},{7,6},{8,9},{9,8},{10,11... | collective-permute-start | bytes 393224 | tf_op jit(solution)/shard_map/ppermute | solution.py:334
  47.2 5.8 %collective-permute-start.20 = (bf16[64,1024]{1,0:T(8,128)(2,1)S(1)}, bf16[64,1024]{1,0:T(8,128)(2,1)S(1)}, u32[]{:S(2)}, u32[]{:S(2)}) collective-permute-start(bf16[64,1024]{1,0:T(8,128)(2,1)S(1)} %fusion), channel_id=1, source_target_pairs={{0,2},{1,3},{2,0},{3,1},{4,6},{5,7},{6,4},{7,5},{8,10},{9,11},{10,... | collective-permute-start | bytes 393224 | tf_op jit(solution)/shard_map/ppermute | solution.py:334
  47.9 5.1 %copy-start = (f32[1024]{0:T(1024)S(1)}, f32[1024]{0:T(1024)}, u32[]{:S(2)}) copy-start(f32[1024]{0:T(1024)} %param.38) | copy-start | bytes 12292
  47.9 5.1 %copy-start.1 = (f32[1024]{0:T(1024)S(1)}, f32[1024]{0:T(1024)}, u32[]{:S(2)}) copy-start(f32[1024]{0:T(1024)} %param.39) | copy-start | bytes 12292
  52.4 1.4 %collective-permute-start.18 = (bf16[1,64,1024]{2,1,0:T(8,128)(2,1)S(1)}, bf16[1,64,1024]{2,1,0:T(8,128)(2,1)S(1)}, u32[]{:S(2)}, u32[]{:S(2)}) collective-permute-start(bf16[1,64,1024]{2,1,0:T(8,128)(2,1)S(1)} %get-tuple-element.102), channel_id=1, source_target_pairs={{0,1},{1,0},{2,3},{3,2},{4,5},{5,4},{6,7},{7,6},{8,9},{9,8},{10,11... | collective-permute-start | bytes 393224 | tf_op jit(solution)/shard_map/ppermute | solution.py:334
  52.4 2.8 %collective-permute-start.21 = (bf16[64,1024]{1,0:T(8,128)(2,1)S(1)}, bf16[64,1024]{1,0:T(8,128)(2,1)S(1)}, u32[]{:S(2)}, u32[]{:S(2)}) collective-permute-start(bf16[64,1024]{1,0:T(8,128)(2,1)S(1)} %get-tuple-element.108), channel_id=1, source_target_pairs={{0,1},{1,0},{2,3},{3,2},{4,5},{5,4},{6,7},{7,6},{8,9},{9,8},{10,11... | collective-permute-start | bytes 393224 | tf_op jit(solution)/shard_map/ppermute | solution.py:334
  53.8 5.6 %collective-permute-start.22 = (bf16[64,1024]{1,0:T(8,128)(2,1)S(1)}, bf16[64,1024]{1,0:T(8,128)(2,1)S(1)}, u32[]{:S(2)}, u32[]{:S(2)}) collective-permute-start(bf16[64,1024]{1,0:T(8,128)(2,1)S(1)} %fusion.1), channel_id=1, source_target_pairs={{0,2},{1,3},{2,0},{3,1},{4,6},{5,7},{6,4},{7,5},{8,10},{9,11},{10,... | collective-permute-start | bytes 393224 | tf_op jit(solution)/shard_map/ppermute | solution.py:334

commit v13 on v8

--- a/solution.py
+++ b/solution.py
@@ -417,6 +417,8 @@
     w_all, w1, w2, downs, up_all = near(w_all, w1, w2, downs, up_all)
     x_far[0], begun = lax.optimization_barrier((x_far[0], begun))
     x_far[0] = second_hop(x_far[0])
+    x_far = lax.optimization_barrier(x_far)
+    x_far[1:] = [second_hop(pieces) for pieces in x_far[1:]]
 
     consts = near(
         out_up, fc1_down.T, fc1_up, fc2_down.T, fc2_up, norm1_gain[None], norm1_bias[None]
@@ -425,17 +427,14 @@
     steps = []
     for c in range(count):
         if c:
-            x_far[c], w_far, steps[0][0] = lax.optimization_barrier(
-                (x_far[c], w_far, steps[0][0])
-            )
-            x_far[c] = second_hop(x_far[c])
+            w_far, steps[0][0] = lax.optimization_barrier((w_far, steps[0][0]))
         attended, x_full = pl.pallas_call(
             functools.partial(attn_kernel, n_tp, c),
             out_shape=[pltpu.VMEM((rows, width), BF), pltpu.VMEM((rows, feat), BF)],
             in_specs=[SMEM] + [VM] * (n_tp + 7),
             out_specs=[VM] * 2,
             compiler_params=params(12),
-            cost_estimate=work(2 * rows * feat * 3 * width + 4 * rows * width * 2 * CAP, rows),
+            cost_estimate=work(8 * rows * feat * 3 * width + 16 * rows * width * 2 * CAP, rows),
             name="attend",
         )(me, *near(arrived, beside, *x_far[c], *begun), w_all, downs, up_all)
         y_got = [swap(attended, 2 * y) for y in range(1, half)]

time: 75.4 us -> 75.2 us (level)
  waiting for transfers between devices: 22.9 us -> 21.1 us
  starting transfers between devices: 17.1 us -> 18.2 us
    all_to_all x1, waiting for transfers between devices: 3.39 us -> 2.27 us  [body(): lax.all_to_all(packed, 'req', split_axis=0, concat_axis=0, tiled=True)]
    ppermute x23, starting transfers between devices: 11.3 us -> 12.4 us  [swap(): return lax.ppermute(value, 'tp', [(i, i ^ r) for i in range(n_tp)])]
  transfers between devices with their start and end apart: 24 -> 24, of which waited for: 14 -> 12; matrix products, arithmetic and copies ran while one was open for 0% -> 0% of each run, Pallas kernels for 23% -> 23%
where the time goes in v13:
time: 75.2 us; the launch traced here: 74.9 us
  waiting for transfers between devices  21.1 us (28%)
  Pallas kernels  20.9 us (28%)
  starting transfers between devices  18.2 us (24%)
  blocking collectives  14.3 us (19%)
    ppermute x23, waiting for transfers between devices, swap(): return lax.ppermute(value, 'tp', [(i, i ^ r) for i in range(n_tp)])  18.8 us
    all_to_all x1, blocking collectives, body(): lax.all_to_all(done.reshape(n_req * n_tp, share, width), ('req', 'tp'), s...  14.3 us
    ppermute x23, starting transfers between devices, swap(): return lax.ppermute(value, 'tp', [(i, i ^ r) for i in range(n_tp)])  12.4 us
    pallas_call x2, Pallas kernels, body(): pl.pallas_call(functools.partial(ffn_kernel, n_tp, c), out_shape=[pltpu.V...  8.94 us
    all_to_all x1, starting transfers between devices, body(): lax.all_to_all(packed, 'req', split_axis=0, concat_axis=0, tiled=True)  5.81 us
    pallas_call x2, Pallas kernels, body(): pl.pallas_call(functools.partial(attn_kernel, n_tp, c), out_shape=[pltpu....  5.52 us
    pallas_call x1, Pallas kernels, body(): pl.pallas_call(begin_kernel, out_shape=[pltpu.VMEM((3, count * rows, widt...  2.86 us
    all_to_all x1, waiting for transfers between devices, body(): lax.all_to_all(packed, 'req', split_axis=0, concat_axis=0, tiled=True)  2.27 us
  transfers between devices with their start and end apart: 24, of which 12 were waited for; matrix products, arithmetic and copies ran while one was open for 0% of the time, Pallas kernels for 23%

profile of v13, /device:TPU:0, one launch (start us, length us, event | category | flops | bytes accessed | tf_op | source)
XLA Modules:
  0.0 74.9 jit_solution(10739025122250170628)
XLA Ops:
  0.0 1.8 %pack.1 = (bf16[8,72,256]{2,1,0:T(8,128)(2,1)}, s32[8]{0:T(128)S(1)}) custom-call(s32[4,8]{1,0:T(4,128)} %bitcast.42, s32[4,8]{1,0:T(4,128)} %bitcast.43, s32[16]{0:T(128)} %slots_in.1, bf16[8,64,256]{2,1,0:T(8,128)(2,1)} %bitcast.40), custom_call_target="tpu_custom_call" | custom-call | tf_op jit(solution)/shard_map/pack/pallas_call | solution.py:342
  1.8 0.5 collective-permute-start.1
  2.4 2.6 %collective-permute-start = (bf16[256,1024]{1,0:T(8,128)(2,1)}, bf16[256,1024]{1,0:T(8,128)(2,1)S(1)}, u32[]{:S(2)}, u32[]{:S(2)}) collective-permute-start(bf16[256,1024]{1,0:T(8,128)(2,1)} %refs_4_.3), channel_id=1, source_target_pairs={{0,2},{1,3},{2,0},{3,1},{4,6},{5,7},{6,4},{7,5},{8,10},{9,11},{10,... | collective-permute-start | bytes 1572872 | tf_op jit(solution)/shard_map/ppermute | solution.py:337
  5.0 5.8 %all-to-all-start = ((bf16[8,72,256]{2,1,0:T(8,128)(2,1)}), bf16[8,72,256]{2,1,0:T(8,128)(2,1)S(1)}, u32[]{:S(2)}, u32[]{:S(2)}) async-start(bf16[8,72,256]{2,1,0:T(8,128)(2,1)} %get-tuple-element.61), calls=%async_computation | async-start | bytes 589824 | tf_op jit(solution)/shard_map/all_to_all | solution.py:370
  10.8 1.5 %collective-permute-start.3 = (bf16[32,256]{1,0:T(8,128)(2,1)}, bf16[32,256]{1,0:T(8,128)(2,1)S(1)}, u32[]{:S(2)}, u32[]{:S(2)}) collective-permute-start(bf16[32,256]{1,0:T(8,128)(2,1)} %bitcast.32), channel_id=1, source_target_pairs={{0,2},{1,3},{2,0},{3,1},{4,6},{5,7},{6,4},{7,5},{8,10},{9,11},{10,... | collective-permute-start | bytes 49160 | tf_op jit(solution)/shard_map/ppermute | solution.py:337
  12.3 0.3 collective-permute-start.2
  12.6 5.1 %collective-permute-done.4.refs_11_ = bf16[32,256]{1,0:T(8,128)(2,1)S(1)} collective-permute-done((bf16[32,256]{1,0:T(8,128)(2,1)}, bf16[32,256]{1,0:T(8,128)(2,1)S(1)}, u32[]{:S(2)}, u32[]{:S(2)}) %collective-permute-start.4) | collective-permute-done | bytes 16416 | tf_op jit(solution)/shard_map/ppermute | solution.py:337
  17.8 0.6 collective-permute-done.3.refs_10_
  18.4 2.3 %all-to-all-done.own.refs_0_ = bf16[8,72,256]{2,1,0:T(8,128)(2,1)S(1)} async-done(((bf16[8,72,256]{2,1,0:T(8,128)(2,1)}), bf16[8,72,256]{2,1,0:T(8,128)(2,1)S(1)}, u32[]{:S(2)}, u32[]{:S(2)}) %all-to-all-start) | async-done | bytes 294944 | tf_op jit(solution)/shard_map/all_to_all | solution.py:370
  20.7 0.6 collective-permute-start.6
  21.3 1.5 %collective-permute-start.8 = (bf16[4,72,256]{2,1,0:T(8,128)(2,1)S(1)}, bf16[4,72,256]{2,1,0:T(8,128)(2,1)S(1)}, u32[]{:S(2)}, u32[]{:S(2)}) collective-permute-start(bf16[4,72,256]{2,1,0:T(8,128)(2,1)S(1)} %get-tuple-element.111), channel_id=1, source_target_pairs={{0,2},{1,3},{2,0},{3,1},{4,6},{5,7},{6,4},{7,5},{8,10},{9,11},{10,... | collective-permute-start | bytes 442376 | tf_op jit(solution)/shard_map/ppermute | solution.py:337
  22.8 2.9 %begin.1 = (f32[3,512,256]{2,1,0:T(8,128)S(1)}, f32[512,96]{1,0:T(8,128)S(1)}, bf16[512,128]{1,0:T(8,128)(2,1)S(1)}, f32[512,128]{1,0:T(8,128)S(1)}, bf16[3,1024...) custom-call(s32[1]{0:T(128)} %bitcast.3.me, ...), custom_call_target="tpu_custom_call" | custom-call | flops 1006632960 | bytes 2097152 | tf_op jit(solution)/shard_map/begin/pallas_call | solution.py:384
  25.7 1.7 %collective-permute-done.6.refs_2_ = bf16[4,72,256]{2,1,0:T(8,128)(2,1)S(1)} collective-permute-done((bf16[4,72,256]{2,1,0:T(8,128)(2,1)S(1)}, bf16[4,72,256]{2,1,0:T(8,128)(2,1)S(1)}, u32[]{:S(2)}, u32[]{:S(2)}) %collective-permute-start.6) | collective-permute-done | bytes 147488 | tf_op jit(solution)/shard_map/ppermute | solution.py:337
  27.4 2.8 %collective-permute-done.8.refs_2_ = bf16[4,72,256]{2,1,0:T(8,128)(2,1)S(1)} collective-permute-done((bf16[4,72,256]{2,1,0:T(8,128)(2,1)S(1)}, bf16[4,72,256]{2,1,0:T(8,128)(2,1)S(1)}, u32[]{:S(2)}, u32[]{:S(2)}) %collective-permute-start.8) | collective-permute-done | bytes 147488 | tf_op jit(solution)/shard_map/ppermute | solution.py:337
  30.2 2.8 %attend.2 = (bf16[256,256]{1,0:T(8,128)(2,1)S(1)}, bf16[256,1024]{1,0:T(8,128)(2,1)S(1)}) custom-call(s32[1]{0:T(128)} %bitcast.3.me, bf16[8,72,256]{2,1,0:T(8,128)(2,1)S(1)} %all-to-all-done.own.refs_0_, bf16[8,72,256]{2,1,0:T(8,128)(2,1)S(1)} %collective-permute-done.5.beside.refs_1_, bf16[4,72,256]{2,1,0:T(8,128)(2,1)S(1)} %collective-permute-done.6.refs_2_, ...), custom_call_target="tpu_custom_call" | custom-call | flops 8724152320 | bytes 2097152 | tf_op jit(solution)/shard_map/attend/pallas_call | solution.py:431
  33.0 0.0 copy-start.2
  33.0 0.0 copy-start.3
  33.0 0.0 copy-start.4
  33.0 0.0 copy-start.5
  33.0 0.0 copy-start.6
  33.0 0.0 copy-start.8
  33.0 0.0 copy-start.9
  33.1 0.6 collective-permute-start.9
  33.6 0.2 collective-permute-start.14
  33.9 0.3 collective-permute-start.16
  34.2 2.8 %attend.3 = (bf16[256,256]{1,0:T(8,128)(2,1)S(1)}, bf16[256,1024]{1,0:T(8,128)(2,1)S(1)}) custom-call(s32[1]{0:T(128)} %bitcast.3.me, bf16[8,72,256]{2,1,0:T(8,128)(2,1)S(1)} %all-to-all-done.own.refs_0_, bf16[8,72,256]{2,1,0:T(8,128)(2,1)S(1)} %collective-permute-done.5.beside.refs_1_, bf16[4,72,256]{2,1,0:T(8,128)(2,1)S(1)} %collective-permute-done.8.refs_2_, ...), custom_call_target="tpu_custom_call" | custom-call | flops 8724152320 | bytes 2097152 | tf_op jit(solution)/shard_map/attend/pallas_call | solution.py:431
  36.9 2.1 %collective-permute-done.9.refs_2_ = bf16[256,256]{1,0:T(8,128)(2,1)S(1)} collective-permute-done((bf16[256,256]{1,0:T(8,128)(2,1)S(1)}, bf16[256,256]{1,0:T(8,128)(2,1)S(1)}, u32[]{:S(2)}, u32[]{:S(2)}) %collective-permute-start.9) | collective-permute-done | bytes 131104 | tf_op jit(solution)/shard_map/ppermute | solution.py:337
  39.1 0.5 collective-permute-start.12
  39.6 0.8 %collective-permute-done.15.refs_3_ = bf16[256,256]{1,0:T(8,128)(2,1)S(1)} collective-permute-done((bf16[256,256]{1,0:T(8,128)(2,1)S(1)}, bf16[256,256]{1,0:T(8,128)(2,1)S(1)}, u32[]{:S(2)}, u32[]{:S(2)}) %collective-permute-start.15) | collective-permute-done | bytes 131104 | tf_op jit(solution)/shard_map/ppermute | solution.py:337
  40.5 4.5 %feed.2 = (f32[2,64,1024]{2,1,0:T(8,128)S(1)}, bf16[64,1024]{1,0:T(8,128)(2,1)S(1)}, bf16[1,64,1024]{2,1,0:T(8,128)(2,1)S(1)}, bf16[64,1024]{1,0:T(8,128)(2,1)S(1)}) custom-call(s32[1]{0:T(128)} %bitcast.3.me, bf16[256,256]{1,0:T(8,128)(2,1)S(1)} %get-tuple-element.84.refs_0_, bf16[256,256]{1,0:T(8,128)(2,1)S(1)} %collective-permute-done.14.refs_1_, ...), custom_call_target="tpu_custom_call" | custom-call | flops 8053063680 | bytes 2097152 | tf_op jit(solution)/shard_map/feed/pallas_call | solution.py:464
  45.0 0.2 collective-permute-start.17
  45.2 0.4 collective-permute-start.11
  45.5 0.1 collective-permute-start.13
  45.7 0.4 collective-permute-start.19
  46.0 0.3 collective-permute-done.17
  46.4 0.2 collective-permute-done.11.refs_1_
  46.6 0.3 collective-permute-done.13.refs_3_
  46.9 0.7 collective-permute-start.20
  47.6 4.5 %feed.3 = (f32[2,64,1024]{2,1,0:T(8,128)S(1)}, bf16[64,1024]{1,0:T(8,128)(2,1)S(1)}, bf16[1,64,1024]{2,1,0:T(8,128)(2,1)S(1)}, bf16[64,1024]{1,0:T(8,128)(2,1)S(1)}) custom-call(s32[1]{0:T(128)} %bitcast.3.me, bf16[256,256]{1,0:T(8,128)(2,1)S(1)} %get-tuple-element.97.refs_0_, bf16[256,256]{1,0:T(8,128)(2,1)S(1)} %collective-permute-done.11.refs_1_, ...), custom_call_target="tpu_custom_call" | custom-call | flops 8053063680 | bytes 2097152 | tf_op jit(solution)/shard_map/feed/pallas_call | solution.py:464
  52.1 0.1 collective-permute-start.18
  52.2 0.5 collective-permute-start.21
  52.7 0.2 finish.2.refs_0_
  52.9 0.6 collective-permute-done.18
  53.5 1.4 %collective-permute-start.22 = (bf16[64,1024]{1,0:T(8,128)(2,1)S(1)}, bf16[64,1024]{1,0:T(8,128)(2,1)S(1)}, u32[]{:S(2)}, u32[]{:S(2)}) collective-permute-start(bf16[64,1024]{1,0:T(8,128)(2,1)S(1)} %fusion.1), channel_id=1, source_target_pairs={{0,2},{1,3},{2,0},{3,1},{4,6},{5,7},{6,4},{7,5},{8,10},{9,11},{10,... | collective-permute-start | bytes 393224 | tf_op jit(solution)/shard_map/ppermute | solution.py:337
  54.9 4.2 %collective-permute-done.22.refs_4_ = bf16[64,1024]{1,0:T(8,128)(2,1)S(1)} collective-permute-done((bf16[64,1024]{1,0:T(8,128)(2,1)S(1)}, bf16[64,1024]{1,0:T(8,128)(2,1)S(1)}, u32[]{:S(2)}, u32[]{:S(2)}) %collective-permute-start.22) | collective-permute-done | bytes 131104 | tf_op jit(solution)/shard_map/ppermute | solution.py:337
  59.1 0.2 finish.3
  59.4 14.3 %all_to_all.10 = bf16[32,16,256]{2,1,0:T(8,128)(2,1)S(1)} all-to-all(bf16[32,16,256]{2,1,0:T(8,128)(2,1)S(1)} %bitcast.21), channel_id=1, replica_groups=mesh['req'=8,'tp'=4] {'req','tp'}, dimensions={0} | all-to-all | bytes 524288 | tf_op jit(solution)/shard_map/all_to_all | solution.py:490
  73.7 1.3 %unpack.1 = bf16[8,64,256]{2,1,0:T(8,128)(2,1)} custom-call(s32[8]{0:T(128)S(1)} %get-tuple-element.58.owners, bf16[8,64,256]{2,1,0:T(8,128)(2,1)S(1)} %bitcast.22), custom_call_target="tpu_custom_call" | custom-call | tf_op jit(solution)/shard_map/unpack/pallas_call | solution.py:497
  (35 shorter events, 0.2 us)
Async XLA Ops:
  1.8 18.8 %collective-permute-start.1 = (bf16[256,1024]{1,0:T(8,128)(2,1)}, bf16[256,1024]{1,0:T(8,128)(2,1)S(1)}, u32[]{:S(2)}, u32[]{:S(2)}) collective-permute-start(bf16[256,1024]{1,0:T(8,128)(2,1)} %refs_4_.3), channel_id=1, source_target_pairs={{0,1},{1,0},{2,3},{3,2},{4,5},{5,4},{6,7},{7,6},{8,9},{9,8},{10,11... | collective-permute-start | bytes 1572872 | tf_op jit(solution)/shard_map/ppermute | solution.py:337
  2.4 18.3 %collective-permute-start = (bf16[256,1024]{1,0:T(8,128)(2,1)}, bf16[256,1024]{1,0:T(8,128)(2,1)S(1)}, u32[]{:S(2)}, u32[]{:S(2)}) collective-permute-start(bf16[256,1024]{1,0:T(8,128)(2,1)} %refs_4_.3), channel_id=1, source_target_pairs={{0,2},{1,3},{2,0},{3,1},{4,6},{5,7},{6,4},{7,5},{8,10},{9,11},{10,... | collective-permute-start | bytes 1572872 | tf_op jit(solution)/shard_map/ppermute | solution.py:337
  5.0 15.7 %all-to-all-start = ((bf16[8,72,256]{2,1,0:T(8,128)(2,1)}), bf16[8,72,256]{2,1,0:T(8,128)(2,1)S(1)}, u32[]{:S(2)}, u32[]{:S(2)}) async-start(bf16[8,72,256]{2,1,0:T(8,128)(2,1)} %get-tuple-element.61), calls=%async_computation | async-start | bytes 589824 | tf_op jit(solution)/shard_map/all_to_all | solution.py:370
  10.8 7.0 %collective-permute-start.4 = (bf16[32,256]{1,0:T(8,128)(2,1)}, bf16[32,256]{1,0:T(8,128)(2,1)S(1)}, u32[]{:S(2)}, u32[]{:S(2)}) collective-permute-start(bf16[32,256]{1,0:T(8,128)(2,1)} %bitcast.31), channel_id=1, source_target_pairs={{0,3},{1,2},{2,1},{3,0},{4,7},{5,6},{6,5},{7,4},{8,11},{9,10},{10,... | collective-permute-start | bytes 49160 | tf_op jit(solution)/shard_map/ppermute | solution.py:337
  10.8 7.6 %collective-permute-start.3 = (bf16[32,256]{1,0:T(8,128)(2,1)}, bf16[32,256]{1,0:T(8,128)(2,1)S(1)}, u32[]{:S(2)}, u32[]{:S(2)}) collective-permute-start(bf16[32,256]{1,0:T(8,128)(2,1)} %bitcast.32), channel_id=1, source_target_pairs={{0,2},{1,3},{2,0},{3,1},{4,6},{5,7},{6,4},{7,5},{8,10},{9,11},{10,... | collective-permute-start | bytes 49160 | tf_op jit(solution)/shard_map/ppermute | solution.py:337
  12.3 6.1 %collective-permute-start.2 = (bf16[32,256]{1,0:T(8,128)(2,1)}, bf16[32,256]{1,0:T(8,128)(2,1)S(1)}, u32[]{:S(2)}, u32[]{:S(2)}) collective-permute-start(bf16[32,256]{1,0:T(8,128)(2,1)} %bitcast.33), channel_id=1, source_target_pairs={{0,1},{1,0},{2,3},{3,2},{4,5},{5,4},{6,7},{7,6},{8,9},{9,8},{10,11... | collective-permute-start | bytes 49160 | tf_op jit(solution)/shard_map/ppermute | solution.py:337
  20.7 2.1 %collective-permute-start.5 = (bf16[8,72,256]{2,1,0:T(8,128)(2,1)S(1)}, bf16[8,72,256]{2,1,0:T(8,128)(2,1)S(1)}, u32[]{:S(2)}, u32[]{:S(2)}) collective-permute-start(bf16[8,72,256]{2,1,0:T(8,128)(2,1)S(1)} %all-to-all-done.own.refs_0_), channel_id=1, source_target_pairs={{0,1},{1,0},{2,3},{3,2},{4,5},{5,4},{6,7},{7,6},{8,9},{9,8},{10,11... | collective-permute-start | bytes 884744 | tf_op jit(solution)/shard_map/ppermute | solution.py:337
  20.7 6.7 %collective-permute-start.6 = (bf16[4,72,256]{2,1,0:T(8,128)(2,1)S(1)}, bf16[4,72,256]{2,1,0:T(8,128)(2,1)S(1)}, u32[]{:S(2)}, u32[]{:S(2)}) collective-permute-start(bf16[4,72,256]{2,1,0:T(8,128)(2,1)S(1)} %get-tuple-element.112), channel_id=1, source_target_pairs={{0,2},{1,3},{2,0},{3,1},{4,6},{5,7},{6,4},{7,5},{8,10},{9,11},{10,... | collective-permute-start | bytes 442376 | tf_op jit(solution)/shard_map/ppermute | solution.py:337
  21.3 8.9 %collective-permute-start.8 = (bf16[4,72,256]{2,1,0:T(8,128)(2,1)S(1)}, bf16[4,72,256]{2,1,0:T(8,128)(2,1)S(1)}, u32[]{:S(2)}, u32[]{:S(2)}) collective-permute-start(bf16[4,72,256]{2,1,0:T(8,128)(2,1)S(1)} %get-tuple-element.111), channel_id=1, source_target_pairs={{0,2},{1,3},{2,0},{3,1},{4,6},{5,7},{6,4},{7,5},{8,10},{9,11},{10,... | collective-permute-start | bytes 442376 | tf_op jit(solution)/shard_map/ppermute | solution.py:337
  27.4 2.8 %collective-permute-start.7 = (bf16[4,72,256]{2,1,0:T(8,128)(2,1)S(1)}, bf16[4,72,256]{2,1,0:T(8,128)(2,1)S(1)}, u32[]{:S(2)}, u32[]{:S(2)}) collective-permute-start(bf16[4,72,256]{2,1,0:T(8,128)(2,1)S(1)} %collective-permute-done.6.refs_2_), channel_id=1, source_target_pairs={{0,1},{1,0},{2,3},{3,2},{4,5},{5,4},{6,7},{7,6},{8,9},{9,8},{10,11... | collective-permute-start | bytes 442376 | tf_op jit(solution)/shard_map/ppermute | solution.py:337
  30.2 4.0 %collective-permute-start.10 = (bf16[4,72,256]{2,1,0:T(8,128)(2,1)S(1)}, bf16[4,72,256]{2,1,0:T(8,128)(2,1)S(1)}, u32[]{:S(2)}, u32[]{:S(2)}) collective-permute-start(bf16[4,72,256]{2,1,0:T(8,128)(2,1)S(1)} %collective-permute-done.8.refs_2_), channel_id=1, source_target_pairs={{0,1},{1,0},{2,3},{3,2},{4,5},{5,4},{6,7},{7,6},{8,9},{9,8},{10,11... | collective-permute-start | bytes 442376 | tf_op jit(solution)/shard_map/ppermute | solution.py:337
  33.0 7.4 %copy-start.2 = (bf16[256,1024]{1,0:T(8,128)(2,1)S(1)}, bf16[256,1024]{1,0:T(8,128)(2,1)}, u32[]{:S(2)}) copy-start(bf16[256,1024]{1,0:T(8,128)(2,1)} %refs_4_.3) | copy-start | bytes 1572868
  33.0 7.4 %copy-start.3 = (bf16[32,1024]{1,0:T(8,128)(2,1)S(1)}, bf16[32,1024]{1,0:T(8,128)(2,1)}, u32[]{:S(2)}) copy-start(bf16[32,1024]{1,0:T(8,128)(2,1)} %refs_14_.3) | copy-start | bytes 196612
  33.0 7.4 %copy-start.4 = (bf16[1024,32]{0,1:T(8,128)(2,1)S(1)}, bf16[1024,32]{0,1:T(8,128)(2,1)}, u32[]{:S(2)}) copy-start(bf16[1024,32]{0,1:T(8,128)(2,1)} %param.32) | copy-start | bytes 196612
  33.0 7.4 %copy-start.5 = (bf16[32,1024]{1,0:T(8,128)(2,1)S(1)}, bf16[32,1024]{1,0:T(8,128)(2,1)}, u32[]{:S(2)}) copy-start(bf16[32,1024]{1,0:T(8,128)(2,1)} %refs_16_.3) | copy-start | bytes 196612
  33.0 7.4 %copy-start.6 = (bf16[1024,32]{0,1:T(8,128)(2,1)S(1)}, bf16[1024,32]{0,1:T(8,128)(2,1)}, u32[]{:S(2)}) copy-start(bf16[1024,32]{0,1:T(8,128)(2,1)} %param.34) | copy-start | bytes 196612
  33.0 7.4 %copy-start.7 = (bf16[32,1024]{1,0:T(8,128)(2,1)S(1)}, bf16[32,1024]{1,0:T(8,128)(2,1)}, u32[]{:S(2)}) copy-start(bf16[32,1024]{1,0:T(8,128)(2,1)} %refs_18_.3) | copy-start | bytes 196612
  33.0 7.4 %copy-start.8 = (bf16[256,32]{0,1:T(8,128)(2,1)S(1)}, bf16[256,32]{0,1:T(8,128)(2,1)}, u32[]{:S(2)}) copy-start(bf16[256,32]{0,1:T(8,128)(2,1)} %param.30) | copy-start | bytes 49156
  33.0 7.4 %copy-start.9 = (f32[1024]{0:T(1024)S(1)}, f32[1024]{0:T(1024)}, u32[]{:S(2)}) copy-start(f32[1024]{0:T(1024)} %param.36) | copy-start | bytes 12292
  33.1 7.4 %copy-start.10 = (f32[1024]{0:T(1024)S(1)}, f32[1024]{0:T(1024)}, u32[]{:S(2)}) copy-start(f32[1024]{0:T(1024)} %param.37) | copy-start | bytes 12292
  33.1 6.0 %collective-permute-start.9 = (bf16[256,256]{1,0:T(8,128)(2,1)S(1)}, bf16[256,256]{1,0:T(8,128)(2,1)S(1)}, u32[]{:S(2)}, u32[]{:S(2)}) collective-permute-start(bf16[256,256]{1,0:T(8,128)(2,1)S(1)} %get-tuple-element.84.refs_0_), channel_id=1, source_target_pairs={{0,2},{1,3},{2,0},{3,1},{4,6},{5,7},{6,4},{7,5},{8,10},{9,11},{10,... | collective-permute-start | bytes 393224 | tf_op jit(solution)/shard_map/ppermute | solution.py:337
  33.6 5.9 %collective-permute-start.14 = (bf16[256,256]{1,0:T(8,128)(2,1)S(1)}, bf16[256,256]{1,0:T(8,128)(2,1)S(1)}, u32[]{:S(2)}, u32[]{:S(2)}) collective-permute-start(bf16[256,256]{1,0:T(8,128)(2,1)S(1)} %get-tuple-element.84.refs_0_), channel_id=1, source_target_pairs={{0,1},{1,0},{2,3},{3,2},{4,5},{5,4},{6,7},{7,6},{8,9},{9,8},{10,11... | collective-permute-start | bytes 393224 | tf_op jit(solution)/shard_map/ppermute | solution.py:337
  33.9 6.5 %collective-permute-start.16 = (bf16[256,1024]{1,0:T(8,128)(2,1)S(1)}, bf16[256,1024]{1,0:T(8,128)(2,1)S(1)}, u32[]{:S(2)}, u32[]{:S(2)}) collective-permute-start(bf16[256,1024]{1,0:T(8,128)(2,1)S(1)} %collective-permute-done.refs_6_), channel_id=1, source_target_pairs={{0,1},{1,0},{2,3},{3,2},{4,5},{5,4},{6,7},{7,6},{8,9},{9,8},{10,11... | collective-permute-start | bytes 1572872 | tf_op jit(solution)/shard_map/ppermute | solution.py:337
  39.0 1.3 %collective-permute-start.15 = (bf16[256,256]{1,0:T(8,128)(2,1)S(1)}, bf16[256,256]{1,0:T(8,128)(2,1)S(1)}, u32[]{:S(2)}, u32[]{:S(2)}) collective-permute-start(bf16[256,256]{1,0:T(8,128)(2,1)S(1)} %collective-permute-done.9.refs_2_), channel_id=1, source_target_pairs={{0,1},{1,0},{2,3},{3,2},{4,5},{5,4},{6,7},{7,6},{8,9},{9,8},{10,11... | collective-permute-start | bytes 393224 | tf_op jit(solution)/shard_map/ppermute | solution.py:337
  39.1 6.5 %collective-permute-start.12 = (bf16[256,256]{1,0:T(8,128)(2,1)S(1)}, bf16[256,256]{1,0:T(8,128)(2,1)S(1)}, u32[]{:S(2)}, u32[]{:S(2)}) collective-permute-start(bf16[256,256]{1,0:T(8,128)(2,1)S(1)} %get-tuple-element.97.refs_0_), channel_id=1, source_target_pairs={{0,2},{1,3},{2,0},{3,1},{4,6},{5,7},{6,4},{7,5},{8,10},{9,11},{10,... | collective-permute-start | bytes 393224 | tf_op jit(solution)/shard_map/ppermute | solution.py:337
  45.0 1.4 %collective-permute-start.17 = (bf16[1,64,1024]{2,1,0:T(8,128)(2,1)S(1)}, bf16[1,64,1024]{2,1,0:T(8,128)(2,1)S(1)}, u32[]{:S(2)}, u32[]{:S(2)}) collective-permute-start(bf16[1,64,1024]{2,1,0:T(8,128)(2,1)S(1)} %get-tuple-element.96), channel_id=1, source_target_pairs={{0,1},{1,0},{2,3},{3,2},{4,5},{5,4},{6,7},{7,6},{8,9},{9,8},{10,11... | collective-permute-start | bytes 393224 | tf_op jit(solution)/shard_map/ppermute | solution.py:337
  45.2 1.4 %collective-permute-start.11 = (bf16[256,256]{1,0:T(8,128)(2,1)S(1)}, bf16[256,256]{1,0:T(8,128)(2,1)S(1)}, u32[]{:S(2)}, u32[]{:S(2)}) collective-permute-start(bf16[256,256]{1,0:T(8,128)(2,1)S(1)} %get-tuple-element.97.refs_0_), channel_id=1, source_target_pairs={{0,1},{1,0},{2,3},{3,2},{4,5},{5,4},{6,7},{7,6},{8,9},{9,8},{10,11... | collective-permute-start | bytes 393224 | tf_op jit(solution)/shard_map/ppermute | solution.py:337
  45.5 1.3 %collective-permute-start.13 = (bf16[256,256]{1,0:T(8,128)(2,1)S(1)}, bf16[256,256]{1,0:T(8,128)(2,1)S(1)}, u32[]{:S(2)}, u32[]{:S(2)}) collective-permute-start(bf16[256,256]{1,0:T(8,128)(2,1)S(1)} %collective-permute-done.12.refs_2_), channel_id=1, source_target_pairs={{0,1},{1,0},{2,3},{3,2},{4,5},{5,4},{6,7},{7,6},{8,9},{9,8},{10,11... | collective-permute-start | bytes 393224 | tf_op jit(solution)/shard_map/ppermute | solution.py:337
  45.7 7.0 %collective-permute-start.19 = (bf16[64,1024]{1,0:T(8,128)(2,1)S(1)}, bf16[64,1024]{1,0:T(8,128)(2,1)S(1)}, u32[]{:S(2)}, u32[]{:S(2)}) collective-permute-start(bf16[64,1024]{1,0:T(8,128)(2,1)S(1)} %get-tuple-element.103), channel_id=1, source_target_pairs={{0,1},{1,0},{2,3},{3,2},{4,5},{5,4},{6,7},{7,6},{8,9},{9,8},{10,11... | collective-permute-start | bytes 393224 | tf_op jit(solution)/shard_map/ppermute | solution.py:337
  46.9 5.8 %collective-permute-start.20 = (bf16[64,1024]{1,0:T(8,128)(2,1)S(1)}, bf16[64,1024]{1,0:T(8,128)(2,1)S(1)}, u32[]{:S(2)}, u32[]{:S(2)}) collective-permute-start(bf16[64,1024]{1,0:T(8,128)(2,1)S(1)} %fusion), channel_id=1, source_target_pairs={{0,2},{1,3},{2,0},{3,1},{4,6},{5,7},{6,4},{7,5},{8,10},{9,11},{10,... | collective-permute-start | bytes 393224 | tf_op jit(solution)/shard_map/ppermute | solution.py:337
  47.6 5.1 %copy-start = (f32[1024]{0:T(1024)S(1)}, f32[1024]{0:T(1024)}, u32[]{:S(2)}) copy-start(f32[1024]{0:T(1024)} %param.38) | copy-start | bytes 12292
  47.6 5.1 %copy-start.1 = (f32[1024]{0:T(1024)S(1)}, f32[1024]{0:T(1024)}, u32[]{:S(2)}) copy-start(f32[1024]{0:T(1024)} %param.39) | copy-start | bytes 12292
  52.1 1.4 %collective-permute-start.18 = (bf16[1,64,1024]{2,1,0:T(8,128)(2,1)S(1)}, bf16[1,64,1024]{2,1,0:T(8,128)(2,1)S(1)}, u32[]{:S(2)}, u32[]{:S(2)}) collective-permute-start(bf16[1,64,1024]{2,1,0:T(8,128)(2,1)S(1)} %get-tuple-element.102), channel_id=1, source_target_pairs={{0,1},{1,0},{2,3},{3,2},{4,5},{5,4},{6,7},{7,6},{8,9},{9,8},{10,11... | collective-permute-start | bytes 393224 | tf_op jit(solution)/shard_map/ppermute | solution.py:337
  52.2 2.8 %collective-permute-start.21 = (bf16[64,1024]{1,0:T(8,128)(2,1)S(1)}, bf16[64,1024]{1,0:T(8,128)(2,1)S(1)}, u32[]{:S(2)}, u32[]{:S(2)}) collective-permute-start(bf16[64,1024]{1,0:T(8,128)(2,1)S(1)} %get-tuple-element.108), channel_id=1, source_target_pairs={{0,1},{1,0},{2,3},{3,2},{4,5},{5,4},{6,7},{7,6},{8,9},{9,8},{10,11... | collective-permute-start | bytes 393224 | tf_op jit(solution)/shard_map/ppermute | solution.py:337
  53.5 5.6 %collective-permute-start.22 = (bf16[64,1024]{1,0:T(8,128)(2,1)S(1)}, bf16[64,1024]{1,0:T(8,128)(2,1)S(1)}, u32[]{:S(2)}, u32[]{:S(2)}) collective-permute-start(bf16[64,1024]{1,0:T(8,128)(2,1)S(1)} %fusion.1), channel_id=1, source_target_pairs={{0,2},{1,3},{2,0},{3,1},{4,6},{5,7},{6,4},{7,5},{8,10},{9,11},{10,... | collective-permute-start | bytes 393224 | tf_op jit(solution)/shard_map/ppermute | solution.py:337
